TPU v7x, 32 devices: a whole 2x2x4 slice. The times are simulated.
32 devices in a mesh: dp: 16 (over z, y, core), tensor: 2 (over x).
Axes of the slice: x: 2, y: 2, z: 4, core: 2. Of those that a mesh axis runs over, the one named last changes fastest.
Arguments:
- tokens: bfloat16 [16384, 1024], P(('dp', 'tensor')), may hold values from -6 to 6
- cotangent: bfloat16 [16384, 1024], P(('dp', 'tensor')), may hold values from -6 to 6
- lengths: int32 [16], P('dp'), may hold values from 256 to 1024, as said below
- expert_ids: int32 [16384, 8], P(('dp', 'tensor')), may hold values from 0 to 31, all different within a row; in each aligned block of 1024 rows (0 to 1023, 1024 to 2047, ...) at most 288 rows name the same one
- gate_values: bfloat16 [16384, 8], P(('dp', 'tensor')), may hold values from 0.049804688 to 0.29882812
- first_gain: float32 [1024], replicated, may hold values from 0.5 to 1.5
- qkv_weight: bfloat16 [1024, 8, 256], P('dp', 'tensor'), may hold values from -0.1875 to 0.1875
- attn_out_weight: bfloat16 [1024, 1024], P('tensor', 'dp'), may hold values from -0.75 to 0.75
- second_gain: float32 [1024], replicated, may hold values from 0.5 to 1.5
- expert_in_weight: bfloat16 [32, 1024, 1024], P('tensor', 'dp'), may hold values from -0.1875 to 0.1875
- expert_out_weight: bfloat16 [32, 512, 1024], P('tensor', 'dp'), may hold values from -0.25 to 0.25
Outputs:
- output: bfloat16 [16384, 1024], P(('dp', 'tensor'))
- tokens_grad: float32 [16384, 1024], P(('dp', 'tensor'))
- first_gain_grad: float32 [1024], replicated
- qkv_grad: float32 [1024, 8, 256], P('dp', 'tensor')
- attn_out_grad: float32 [1024, 1024], P('tensor', 'dp')
- second_gain_grad: float32 [1024], replicated
- expert_in_grad: float32 [32, 1024, 1024], P('tensor', 'dp')
- expert_out_grad: float32 [32, 512, 1024], P('tensor', 'dp')
Inputs may be any that keep to these rules, and one draw needn't show every extreme that they name: Each slot holds one sequence of lengths[s] tokens from its first position on; the rest of its 1024 positions is padding. `expert_ids`: each row names 8 different experts; within each aligned block of 1024 rows (one slot) no expert is named by more than 288 rows.
All inputs are finite; a program needn't handle non-finite values.
Results may differ from a plain program's by a relative error of at most 0.018.
Values may be sent and summed in bfloat16 or wider, within the bound.
A program may use at most 256 MiB of HBM per device.

v0:
```python
import math

import jax
import jax.numpy as jnp
from jax import lax
from jax.sharding import PartitionSpec as P

D = 1024
HD = 64
FF = 512
G = 2
CAP = 288


EPSILON = 1e-06
THETA = 10000.0
NEGATIVE = -1e30


def rope_tables(total_rows, head_size):
    half_size = head_size // 2
    positions = jnp.arange(total_rows).astype(jnp.float32)
    frequency = THETA ** (-(jnp.arange(half_size).astype(jnp.float32) * 2.0 / head_size))
    angles = positions[:, None] * frequency[None, :]
    return (jnp.cos(angles), jnp.sin(angles))


def table_shape(tensor_in, cosine_table, sine_table):
    half_size = tensor_in.shape[-1] // 2
    shape_out = (tensor_in.shape[0],) + (1,) * (tensor_in.ndim - 2) + (half_size,)
    return (half_size, cosine_table.reshape(shape_out), sine_table.reshape(shape_out))


def rotate(tensor_in, cosine_table, sine_table):
    half_size, cos_part, sin_part = table_shape(tensor_in, cosine_table, sine_table)
    first_half = tensor_in[..., :half_size]
    second_half = tensor_in[..., half_size:]
    return jnp.concatenate(
        [
            first_half * cos_part - second_half * sin_part,
            second_half * cos_part + first_half * sin_part,
        ],
        axis=-1,
    )


def rotate_back(grad_in, cosine_table, sine_table):
    half_size, cos_part, sin_part = table_shape(grad_in, cosine_table, sine_table)
    first_half = grad_in[..., :half_size]
    second_half = grad_in[..., half_size:]
    return jnp.concatenate(
        [
            first_half * cos_part + second_half * sin_part,
            second_half * cos_part - first_half * sin_part,
        ],
        axis=-1,
    )


def dispatch(routes, route_gates, first_expert, expert_count, capacity, total_rows):
    flat_routes = routes.reshape(-1) - first_expert
    inside = (flat_routes >= 0) & (flat_routes < expert_count)
    one_hot = (flat_routes[:, None] == jnp.arange(expert_count, dtype=jnp.int32)[None, :]).astype(
        jnp.int32
    )
    before = jnp.cumsum(one_hot, axis=0, dtype=jnp.int32) - one_hot
    position = jnp.sum(before * one_hot, axis=1, dtype=jnp.int32)
    target = jnp.where(inside, flat_routes * capacity + position, expert_count * capacity).astype(
        jnp.int32
    )
    owner = jnp.arange(flat_routes.shape[0], dtype=jnp.int32) // routes.shape[1]
    slot_token = (
        jnp.full((expert_count * capacity + 1,), total_rows, jnp.int32)
        .at[target]
        .set(owner)[: expert_count * capacity]
    )
    slot_gate = (
        jnp.zeros((expert_count * capacity + 1,), jnp.float32)
        .at[target]
        .set(route_gates.reshape(-1).astype(jnp.float32))[: expert_count * capacity]
    )
    return (slot_token, slot_gate)


def norm_back(normed_grad, source, inverse, gain):
    scaled = normed_grad * gain
    gain_part = jnp.sum(normed_grad * source * inverse, axis=0)
    cubed = inverse * inverse * inverse
    back = inverse * scaled - source * cubed * jnp.mean(scaled * source, axis=-1, keepdims=True)
    return (gain_part, back)


def body(
    tokens,
    cotangent,
    lengths,
    expert_ids,
    gate_values,
    first_gain,
    qkv_weight,
    attn_out_weight,
    second_gain,
    expert_in_weight,
    expert_out_weight,
):
    rows_local = tokens.shape[0]
    tensor_rank = lax.axis_index("tensor")
    slot_rows = rows_local * lax.axis_size("tensor")
    length = lengths[0]
    positions = tensor_rank * rows_local + jnp.arange(rows_local, dtype=jnp.int32)
    valid_rows = (positions < length)[:, None]
    cosine_table, sine_table = rope_tables(slot_rows, HD)
    kv_local = qkv_weight.shape[1]
    heads_width = attn_out_weight.shape[0]
    experts_local = expert_in_weight.shape[0]
    first_expert = tensor_rank * experts_local
    block_rows = min(512, slot_rows)
    block_count = slot_rows // block_rows
    score_scale = 1.0 / math.sqrt(HD)

    def allowed_of(block_start):
        query_pos = block_start + jnp.arange(block_rows, dtype=jnp.int32)
        key_pos = jnp.arange(slot_rows, dtype=jnp.int32)
        return (key_pos[None, :] <= query_pos[:, None]) & (key_pos[None, :] < length)

    def forward(inputs):
        input_rows, gates_in, routes_in, qkv_in, out_in, expert_in, expert_down = inputs
        qkv_full, out_full = (
            lax.all_gather(qkv_in, "dp", axis=0, tiled=True),
            lax.all_gather(out_in, "dp", axis=1, tiled=True),
        )
        in_full, down_full = (
            lax.all_gather(expert_in, "dp", axis=1, tiled=True),
            lax.all_gather(expert_down, "dp", axis=1, tiled=True),
        )
        inputs_f = input_rows.astype(jnp.float32)
        inverse_one = lax.rsqrt(jnp.mean(inputs_f * inputs_f, axis=-1, keepdims=True) + EPSILON)
        normed_one = (inputs_f * inverse_one * first_gain).astype(jnp.bfloat16)
        normed_all = lax.all_gather(normed_one, "tensor", axis=0, tiled=True)
        projected = jnp.einsum(
            "sd,dkc->skc", normed_all, qkv_full, preferred_element_type=jnp.float32
        )
        queries = rotate(
            projected[:, :, : G * HD].reshape(slot_rows, kv_local, G, HD), cosine_table, sine_table
        ).astype(jnp.bfloat16)
        key_heads = rotate(projected[:, :, G * HD : (G + 1) * HD], cosine_table, sine_table).astype(
            jnp.bfloat16
        )
        value_heads = projected[:, :, (G + 1) * HD :].astype(jnp.bfloat16)

        def attend(block_start):
            query_block = lax.dynamic_slice_in_dim(queries, block_start, block_rows, 0)
            scores = (
                jnp.einsum(
                    "qkgd,tkd->kgqt", query_block, key_heads, preferred_element_type=jnp.float32
                )
                * score_scale
            )
            scores = jnp.where(allowed_of(block_start), scores, NEGATIVE)
            largest = jnp.max(scores, axis=-1, keepdims=True)
            expon = jnp.exp(scores - largest)
            totals = jnp.sum(expon, axis=-1, keepdims=True)
            probabilities = (expon / totals).astype(jnp.bfloat16)
            attended = jnp.einsum(
                "kgqt,tkd->qkgd", probabilities, value_heads, preferred_element_type=jnp.float32
            )
            return (attended.astype(jnp.bfloat16), (largest + jnp.log(totals))[..., 0])

        block_starts = jnp.arange(block_count, dtype=jnp.int32) * block_rows
        attended_blocks, lse_all = lax.map(attend, block_starts)
        attn_all = attended_blocks.reshape(slot_rows, heads_width)
        branch = lax.psum_scatter(
            jnp.dot(attn_all, out_full, preferred_element_type=jnp.float32),
            "tensor",
            scatter_dimension=0,
            tiled=True,
        )
        hidden = inputs_f + branch
        inverse_two = lax.rsqrt(jnp.mean(hidden * hidden, axis=-1, keepdims=True) + EPSILON)
        normed_two = (hidden * inverse_two * second_gain).astype(jnp.bfloat16)
        normed_two_all, routes_all, gates_all = (
            lax.all_gather(normed_two, "tensor", axis=0, tiled=True),
            lax.all_gather(routes_in, "tensor", axis=0, tiled=True),
            lax.all_gather(gates_in, "tensor", axis=0, tiled=True),
        )
        slot_token, slot_gate = dispatch(
            routes_all, gates_all, first_expert, experts_local, CAP, slot_rows
        )
        padded = jnp.concatenate([normed_two_all, jnp.zeros((1, D), jnp.bfloat16)], axis=0)
        expert_rows = padded[slot_token].reshape(experts_local, CAP, D)
        gate_up = jnp.einsum(
            "ecd,edf->ecf", expert_rows, in_full, preferred_element_type=jnp.float32
        )
        activated = (jax.nn.silu(gate_up[..., :FF]) * gate_up[..., FF:]).astype(jnp.bfloat16)
        expert_out = jnp.einsum(
            "ecf,efd->ecd", activated, down_full, preferred_element_type=jnp.float32
        )
        weighted = expert_out * slot_gate.reshape(experts_local, CAP, 1)
        combined = (
            jnp.zeros((slot_rows + 1, D), jnp.float32)
            .at[slot_token]
            .add(weighted.reshape(-1, D))[:slot_rows]
        )
        mixture = lax.psum_scatter(
            combined.astype(jnp.bfloat16), "tensor", scatter_dimension=0, tiled=True
        ).astype(jnp.float32)
        output = jnp.where(valid_rows, hidden + mixture, 0.0).astype(jnp.bfloat16)
        saved = (
            qkv_full,
            out_full,
            in_full,
            down_full,
            inputs_f,
            inverse_one,
            normed_all,
            queries,
            key_heads,
            value_heads,
            attn_all,
            lse_all,
            hidden,
            inverse_two,
            slot_token,
            slot_gate,
            expert_rows,
            gate_up,
            activated,
        )
        return (output, saved)

    inputs = (
        tokens,
        gate_values,
        expert_ids,
        qkv_weight,
        attn_out_weight,
        expert_in_weight,
        expert_out_weight,
    )
    output, unused_state = forward(inputs)
    again_inputs, output = lax.optimization_barrier((inputs, output))
    saved = forward(again_inputs)[1]
    (
        qkv_full,
        out_full,
        in_full,
        down_full,
        inputs_f,
        inverse_one,
        normed_all,
        queries,
        key_heads,
        value_heads,
        attn_all,
        lse_all,
        hidden,
        inverse_two,
        slot_token,
        slot_gate,
        expert_rows,
        gate_up,
        activated,
    ) = saved
    dy_masked = jnp.where(valid_rows, cotangent, jnp.zeros_like(cotangent))
    dy_float = dy_masked.astype(jnp.float32)
    dy_all = lax.all_gather(dy_masked, "tensor", axis=0, tiled=True)
    dy_padded = jnp.concatenate([dy_all, jnp.zeros((1, D), jnp.bfloat16)], axis=0)
    out_grad = (
        dy_padded[slot_token].reshape(experts_local, CAP, D).astype(jnp.float32)
        * slot_gate.reshape(experts_local, CAP, 1)
    ).astype(jnp.bfloat16)
    down_part = jnp.einsum("ecf,ecd->efd", activated, out_grad, preferred_element_type=jnp.float32)
    act_grad = jnp.einsum("ecd,efd->ecf", out_grad, down_full, preferred_element_type=jnp.float32)
    gate_part = gate_up[..., :FF]
    up_part = gate_up[..., FF:]
    sigmoid_gate = jax.nn.sigmoid(gate_part)
    gate_grad = act_grad * up_part * sigmoid_gate * (1.0 + gate_part * (1.0 - sigmoid_gate))
    up_grad = act_grad * gate_part * sigmoid_gate
    gate_up_grad = jnp.concatenate([gate_grad, up_grad], axis=-1).astype(jnp.bfloat16)
    in_part = jnp.einsum(
        "ecd,ecf->edf", expert_rows, gate_up_grad, preferred_element_type=jnp.float32
    )
    rows_grad = jnp.einsum(
        "ecf,edf->ecd", gate_up_grad, in_full, preferred_element_type=jnp.float32
    )
    normed_two_part = (
        jnp.zeros((slot_rows + 1, D), jnp.float32)
        .at[slot_token]
        .add(rows_grad.reshape(-1, D))[:slot_rows]
    )
    normed_two_grad = lax.psum_scatter(
        normed_two_part.astype(jnp.bfloat16), "tensor", scatter_dimension=0, tiled=True
    ).astype(jnp.float32)
    second_gain_part, hidden_back = norm_back(normed_two_grad, hidden, inverse_two, second_gain)
    hidden_grad = dy_float + hidden_back
    shard_piece = lax.all_gather(hidden_grad.astype(jnp.bfloat16), "tensor", axis=0, tiled=True)
    out_total = jnp.einsum("sh,sd->hd", attn_all, shard_piece, preferred_element_type=jnp.float32)
    grad_piece = jnp.einsum(
        "sd,hd->sh", shard_piece, out_full, preferred_element_type=jnp.float32
    ).astype(jnp.bfloat16)
    attn_grad_all = grad_piece
    attn_grad_heads = attn_grad_all.reshape(slot_rows, kv_local, G, HD)

    def back_block(carried, block_index):
        keys_total, values_total = carried
        block_start = block_index * block_rows
        query_block = lax.dynamic_slice_in_dim(queries, block_start, block_rows, 0)
        grad_block = lax.dynamic_slice_in_dim(attn_grad_heads, block_start, block_rows, 0)
        lse_block = lse_all[block_index]
        scores = (
            jnp.einsum("qkgd,tkd->kgqt", query_block, key_heads, preferred_element_type=jnp.float32)
            * score_scale
        )
        probabilities = jnp.where(
            allowed_of(block_start), jnp.exp(scores - lse_block[..., None]), 0.0
        )
        prob_grad = jnp.einsum(
            "qkgd,tkd->kgqt", grad_block, value_heads, preferred_element_type=jnp.float32
        )
        center = jnp.sum(probabilities * prob_grad, axis=-1, keepdims=True)
        score_grad = (probabilities * (prob_grad - center)).astype(jnp.bfloat16)
        query_grad = (
            jnp.einsum("kgqt,tkd->qkgd", score_grad, key_heads, preferred_element_type=jnp.float32)
            * score_scale
        )
        keys_total = (
            keys_total
            + jnp.einsum(
                "kgqt,qkgd->tkd", score_grad, query_block, preferred_element_type=jnp.float32
            )
            * score_scale
        )
        values_total = values_total + jnp.einsum(
            "kgqt,qkgd->tkd",
            probabilities.astype(jnp.bfloat16),
            grad_block,
            preferred_element_type=jnp.float32,
        )
        return ((keys_total, values_total), query_grad)

    zero_heads = jnp.zeros((slot_rows, kv_local, HD), jnp.float32)
    (keys_grad, values_grad), query_grads = lax.scan(
        back_block, (zero_heads, zero_heads), jnp.arange(block_count, dtype=jnp.int32)
    )
    query_grad_all = rotate_back(
        query_grads.reshape(slot_rows, kv_local, G, HD), cosine_table, sine_table
    ).reshape(slot_rows, kv_local, G * HD)
    keys_grad_back = rotate_back(keys_grad, cosine_table, sine_table)
    projected_grad = jnp.concatenate([query_grad_all, keys_grad_back, values_grad], axis=-1).astype(
        jnp.bfloat16
    )
    qkv_part = jnp.einsum(
        "sd,skc->dkc", normed_all, projected_grad, preferred_element_type=jnp.float32
    )
    grad_piece = projected_grad
    normed_one_grad = lax.psum_scatter(
        jnp.einsum("skc,dkc->sd", grad_piece, qkv_full, preferred_element_type=jnp.float32).astype(
            jnp.bfloat16
        ),
        "tensor",
        scatter_dimension=0,
        tiled=True,
    ).astype(jnp.float32)
    first_gain_part, input_back = norm_back(normed_one_grad, inputs_f, inverse_one, first_gain)
    tokens_grad = hidden_grad + input_back
    qkv_grad, attn_out_grad, expert_in_grad, expert_out_grad = (
        lax.psum_scatter(
            qkv_part.astype(jnp.bfloat16), "dp", scatter_dimension=0, tiled=True
        ).astype(jnp.float32),
        lax.psum_scatter(
            out_total.astype(jnp.bfloat16), "dp", scatter_dimension=1, tiled=True
        ).astype(jnp.float32),
        lax.psum_scatter(
            in_part.astype(jnp.bfloat16), "dp", scatter_dimension=1, tiled=True
        ).astype(jnp.float32),
        lax.psum_scatter(
            down_part.astype(jnp.bfloat16), "dp", scatter_dimension=1, tiled=True
        ).astype(jnp.float32),
    )
    first_gain_grad, second_gain_grad = lax.psum(
        (first_gain_part, second_gain_part), ("dp", "tensor")
    )
    return (
        output,
        tokens_grad,
        first_gain_grad,
        qkv_grad,
        attn_out_grad,
        second_gain_grad,
        expert_in_grad,
        expert_out_grad,
    )


def solution(mesh):
    placed = (
        P(("dp", "tensor"), None),
        P(("dp", "tensor"), None),
        P("dp"),
        P(("dp", "tensor"), None),
        P(("dp", "tensor"), None),
        P(),
        P("dp", "tensor", None),
        P("tensor", "dp"),
        P(),
        P("tensor", "dp", None),
        P("tensor", "dp", None),
    )
    return jax.shard_map(
        body,
        mesh=mesh,
        in_specs=placed,
        out_specs=(
            P(("dp", "tensor"), None),
            P(("dp", "tensor"), None),
            P(),
            P("dp", "tensor", None),
            P("tensor", "dp"),
            P(),
            P("tensor", "dp", None),
            P("tensor", "dp", None),
        ),
        check_vma=False,
    )
```

profile of v0, /device:TPU:9, one launch (start us, length us, event | category | flops | bytes accessed | tf_op | source)
XLA Modules:
  0.0 2168.4 jit_solution(9184768351693709523)
XLA Ops:
  13.4 32.3 %all-gather.15.cloned.1.call-done = bf16[1024,1024]{1,0:T(8,128)(2,1)} async-done(((bf16[512,1024]{1,0:T(8,128)(2,1)}), bf16[1024,1024]{1,0:T(8,128)(2,1)}) %all-gather.15.cloned.1.call-update) | async-done | bytes 2097168 | tf_op jit(solution)/shard_map/all_gather | solution.py:139
  45.7 43.7 %all-gather.17.cloned.1.call-done = bf16[1024,4,256]{2,0,1:T(8,128)(2,1)} async-done(((bf16[64,4,256]{2,0,1:T(8,128)(2,1)}), bf16[1024,4,256]{2,0,1:T(8,128)(2,1)}) %all-gather.17.cloned.1.call-update) | async-done | bytes 2097168 | tf_op jit(solution)/shard_map/all_gather | solution.py:129
  89.4 4.6 fusion.114
  95.9 46.7 %while.37 = (s32[]{:T(128)}, bf16[2,512,4,2,64]{1,4,3,2,0:T(8,128)(2,1)S(1)}, s32[2]{0:T(128)S(1)}, s32[]{:T(128)}, bf16[1024,4,2,64]{0,3,2,1:T(8,128)(2,1)S(1)}...) while((s32[]{:T(128)}, ...), condition=%wide.region_4.5_spmd, body=%wide.region_1.4_spmd.sunk | while | flops 1100220928 | bytes 36739232 | solution.py:170
  100.4 10.4 fusion.206
  110.8 8.6 fusion.207
  123.7 10.4 fusion.206
  134.1 8.5 fusion.207
  144.0 4.5 fusion.152
  148.6 53.7 %reduce-scatter.10.cloned.1.call-done = f32[512,1024]{1,0:T(8,128)} async-done(((f32[1024,1024]{1,0:T(8,128)}), f32[512,1024]{1,0:T(8,128)}) %reduce-scatter.10.cloned.1.call-update) | async-done | bytes 2097168 | tf_op jit(solution)/shard_map/reduce_scatter | solution.py:172
  211.3 4.8 reduce-window.14
  223.3 30.5 %scatter_custom_fusion = s32[4609]{0:T(1024)S(1)} fusion(s32[8192]{0:T(1024)S(1)} %bitcast.308, s32[8192]{0:T(1024)S(1)} %add_select_fusion, s32[]{:T(128)} %constant.128.clone.1), kind=kCustom, calls=%fused_computation.230 | custom fusion | bytes 18440 | tf_op jit(solution)/shard_map/scatter | solution.py:75
  253.8 30.5 %scatter_custom_fusion.1 = f32[4609]{0:T(1024)S(1)} fusion(s32[8192]{0:T(1024)S(1)} %bitcast.309, f32[8192]{0:T(1024)S(1)} %reshape.495, f32[]{:T(128)} %constant.82.clone.1), kind=kCustom, calls=%fused_computation.226 | custom fusion | bytes 18440 | tf_op jit(solution)/shard_map/scatter | solution.py:80
  286.2 15.0 gather_fusion
  301.2 108.2 %all-gather.23.cloned.1.call-done = bf16[16,1024,1024]{2,1,0:T(8,128)(2,1)} async-done(((bf16[16,64,1024]{2,1,0:T(8,128)(2,1)}), bf16[16,1024,1024]{2,1,0:T(8,128)(2,1)}) %all-gather.23.cloned.1.call-update) | async-done | bytes 33554448 | tf_op jit(solution)/shard_map/all_gather | solution.py:133
  409.4 31.0 %fusion.153 = f32[16,288,1024]{2,1,0:T(8,128)} fusion(bf16[16,288,1024]{2,1,0:T(8,128)(2,1)} %bitcast.289, bf16[16,1024,1024]{2,1,0:T(8,128)(2,1)} %all-gather.23.cloned.1.call-done), kind=kOutput, calls=%fused_computation.251 | convolution fusion | flops 9663676416 | bytes 61865984 | tf_op jit(solution)/shard_map/ecd,edf->ecf/dot_general | solution.py:191
  440.4 96.5 %all-gather.25.cloned.1.call-done = bf16[16,512,1024]{2,1,0:T(8,128)(2,1)} async-done(((bf16[16,32,1024]{2,1,0:T(8,128)(2,1)}), bf16[16,512,1024]{2,1,0:T(8,128)(2,1)}) %all-gather.25.cloned.1.call-update) | async-done | bytes 16777232 | tf_op jit(solution)/shard_map/all_gather | solution.py:134
  536.9 19.2 broadcast_multiply_fusion
  556.0 43.3 %scatter_custom_fusion.2 = f32[1025,1024]{1,0:T(8,128)} fusion(s32[4608]{0:T(1024)S(1)} %compare_select_fusion.3, f32[4608,1024]{1,0:T(8,128)} %bitcast.310, f32[]{:T(128)} %constant.82.clone.1), kind=kCustom, calls=%fused_computation.131 | custom fusion | flops 4718592 | bytes 4198912 | tf_op jit(solution)/shard_map/scatter-add | solution.py:202
  603.9 30.8 %reduce-scatter.12.cloned.1.call-done = bf16[512,1024]{1,0:T(8,128)(2,1)} async-done(((bf16[1024,1024]{1,0:T(8,128)(2,1)}), bf16[512,1024]{1,0:T(8,128)(2,1)}) %reduce-scatter.12.cloned.1.call-update) | async-done | bytes 1048592 | tf_op jit(solution)/shard_map/reduce_scatter | solution.py:204
  641.1 31.7 %all-gather.27.cloned.1.call-done = bf16[1024,1024]{1,0:T(8,128)(2,1)} async-done(((bf16[512,1024]{1,0:T(8,128)(2,1)}), bf16[1024,1024]{1,0:T(8,128)(2,1)}) %all-gather.27.cloned.1.call-update) | async-done | bytes 2097168 | tf_op jit(solution)/shard_map/all_gather | solution.py:139
  672.8 43.5 %all-gather.29.cloned.1.call-done = bf16[1024,4,256]{2,0,1:T(8,128)(2,1)} async-done(((bf16[64,4,256]{2,0,1:T(8,128)(2,1)}), bf16[1024,4,256]{2,0,1:T(8,128)(2,1)}) %all-gather.29.cloned.1.call-update) | async-done | bytes 2097168 | tf_op jit(solution)/shard_map/all_gather | solution.py:129
  716.3 4.6 fusion.112
  722.8 37.3 %while.38 = (s32[]{:T(128)}, bf16[2,512,4,2,64]{1,4,3,2,0:T(8,128)(2,1)S(1)}, f32[2,4,2,512]{3,2,1,0:T(2,128)}, s32[2]{0:T(128)S(1)}, s32[]{:T(128)}, /*index=5*...) while((s32[]{:T(128)}, ...), condition=%wide.region_18.19_spmd, body=%wide.region_15.18_spmd.sunk | while | flops 1125381632 | bytes 54663852 | solution.py:170
  736.0 5.7 fusion.211
  754.4 5.7 fusion.211
  769.6 51.3 %reduce-scatter.14.cloned.1.call-done = f32[512,1024]{1,0:T(8,128)} async-done(((f32[1024,1024]{1,0:T(8,128)}), f32[512,1024]{1,0:T(8,128)}) %reduce-scatter.14.cloned.1.call-update) | async-done | bytes 2097168 | tf_op jit(solution)/shard_map/reduce_scatter | solution.py:172
  825.7 29.9 %all-gather.33.cloned.1.call-done = bf16[1024,1024]{1,0:T(8,128)(2,1)} async-done(((bf16[512,1024]{1,0:T(8,128)(2,1)}), bf16[1024,1024]{1,0:T(8,128)(2,1)}) %all-gather.33.cloned.1.call-update) | async-done | bytes 2097168 | tf_op jit(solution)/shard_map/all_gather | solution.py:266
  865.1 9.9 reduce-window.16
  887.4 30.7 %scatter_custom_fusion.3 = s32[4609]{0:T(1024)S(1)} fusion(s32[8192]{0:T(1024)S(1)} %bitcast.306, s32[8192]{0:T(1024)} %copy-done.41, s32[]{:T(128)} %constant.128.clone.1), kind=kCustom, calls=%fused_computation.228 | custom fusion | bytes 18948 | tf_op jit(solution)/shard_map/scatter | solution.py:75
  918.0 30.5 %scatter_custom_fusion.4 = f32[4609]{0:T(1024)S(1)} fusion(s32[8192]{0:T(1024)S(1)} %bitcast.307, f32[8192]{0:T(1024)S(1)} %reshape.519, f32[]{:T(128)} %constant.82.clone.1), kind=kCustom, calls=%fused_computation.224 | custom fusion | bytes 18440 | tf_op jit(solution)/shard_map/scatter | solution.py:80
  948.6 15.1 gather_fusion.1
  965.6 15.0 gather_fusion.2
  980.5 80.5 %all-gather.39.cloned.1.call-done = bf16[16,1024,1024]{2,1,0:T(8,128)(2,1)} async-done(((bf16[16,64,1024]{2,1,0:T(8,128)(2,1)}), bf16[16,1024,1024]{2,1,0:T(8,128)(2,1)}) %all-gather.39.cloned.1.call-update) | async-done | bytes 33554448 | tf_op jit(solution)/shard_map/all_gather | solution.py:133
  1061.0 31.1 %fusion.155 = f32[16,288,1024]{2,1,0:T(8,128)} fusion(bf16[16,288,1024]{2,1,0:T(8,128)(2,1)} %bitcast.285, bf16[16,1024,1024]{2,1,0:T(8,128)(2,1)} %all-gather.39.cloned.1.call-done), kind=kOutput, calls=%fused_computation.253 | convolution fusion | flops 9663676416 | bytes 61865984 | tf_op jit(solution)/shard_map/ecd,edf->ecf/dot_general | solution.py:191
  1092.1 96.3 %all-gather.35.cloned.1.call-done = bf16[16,512,1024]{2,1,0:T(8,128)(2,1)} async-done(((bf16[16,32,1024]{2,1,0:T(8,128)(2,1)}), bf16[16,512,1024]{2,1,0:T(8,128)(2,1)}) %all-gather.35.cloned.1.call-update) | async-done | bytes 16777232 | tf_op jit(solution)/shard_map/all_gather | solution.py:134
  1188.4 24.5 %multiply_convert_fusion.2 = (bf16[16,288,512]{2,1,0:T(8,128)(2,1)}, bf16[16,288,512]{2,1,0:T(8,128)(2,1)}) fusion(f32[16,288,1024]{2,1,0:T(8,128)} %fusion.155, bf16[16,512,1024]{2,1,0:T(8,128)(2,1)} %all-gather.35.cloned.1.call-done, bf16[16,288,1024]{2,1,0:T(8,128)(2,1)} %bitcast.287, f32[16,288]{1,0:T(8,128)S(1)} %mul.727), kind=kOutput, calls=%fused_computation.104 | convolution fusion | flops 4876664832 | bytes 54544384 | tf_op jit(solution)/shard_map/ecd,efd->ecf/dot_general | solution.py:273
  1212.9 23.2 %fusion.82 = f32[16,288,1024]{2,1,0:T(8,128)} fusion(bf16[16,1024,1024]{2,1,0:T(8,128)(2,1)} %all-gather.39.cloned.1.call-done, bf16[16,288,512]{2,1,0:T(8,128)(2,1)} %get-tuple-element.298, bf16[16,288,512]{2,1,0:T(8,128)(2,1)} %get-tuple-element.297), kind=kOutput, calls=%fused_computation.108 | convolution fusion | flops 9682550784 | bytes 61865984 | tf_op jit(solution)/shard_map/ecf,edf->ecd/dot_general | solution.py:283
  1236.1 43.2 %scatter_custom_fusion.5 = f32[1025,1024]{1,0:T(8,128)} fusion(s32[4608]{0:T(1024)S(1)} %compare_select_fusion.2, f32[4608,1024]{1,0:T(8,128)} %bitcast.311, f32[]{:T(128)} %constant.82.clone.1), kind=kCustom, calls=%fused_computation.129 | custom fusion | flops 4718592 | bytes 4198912 | tf_op jit(solution)/shard_map/scatter-add | solution.py:289
  1283.2 31.5 %reduce-scatter.16.cloned.1.call-done = bf16[512,1024]{1,0:T(8,128)(2,1)} async-done(((bf16[1024,1024]{1,0:T(8,128)(2,1)}), bf16[512,1024]{1,0:T(8,128)(2,1)}) %reduce-scatter.16.cloned.1.call-update) | async-done | bytes 1048592 | tf_op jit(solution)/shard_map/reduce_scatter | solution.py:291
  1319.5 33.2 %all-gather.41.cloned.1.call-done = bf16[1024,1024]{1,0:T(8,128)(2,1)} async-done(((bf16[512,1024]{1,0:T(8,128)(2,1)}), bf16[1024,1024]{1,0:T(8,128)(2,1)}) %all-gather.41.cloned.1.call-update) | async-done | bytes 2097168 | tf_op jit(solution)/shard_map/all_gather | solution.py:296
  1360.7 165.5 %while.39 = (s32[]{:T(128)}, f32[1024,4,64]{0,2,1:T(8,128)}, f32[1024,4,64]{0,2,1:T(8,128)}, f32[2,512,4,2,64]{1,0,4,3,2:T(2,128)}, s32[2]{0:T(128)S(1)}, /*inde...) while((s32[]{:T(128)}, f32[1024,4,64]{0,2,1:T(8,128)}, ...), condition=%wide.region_31.32_spmd.clone, body=%wide.region_29.31_spmd.clone.sunk | while | flops 2724722176 | bytes 202987984 | solution.py:342
  1362.3 9.5 fusion.220
  1376.1 15.5 fusion.222
  1392.7 9.4 fusion.223
  1402.1 6.1 fusion.226
  1409.4 19.6 dynamic_update_slice.26
  1429.0 6.0 fusion.224
  1435.0 7.7 fusion.225
  1444.9 9.3 fusion.220
  1458.5 15.4 fusion.222
  1475.1 9.4 fusion.223
  1484.5 6.1 fusion.226
  1491.6 19.6 dynamic_update_slice.26
  1511.2 6.3 fusion.224
  1517.5 7.7 fusion.225
  1537.1 6.5 fusion.116
  1543.7 5.6 bitcast_convert_fusion
  1549.4 20.8 convolution_convert_fusion.1
  1570.3 28.2 %convolution_convert_fusion = bf16[16,1024,1024]{2,1,0:T(8,128)(2,1)} fusion(bf16[16,288,1024]{2,1,0:T(8,128)(2,1)} %bitcast.286, bf16[16,288,512]{2,1,0:T(8,128)(2,1)} %get-tuple-element.298, bf16[16,288,512]{2,1,0:T(8,128)(2,1)} %get-tuple-element.297), kind=kOutput, calls=%fused_computation.95 | convolution fusion | flops 9699328000 | bytes 52428800 | tf_op jit(solution)/shard_map/ecd,ecf->edf/dot_general | solution.py:280
  1605.0 34.1 %reduce-scatter.18.cloned.1.call-done = bf16[512,1024]{1,0:T(8,128)(2,1)} async-done(((bf16[1024,1024]{1,0:T(8,128)(2,1)}), bf16[512,1024]{1,0:T(8,128)(2,1)}) %reduce-scatter.18.cloned.1.call-update) | async-done | bytes 1048592 | tf_op jit(solution)/shard_map/reduce_scatter | solution.py:356
  1641.2 38.9 %all-reduce.3 = (f32[1024]{0:T(1024)}, f32[1024]{0:T(1024)}) all-reduce(f32[1024]{0:T(1024)S(1)} %get-tuple-element.231, f32[1024]{0:T(1024)S(1)} %copy-done.50), channel_id=1, replica_groups=mesh['dp'=16,'tensor'=2] {'dp','tensor'}, use_global_device_ids=true, to_apply=%region_35.36 | all-reduce | flops 2048 | bytes 16384 | tf_op jit(solution)/shard_map/psum | solution.py:380
  1684.5 136.3 %reduce-scatter.26.cloned.1.call-done = bf16[16,32,1024]{2,1,0:T(8,128)(2,1)} async-done(((bf16[16,512,1024]{2,1,0:T(8,128)(2,1)}), bf16[16,32,1024]{2,1,0:T(8,128)(2,1)}) %reduce-scatter.26.cloned.1.call-update) | async-done | bytes 1048592 | tf_op jit(solution)/shard_map/reduce_scatter | solution.py:376
  1823.5 334.0 %reduce-scatter.24.cloned.1.call-done = bf16[16,64,1024]{2,1,0:T(8,128)(2,1)} async-done(((bf16[16,1024,1024]{2,1,0:T(8,128)(2,1)}), bf16[16,64,1024]{2,1,0:T(8,128)(2,1)}) %reduce-scatter.24.cloned.1.call-update) | async-done | bytes 2097168 | tf_op jit(solution)/shard_map/reduce_scatter | solution.py:373
  (338 shorter events, 162.8 us)
Async XLA Ops:
  7.2 38.6 %all-gather.15.cloned.1.call-start = ((), (), s32[]{:S(2)}) async-start(), calls=%async_computation.9 | async-start | bytes 3145728 | tf_op jit(solution)/shard_map/all_gather | solution.py:139
  11.3 78.1 %all-gather.17.cloned.1.call-start = ((), (), s32[]{:S(2)}) async-start(), calls=%async_computation.10 | async-start | bytes 2228224 | tf_op jit(solution)/shard_map/all_gather | solution.py:129
  12.1 131.9 %all-gather.19.cloned.1.call-start = ((), (), s32[]{:S(2)}) async-start(), calls=%async_computation.11 | async-start | bytes 1114112 | tf_op jit(solution)/shard_map/all_gather | solution.py:130
  12.8 189.5 %reduce-scatter.10.cloned.1.call-start = ((), (), s32[]{:S(2)}) async-start(), calls=%async_computation.12 | async-start | bytes 6291456 | tf_op jit(solution)/shard_map/reduce_scatter | solution.py:172
  13.4 81.1 %copy-start.19 = (f32[1024,32]{0,1:T(8,128)}, f32[1024,32]{0,1:T(8,128)S(1)}, u32[]{:S(2)}) copy-start(f32[1024,32]{0,1:T(8,128)S(1)} %get-tuple-element.311) | copy-start | bytes 393220
  13.4 81.1 %copy-start.22 = (f32[1024,32]{0,1:T(8,128)}, f32[1024,32]{0,1:T(8,128)S(1)}, u32[]{:S(2)}) copy-start(f32[1024,32]{0,1:T(8,128)S(1)} %get-tuple-element.312) | copy-start | bytes 393220
  148.5 53.8 %copy-start = (bf16[512,1024]{1,0:T(8,128)(2,1)S(1)}, bf16[512,1024]{1,0:T(8,128)(2,1)}, u32[]{:S(2)}) copy-start(bf16[512,1024]{1,0:T(8,128)(2,1)} %param.17) | copy-start | bytes 3145732
  148.5 55.9 %copy-start.30 = (f32[1024]{0:T(1024)S(1)}, f32[1024]{0:T(1024)}, u32[]{:S(2)}) copy-start(f32[1024]{0:T(1024)} %param.25) | copy-start | bytes 12292
  148.6 135.9 %all-gather.21.cloned.1.call-start = ((), (), s32[]{:S(2)}) async-start(), calls=%async_computation.13 | async-start | bytes 3145728 | tf_op jit(solution)/shard_map/all_gather | solution.py:182
  205.9 203.4 %all-gather.23.cloned.1.call-start = ((), (), s32[]{:S(2)}) async-start(), calls=%async_computation.14 | async-start | bytes 35651584 | tf_op jit(solution)/shard_map/all_gather | solution.py:133
  206.5 330.4 %all-gather.25.cloned.1.call-start = ((), (), s32[]{:S(2)}) async-start(), calls=%async_computation.15 | async-start | bytes 17825792 | tf_op jit(solution)/shard_map/all_gather | solution.py:134
  207.3 427.5 %reduce-scatter.12.cloned.1.call-start = ((), (), s32[]{:S(2)}) async-start(), calls=%async_computation.16 | async-start | bytes 3145728 | tf_op jit(solution)/shard_map/reduce_scatter | solution.py:204
  222.6 61.8 %copy-start.41 = (s32[8192]{0:T(1024)}, s32[8192]{0:T(1024)S(1)}, u32[]{:S(2)}) copy-start(s32[8192]{0:T(1024)S(1)} %add_select_fusion) | copy-start | bytes 98308
  556.0 78.7 %copy-start.15 = (f32[512,1024]{1,0:T(8,128)S(1)}, f32[512,1024]{1,0:T(8,128)}, u32[]{:S(2)}) copy-start(f32[512,1024]{1,0:T(8,128)} %reduce-scatter.10.cloned.1.call-done) | copy-start | bytes 6291460
  603.1 35.1 %copy-start.33 = (f32[1024]{0:T(1024)S(1)}, f32[1024]{0:T(1024)}, u32[]{:S(2)}) copy-start(f32[1024]{0:T(1024)} %param.22) | copy-start | bytes 12292
  603.2 69.6 %all-gather.27.cloned.1.call-start = ((), (), s32[]{:S(2)}) async-start(), calls=%async_computation.17 | async-start | bytes 3145728 | tf_op jit(solution)/shard_map/all_gather | solution.py:139
  603.9 33.4 %copy-start.51 = (pred[512]{0:T(512)(128)(4,1)}, pred[512]{0:T(512)(128)(4,1)S(1)}, u32[]{:S(2)}) copy-start(pred[512]{0:T(512)(128)(4,1)S(1)} %add_compare_fusion) | copy-start | bytes 1540
  603.9 35.7 %copy-start.29 = (bf16[64,4,256]{2,1,0:T(4,128)(2,1)S(1)}, bf16[64,4,256]{2,1,0:T(4,128)(2,1)}, u32[]{:S(2)}) copy-start(bf16[64,4,256]{2,1,0:T(4,128)(2,1)} %param.23) | copy-start | bytes 393220
  638.2 82.7 %copy-start.42 = (f32[512]{0:T(512)}, f32[512]{0:T(512)S(1)}, u32[]{:S(2)}) copy-start(f32[512]{0:T(512)S(1)} %get-tuple-element.314) | copy-start | bytes 6148
  639.5 76.8 %all-gather.29.cloned.1.call-start = ((), (), s32[]{:S(2)}) async-start(), calls=%async_computation.18 | async-start | bytes 2228224 | tf_op jit(solution)/shard_map/all_gather | solution.py:129
  640.3 121.3 %all-gather.31.cloned.1.call-start = ((), (), s32[]{:S(2)}) async-start(), calls=%async_computation.19 | async-start | bytes 1114112 | tf_op jit(solution)/shard_map/all_gather | solution.py:130
  641.0 79.9 %copy-start.20 = (f32[1024,32]{0,1:T(8,128)S(1)}, f32[1024,32]{0,1:T(8,128)}, u32[]{:S(2)}) copy-start(f32[1024,32]{0,1:T(8,128)} %copy-done.19) | copy-start | bytes 393220
  641.0 79.9 %copy-start.23 = (f32[1024,32]{0,1:T(8,128)S(1)}, f32[1024,32]{0,1:T(8,128)}, u32[]{:S(2)}) copy-start(f32[1024,32]{0,1:T(8,128)} %copy-done.22) | copy-start | bytes 393220
  641.0 179.9 %reduce-scatter.14.cloned.1.call-start = ((), (), s32[]{:S(2)}) async-start(), calls=%async_computation.20 | async-start | bytes 6291456 | tf_op jit(solution)/shard_map/reduce_scatter | solution.py:172
  767.1 53.8 %copy-start.1 = (bf16[512,1024]{1,0:T(8,128)(2,1)S(1)}, bf16[512,1024]{1,0:T(8,128)(2,1)}, u32[]{:S(2)}) copy-start(bf16[512,1024]{1,0:T(8,128)(2,1)} %param.17) | copy-start | bytes 3145732
  767.1 55.9 %copy-start.31 = (f32[1024]{0:T(1024)S(1)}, f32[1024]{0:T(1024)}, u32[]{:S(2)}) copy-start(f32[1024]{0:T(1024)} %param.25) | copy-start | bytes 12292
  767.1 88.5 %all-gather.33.cloned.1.call-start = ((), (), s32[]{:S(2)}) async-start(), calls=%async_computation.21 | async-start | bytes 3145728 | tf_op jit(solution)/shard_map/all_gather | solution.py:266
  769.6 194.2 %all-gather.37.cloned.1.call-start = ((), (), s32[]{:S(2)}) async-start(), calls=%async_computation.23 | async-start | bytes 3145728 | tf_op jit(solution)/shard_map/all_gather | solution.py:182
  823.0 494.5 %copy-start.37 = (f32[512]{0:T(512)}, f32[512]{0:T(512)S(1)}, u32[]{:S(2)}) copy-start(f32[512]{0:T(512)S(1)} %get-tuple-element.316) | copy-start | bytes 6148
  823.0 494.5 %copy-start.46 = (f32[512]{0:T(512)}, f32[512]{0:T(512)S(1)}, u32[]{:S(2)}) copy-start(f32[512]{0:T(512)S(1)} %get-tuple-element.315) | copy-start | bytes 6148
  824.5 33.0 %copy-start.36 = (s32[512,8]{0,1:T(8,128)S(1)}, s32[512,8]{0,1:T(8,128)}, u32[]{:S(2)}) copy-start(s32[512,8]{0,1:T(8,128)} %param.20) | copy-start | bytes 49156
  824.5 236.6 %all-gather.39.cloned.1.call-start = ((), (), s32[]{:S(2)}) async-start(), calls=%async_computation.24 | async-start | bytes 35651584 | tf_op jit(solution)/shard_map/all_gather | solution.py:133
  825.1 363.3 %all-gather.35.cloned.1.call-start = ((), (), s32[]{:S(2)}) async-start(), calls=%async_computation.22 | async-start | bytes 17825792 | tf_op jit(solution)/shard_map/all_gather | solution.py:134
  825.7 54.0 %copy-start.40 = (bf16[512,8]{0,1:T(8,128)(2,1)S(1)}, bf16[512,8]{0,1:T(8,128)(2,1)}, u32[]{:S(2)}) copy-start(bf16[512,8]{0,1:T(8,128)(2,1)} %param.21) | copy-start | bytes 24580
  825.7 489.1 %reduce-scatter.16.cloned.1.call-start = ((), (), s32[]{:S(2)}) async-start(), calls=%async_computation.25 | async-start | bytes 3145728 | tf_op jit(solution)/shard_map/reduce_scatter | solution.py:291
  948.6 239.8 %copy-start.44 = (f32[16,288]{1,0:T(8,128)}, f32[16,288]{1,0:T(8,128)S(1)}, u32[]{:S(2)}) copy-start(f32[16,288]{1,0:T(8,128)S(1)} %mul.727) | copy-start | bytes 55300
  1236.1 78.6 %copy-start.6 = (f32[512,1024]{1,0:T(8,128)S(1)}, f32[512,1024]{1,0:T(8,128)}, u32[]{:S(2)}) copy-start(f32[512,1024]{1,0:T(8,128)} %reduce-scatter.14.cloned.1.call-done) | copy-start | bytes 6291460
  1283.1 69.6 %all-gather.41.cloned.1.call-start = ((), (), s32[]{:S(2)}) async-start(), calls=%async_computation.26 | async-start | bytes 3145728 | tf_op jit(solution)/shard_map/all_gather | solution.py:296
  1317.5 39.5 %copy-start.48 = (f32[512]{0:T(512)}, f32[512]{0:T(512)S(1)}, u32[]{:S(2)}) copy-start(f32[512]{0:T(512)S(1)} %broadcast_multiply_fusion.4) | copy-start | bytes 6148
  1319.4 279.2 %reduce-scatter.22.cloned.1.call-start = ((), (), s32[]{:S(2)}) async-start(), calls=%async_computation.29 | async-start | bytes 1114112 | tf_op jit(solution)/shard_map/reduce_scatter | solution.py:370
  1357.1 246.2 %reduce-scatter.20.cloned.1.call-start = ((), (), s32[]{:S(2)}) async-start(), calls=%async_computation.28 | async-start | bytes 2228224 | tf_op jit(solution)/shard_map/reduce_scatter | solution.py:367
  1376.0 15.5 slice-start
  1376.0 15.5 slice-start.1
  1376.0 15.5 slice-start.2
  1376.0 16.7 slice-start.3
  1408.3 20.7 copy-start.9
  1458.4 15.5 slice-start
  1458.5 15.5 slice-start.1
  1458.5 16.6 slice-start.3
  1490.5 20.7 copy-start.9
  1543.6 95.4 %reduce-scatter.18.cloned.1.call-start = ((), (), s32[]{:S(2)}) async-start(), calls=%async_computation.27 | async-start | bytes 3145728 | tf_op jit(solution)/shard_map/reduce_scatter | solution.py:356
  1549.4 271.4 %reduce-scatter.26.cloned.1.call-start = ((), (), s32[]{:S(2)}) async-start(), calls=%async_computation.31 | async-start | bytes 17825792 | tf_op jit(solution)/shard_map/reduce_scatter | solution.py:376
  1570.2 587.3 %reduce-scatter.24.cloned.1.call-start = ((), (), s32[]{:S(2)}) async-start(), calls=%async_computation.30 | async-start | bytes 35651584 | tf_op jit(solution)/shard_map/reduce_scatter | solution.py:373
  1598.5 40.6 %copy-start.2 = (bf16[512,1024]{1,0:T(8,128)(2,1)S(1)}, bf16[512,1024]{1,0:T(8,128)(2,1)}, u32[]{:S(2)}) copy-start(bf16[512,1024]{1,0:T(8,128)(2,1)} %param.17) | copy-start | bytes 3145732
  1598.5 40.6 %copy-start.34 = (f32[1024]{0:T(1024)S(1)}, f32[1024]{0:T(1024)}, u32[]{:S(2)}) copy-start(f32[1024]{0:T(1024)} %param.22) | copy-start | bytes 12292
  1598.5 40.6 %copy-start.43 = (f32[512]{0:T(512)S(1)}, f32[512]{0:T(512)}, u32[]{:S(2)}) copy-start(f32[512]{0:T(512)} %copy-done.42) | copy-start | bytes 6148
  1598.5 42.7 %copy-start.50 = (f32[1024]{0:T(1024)S(1)}, f32[1024]{0:T(1024)}, u32[]{:S(2)}) copy-start(f32[1024]{0:T(1024)} %get-tuple-element.229) | copy-start | bytes 12292
  1598.5 81.6 %copy-start.7 = (f32[512,1024]{1,0:T(8,128)S(1)}, f32[512,1024]{1,0:T(8,128)}, u32[]{:S(2)}) copy-start(f32[512,1024]{1,0:T(8,128)} %reduce-scatter.14.cloned.1.call-done) | copy-start | bytes 6291460
  1598.5 81.6 %copy-start.32 = (f32[1024]{0:T(1024)S(1)}, f32[1024]{0:T(1024)}, u32[]{:S(2)}) copy-start(f32[1024]{0:T(1024)} %param.25) | copy-start | bytes 12292
  1598.5 81.6 %copy-start.38 = (f32[512]{0:T(512)S(1)}, f32[512]{0:T(512)}, u32[]{:S(2)}) copy-start(f32[512]{0:T(512)} %copy-done.37) | copy-start | bytes 6148
  1598.5 81.6 %copy-start.47 = (f32[512]{0:T(512)S(1)}, f32[512]{0:T(512)}, u32[]{:S(2)}) copy-start(f32[512]{0:T(512)} %copy-done.46) | copy-start | bytes 6148
  1598.5 81.6 %copy-start.49 = (f32[512]{0:T(512)S(1)}, f32[512]{0:T(512)}, u32[]{:S(2)}) copy-start(f32[512]{0:T(512)} %copy-done.48) | copy-start | bytes 6148
  1598.5 81.6 %copy-start.53 = (pred[512]{0:T(512)(128)(4,1)S(1)}, pred[512]{0:T(512)(128)(4,1)}, u32[]{:S(2)}) copy-start(pred[512]{0:T(512)(128)(4,1)} %copy-done.51) | copy-start | bytes 1540
  1598.5 81.6 %copy-start.54 = (f32[512]{0:T(512)S(1)}, f32[512]{0:T(512)}, u32[]{:S(2)}) copy-start(f32[512]{0:T(512)} %get-tuple-element.313) | copy-start | bytes 6148
  (26 other events, 122.7 us)
Sparse Core Ops, SparseCore 0:
  11.4 34.2 all-gather.14
  48.5 40.8 all-gather.16
  91.6 36.7 all-gather.18
  148.7 53.6 reduce-scatter.9
  206.0 33.2 all-gather.20
  240.8 168.5 all-gather.22
  411.8 125.0 all-gather.24
  603.3 31.4 reduce-scatter.11
  639.6 33.1 all-gather.26
  675.4 40.8 all-gather.28
  718.5 36.7 all-gather.30
  767.2 53.6 reduce-scatter.13
  822.5 33.0 all-gather.32
  857.7 33.2 all-gather.36
  892.5 168.4 all-gather.38
  1063.3 125.0 all-gather.34
  1283.3 31.4 reduce-scatter.15
  1319.6 33.1 all-gather.40
  1357.2 55.4 reduce-scatter.21
  1543.8 59.4 reduce-scatter.19
  1606.1 32.9 reduce-scatter.17
  1643.7 176.9 reduce-scatter.25
  1825.6 331.9 reduce-scatter.23
where the time goes:
time: 2180 us; the launch traced here: 2170 us
  waiting for transfers between devices  1270 us (58%)
  matrix products  362 us (17%)
  local copies, waits for them, and re-layouts  264 us (12%)
  other arithmetic  184 us (8%)
  blocking collectives  53.4 us (2%)
    reduce_scatter x1, waiting for transfers between devices, body(): lax.psum_scatter(in_part.astype(jnp.bfloat16), 'dp', scatter_dimension=1,...  334 us
    all_gather x2, waiting for transfers between devices, forward(): lax.all_gather(expert_down, 'dp', axis=1, tiled=True)  193 us
    all_gather x2, waiting for transfers between devices, forward(): lax.all_gather(expert_in, 'dp', axis=1, tiled=True)  189 us
    reduce_scatter x1, waiting for transfers between devices, body(): lax.psum_scatter(down_part.astype(jnp.bfloat16), 'dp', scatter_dimension=...  136 us
    reduce_scatter x2, waiting for transfers between devices, forward(): lax.psum_scatter(jnp.dot(attn_all, out_full, preferred_element_type=jnp.f...  105 us
    all_gather x2, waiting for transfers between devices, forward(): lax.all_gather(qkv_in, 'dp', axis=0, tiled=True)  87.2 us
    all_gather x2, waiting for transfers between devices, forward(): normed_all = lax.all_gather(normed_one, 'tensor', axis=0, tiled=True)  64 us
    dot_general x2, matrix products, forward(): jnp.einsum('ecd,edf->ecf', expert_rows, in_full, preferred_element_type=j...  62.1 us
  transfers between devices with their start and end apart: 23, of which 18 were waited for; matrix products, arithmetic and copies ran while one was open for 28% of the time, Pallas kernels for 0%

commit v1 on v0

v1 whole, which is shorter than its diff:
```python
import functools
import math

import jax
import jax.numpy as jnp
from jax import lax
from jax.experimental import pallas as pl
from jax.experimental.pallas import tpu as pltpu
from jax.sharding import PartitionSpec as P

D = 1024
HD = 64
FF = 512
G = 2
CAP = 288
GROUP = 4
LANES = 128

EPSILON = 1e-06
THETA = 10000.0
NEGATIVE = -1e30
BF = jnp.bfloat16
F32 = jnp.float32
VMEM_LIMIT = 60 * 1024 * 1024

ANY = pl.BlockSpec(memory_space=pl.ANY)
SMEM = pl.BlockSpec(memory_space=pltpu.SMEM)
VM = pl.BlockSpec(memory_space=pltpu.VMEM)


def mm(a, b):
    return lax.dot_general(a, b, (((1,), (0,)), ((), ())), preferred_element_type=F32)


def mm_nt(a, b):
    return lax.dot_general(a, b, (((1,), (1,)), ((), ())), preferred_element_type=F32)


def mm_tn(a, b):
    return lax.dot_general(a, b, (((0,), (0,)), ((), ())), preferred_element_type=F32)


def call(kernel, name, out_shape, in_specs, out_specs, args, scratch=(), flops=0, moved=0, **more):
    return pl.pallas_call(
        kernel,
        name=name,
        out_shape=out_shape,
        in_specs=in_specs,
        out_specs=out_specs,
        scratch_shapes=list(scratch),
        compiler_params=pltpu.CompilerParams(vmem_limit_bytes=VMEM_LIMIT),
        cost_estimate=pl.CostEstimate(flops=flops, bytes_accessed=moved, transcendentals=0),
        **more,
    )(*args)


def rope_tables(total_rows):
    half = HD // 2
    positions = jnp.arange(total_rows).astype(F32)
    frequency = THETA ** (-(jnp.arange(half).astype(F32) * 2.0 / HD))
    angles = positions[:, None] * frequency[None, :]
    cosine, sine = jnp.cos(angles), jnp.sin(angles)
    return (
        jnp.concatenate([cosine] * 4, axis=1),
        jnp.concatenate([-sine, sine, -sine, sine], axis=1),
    )


def swap_halves(v):
    lane = lax.broadcasted_iota(jnp.int32, v.shape, 1)
    return jnp.where(lane % HD < HD // 2, pltpu.roll(v, LANES - HD // 2, 1), pltpu.roll(v, HD // 2, 1))


def qkv_kernel(n_ref, w_ref, cos_ref, sin_ref, out_ref):
    projected = mm(n_ref[...], w_ref[...])
    cosine, sine = cos_ref[...], sin_ref[...]
    key_lanes = lax.broadcasted_iota(jnp.int32, cosine.shape, 1) < HD
    for g in range(projected.shape[1] // (2 * LANES)):
        q = projected[:, g * 2 * LANES : g * 2 * LANES + LANES]
        kv = projected[:, g * 2 * LANES + LANES : (g + 1) * 2 * LANES]
        q = q * cosine + swap_halves(q) * sine
        kv = jnp.where(key_lanes, kv * cosine + swap_halves(kv) * sine, kv)
        out_ref[:, g * 2 * LANES : g * 2 * LANES + LANES] = q.astype(BF)
        out_ref[:, g * 2 * LANES + LANES : (g + 1) * 2 * LANES] = kv.astype(BF)


def qkv_project(normed, weight, cosine, sine):
    rows, width = normed.shape[0], weight.shape[1]
    block = 256
    return pl.pallas_call(
        qkv_kernel,
        name="qkv_rope",
        grid=(rows // block,),
        out_shape=jax.ShapeDtypeStruct((rows, width), BF),
        in_specs=[
            pl.BlockSpec((block, D), lambda b: (b, 0)),
            pl.BlockSpec((D, width), lambda b: (0, 0)),
            pl.BlockSpec((block, LANES), lambda b: (b, 0)),
            pl.BlockSpec((block, LANES), lambda b: (b, 0)),
        ],
        out_specs=pl.BlockSpec((block, width), lambda b: (b, 0)),
        compiler_params=pltpu.CompilerParams(vmem_limit_bytes=VMEM_LIMIT),
        cost_estimate=pl.CostEstimate(flops=2 * rows * D * width, bytes_accessed=6 << 20, transcendentals=0),
    )(normed, weight, cosine, sine)


def head_pair(v):
    first = lax.broadcasted_iota(jnp.int32, v.shape, 1) < HD
    zero = jnp.zeros_like(v)
    return jnp.concatenate([jnp.where(first, v, zero), jnp.where(first, zero, v)], axis=0)


def head_join(v):
    n = v.shape[0] // 2
    first = lax.broadcasted_iota(jnp.int32, (n, LANES), 1) < HD
    return jnp.where(first, v[:n], v[n:])


def doubled(kv):
    first = lax.broadcasted_iota(jnp.int32, kv.shape, 1) < HD
    other = pltpu.roll(kv.astype(F32), HD, 1).astype(BF)
    return jnp.where(first, kv, other), jnp.where(first, other, kv)


def allowed(n_keys, q_block, q_start, length):
    key = lax.broadcasted_iota(jnp.int32, (n_keys, 2 * q_block), 0)
    lane = lax.broadcasted_iota(jnp.int32, (n_keys, 2 * q_block), 1)
    query = q_start + jnp.where(lane < q_block, lane, lane - q_block)
    return (key <= query) & (key < length)


def attend_kernel(q_block, idx_ref, qkv_ref, *out_refs):
    outs, lse_ref = out_refs[:-1], out_refs[-1]
    rows = qkv_ref.shape[0]
    length = idx_ref[3]
    keys, values = doubled(qkv_ref[:, LANES:])
    for b in range(rows // q_block):
        start, n_keys = b * q_block, (b + 1) * q_block
        q = head_pair(qkv_ref[start : start + q_block, :LANES])
        scores = mm_nt(keys[:n_keys], q) * (1.0 / math.sqrt(HD))
        scores = jnp.where(allowed(n_keys, q_block, start, length), scores, NEGATIVE)
        largest = jnp.max(scores, axis=0, keepdims=True)
        expon = jnp.exp(scores - largest)
        totals = jnp.sum(expon, axis=0, keepdims=True)
        probs = (expon * (1.0 / totals)).astype(BF)
        mixed = head_join(mm_tn(probs, values[:n_keys])).astype(BF)
        lse_ref[0, b : b + 1, :] = largest + jnp.log(totals)
        if len(outs) == 1:
            outs[0][start : start + q_block] = mixed
        else:
            own_rows = rows // 2
            half, at = start // own_rows, start % own_rows
            mine = idx_ref[2] == half

            @pl.when(mine)
            def _():
                outs[0][at : at + q_block] = mixed

            @pl.when(jnp.logical_not(mine))
            def _():
                outs[1][at : at + q_block] = mixed


def attend(idx, qkv, parts, q_block):
    rows, groups = qkv.shape[0], qkv.shape[1] // (2 * LANES)
    out = jax.ShapeDtypeStruct((rows // parts, groups * LANES), BF)
    return pl.pallas_call(
        functools.partial(attend_kernel, q_block),
        name="attend",
        grid=(groups,),
        out_shape=[out] * parts + [jax.ShapeDtypeStruct((groups, rows // q_block, 2 * q_block), F32)],
        in_specs=[SMEM, pl.BlockSpec((rows, 2 * LANES), lambda g: (0, g))],
        out_specs=[pl.BlockSpec((rows // parts, LANES), lambda g: (0, g))] * parts
        + [pl.BlockSpec((1, rows // q_block, 2 * q_block), lambda g: (g, 0, 0))],
        compiler_params=pltpu.CompilerParams(vmem_limit_bytes=VMEM_LIMIT),
        cost_estimate=pl.CostEstimate(flops=14 << 30, bytes_accessed=4 << 20, transcendentals=0),
    )(idx, qkv)


def attend_back_kernel(q_block, n_grads, idx_ref, qkv_ref, lse_ref, cos_ref, sin_ref, *refs):
    grads, outs = refs[:n_grads], refs[n_grads : 2 * n_grads]
    do_ref, dq_ref, dk_ref, dv_ref = refs[2 * n_grads :]
    rows = qkv_ref.shape[0]
    own_rows = rows // n_grads
    length = idx_ref[3]
    for p in range(n_grads):
        at = pl.multiple_of((p ^ idx_ref[2] if n_grads == 2 else 0) * own_rows, own_rows)
        do_ref[pl.ds(at, own_rows), :] = grads[p][...]
    keys, values = doubled(qkv_ref[:, LANES:])
    dk_ref[...] = jnp.zeros_like(dk_ref)
    dv_ref[...] = jnp.zeros_like(dv_ref)
    scale = 1.0 / math.sqrt(HD)
    for b in range(rows // q_block):
        start, n_keys = b * q_block, (b + 1) * q_block
        q = head_pair(qkv_ref[start : start + q_block, :LANES])
        grad = head_pair(do_ref[start : start + q_block, :])
        scores = mm_nt(keys[:n_keys], q) * scale
        probs = jnp.where(
            allowed(n_keys, q_block, start, length), jnp.exp(scores - lse_ref[0, b : b + 1, :]), 0.0
        )
        prob_grad = mm_nt(values[:n_keys], grad)
        center = jnp.sum(probs * prob_grad, axis=0, keepdims=True)
        score_grad = (probs * (prob_grad - center)).astype(BF)
        dq_ref[start : start + q_block, :] = head_join(mm_tn(score_grad, keys[:n_keys])) * scale
        dk_ref[:n_keys, :] += mm(score_grad, q)
        dv_ref[:n_keys, :] += mm(probs.astype(BF), grad)
    cosine, sine = cos_ref[...], sin_ref[...]
    dq = dq_ref[...]
    dq = (dq * cosine - swap_halves(dq) * sine).astype(BF)
    dk, dv = dk_ref[...] * scale, dv_ref[...]
    dk = dk + pltpu.roll(dk, HD, 1)
    dv = dv + pltpu.roll(dv, HD, 1)
    dk = dk * cosine - swap_halves(dk) * sine
    first = lax.broadcasted_iota(jnp.int32, dk.shape, 1) < HD
    dkv = jnp.where(first, dk, dv).astype(BF)
    if n_grads == 1:
        outs[0][:, :LANES] = dq
        outs[0][:, LANES:] = dkv
    else:
        do_ref[...] = dq
        for p in range(2):
            at = pl.multiple_of((p ^ idx_ref[2]) * own_rows, own_rows)
            outs[p][:, :LANES] = do_ref[pl.ds(at, own_rows), :]
        do_ref[...] = dkv
        for p in range(2):
            at = pl.multiple_of((p ^ idx_ref[2]) * own_rows, own_rows)
            outs[p][:, LANES:] = do_ref[pl.ds(at, own_rows), :]


def attend_back(idx, qkv, lse, cosine, sine, grads, q_block):
    rows, groups, parts = qkv.shape[0], qkv.shape[1] // (2 * LANES), len(grads)
    return pl.pallas_call(
        functools.partial(attend_back_kernel, q_block, parts),
        name="attend_back",
        grid=(groups,),
        out_shape=[jax.ShapeDtypeStruct((rows // parts, groups * 2 * LANES), BF)] * parts,
        in_specs=[
            SMEM,
            pl.BlockSpec((rows, 2 * LANES), lambda g: (0, g)),
            pl.BlockSpec((1, rows // q_block, 2 * q_block), lambda g: (g, 0, 0)),
            pl.BlockSpec((rows, LANES), lambda g: (0, 0)),
            pl.BlockSpec((rows, LANES), lambda g: (0, 0)),
        ]
        + [pl.BlockSpec((rows // parts, LANES), lambda g: (0, g))] * parts,
        out_specs=[pl.BlockSpec((rows // parts, 2 * LANES), lambda g: (0, g))] * parts,
        scratch_shapes=[pltpu.VMEM((rows, LANES), BF)] + [pltpu.VMEM((rows, LANES), F32)] * 3,
        compiler_params=pltpu.CompilerParams(vmem_limit_bytes=VMEM_LIMIT),
        cost_estimate=pl.CostEstimate(flops=30 << 30, bytes_accessed=6 << 20, transcendentals=0),
    )(idx, qkv, lse, cosine, sine, *grads)


def project_out_kernel(n_parts, pieces, x_ref, gain_ref, *refs):
    attns, weights = refs[:n_parts], refs[n_parts : 2 * n_parts]
    hidden_ref, normed_refs = refs[2 * n_parts], refs[2 * n_parts + 1 :]
    rows = x_ref.shape[0] // pieces
    for p in range(pieces):
        at = slice(p * rows, (p + 1) * rows)
        hidden = x_ref[at].astype(F32)
        for a, w in zip(attns, weights, strict=True):
            hidden = hidden + mm_nt(a[at], w[...])
        inverse = lax.rsqrt(jnp.mean(hidden * hidden, axis=-1, keepdims=True) + EPSILON)
        hidden_ref[at] = hidden
        normed_refs[p][...] = (hidden * inverse * gain_ref[...]).astype(BF)


def project_out(x, gain, attns, weights, pieces):
    rows = x.shape[0]
    n = len(attns)
    return call(
        functools.partial(project_out_kernel, n, pieces),
        "project_out",
        [jax.ShapeDtypeStruct((rows, D), F32)] + [jax.ShapeDtypeStruct((rows // pieces, D), BF)] * pieces,
        [VM] * (2 + 2 * n),
        [VM] * (1 + pieces),
        (x, gain.reshape(1, D), *attns, *weights),
        flops=2 * rows * D * D,
        moved=7 << 20,
    )


def hidden_back_kernel(n_parts, pieces, n_sums, valid_ref, hidden_ref, cot_ref, gain_ref, *refs):
    sums, refs = refs[: pieces * n_sums], refs[pieces * n_sums :]
    weights, refs = refs[:n_parts], refs[n_parts:]
    grad_ref, low_ref, gain_grad_ref, attn_refs = refs[0], refs[1], refs[2], refs[3:]
    rows = hidden_ref.shape[0] // pieces
    gain = gain_ref[...]
    gain_grad = jnp.zeros((1, D), F32)
    for p in range(pieces):
        at = slice(p * rows, (p + 1) * rows)
        hidden = hidden_ref[at]
        normed_grad = sums[p * n_sums][...].astype(F32)
        for s in sums[p * n_sums + 1 : (p + 1) * n_sums]:
            normed_grad = normed_grad + s[...].astype(F32)
        inverse = lax.rsqrt(jnp.mean(hidden * hidden, axis=-1, keepdims=True) + EPSILON)
        gain_grad = gain_grad + jnp.sum(normed_grad * (hidden * inverse), axis=0, keepdims=True)
        scaled = normed_grad * gain
        back = inverse * scaled - hidden * (
            inverse * inverse * inverse * jnp.mean(scaled * hidden, axis=-1, keepdims=True)
        )
        dy = jnp.where(valid_ref[at] > 0, cot_ref[at].astype(F32), 0.0)
        total = dy + back
        grad_ref[at] = total
        low = total.astype(BF)
        low_ref[at] = low
        for a, w in zip(attn_refs, weights, strict=True):
            a[at] = mm(low, w[...]).astype(BF)
    gain_grad_ref[...] = gain_grad


def hidden_back(valid, hidden, cotangent, gain, sums, weights):
    rows, pieces, n_sums, n = hidden.shape[0], len(sums), len(sums[0]), len(weights)
    heads = weights[0].shape[1]
    return call(
        functools.partial(hidden_back_kernel, n, pieces, n_sums),
        "hidden_back",
        [
            jax.ShapeDtypeStruct((rows, D), F32),
            jax.ShapeDtypeStruct((rows, D), BF),
            jax.ShapeDtypeStruct((1, D), F32),
        ]
        + [jax.ShapeDtypeStruct((rows, heads), BF)] * n,
        [VM] * (4 + pieces * n_sums + n),
        [VM] * (3 + n),
        (valid, hidden, cotangent, gain.reshape(1, D), *[s for piece in sums for s in piece], *weights),
        flops=2 * rows * D * D,
        moved=10 << 20,
    )


def dispatch_kernel(n_pieces, scaled, pos_ref, gate_ref, *refs):
    pieces, out_ref, rows_ref, sems = refs[:n_pieces], refs[n_pieces], refs[n_pieces + 1], refs[n_pieces + 2]
    height = rows_ref.shape[0] // n_pieces
    copies = [
        pltpu.make_async_copy(piece, rows_ref.at[pl.ds(p * height, height)], sems.at[p])
        for p, piece in enumerate(pieces)
    ]
    for c in copies:
        c.start()
    rank = lax.broadcasted_iota(jnp.int32, (CAP, rows_ref.shape[0]), 0)
    for c in copies:
        c.wait()
    for j in range(out_ref.shape[0]):
        chosen = rank == pos_ref[j : j + 1, :]
        value = gate_ref[j : j + 1, :] if scaled else 1.0
        one_hot = jnp.where(chosen, value, 0.0).astype(BF)
        out_ref[j] = mm(one_hot, rows_ref[...]).astype(BF)


def dispatch(pos, gate, pieces, scaled):
    experts, rows = pos.shape
    return call(
        functools.partial(dispatch_kernel, len(pieces), scaled),
        "dispatch_scaled" if scaled else "dispatch",
        jax.ShapeDtypeStruct((experts, CAP, D), BF),
        [VM, VM] + [ANY] * len(pieces),
        VM,
        (pos, gate, *pieces),
        scratch=[pltpu.VMEM((rows, D), BF), pltpu.SemaphoreType.DMA((len(pieces),))],
        flops=2 * experts * CAP * rows * D,
        moved=5 << 20,
    )


def combine_kernel(n_experts, slot, scaled, n_adds, n_outs, pos_ref, gate_ref, *refs):
    sources, refs = refs[:n_experts], refs[n_experts:]
    adds, outs, (held, sems) = refs[:n_adds], refs[n_adds : n_adds + n_outs], refs[n_adds + n_outs :]
    copies = [
        pltpu.make_async_copy(source.at[slot], held.at[pl.ds(j * CAP, CAP)], sems.at[j])
        for j, source in enumerate(sources)
    ]
    for c in copies:
        c.start()
    for c in copies:
        c.wait()
    width = n_experts * CAP
    rows = pos_ref.shape[0]
    block = 256
    per_out = rows // n_outs
    for b in range(rows // block):
        at = slice(b * block, (b + 1) * block)
        tiles = []
        for first in range(0, width, LANES):
            size = min(LANES, width - first)
            lane = first + lax.broadcasted_iota(jnp.int32, (block, size), 1)
            tile = jnp.zeros((block, size), F32)
            for j in range(first // CAP, (first + size - 1) // CAP + 1):
                target = pos_ref[at, j : j + 1]
                target = jnp.where(target >= 0, target + j * CAP, -1)
                tile = jnp.where(lane == target, gate_ref[at, j : j + 1] if scaled else 1.0, tile)
            tiles.append(tile.astype(BF))
        total = mm(jnp.concatenate(tiles, axis=1), held[...])
        out, inner = outs[b * block // per_out], slice(b * block % per_out, b * block % per_out + block)
        if n_adds:
            total = total + adds[0][at].astype(F32)
        out[inner] = total.astype(BF)


def combine(pos, gate, sources, slot, scaled, add, n_outs):
    rows, n_experts = pos.shape
    adds = [] if add is None else [add]
    return call(
        functools.partial(combine_kernel, n_experts, slot, scaled, len(adds), n_outs),
        "combine_scaled" if scaled else "combine",
        [jax.ShapeDtypeStruct((rows // n_outs, D), BF)] * n_outs,
        [VM, VM] + [ANY] * n_experts + [VM] * len(adds),
        [VM] * n_outs,
        (pos, gate, *sources, *adds),
        scratch=[pltpu.VMEM((n_experts * CAP, D), BF), pltpu.SemaphoreType.DMA((n_experts,))],
        flops=2 * n_experts * CAP * rows * D,
        moved=5 << 20,
    )


def expert_kernel(j, outer, in_rows, down_rows, idx_ref, *refs):
    n_hops = outer - 1
    xs, refs = refs[:GROUP], refs[GROUP:]
    gs, refs = refs[:GROUP], refs[GROUP:]
    own, refs = refs[0], refs[1:]
    lefts, refs = refs[:n_hops], refs[n_hops:]
    rights, refs = refs[:n_hops], refs[n_hops:]
    y_ref, dx_ref, dw_ref = refs[:3]
    x_all, g_all, w_in, w_down, act_all, gug_all, sem_x, sem_g, sem_w, sem_d = refs[3:]
    o, i = idx_ref[0], idx_ref[1]

    def rows_of(sources, held, sems):
        return [
            pltpu.make_async_copy(s.at[j], held.at[pl.ds(n * CAP, CAP)], sems.at[n])
            for n, s in enumerate(sources)
        ]

    def weight_copies(source, at, slot):
        made = []
        for m in range(GROUP):
            place = at * GROUP + (i ^ m)
            made.append(
                pltpu.make_async_copy(
                    source.at[m, pl.ds(0, in_rows)],
                    w_in.at[pl.ds(pl.multiple_of(place * in_rows, in_rows), in_rows)],
                    sem_w.at[slot * GROUP + m],
                )
            )
            made.append(
                pltpu.make_async_copy(
                    source.at[m, pl.ds(in_rows, down_rows)],
                    w_down.at[pl.ds(pl.multiple_of(place * down_rows, down_rows), down_rows)],
                    sem_d.at[slot * GROUP + m],
                )
            )
        return made

    def each_weight(act):
        act(weight_copies(own, o, 0))
        for k in range(1, outer):

            @pl.when(o >= k)
            def _():
                act(weight_copies(lefts[k - 1], o - k, k))

            @pl.when(o + k < outer)
            def _():
                act(weight_copies(rights[k - 1], o + k, n_hops + k))

    def start(made):
        for c in made:
            c.start()

    def wait(made):
        for c in made:
            c.wait()

    each_weight(start)
    copy_x, copy_g = rows_of(xs, x_all, sem_x), rows_of(gs, g_all, sem_g)
    start(copy_x)
    start(copy_g)
    each_weight(wait)
    wait(copy_x)
    wait(copy_g)

    def per_slot(s, carry):
        at = pl.ds(pl.multiple_of(s * CAP, CAP), CAP)
        gate_up = mm(x_all[at, :], w_in[...])
        g, u = gate_up[:, :FF], gate_up[:, FF:]
        sigma = 1.0 / (1.0 + jnp.exp(-g))
        silu = g * sigma
        act = (silu * u).astype(BF)
        act_all[at, :] = act
        y_ref[s] = mm(act, w_down[...]).astype(BF)
        act_grad = mm_nt(g_all[at, :], w_down[...])
        gug_all[at, :FF] = (act_grad * u * sigma * (1.0 + g * (1.0 - sigma))).astype(BF)
        gug_all[at, FF:] = (act_grad * silu).astype(BF)
        dx_ref[s] = mm_nt(gug_all[at, :], w_in[...]).astype(BF)
        return carry

    lax.fori_loop(0, GROUP, per_slot, 0)
    for c in range(outer):
        part = mm_tn(x_all[:, c * GROUP * in_rows : (c + 1) * GROUP * in_rows], gug_all[...]).astype(BF)
        for r in range(GROUP):
            dw_ref[c, i ^ r, :in_rows, :] = part[r * in_rows : (r + 1) * in_rows]
        part = mm_tn(act_all[:, c * GROUP * down_rows : (c + 1) * GROUP * down_rows], g_all[...]).astype(BF)
        for r in range(GROUP):
            dw_ref[c, i ^ r, in_rows:, :] = part[r * down_rows : (r + 1) * down_rows]


def expert(idx, j, outer, in_rows, down_rows, xs, gs, own, lefts, rights):
    n_hops = outer - 1
    total = GROUP * CAP
    packed = in_rows + down_rows
    return call(
        functools.partial(expert_kernel, j, outer, in_rows, down_rows),
        "expert",
        [
            jax.ShapeDtypeStruct((GROUP, CAP, D), BF),
            jax.ShapeDtypeStruct((GROUP, CAP, D), BF),
            jax.ShapeDtypeStruct((outer, GROUP, packed, D), BF),
        ],
        [SMEM] + [ANY] * (2 * GROUP + 1 + 2 * n_hops),
        [VM] * 3,
        (idx, *xs, *gs, own, *lefts, *rights),
        scratch=[
            pltpu.VMEM((total, D), BF),
            pltpu.VMEM((total, D), BF),
            pltpu.VMEM((D, 2 * FF), BF),
            pltpu.VMEM((FF, D), BF),
            pltpu.VMEM((total, FF), BF),
            pltpu.VMEM((total, 2 * FF), BF),
            pltpu.SemaphoreType.DMA((GROUP,)),
            pltpu.SemaphoreType.DMA((GROUP,)),
            pltpu.SemaphoreType.DMA(((1 + 2 * n_hops) * GROUP,)),
            pltpu.SemaphoreType.DMA(((1 + 2 * n_hops) * GROUP,)),
        ],
        flops=18 * total * D * FF,
        moved=15 << 20,
    )


def pack_kernel(n_experts, in_rows, down_rows, idx_ref, in_ref, down_ref, *refs):
    outs, sems = refs[:-1], refs[-1]
    i = idx_ref[1]
    copies = []
    for j in range(n_experts):
        for m in range(GROUP):
            n = j * GROUP + m
            source = (i ^ m) * n_experts + j
            copies.append(pltpu.make_async_copy(in_ref.at[source], outs[n].at[pl.ds(0, in_rows)], sems.at[2 * n]))
            copies.append(
                pltpu.make_async_copy(down_ref.at[source], outs[n].at[pl.ds(in_rows, down_rows)], sems.at[2 * n + 1])
            )
    for c in copies:
        c.start()
    for c in copies:
        c.wait()


def pack_weights(idx, expert_in, expert_down):
    experts, in_rows, _ = expert_in.shape
    down_rows = expert_down.shape[1]
    n = experts // GROUP
    flat = call(
        functools.partial(pack_kernel, n, in_rows, down_rows),
        "pack_weights",
        [jax.ShapeDtypeStruct((in_rows + down_rows, D), BF)] * experts,
        [SMEM, ANY, ANY],
        [VM] * experts,
        (idx, expert_in, expert_down),
        scratch=[pltpu.SemaphoreType.DMA((2 * experts,))],
        moved=6 << 20,
    )
    return [[flat[j * GROUP + m] for m in range(GROUP)] for j in range(n)]


def body(
    tokens,
    cotangent,
    lengths,
    expert_ids,
    gate_values,
    first_gain,
    qkv_weight,
    attn_out_weight,
    second_gain,
    expert_in_weight,
    expert_out_weight,
):
    rows = tokens.shape[0]
    n_tensor, n_dp = lax.axis_size("tensor"), lax.axis_size("dp")
    outer = n_dp // GROUP
    slot_rows = rows * n_tensor
    d, t = lax.axis_index("dp"), lax.axis_index("tensor")
    o, i = d // GROUP, d % GROUP
    length = lengths[0]
    idx = jnp.stack([o, i, t, length]).astype(jnp.int32)
    width = qkv_weight.shape[1] * qkv_weight.shape[2]
    experts_local, in_rows, _ = expert_in_weight.shape
    down_rows = expert_out_weight.shape[1]
    own_experts = experts_local // GROUP
    pair = n_tensor == 2
    q_block = 256
    half = rows // 2

    def across(v, m):
        return lax.ppermute(v, "dp", [(a, a ^ m) for a in range(n_dp)])

    def beside(v):
        return lax.ppermute(v, "tensor", [(0, 1), (1, 0)])

    def chain(v):
        up = [(a, a + GROUP) for a in range(n_dp - GROUP)]
        down = [(b, a) for a, b in up]
        lefts, rights = [], []
        a = b = v
        for _ in range(outer - 1):
            a, b = lax.ppermute(a, "dp", up), lax.ppermute(b, "dp", down)
            lefts.append(a)
            rights.append(b)
        return lefts, rights

    def gather_group(pieces):
        if pair:
            a, b = pieces
            ax, by, ay, bx = beside(a), across(b, 2), across(a, 2), beside(b)
            axy, bxy = across(ax, 2), beside(by)
            slots = [[a, ax, b, bx], [ay, axy, by, bxy]]
        else:
            slot = lax.all_gather(pieces[0], "tensor", axis=0, tiled=True)
            slots = [[slot], [across(slot, 2)]]
        return slots + [[across(p, 1) for p in s] for s in slots]

    qkv_full = lax.all_gather(qkv_weight.reshape(qkv_weight.shape[0], width), "dp", axis=0, tiled=True)
    out_full = lax.all_gather(attn_out_weight.T, "dp", axis=0, tiled=True)
    blocks = pack_weights(idx, expert_in_weight, expert_out_weight)
    moved_weights = []
    for per_expert in blocks:
        own = jnp.stack([per_expert[0]] + [across(per_expert[m], m) for m in range(1, GROUP)])
        moved_weights.append((own, *chain(own)))
    if pair:
        out_parts = [out_full, beside(out_full)]
    else:
        gathered = lax.all_gather(out_full, "tensor", axis=0)
        out_parts = [gathered[k] for k in range(n_tensor)]

    x = tokens.astype(F32)
    inverse_one = lax.rsqrt(jnp.mean(x * x, axis=-1, keepdims=True) + EPSILON)
    normed_one = (x * inverse_one * first_gain).astype(BF)
    if pair:
        other = beside(normed_one)
        normed_all = jnp.where(
            t == 0,
            jnp.concatenate([normed_one, other], axis=0),
            jnp.concatenate([other, normed_one], axis=0),
        )
    else:
        normed_all = lax.all_gather(normed_one, "tensor", axis=0, tiled=True)
    cosine, sine = rope_tables(slot_rows)
    qkv = qkv_project(normed_all, qkv_full, cosine, sine)
    *attended, lse = attend(idx, qkv, 2 if pair else 1, q_block)
    if pair:
        attn_parts = [attended[0], beside(attended[1])]
    else:
        heads = attended[0].shape[1]
        exchanged = lax.all_to_all(attended[0].reshape(n_tensor, rows, heads), "tensor", 0, 0)
        attn_parts = [exchanged[k] for k in range(n_tensor)]
    hidden, *normed_two = project_out(tokens, second_gain, attn_parts, out_parts, 2 if pair else 1)

    positions = t * rows + jnp.arange(rows, dtype=jnp.int32)
    valid_rows = positions < length
    n_experts = experts_local * n_tensor
    chosen = expert_ids.T[None] == jnp.arange(n_experts, dtype=jnp.int32)[:, None, None]
    gates = jnp.sum(jnp.where(chosen, gate_values.T[None].astype(F32), 0.0), axis=1)
    gates = jnp.where(valid_rows[None, :], gates, 0.0).astype(BF)
    if pair:
        gates_x = beside(gates)
        slot_gates = jnp.concatenate(
            [gates[:, :half], gates_x[:, :half], gates[:, half:], gates_x[:, half:]], axis=1
        )
    else:
        slot_gates = lax.all_gather(gates, "tensor", axis=1, tiled=True)
    gates_y = across(slot_gates, 2)
    all_gates = jnp.stack([slot_gates, gates_y, across(slot_gates, 1), across(gates_y, 1)])
    own_gates = lax.dynamic_slice_in_dim(
        all_gates, t * experts_local + i * own_experts, own_experts, axis=1
    ).astype(F32)
    named = own_gates > 0
    before = (
        lax.broadcasted_iota(jnp.int32, (slot_rows, slot_rows), 0)
        < lax.broadcasted_iota(jnp.int32, (slot_rows, slot_rows), 1)
    ).astype(BF)
    ranks = jnp.dot(
        named.astype(BF).reshape(GROUP * own_experts, slot_rows), before, preferred_element_type=F32
    ).reshape(GROUP, own_experts, slot_rows)
    pos = jnp.where(named, ranks, -1.0).astype(jnp.int32)
    pos_columns, gate_columns = jnp.swapaxes(pos, 1, 2), jnp.swapaxes(own_gates, 1, 2)

    dy = jnp.where(valid_rows[:, None], cotangent, jnp.zeros_like(cotangent))
    dy_slots = gather_group([dy[:half], dy[half:]] if pair else [dy])
    out_grads = [dispatch(pos[s], own_gates[s], dy_slots[s], True) for s in range(GROUP)]
    normed_slots = gather_group(normed_two)
    expert_rows = [dispatch(pos[s], own_gates[s], normed_slots[s], False) for s in range(GROUP)]

    expert_outs, row_grads, weight_grads = [], [], []
    for j in range(own_experts):
        own, lefts, rights = moved_weights[j]
        y, dx, dw = expert(
            idx, j, outer, in_rows, down_rows, expert_rows, out_grads, own, lefts, rights
        )
        expert_outs.append(y)
        row_grads.append(dx)
        weight_grads.append(dw)

    def sum_group(sources, scaled):
        def part(s, add, n_outs):
            return combine(pos_columns[s], gate_columns[s], sources, s, scaled, add, n_outs)

        far = [part(2, None, 1)[0], part(3, None, 1)[0]]
        near = [across(v, 1) for v in far]
        if pair:
            ay, axy, by, bxy = part(1, near[1], 4)
            a, ax, b, bx = part(0, near[0], 4)

            def add(p, q):
                return (p.astype(F32) + q.astype(F32)).astype(BF)

            a, ax = add(a, across(ay, 2)), add(ax, across(axy, 2))
            b, by = add(b, beside(bx)), add(by, beside(bxy))
            return [[a, beside(ax)], [b, across(by, 2)]]
        (y,) = part(1, near[1], 1)
        (v,) = part(0, near[0], 1)
        v = (v.astype(F32) + across(y, 2).astype(F32)).astype(BF)
        return [[lax.psum_scatter(v, "tensor", scatter_dimension=0, tiled=True)]]

    valid_column = valid_rows.astype(F32)[:, None]
    normed_two_grad = sum_group(row_grads, False)
    hidden_grad, branch_grad, second_gain_part, *attn_grads = hidden_back(
        valid_column, hidden, cotangent, second_gain, normed_two_grad, out_parts
    )
    if pair:
        attn_grads = [attn_grads[0], beside(attn_grads[1])]
    else:
        attn_grads = [
            lax.all_to_all(jnp.stack(attn_grads), "tensor", 0, 0).reshape(slot_rows, attn_grads[0].shape[1])
        ]
    projected_grads = attend_back(idx, qkv, lse, cosine, sine, attn_grads, q_block)

    def first_norm_part(v):
        return lax.dot_general(v, qkv_full, (((1,), (1,)), ((), ())), preferred_element_type=F32).astype(BF)

    if pair:
        theirs = beside(first_norm_part(projected_grads[1]))
        normed_one_grad = first_norm_part(projected_grads[0]).astype(F32) + theirs.astype(F32)
        qkv_part = mm_tn(normed_one, projected_grads[0]) + mm_tn(other, projected_grads[1])
    else:
        normed_one_grad = lax.psum_scatter(
            first_norm_part(projected_grads[0]), "tensor", scatter_dimension=0, tiled=True
        ).astype(F32)
        qkv_part = mm_tn(normed_all, projected_grads[0])
    first_gain_part = jnp.sum(normed_one_grad * (x * inverse_one), axis=0)
    scaled = normed_one_grad * first_gain
    tokens_grad = (
        hidden_grad
        + inverse_one * scaled
        - x * (inverse_one * inverse_one * inverse_one * jnp.mean(scaled * x, axis=-1, keepdims=True))
    )

    mixture = sum_group(expert_outs, True)
    mixture = jnp.concatenate([sum(v.astype(F32) for v in terms) for terms in mixture], axis=0)
    output = jnp.where(valid_rows[:, None], hidden + mixture, 0.0).astype(BF)

    outer_groups = [[a * GROUP + b for a in range(outer)] for b in range(GROUP)]
    received = [[] for _ in range(GROUP)]
    for dw in weight_grads:
        mine = lax.psum_scatter(dw, "dp", scatter_dimension=0, tiled=True, axis_index_groups=outer_groups)
        for m in range(GROUP):
            block = mine[0, m]
            received[m].append(block if m == 0 else across(block, m))
    by_distance = jnp.stack([jnp.stack(v) for v in received])
    by_source = jnp.take(by_distance, jnp.arange(GROUP) ^ i, axis=0).reshape(
        experts_local, in_rows + down_rows, D
    )
    expert_in_grad = by_source[:, :in_rows].astype(F32)
    expert_out_grad = by_source[:, in_rows:].astype(F32)

    attn_out_parts = [mm_tn(branch_grad, part).astype(BF) for part in attn_parts]
    if pair:
        attn_out_part = (attn_out_parts[0].astype(F32) + beside(attn_out_parts[1]).astype(F32)).astype(BF)
    else:
        attn_out_part = lax.psum_scatter(jnp.stack(attn_out_parts), "tensor", scatter_dimension=0, tiled=True)[0]
    qkv_grad = lax.psum_scatter(qkv_part.astype(BF), "dp", scatter_dimension=0, tiled=True).astype(F32)
    attn_out_grad = lax.psum_scatter(attn_out_part, "dp", scatter_dimension=0, tiled=True).astype(F32).T

    gains = jnp.stack([first_gain_part, second_gain_part[0]])
    if pair:
        gains = gains + beside(gains)
    else:
        gains = lax.psum(gains, "tensor")
    step = 1
    while step < n_dp:
        gains = gains + across(gains, step)
        step *= 2
    return (
        output,
        tokens_grad,
        gains[0],
        qkv_grad.reshape(qkv_weight.shape),
        attn_out_grad,
        gains[1],
        expert_in_grad,
        expert_out_grad,
    )


def solution(mesh):
    placed = (
        P(("dp", "tensor"), None),
        P(("dp", "tensor"), None),
        P("dp"),
        P(("dp", "tensor"), None),
        P(("dp", "tensor"), None),
        P(),
        P("dp", "tensor", None),
        P("tensor", "dp"),
        P(),
        P("tensor", "dp", None),
        P("tensor", "dp", None),
    )
    return jax.shard_map(
        body,
        mesh=mesh,
        in_specs=placed,
        out_specs=(
            P(("dp", "tensor"), None),
            P(("dp", "tensor"), None),
            P(),
            P("dp", "tensor", None),
            P("tensor", "dp"),
            P(),
            P("tensor", "dp", None),
            P("tensor", "dp", None),
        ),
        check_vma=False,
    )
```

time: 2180 us -> 980 us (0.45)
  waiting for transfers between devices: 1270 us -> 436 us
  matrix products: 362 us -> 18.5 us
  Pallas kernels: 0 us -> 255 us
  local copies, waits for them, and re-layouts: 264 us -> 43.7 us
  starting transfers between devices: 0.94 us -> 151 us
  other arithmetic: 184 us -> 44.6 us
  blocking collectives: 53.4 us -> 0 us
    reduce_scatter x9 -> x6, waiting for transfers between devices: 675 us -> 31.9 us  [the longest x1 26.7 us: body(): lax.psum_scatter(qkv_part.astype(BF), 'dp', scatter_dimension=0, tiled=True)]
    all_gather x14 -> x2, waiting for transfers between devices: 596 us -> 1.42 us  [the longest x1 1.42 us: body(): out_full = lax.all_gather(attn_out_weight.T, 'dp', axis=0, tiled=True)]
    ppermute x0 -> x107, waiting for transfers between devices: none -> 403 us  [the longest x24 250 us: chain(): a, b = (lax.ppermute(a, 'dp', up), lax.ppermute(b, 'dp', down))]
    dot_general x31 -> x7, matrix products: 341 us -> 18.5 us  [the longest x2 9.35 us: first_norm_part(): lax.dot_general(v, qkv_full, (((1,), (1,)), ((), ())), preferred_element_...]
    pallas_call x0 -> x26, Pallas kernels: none -> 255 us  [the longest x23 204 us: call(): pl.pallas_call(kernel, name=name, out_shape=out_shape, in_specs=in_specs,...]
    ppermute x0 -> x107, starting transfers between devices: none -> 150 us  [the longest x24 67.3 us: chain(): a, b = (lax.ppermute(a, 'dp', up), lax.ppermute(b, 'dp', down))]
    scatter x4 -> x0, local copies, waits for them, and re-layouts: 122 us -> none  [the longest x2 61.1 us: dispatch(): slot_token = jnp.full((expert_count * capacity + 1,), total_rows, jnp.int...]
    scatter-add x2 -> x0, other arithmetic: 86.4 us -> none  [the longest x1 43.3 us: forward(): combined = jnp.zeros((slot_rows + 1, D), jnp.float32).at[slot_token].add(...]
  transfers between devices with their start and end apart: 23 -> 115, of which waited for: 18 -> 41; matrix products, arithmetic and copies ran while one was open for 28% -> 10% of each run, Pallas kernels for 0% -> 24%
where the time goes in v1:
time: 980 us; the launch traced here: 965 us
  waiting for transfers between devices  436 us (44%)
  Pallas kernels  255 us (26%)
  starting transfers between devices  151 us (15%)
  other arithmetic  44.6 us (5%)
  local copies, waits for them, and re-layouts  43.7 us (4%)
  matrix products  18.5 us (2%)
  between operations  16.7 us (2%)
    ppermute x24, waiting for transfers between devices, chain(): a, b = (lax.ppermute(a, 'dp', up), lax.ppermute(b, 'dp', down))  250 us
    pallas_call x23, Pallas kernels, call(): pl.pallas_call(kernel, name=name, out_shape=out_shape, in_specs=in_specs,...  204 us
    ppermute x63, waiting for transfers between devices, across(): return lax.ppermute(v, 'dp', [(a, a ^ m) for a in range(n_dp)])  95.3 us
    ppermute x24, starting transfers between devices, chain(): a, b = (lax.ppermute(a, 'dp', up), lax.ppermute(b, 'dp', down))  67.3 us
    ppermute x63, starting transfers between devices, across(): return lax.ppermute(v, 'dp', [(a, a ^ m) for a in range(n_dp)])  65.6 us
    ppermute x20, waiting for transfers between devices, beside(): return lax.ppermute(v, 'tensor', [(0, 1), (1, 0)])  57.9 us
    reduce_scatter x1, waiting for transfers between devices, body(): lax.psum_scatter(qkv_part.astype(BF), 'dp', scatter_dimension=0, tiled=True)  26.7 us
    pallas_call x1, Pallas kernels, attend_back(): pl.pallas_call(functools.partial(attend_back_kernel, q_block, parts), nam...  24 us
  transfers between devices with their start and end apart: 115, of which 41 were waited for; matrix products, arithmetic and copies ran while one was open for 10% of the time, Pallas kernels for 24%

profile of v1, /device:TPU:9, one launch (start us, length us, event | category | flops | bytes accessed | tf_op | source)
XLA Modules:
  0.0 965.4 jit_solution(14634104559619611496)
XLA Ops:
  15.6 4.5 pack_weights.1
  21.4 15.4 %collective-permute-done.3 = bf16[32,512]{1,0:T(8,128)(2,1)S(1)} collective-permute-done((bf16[32,512]{1,0:T(8,128)(2,1)S(1)}, bf16[32,512]{1,0:T(8,128)(2,1)S(1)}, u32[]{:S(2)}, u32[]{:S(2)}) %collective-permute-start.3) | collective-permute-done | bytes 32800 | tf_op jit(solution)/shard_map/ppermute | solution.py:604
  45.9 14.9 %collective-permute-done.63 = bf16[96,1024]{1,0:T(8,128)(2,1)S(1)} collective-permute-done((bf16[96,1024]{1,0:T(8,128)(2,1)S(1)}, bf16[96,1024]{1,0:T(8,128)(2,1)S(1)}, u32[]{:S(2)}, u32[]{:S(2)}) %collective-permute-start.63) | collective-permute-done | bytes 196640 | tf_op jit(solution)/shard_map/ppermute | solution.py:601
  76.6 3.7 pad_maximum_fusion.5
  82.6 7.1 qkv_rope.1.qkv_ref
  98.4 19.7 %attend.1 = (bf16[512,512]{1,0:T(8,128)(2,1)}, bf16[512,512]{1,0:T(8,128)(2,1)}, f32[4,4,512]{2,1,0:T(4,128)}) custom-call(s32[4]{0:T(128)} %pad_add_fusion.idx_ref, bf16[1024,1024]{1,0:T(8,128)(2,1)} %qkv_rope.1.qkv_ref), custom_call_target="tpu_custom_call" | custom-call | flops 15032385536 | bytes 4194304 | tf_op jit(solution)/shard_map/attend/pallas_call | solution.py:167
  120.3 6.9 collective-permute-done.2.refs_3_.refs_5_
  129.3 9.2 collective-permute-done.1.refs_1_
  142.0 5.0 project_out.1
  180.1 6.3 dispatch_scaled.4.refs_4_
  188.8 6.3 dispatch_scaled.5.refs_5_
  195.1 6.3 dispatch_scaled.6.refs_6_
  201.5 6.7 dispatch_scaled.7.refs_7_
  208.2 3.6 collective-permute-start.67
  215.2 6.3 dispatch.4.refs_0_
  221.5 6.3 dispatch.5.refs_1_
  227.8 6.3 dispatch.6.refs_2_
  235.0 6.3 dispatch.7.refs_3_
  242.2 19.6 %expert.7 = (bf16[4,288,1024]{2,1,0:T(8,128)(2,1)}, bf16[4,288,1024]{2,1,0:T(8,128)(2,1)}, bf16[4,4,96,1024]{3,2,1,0:T(8,128)(2,1)}) custom-call(s32[4]{0:T(128)} %pad_add_fusion.idx_ref, bf16[4,288,1024]{2,1,0:T(8,128)(2,1)} %dispatch.4.refs_0_, bf16[4,288,1024]{2,1,0:T(8,128)(2,1)} %dispatch.5.refs_1_, bf16[4,288,1024]{2,1,0:T(8,128)(2,1)} %dispatch.6.refs_2_, ...), custom_call_target="tpu_custom_call" | custom-call | flops 10871635968 | bytes 15728640 | tf_op jit(solution)/shard_map/expert/pallas_call | solution.py:44
  264.9 4.0 collective-permute-done.54
  268.9 5.2 collective-permute-done.55
  274.2 3.6 collective-permute-start.56
  279.7 48.9 %collective-permute-done.56.refs_9_ = bf16[4,96,1024]{2,1,0:T(8,128)(2,1)S(1)} collective-permute-done((bf16[4,96,1024]{2,1,0:T(8,128)(2,1)S(1)}, bf16[4,96,1024]{2,1,0:T(8,128)(2,1)S(1)}, u32[]{:S(2)}, u32[]{:S(2)}) %collective-permute-start.56) | collective-permute-done | bytes 786464 | tf_op jit(solution)/shard_map/ppermute | solution.py:612
  328.6 4.4 collective-permute-start.57
  335.2 19.1 %collective-permute-done.57.refs_10_ = bf16[4,96,1024]{2,1,0:T(8,128)(2,1)S(1)} collective-permute-done((bf16[4,96,1024]{2,1,0:T(8,128)(2,1)S(1)}, bf16[4,96,1024]{2,1,0:T(8,128)(2,1)S(1)}, u32[]{:S(2)}, u32[]{:S(2)}) %collective-permute-start.57) | collective-permute-done | bytes 786464 | tf_op jit(solution)/shard_map/ppermute | solution.py:612
  359.7 15.9 %collective-permute-done.58.refs_11_ = bf16[4,96,1024]{2,1,0:T(8,128)(2,1)S(1)} collective-permute-done((bf16[4,96,1024]{2,1,0:T(8,128)(2,1)S(1)}, bf16[4,96,1024]{2,1,0:T(8,128)(2,1)S(1)}, u32[]{:S(2)}, u32[]{:S(2)}) %collective-permute-start.58) | collective-permute-done | bytes 786464 | tf_op jit(solution)/shard_map/ppermute | solution.py:612
  377.5 19.7 %expert.6 = (bf16[4,288,1024]{2,1,0:T(8,128)(2,1)}, bf16[4,288,1024]{2,1,0:T(8,128)(2,1)}, bf16[4,4,96,1024]{3,2,1,0:T(8,128)(2,1)}) custom-call(s32[4]{0:T(128)} %pad_add_fusion.idx_ref, bf16[4,288,1024]{2,1,0:T(8,128)(2,1)} %dispatch.4.refs_0_, bf16[4,288,1024]{2,1,0:T(8,128)(2,1)} %dispatch.5.refs_1_, bf16[4,288,1024]{2,1,0:T(8,128)(2,1)} %dispatch.6.refs_2_, ...), custom_call_target="tpu_custom_call" | custom-call | flops 10871635968 | bytes 15728640 | tf_op jit(solution)/shard_map/expert/pallas_call | solution.py:44
  401.6 4.8 collective-permute-done.45
  406.5 4.7 collective-permute-done.46
  416.6 47.9 %collective-permute-done.47.refs_9_ = bf16[4,96,1024]{2,1,0:T(8,128)(2,1)S(1)} collective-permute-done((bf16[4,96,1024]{2,1,0:T(8,128)(2,1)S(1)}, bf16[4,96,1024]{2,1,0:T(8,128)(2,1)S(1)}, u32[]{:S(2)}, u32[]{:S(2)}) %collective-permute-start.47) | collective-permute-done | bytes 786464 | tf_op jit(solution)/shard_map/ppermute | solution.py:612
  464.5 4.7 collective-permute-start.48
  471.2 18.4 %collective-permute-done.48.refs_10_ = bf16[4,96,1024]{2,1,0:T(8,128)(2,1)S(1)} collective-permute-done((bf16[4,96,1024]{2,1,0:T(8,128)(2,1)S(1)}, bf16[4,96,1024]{2,1,0:T(8,128)(2,1)S(1)}, u32[]{:S(2)}, u32[]{:S(2)}) %collective-permute-start.48) | collective-permute-done | bytes 786464 | tf_op jit(solution)/shard_map/ppermute | solution.py:612
  495.0 14.7 %collective-permute-done.49.refs_11_ = bf16[4,96,1024]{2,1,0:T(8,128)(2,1)S(1)} collective-permute-done((bf16[4,96,1024]{2,1,0:T(8,128)(2,1)S(1)}, bf16[4,96,1024]{2,1,0:T(8,128)(2,1)S(1)}, u32[]{:S(2)}, u32[]{:S(2)}) %collective-permute-start.49) | collective-permute-done | bytes 786464 | tf_op jit(solution)/shard_map/ppermute | solution.py:612
  512.7 19.7 %expert.5 = (bf16[4,288,1024]{2,1,0:T(8,128)(2,1)}, bf16[4,288,1024]{2,1,0:T(8,128)(2,1)}, bf16[4,4,96,1024]{3,2,1,0:T(8,128)(2,1)}) custom-call(s32[4]{0:T(128)} %pad_add_fusion.idx_ref, bf16[4,288,1024]{2,1,0:T(8,128)(2,1)} %dispatch.4.refs_0_, bf16[4,288,1024]{2,1,0:T(8,128)(2,1)} %dispatch.5.refs_1_, bf16[4,288,1024]{2,1,0:T(8,128)(2,1)} %dispatch.6.refs_2_, ...), custom_call_target="tpu_custom_call" | custom-call | flops 10871635968 | bytes 15728640 | tf_op jit(solution)/shard_map/expert/pallas_call | solution.py:44
  537.1 4.8 collective-permute-done.36
  541.9 4.7 collective-permute-done.37
  552.1 48.9 %collective-permute-done.38.refs_9_ = bf16[4,96,1024]{2,1,0:T(8,128)(2,1)S(1)} collective-permute-done((bf16[4,96,1024]{2,1,0:T(8,128)(2,1)S(1)}, bf16[4,96,1024]{2,1,0:T(8,128)(2,1)S(1)}, u32[]{:S(2)}, u32[]{:S(2)}) %collective-permute-start.38) | collective-permute-done | bytes 786464 | tf_op jit(solution)/shard_map/ppermute | solution.py:612
  601.0 4.2 collective-permute-start.39
  607.2 18.3 %collective-permute-done.39.refs_10_ = bf16[4,96,1024]{2,1,0:T(8,128)(2,1)S(1)} collective-permute-done((bf16[4,96,1024]{2,1,0:T(8,128)(2,1)S(1)}, bf16[4,96,1024]{2,1,0:T(8,128)(2,1)S(1)}, u32[]{:S(2)}, u32[]{:S(2)}) %collective-permute-start.39) | collective-permute-done | bytes 786464 | tf_op jit(solution)/shard_map/ppermute | solution.py:612
  635.2 10.7 %collective-permute-done.40.refs_11_ = bf16[4,96,1024]{2,1,0:T(8,128)(2,1)S(1)} collective-permute-done((bf16[4,96,1024]{2,1,0:T(8,128)(2,1)S(1)}, bf16[4,96,1024]{2,1,0:T(8,128)(2,1)S(1)}, u32[]{:S(2)}, u32[]{:S(2)}) %collective-permute-start.40) | collective-permute-done | bytes 786464 | tf_op jit(solution)/shard_map/ppermute | solution.py:612
  648.4 19.9 %expert.4 = (bf16[4,288,1024]{2,1,0:T(8,128)(2,1)}, bf16[4,288,1024]{2,1,0:T(8,128)(2,1)}, bf16[4,4,96,1024]{3,2,1,0:T(8,128)(2,1)}) custom-call(s32[4]{0:T(128)} %pad_add_fusion.idx_ref, bf16[4,288,1024]{2,1,0:T(8,128)(2,1)} %dispatch.4.refs_0_, bf16[4,288,1024]{2,1,0:T(8,128)(2,1)} %dispatch.5.refs_1_, bf16[4,288,1024]{2,1,0:T(8,128)(2,1)} %dispatch.6.refs_2_, ...), custom_call_target="tpu_custom_call" | custom-call | flops 10871635968 | bytes 15728640 | tf_op jit(solution)/shard_map/expert/pallas_call | solution.py:44
  668.3 7.1 combine.6
  677.5 7.1 combine.4
  684.7 7.1 combine_scaled.6
  692.4 7.4 combine_scaled.4
  700.9 7.4 combine.7
  709.5 7.4 combine.5
  718.7 7.4 combine_scaled.7
  727.5 7.4 combine_scaled.5
  743.9 8.5 collective-permute-done.74
  754.8 20.0 %collective-permute-done.86.refs_3_ = bf16[256,1024]{1,0:T(8,128)(2,1)S(1)} collective-permute-done((bf16[256,1024]{1,0:T(8,128)(2,1)S(1)}, bf16[256,1024]{1,0:T(8,128)(2,1)S(1)}, u32[]{:S(2)}, u32[]{:S(2)}) %collective-permute-start.86) | collective-permute-done | bytes 524320 | tf_op jit(solution)/shard_map/ppermute | solution.py:601
  776.7 6.7 hidden_back.1
  789.3 8.4 collective-permute-done.87.refs_1_
  798.7 24.0 %attend_back.1 = (bf16[512,1024]{1,0:T(8,128)(2,1)}, bf16[512,1024]{1,0:T(8,128)(2,1)}) custom-call(s32[4]{0:T(128)} %pad_add_fusion.idx_ref, bf16[1024,1024]{1,0:T(8,128)(2,1)} %qkv_rope.1.qkv_ref, f32[4,4,512]{2,1,0:T(4,128)} %get-tuple-element.111.lse_ref, f32[1024,128]{1,0:T(8,128)} %get-tuple-element.172.cos_ref, ...), custom_call_target="tpu_custom_call" | custom-call | flops 32212254720 | bytes 6291456 | tf_op jit(solution)/shard_map/attend_back/pallas_call | solution.py:232
  822.7 4.3 convolution_convert_fusion
  833.6 15.2 %collective-permute-done.88 = bf16[512,1024]{1,0:T(8,128)(2,1)} collective-permute-done((bf16[512,1024]{1,0:T(8,128)(2,1)}, bf16[512,1024]{1,0:T(8,128)(2,1)}, u32[]{:S(2)}, u32[]{:S(2)}) %collective-permute-start.88) | collective-permute-done | bytes 1048608 | tf_op jit(solution)/shard_map/ppermute | solution.py:604
  848.8 5.1 fusion.6
  856.5 5.3 collective-permute-start.90
  870.9 3.5 fusion.9
  886.4 5.2 reduce-scatter.9.cloned.1.call-done
  903.9 5.0 collective-permute-done.106
  908.9 4.2 collective-permute-done.105
  913.2 4.2 collective-permute-done.104
  929.7 26.7 %reduce-scatter.7.cloned.1.call-done = bf16[64,1024]{1,0:T(8,128)(2,1)} async-done(((bf16[1024,1024]{1,0:T(8,128)(2,1)}), bf16[64,1024]{1,0:T(8,128)(2,1)}) %reduce-scatter.7.cloned.1.call-update) | async-done | bytes 131088 | tf_op jit(solution)/shard_map/reduce_scatter | solution.py:786
  (447 shorter events, 236.5 us)
Async XLA Ops:
  7.2 75.4 %all-gather.3.cloned.1.call-start = ((), (), s32[]{:S(2)}) async-start(), calls=%async_computation.6 | async-start | bytes 2228224 | tf_op jit(solution)/shard_map/all_gather | solution.py:628
  8.9 88.9 %all-gather.5.cloned.1.call-start = ((), (), s32[]{:S(2)}) async-start(), calls=%async_computation.7 | async-start | bytes 1114112 | tf_op jit(solution)/shard_map/all_gather | solution.py:629
  12.1 64.4 %collective-permute-start = (bf16[512,1024]{1,0:T(8,128)(2,1)S(1)}, bf16[512,1024]{1,0:T(8,128)(2,1)S(1)}, u32[]{:S(2)}, u32[]{:S(2)}) collective-permute-start(bf16[512,1024]{1,0:T(8,128)(2,1)S(1)} %fusion.5), channel_id=1, source_target_pairs={{0,1},{1,0},{2,3},{3,2},{4,5},{5,4},{6,7},{7,6},{8,9},{9,8},{10,11... | collective-permute-start | bytes 3145736 | tf_op jit(solution)/shard_map/ppermute | solution.py:604
  14.2 22.6 %collective-permute-start.3 = (bf16[32,512]{1,0:T(8,128)(2,1)S(1)}, bf16[32,512]{1,0:T(8,128)(2,1)S(1)}, u32[]{:S(2)}, u32[]{:S(2)}) collective-permute-start(bf16[32,512]{1,0:T(8,128)(2,1)S(1)} %select_convert_fusion.1), channel_id=1, source_target_pairs={{0,1},{1,0},{2,3},{3,2},{4,5},{5,4},{6,7},{7,6},{8,9},{9,8},{10,11... | collective-permute-start | bytes 98312 | tf_op jit(solution)/shard_map/ppermute | solution.py:604
  20.1 22.8 %collective-permute-start.62 = (bf16[96,1024]{1,0:T(8,128)(2,1)}, bf16[96,1024]{1,0:T(8,128)(2,1)}, u32[]{:S(2)}, u32[]{:S(2)}) collective-permute-start(bf16[96,1024]{1,0:T(8,128)(2,1)} %get-tuple-element.86), channel_id=1, source_target_pairs={{0,2},{2,0},{4,6},{6,4},{8,10},{10,8},{12,14},{14,12},{16,18},{18,... | collective-permute-start | bytes 589832 | tf_op jit(solution)/shard_map/ppermute | solution.py:601
  21.2 853.9 %reduce-scatter.17.cloned.1.call-start = ((), (), s32[]{:S(2)}) async-start(), calls=%async_computation.13 | async-start | bytes 3932160 | tf_op jit(solution)/shard_map/reduce_scatter | solution.py:770
  39.2 34.7 %collective-permute-start.21 = (bf16[256,1024]{1,0:T(8,128)(2,1)}, bf16[256,1024]{1,0:T(8,128)(2,1)}, u32[]{:S(2)}, u32[]{:S(2)}) collective-permute-start(bf16[256,1024]{1,0:T(8,128)(2,1)} %get-tuple-element.141.refs_0_), channel_id=1, source_target_pairs={{0,1},{1,0},{2,3},{3,2},{4,5},{5,4},{6,7},{7,6},{8,9},{9,8},{10,11... | collective-permute-start | bytes 1572872 | tf_op jit(solution)/shard_map/ppermute | solution.py:604
  40.4 34.7 %collective-permute-start.25 = (bf16[256,1024]{1,0:T(8,128)(2,1)}, bf16[256,1024]{1,0:T(8,128)(2,1)}, u32[]{:S(2)}, u32[]{:S(2)}) collective-permute-start(bf16[256,1024]{1,0:T(8,128)(2,1)} %get-tuple-element.140.refs_2_), channel_id=1, source_target_pairs={{0,4},{2,6},{4,0},{6,2},{8,12},{10,14},{12,8},{14,10},{16,20},{18,... | collective-permute-start | bytes 1572872 | tf_op jit(solution)/shard_map/ppermute | solution.py:601
  42.9 22.7 %collective-permute-start.64 = (bf16[96,1024]{1,0:T(8,128)(2,1)S(1)}, bf16[96,1024]{1,0:T(8,128)(2,1)S(1)}, u32[]{:S(2)}, u32[]{:S(2)}) collective-permute-start(bf16[96,1024]{1,0:T(8,128)(2,1)S(1)} %copy-done.79), channel_id=1, source_target_pairs={{0,6},{2,4},{4,2},{6,0},{8,14},{10,12},{12,10},{14,8},{16,22},{18,... | collective-permute-start | bytes 589832 | tf_op jit(solution)/shard_map/ppermute | solution.py:601
  67.6 28.8 %collective-permute-start.65 = (bf16[4,96,1024]{2,1,0:T(8,128)(2,1)}, bf16[4,96,1024]{2,1,0:T(8,128)(2,1)}, u32[]{:S(2)}, u32[]{:S(2)}) collective-permute-start(bf16[4,96,1024]{2,1,0:T(8,128)(2,1)} %pad_maximum_fusion.4.refs_8_), channel_id=1, source_target_pairs={{0,8},{2,10},{4,12},{6,14},{8,16},{10,18},{12,20},{14,22},{16,24},... | collective-permute-start | bytes 2359304 | tf_op jit(solution)/shard_map/ppermute | solution.py:612
  89.7 28.4 %collective-permute-start.68 = (bf16[4,96,1024]{2,1,0:T(8,128)(2,1)}, bf16[4,96,1024]{2,1,0:T(8,128)(2,1)}, u32[]{:S(2)}, u32[]{:S(2)}) collective-permute-start(bf16[4,96,1024]{2,1,0:T(8,128)(2,1)} %pad_maximum_fusion.4.refs_8_), channel_id=1, source_target_pairs={{8,0},{10,2},{12,4},{14,6},{16,8},{18,10},{20,12},{22,14},{24,16},... | collective-permute-start | bytes 2359304 | tf_op jit(solution)/shard_map/ppermute | solution.py:612
  92.8 27.0 %collective-permute-start.26 = (bf16[256,1024]{1,0:T(8,128)(2,1)}, bf16[256,1024]{1,0:T(8,128)(2,1)S(1)}, u32[]{:S(2)}, u32[]{:S(2)}) collective-permute-start(bf16[256,1024]{1,0:T(8,128)(2,1)} %collective-permute-done.25.refs_2_), channel_id=1, source_target_pairs={{0,1},{1,0},{2,3},{3,2},{4,5},{5,4},{6,7},{7,6},{8,9},{9,8},{10,11... | collective-permute-start | bytes 1572872 | tf_op jit(solution)/shard_map/ppermute | solution.py:604
  93.8 26.0 %collective-permute-start.33 = (bf16[256,1024]{1,0:T(8,128)(2,1)}, bf16[256,1024]{1,0:T(8,128)(2,1)S(1)}, u32[]{:S(2)}, u32[]{:S(2)}) collective-permute-start(bf16[256,1024]{1,0:T(8,128)(2,1)} %collective-permute-done.25.refs_2_), channel_id=1, source_target_pairs={{0,2},{2,0},{4,6},{6,4},{8,10},{10,8},{12,14},{14,12},{16,18},{18,... | collective-permute-start | bytes 1572872 | tf_op jit(solution)/shard_map/ppermute | solution.py:601
  96.1 23.0 %collective-permute-start.24 = (bf16[256,1024]{1,0:T(8,128)(2,1)}, bf16[256,1024]{1,0:T(8,128)(2,1)}, u32[]{:S(2)}, u32[]{:S(2)}) collective-permute-start(bf16[256,1024]{1,0:T(8,128)(2,1)} %collective-permute-done.21.refs_1_), channel_id=1, source_target_pairs={{0,4},{2,6},{4,0},{6,2},{8,12},{10,14},{12,8},{14,10},{16,20},{18,... | collective-permute-start | bytes 1572872 | tf_op jit(solution)/shard_map/ppermute | solution.py:601
  97.8 29.4 %collective-permute-start.2 = (bf16[1024,512]{1,0:T(8,128)(2,1)}, bf16[1024,512]{1,0:T(8,128)(2,1)S(1)}, u32[]{:S(2)}, u32[]{:S(2)}) collective-permute-start(bf16[1024,512]{1,0:T(8,128)(2,1)} %all-gather.5.cloned.1.call-done.refs_2_.refs_4_), channel_id=1, source_target_pairs={{0,1},{1,0},{2,3},{3,2},{4,5},{5,4},{6,7},{7,6},{8,9},{9,8},{10,11... | collective-permute-start | bytes 3145736 | tf_op jit(solution)/shard_map/ppermute | solution.py:604
  119.0 28.0 %collective-permute-start.31 = (bf16[256,1024]{1,0:T(8,128)(2,1)}, bf16[256,1024]{1,0:T(8,128)(2,1)}, u32[]{:S(2)}, u32[]{:S(2)}) collective-permute-start(bf16[256,1024]{1,0:T(8,128)(2,1)} %collective-permute-done.23.refs_0_), channel_id=1, source_target_pairs={{0,2},{2,0},{4,6},{6,4},{8,10},{10,8},{12,14},{14,12},{16,18},{18,... | collective-permute-start | bytes 1572872 | tf_op jit(solution)/shard_map/ppermute | solution.py:601
  119.8 29.8 %collective-permute-start.28 = (bf16[256,1024]{1,0:T(8,128)(2,1)}, bf16[256,1024]{1,0:T(8,128)(2,1)}, u32[]{:S(2)}, u32[]{:S(2)}) collective-permute-start(bf16[256,1024]{1,0:T(8,128)(2,1)} %collective-permute-done.21.refs_1_), channel_id=1, source_target_pairs={{0,2},{2,0},{4,6},{6,4},{8,10},{10,8},{12,14},{14,12},{16,18},{18,... | collective-permute-start | bytes 1572872 | tf_op jit(solution)/shard_map/ppermute | solution.py:601
  119.9 29.8 %collective-permute-start.30 = (bf16[256,1024]{1,0:T(8,128)(2,1)}, bf16[256,1024]{1,0:T(8,128)(2,1)}, u32[]{:S(2)}, u32[]{:S(2)}) collective-permute-start(bf16[256,1024]{1,0:T(8,128)(2,1)} %collective-permute-done.22.refs_3_), channel_id=1, source_target_pairs={{0,2},{2,0},{4,6},{6,4},{8,10},{10,8},{12,14},{14,12},{16,18},{18,... | collective-permute-start | bytes 1572872 | tf_op jit(solution)/shard_map/ppermute | solution.py:601
  127.2 28.0 %collective-permute-start.66 = (bf16[4,96,1024]{2,1,0:T(8,128)(2,1)}, bf16[4,96,1024]{2,1,0:T(8,128)(2,1)}, u32[]{:S(2)}, u32[]{:S(2)}) collective-permute-start(bf16[4,96,1024]{2,1,0:T(8,128)(2,1)} %collective-permute-done.65.refs_9_), channel_id=1, source_target_pairs={{0,8},{2,10},{4,12},{6,14},{8,16},{10,18},{12,20},{14,22},{16,24},... | collective-permute-start | bytes 2359304 | tf_op jit(solution)/shard_map/ppermute | solution.py:612
  153.7 34.0 %collective-permute-start.9 = (bf16[256,1024]{1,0:T(8,128)(2,1)}, bf16[256,1024]{1,0:T(8,128)(2,1)}, u32[]{:S(2)}, u32[]{:S(2)}) collective-permute-start(bf16[256,1024]{1,0:T(8,128)(2,1)} %get-tuple-element.68.refs_0_), channel_id=1, source_target_pairs={{0,4},{2,6},{4,0},{6,2},{8,12},{10,14},{12,8},{14,10},{16,20},{18,... | collective-permute-start | bytes 1572872 | tf_op jit(solution)/shard_map/ppermute | solution.py:601
  154.2 32.3 %collective-permute-start.11 = (bf16[256,1024]{1,0:T(8,128)(2,1)}, bf16[256,1024]{1,0:T(8,128)(2,1)}, u32[]{:S(2)}, u32[]{:S(2)}) collective-permute-start(bf16[256,1024]{1,0:T(8,128)(2,1)} %get-tuple-element.69.refs_2_), channel_id=1, source_target_pairs={{0,4},{2,6},{4,0},{6,2},{8,12},{10,14},{12,8},{14,10},{16,20},{18,... | collective-permute-start | bytes 1572872 | tf_op jit(solution)/shard_map/ppermute | solution.py:601
  155.2 32.9 %collective-permute-start.8 = (bf16[256,1024]{1,0:T(8,128)(2,1)}, bf16[256,1024]{1,0:T(8,128)(2,1)}, u32[]{:S(2)}, u32[]{:S(2)}) collective-permute-start(bf16[256,1024]{1,0:T(8,128)(2,1)} %get-tuple-element.69.refs_2_), channel_id=1, source_target_pairs={{0,1},{1,0},{2,3},{3,2},{4,5},{5,4},{6,7},{7,6},{8,9},{9,8},{10,11... | collective-permute-start | bytes 1572872 | tf_op jit(solution)/shard_map/ppermute | solution.py:604
  157.2 31.1 %collective-permute-start.13 = (bf16[256,1024]{1,0:T(8,128)(2,1)}, bf16[256,1024]{1,0:T(8,128)(2,1)}, u32[]{:S(2)}, u32[]{:S(2)}) collective-permute-start(bf16[256,1024]{1,0:T(8,128)(2,1)} %get-tuple-element.68.refs_0_), channel_id=1, source_target_pairs={{0,2},{2,0},{4,6},{6,4},{8,10},{10,8},{12,14},{14,12},{16,18},{18,... | collective-permute-start | bytes 1572872 | tf_op jit(solution)/shard_map/ppermute | solution.py:601
  163.1 25.7 %collective-permute-start.15 = (bf16[256,1024]{1,0:T(8,128)(2,1)}, bf16[256,1024]{1,0:T(8,128)(2,1)}, u32[]{:S(2)}, u32[]{:S(2)}) collective-permute-start(bf16[256,1024]{1,0:T(8,128)(2,1)} %get-tuple-element.69.refs_2_), channel_id=1, source_target_pairs={{0,2},{2,0},{4,6},{6,4},{8,10},{10,8},{12,14},{14,12},{16,18},{18,... | collective-permute-start | bytes 1572872 | tf_op jit(solution)/shard_map/ppermute | solution.py:601
  187.7 27.0 %collective-permute-start.14 = (bf16[256,1024]{1,0:T(8,128)(2,1)S(1)}, bf16[256,1024]{1,0:T(8,128)(2,1)}, u32[]{:S(2)}, u32[]{:S(2)}) collective-permute-start(bf16[256,1024]{1,0:T(8,128)(2,1)S(1)} %copy-done.65), channel_id=1, source_target_pairs={{0,2},{2,0},{4,6},{6,4},{8,10},{10,8},{12,14},{14,12},{16,18},{18,... | collective-permute-start | bytes 1572872 | tf_op jit(solution)/shard_map/ppermute | solution.py:601
  188.0 23.8 %collective-permute-start.12 = (bf16[256,1024]{1,0:T(8,128)(2,1)}, bf16[256,1024]{1,0:T(8,128)(2,1)}, u32[]{:S(2)}, u32[]{:S(2)}) collective-permute-start(bf16[256,1024]{1,0:T(8,128)(2,1)} %collective-permute-done.11.refs_2_), channel_id=1, source_target_pairs={{0,1},{1,0},{2,3},{3,2},{4,5},{5,4},{6,7},{7,6},{8,9},{9,8},{10,11... | collective-permute-start | bytes 1572872 | tf_op jit(solution)/shard_map/ppermute | solution.py:604
  188.3 25.5 %collective-permute-start.17 = (bf16[256,1024]{1,0:T(8,128)(2,1)}, bf16[256,1024]{1,0:T(8,128)(2,1)}, u32[]{:S(2)}, u32[]{:S(2)}) collective-permute-start(bf16[256,1024]{1,0:T(8,128)(2,1)} %collective-permute-done.9.refs_0_), channel_id=1, source_target_pairs={{0,2},{2,0},{4,6},{6,4},{8,10},{10,8},{12,14},{14,12},{16,18},{18,... | collective-permute-start | bytes 1572872 | tf_op jit(solution)/shard_map/ppermute | solution.py:601
  188.8 26.0 %collective-permute-start.16 = (bf16[256,1024]{1,0:T(8,128)(2,1)}, bf16[256,1024]{1,0:T(8,128)(2,1)}, u32[]{:S(2)}, u32[]{:S(2)}) collective-permute-start(bf16[256,1024]{1,0:T(8,128)(2,1)} %collective-permute-done.8.refs_3_), channel_id=1, source_target_pairs={{0,2},{2,0},{4,6},{6,4},{8,10},{10,8},{12,14},{14,12},{16,18},{18,... | collective-permute-start | bytes 1572872 | tf_op jit(solution)/shard_map/ppermute | solution.py:601
  208.2 33.0 %collective-permute-start.67 = (bf16[4,96,1024]{2,1,0:T(8,128)(2,1)}, bf16[4,96,1024]{2,1,0:T(8,128)(2,1)S(1)}, u32[]{:S(2)}, u32[]{:S(2)}) collective-permute-start(bf16[4,96,1024]{2,1,0:T(8,128)(2,1)} %collective-permute-done.66.refs_10_), channel_id=1, source_target_pairs={{0,8},{2,10},{4,12},{6,14},{8,16},{10,18},{12,20},{14,22},{16,24},... | collective-permute-start | bytes 2359304 | tf_op jit(solution)/shard_map/ppermute | solution.py:612
  211.9 29.4 %collective-permute-start.70 = (bf16[4,96,1024]{2,1,0:T(8,128)(2,1)}, bf16[4,96,1024]{2,1,0:T(8,128)(2,1)}, u32[]{:S(2)}, u32[]{:S(2)}) collective-permute-start(bf16[4,96,1024]{2,1,0:T(8,128)(2,1)} %collective-permute-done.69.refs_13_), channel_id=1, source_target_pairs={{8,0},{10,2},{12,4},{14,6},{16,8},{18,10},{20,12},{22,14},{24,16},... | collective-permute-start | bytes 2359304 | tf_op jit(solution)/shard_map/ppermute | solution.py:612
  261.9 616.0 %reduce-scatter.15.cloned.1.call-start = ((), (), s32[]{:S(2)}) async-start(), calls=%async_computation.12 | async-start | bytes 3932160 | tf_op jit(solution)/shard_map/reduce_scatter | solution.py:770
  274.2 54.4 %collective-permute-start.56 = (bf16[4,96,1024]{2,1,0:T(8,128)(2,1)S(1)}, bf16[4,96,1024]{2,1,0:T(8,128)(2,1)S(1)}, u32[]{:S(2)}, u32[]{:S(2)}) collective-permute-start(bf16[4,96,1024]{2,1,0:T(8,128)(2,1)S(1)} %pad_maximum_fusion.3.refs_8_), channel_id=1, source_target_pairs={{0,8},{2,10},{4,12},{6,14},{8,16},{10,18},{12,20},{14,22},{16,24},... | collective-permute-start | bytes 2359304 | tf_op jit(solution)/shard_map/ppermute | solution.py:612
  277.8 55.5 %collective-permute-start.59 = (bf16[4,96,1024]{2,1,0:T(8,128)(2,1)S(1)}, bf16[4,96,1024]{2,1,0:T(8,128)(2,1)S(1)}, u32[]{:S(2)}, u32[]{:S(2)}) collective-permute-start(bf16[4,96,1024]{2,1,0:T(8,128)(2,1)S(1)} %pad_maximum_fusion.3.refs_8_), channel_id=1, source_target_pairs={{8,0},{10,2},{12,4},{14,6},{16,8},{18,10},{20,12},{22,14},{24,16},... | collective-permute-start | bytes 2359304 | tf_op jit(solution)/shard_map/ppermute | solution.py:612
  328.6 25.8 %collective-permute-start.57 = (bf16[4,96,1024]{2,1,0:T(8,128)(2,1)S(1)}, bf16[4,96,1024]{2,1,0:T(8,128)(2,1)S(1)}, u32[]{:S(2)}, u32[]{:S(2)}) collective-permute-start(bf16[4,96,1024]{2,1,0:T(8,128)(2,1)S(1)} %collective-permute-done.56.refs_9_), channel_id=1, source_target_pairs={{0,8},{2,10},{4,12},{6,14},{8,16},{10,18},{12,20},{14,22},{16,24},... | collective-permute-start | bytes 2359304 | tf_op jit(solution)/shard_map/ppermute | solution.py:612
  333.3 23.9 %collective-permute-start.60 = (bf16[4,96,1024]{2,1,0:T(8,128)(2,1)S(1)}, bf16[4,96,1024]{2,1,0:T(8,128)(2,1)S(1)}, u32[]{:S(2)}, u32[]{:S(2)}) collective-permute-start(bf16[4,96,1024]{2,1,0:T(8,128)(2,1)S(1)} %collective-permute-done.59.refs_12_), channel_id=1, source_target_pairs={{8,0},{10,2},{12,4},{14,6},{16,8},{18,10},{20,12},{22,14},{24,16},... | collective-permute-start | bytes 2359304 | tf_op jit(solution)/shard_map/ppermute | solution.py:612
  397.3 482.6 %reduce-scatter.13.cloned.1.call-start = ((), (), s32[]{:S(2)}) async-start(), calls=%async_computation.11 | async-start | bytes 3932160 | tf_op jit(solution)/shard_map/reduce_scatter | solution.py:770
  411.3 53.3 %collective-permute-start.47 = (bf16[4,96,1024]{2,1,0:T(8,128)(2,1)S(1)}, bf16[4,96,1024]{2,1,0:T(8,128)(2,1)S(1)}, u32[]{:S(2)}, u32[]{:S(2)}) collective-permute-start(bf16[4,96,1024]{2,1,0:T(8,128)(2,1)S(1)} %pad_maximum_fusion.2.refs_8_), channel_id=1, source_target_pairs={{0,8},{2,10},{4,12},{6,14},{8,16},{10,18},{12,20},{14,22},{16,24},... | collective-permute-start | bytes 2359304 | tf_op jit(solution)/shard_map/ppermute | solution.py:612
  414.1 55.1 %collective-permute-start.50 = (bf16[4,96,1024]{2,1,0:T(8,128)(2,1)S(1)}, bf16[4,96,1024]{2,1,0:T(8,128)(2,1)S(1)}, u32[]{:S(2)}, u32[]{:S(2)}) collective-permute-start(bf16[4,96,1024]{2,1,0:T(8,128)(2,1)S(1)} %pad_maximum_fusion.2.refs_8_), channel_id=1, source_target_pairs={{8,0},{10,2},{12,4},{14,6},{16,8},{18,10},{20,12},{22,14},{24,16},... | collective-permute-start | bytes 2359304 | tf_op jit(solution)/shard_map/ppermute | solution.py:612
  464.5 25.1 %collective-permute-start.48 = (bf16[4,96,1024]{2,1,0:T(8,128)(2,1)S(1)}, bf16[4,96,1024]{2,1,0:T(8,128)(2,1)S(1)}, u32[]{:S(2)}, u32[]{:S(2)}) collective-permute-start(bf16[4,96,1024]{2,1,0:T(8,128)(2,1)S(1)} %collective-permute-done.47.refs_9_), channel_id=1, source_target_pairs={{0,8},{2,10},{4,12},{6,14},{8,16},{10,18},{12,20},{14,22},{16,24},... | collective-permute-start | bytes 2359304 | tf_op jit(solution)/shard_map/ppermute | solution.py:612
  469.3 23.3 %collective-permute-start.51 = (bf16[4,96,1024]{2,1,0:T(8,128)(2,1)S(1)}, bf16[4,96,1024]{2,1,0:T(8,128)(2,1)S(1)}, u32[]{:S(2)}, u32[]{:S(2)}) collective-permute-start(bf16[4,96,1024]{2,1,0:T(8,128)(2,1)S(1)} %collective-permute-done.50.refs_12_), channel_id=1, source_target_pairs={{8,0},{10,2},{12,4},{14,6},{16,8},{18,10},{20,12},{22,14},{24,16},... | collective-permute-start | bytes 2359304 | tf_op jit(solution)/shard_map/ppermute | solution.py:612
  532.5 349.8 %reduce-scatter.11.cloned.1.call-start = ((), (), s32[]{:S(2)}) async-start(), calls=%async_computation.10 | async-start | bytes 3932160 | tf_op jit(solution)/shard_map/reduce_scatter | solution.py:770
  546.7 54.3 %collective-permute-start.38 = (bf16[4,96,1024]{2,1,0:T(8,128)(2,1)S(1)}, bf16[4,96,1024]{2,1,0:T(8,128)(2,1)S(1)}, u32[]{:S(2)}, u32[]{:S(2)}) collective-permute-start(bf16[4,96,1024]{2,1,0:T(8,128)(2,1)S(1)} %pad_maximum_fusion.1.refs_8_), channel_id=1, source_target_pairs={{0,8},{2,10},{4,12},{6,14},{8,16},{10,18},{12,20},{14,22},{16,24},... | collective-permute-start | bytes 2359304 | tf_op jit(solution)/shard_map/ppermute | solution.py:612
  550.1 55.1 %collective-permute-start.41 = (bf16[4,96,1024]{2,1,0:T(8,128)(2,1)S(1)}, bf16[4,96,1024]{2,1,0:T(8,128)(2,1)S(1)}, u32[]{:S(2)}, u32[]{:S(2)}) collective-permute-start(bf16[4,96,1024]{2,1,0:T(8,128)(2,1)S(1)} %pad_maximum_fusion.1.refs_8_), channel_id=1, source_target_pairs={{8,0},{10,2},{12,4},{14,6},{16,8},{18,10},{20,12},{22,14},{24,16},... | collective-permute-start | bytes 2359304 | tf_op jit(solution)/shard_map/ppermute | solution.py:612
  601.0 24.5 %collective-permute-start.39 = (bf16[4,96,1024]{2,1,0:T(8,128)(2,1)S(1)}, bf16[4,96,1024]{2,1,0:T(8,128)(2,1)S(1)}, u32[]{:S(2)}, u32[]{:S(2)}) collective-permute-start(bf16[4,96,1024]{2,1,0:T(8,128)(2,1)S(1)} %collective-permute-done.38.refs_9_), channel_id=1, source_target_pairs={{0,8},{2,10},{4,12},{6,14},{8,16},{10,18},{12,20},{14,22},{16,24},... | collective-permute-start | bytes 2359304 | tf_op jit(solution)/shard_map/ppermute | solution.py:612
  605.3 22.7 %collective-permute-start.42 = (bf16[4,96,1024]{2,1,0:T(8,128)(2,1)S(1)}, bf16[4,96,1024]{2,1,0:T(8,128)(2,1)S(1)}, u32[]{:S(2)}, u32[]{:S(2)}) collective-permute-start(bf16[4,96,1024]{2,1,0:T(8,128)(2,1)S(1)} %collective-permute-done.41.refs_12_), channel_id=1, source_target_pairs={{8,0},{10,2},{12,4},{14,6},{16,8},{18,10},{20,12},{22,14},{24,16},... | collective-permute-start | bytes 2359304 | tf_op jit(solution)/shard_map/ppermute | solution.py:612
  675.4 25.4 %collective-permute-start.80 = (bf16[1024,1024]{1,0:T(8,128)(2,1)}, bf16[1024,1024]{1,0:T(8,128)(2,1)}, u32[]{:S(2)}, u32[]{:S(2)}) collective-permute-start(bf16[1024,1024]{1,0:T(8,128)(2,1)} %combine.6), channel_id=1, source_target_pairs={{0,2},{2,0},{4,6},{6,4},{8,10},{10,8},{12,14},{14,12},{16,18},{18,... | collective-permute-start | bytes 6291464 | tf_op jit(solution)/shard_map/ppermute | solution.py:601
  684.6 24.9 %collective-permute-start.79 = (bf16[1024,1024]{1,0:T(8,128)(2,1)}, bf16[1024,1024]{1,0:T(8,128)(2,1)}, u32[]{:S(2)}, u32[]{:S(2)}) collective-permute-start(bf16[1024,1024]{1,0:T(8,128)(2,1)} %combine.4), channel_id=1, source_target_pairs={{0,2},{2,0},{4,6},{6,4},{8,10},{10,8},{12,14},{14,12},{16,18},{18,... | collective-permute-start | bytes 6291464 | tf_op jit(solution)/shard_map/ppermute | solution.py:601
  691.8 26.6 %collective-permute-start.72 = (bf16[1024,1024]{1,0:T(8,128)(2,1)}, bf16[1024,1024]{1,0:T(8,128)(2,1)}, u32[]{:S(2)}, u32[]{:S(2)}) collective-permute-start(bf16[1024,1024]{1,0:T(8,128)(2,1)} %combine_scaled.6), channel_id=1, source_target_pairs={{0,2},{2,0},{4,6},{6,4},{8,10},{10,8},{12,14},{14,12},{16,18},{18,... | collective-permute-start | bytes 6291464 | tf_op jit(solution)/shard_map/ppermute | solution.py:601
  699.8 26.4 %collective-permute-start.71 = (bf16[1024,1024]{1,0:T(8,128)(2,1)}, bf16[1024,1024]{1,0:T(8,128)(2,1)S(1)}, u32[]{:S(2)}, u32[]{:S(2)}) collective-permute-start(bf16[1024,1024]{1,0:T(8,128)(2,1)} %combine_scaled.4), channel_id=1, source_target_pairs={{0,2},{2,0},{4,6},{6,4},{8,10},{10,8},{12,14},{14,12},{16,18},{18,... | collective-permute-start | bytes 6291464 | tf_op jit(solution)/shard_map/ppermute | solution.py:601
  700.8 190.9 %reduce-scatter.9.cloned.1.call-start = ((), (), s32[]{:S(2)}) async-start(), calls=%async_computation.9 | async-start | bytes 1114112 | tf_op jit(solution)/shard_map/reduce_scatter | solution.py:787
  708.3 26.6 %collective-permute-start.85 = (bf16[256,1024]{1,0:T(8,128)(2,1)}, bf16[256,1024]{1,0:T(8,128)(2,1)}, u32[]{:S(2)}, u32[]{:S(2)}) collective-permute-start(bf16[256,1024]{1,0:T(8,128)(2,1)} %get-tuple-element.109), channel_id=1, source_target_pairs={{0,1},{1,0},{2,3},{3,2},{4,5},{5,4},{6,7},{7,6},{8,9},{9,8},{10,11... | collective-permute-start | bytes 1572872 | tf_op jit(solution)/shard_map/ppermute | solution.py:604
  717.2 23.6 %collective-permute-start.82 = (bf16[256,1024]{1,0:T(8,128)(2,1)}, bf16[256,1024]{1,0:T(8,128)(2,1)}, u32[]{:S(2)}, u32[]{:S(2)}) collective-permute-start(bf16[256,1024]{1,0:T(8,128)(2,1)} %get-tuple-element.105), channel_id=1, source_target_pairs={{0,4},{2,6},{4,0},{6,2},{8,12},{10,14},{12,8},{14,10},{16,20},{18,... | collective-permute-start | bytes 1572872 | tf_op jit(solution)/shard_map/ppermute | solution.py:601
  718.4 23.9 %collective-permute-start.81 = (bf16[256,1024]{1,0:T(8,128)(2,1)}, bf16[256,1024]{1,0:T(8,128)(2,1)S(1)}, u32[]{:S(2)}, u32[]{:S(2)}) collective-permute-start(bf16[256,1024]{1,0:T(8,128)(2,1)} %get-tuple-element.103), channel_id=1, source_target_pairs={{0,4},{2,6},{4,0},{6,2},{8,12},{10,14},{12,8},{14,10},{16,20},{18,... | collective-permute-start | bytes 1572872 | tf_op jit(solution)/shard_map/ppermute | solution.py:601
  726.2 26.2 %collective-permute-start.74 = (bf16[256,1024]{1,0:T(8,128)(2,1)}, bf16[256,1024]{1,0:T(8,128)(2,1)}, u32[]{:S(2)}, u32[]{:S(2)}) collective-permute-start(bf16[256,1024]{1,0:T(8,128)(2,1)} %get-tuple-element.93), channel_id=1, source_target_pairs={{0,4},{2,6},{4,0},{6,2},{8,12},{10,14},{12,8},{14,10},{16,20},{18,... | collective-permute-start | bytes 1572872 | tf_op jit(solution)/shard_map/ppermute | solution.py:601
  734.9 92.0 %collective-permute-start.73 = (bf16[256,1024]{1,0:T(8,128)(2,1)}, bf16[256,1024]{1,0:T(8,128)(2,1)S(1)}, u32[]{:S(2)}, u32[]{:S(2)}) collective-permute-start(bf16[256,1024]{1,0:T(8,128)(2,1)} %get-tuple-element.91), channel_id=1, source_target_pairs={{0,4},{2,6},{4,0},{6,2},{8,12},{10,14},{12,8},{14,10},{16,20},{18,... | collective-permute-start | bytes 1572872 | tf_op jit(solution)/shard_map/ppermute | solution.py:601
  737.5 46.7 %collective-permute-start.77 = (bf16[256,1024]{1,0:T(8,128)(2,1)}, bf16[256,1024]{1,0:T(8,128)(2,1)S(1)}, u32[]{:S(2)}, u32[]{:S(2)}) collective-permute-start(bf16[256,1024]{1,0:T(8,128)(2,1)} %get-tuple-element.97), channel_id=1, source_target_pairs={{0,1},{1,0},{2,3},{3,2},{4,5},{5,4},{6,7},{7,6},{8,9},{9,8},{10,11... | collective-permute-start | bytes 1572872 | tf_op jit(solution)/shard_map/ppermute | solution.py:604
  740.8 33.9 %collective-permute-start.86 = (bf16[256,1024]{1,0:T(8,128)(2,1)S(1)}, bf16[256,1024]{1,0:T(8,128)(2,1)S(1)}, u32[]{:S(2)}, u32[]{:S(2)}) collective-permute-start(bf16[256,1024]{1,0:T(8,128)(2,1)S(1)} %add_convert_fusion.2), channel_id=1, source_target_pairs={{0,4},{2,6},{4,0},{6,2},{8,12},{10,14},{12,8},{14,10},{16,20},{18,... | collective-permute-start | bytes 1572872 | tf_op jit(solution)/shard_map/ppermute | solution.py:601
  742.3 33.6 %collective-permute-start.83 = (bf16[256,1024]{1,0:T(8,128)(2,1)S(1)}, bf16[256,1024]{1,0:T(8,128)(2,1)S(1)}, u32[]{:S(2)}, u32[]{:S(2)}) collective-permute-start(bf16[256,1024]{1,0:T(8,128)(2,1)S(1)} %add_convert_fusion.4), channel_id=1, source_target_pairs={{0,1},{1,0},{2,3},{3,2},{4,5},{5,4},{6,7},{7,6},{8,9},{9,8},{10,11... | collective-permute-start | bytes 1572872 | tf_op jit(solution)/shard_map/ppermute | solution.py:604
  752.4 76.1 %collective-permute-start.76 = (bf16[256,1024]{1,0:T(8,128)(2,1)}, bf16[256,1024]{1,0:T(8,128)(2,1)S(1)}, u32[]{:S(2)}, u32[]{:S(2)}) collective-permute-start(bf16[256,1024]{1,0:T(8,128)(2,1)} %get-tuple-element.95), channel_id=1, source_target_pairs={{0,1},{1,0},{2,3},{3,2},{4,5},{5,4},{6,7},{7,6},{8,9},{9,8},{10,11... | collective-permute-start | bytes 1572872 | tf_op jit(solution)/shard_map/ppermute | solution.py:604
  774.8 53.4 %collective-permute-start.75 = (bf16[256,1024]{1,0:T(8,128)(2,1)S(1)}, bf16[256,1024]{1,0:T(8,128)(2,1)S(1)}, u32[]{:S(2)}, u32[]{:S(2)}) collective-permute-start(bf16[256,1024]{1,0:T(8,128)(2,1)S(1)} %add_convert_fusion.8), channel_id=1, source_target_pairs={{0,1},{1,0},{2,3},{3,2},{4,5},{5,4},{6,7},{7,6},{8,9},{9,8},{10,11... | collective-permute-start | bytes 1572872 | tf_op jit(solution)/shard_map/ppermute | solution.py:604
  785.2 43.3 %collective-permute-start.78 = (bf16[256,1024]{1,0:T(8,128)(2,1)}, bf16[256,1024]{1,0:T(8,128)(2,1)S(1)}, u32[]{:S(2)}, u32[]{:S(2)}) collective-permute-start(bf16[256,1024]{1,0:T(8,128)(2,1)} %add_convert_fusion.6), channel_id=1, source_target_pairs={{0,4},{2,6},{4,0},{6,2},{8,12},{10,14},{12,8},{14,10},{16,20},{18,... | collective-permute-start | bytes 1572872 | tf_op jit(solution)/shard_map/ppermute | solution.py:601
  797.7 32.9 %collective-permute-start.94 = (bf16[1024,512]{1,0:T(8,128)(2,1)}, bf16[1024,512]{1,0:T(8,128)(2,1)}, u32[]{:S(2)}, u32[]{:S(2)}) collective-permute-start(bf16[1024,512]{1,0:T(8,128)(2,1)} %convolution_convert_fusion.2), channel_id=1, source_target_pairs={{0,1},{1,0},{2,3},{3,2},{4,5},{5,4},{6,7},{7,6},{8,9},{9,8},{10,11... | collective-permute-start | bytes 3145736 | tf_op jit(solution)/shard_map/ppermute | solution.py:604
  826.9 21.8 %collective-permute-start.88 = (bf16[512,1024]{1,0:T(8,128)(2,1)}, bf16[512,1024]{1,0:T(8,128)(2,1)}, u32[]{:S(2)}, u32[]{:S(2)}) collective-permute-start(bf16[512,1024]{1,0:T(8,128)(2,1)} %convolution_convert_fusion), channel_id=1, source_target_pairs={{0,1},{1,0},{2,3},{3,2},{4,5},{5,4},{6,7},{7,6},{8,9},{9,8},{10,11... | collective-permute-start | bytes 3145736 | tf_op jit(solution)/shard_map/ppermute | solution.py:604
  833.3 123.1 %reduce-scatter.7.cloned.1.call-start = ((), (), s32[]{:S(2)}) async-start(), calls=%async_computation.8 | async-start | bytes 2228224 | tf_op jit(solution)/shard_map/reduce_scatter | solution.py:786
  (132 other events, 1638.2 us)
Sparse Core Ops, SparseCore 0:
  10.8 44.9 all-gather.2
  57.9 39.8 all-gather.4
  262.0 77.5 reduce-scatter.16
  397.4 77.7 reduce-scatter.14
  532.6 78.2 reduce-scatter.12
  700.9 59.8 reduce-scatter.10
  833.4 58.2 reduce-scatter.8
  895.9 60.4 reduce-scatter.6

commit v2 on v1

--- a/solution.py
+++ b/solution.py
@@ -22,6 +22,7 @@
 BF = jnp.bfloat16
 F32 = jnp.float32
 VMEM_LIMIT = 60 * 1024 * 1024
+MESH = pl.DeviceIdType.MESH
 
 ANY = pl.BlockSpec(memory_space=pl.ANY)
 SMEM = pl.BlockSpec(memory_space=pltpu.SMEM)
@@ -541,9 +542,13 @@
         for m in range(GROUP):
             n = j * GROUP + m
             source = (i ^ m) * n_experts + j
-            copies.append(pltpu.make_async_copy(in_ref.at[source], outs[n].at[pl.ds(0, in_rows)], sems.at[2 * n]))
             copies.append(
-                pltpu.make_async_copy(down_ref.at[source], outs[n].at[pl.ds(in_rows, down_rows)], sems.at[2 * n + 1])
+                pltpu.make_async_copy(in_ref.at[source], outs[m].at[j, pl.ds(0, in_rows)], sems.at[2 * n])
+            )
+            copies.append(
+                pltpu.make_async_copy(
+                    down_ref.at[source], outs[m].at[j, pl.ds(in_rows, down_rows)], sems.at[2 * n + 1]
+                )
             )
     for c in copies:
         c.start()
@@ -555,20 +560,590 @@
     experts, in_rows, _ = expert_in.shape
     down_rows = expert_down.shape[1]
     n = experts // GROUP
-    flat = call(
+    return call(
         functools.partial(pack_kernel, n, in_rows, down_rows),
         "pack_weights",
-        [jax.ShapeDtypeStruct((in_rows + down_rows, D), BF)] * experts,
+        [jax.ShapeDtypeStruct((n, in_rows + down_rows, D), BF)] * GROUP,
         [SMEM, ANY, ANY],
-        [VM] * experts,
+        [VM] * GROUP,
         (idx, expert_in, expert_down),
         scratch=[pltpu.SemaphoreType.DMA((2 * experts,))],
         moved=6 << 20,
     )
-    return [[flat[j * GROUP + m] for m in range(GROUP)] for j in range(n)]
-
-
-def body(
+
+
+def place():
+    d, t = lax.axis_index("dp"), lax.axis_index("tensor")
+    return d, t, d // GROUP, d % GROUP
+
+
+def flip(v, m):
+    first, second = v % 2, (v // 2) % 2
+    if m & 1:
+        v = v + 1 - 2 * first
+    if m & 2:
+        v = v + 2 - 4 * second
+    return v
+
+
+def greet(outer, distances, tensor):
+    d, t, o, _ = place()
+    barrier = pltpu.get_barrier_semaphore()
+    count = 0
+    for m in distances:
+        pl.semaphore_signal(barrier, inc=1, device_id=(flip(d, m), t), device_id_type=MESH)
+        count += 1
+    if tensor:
+        pl.semaphore_signal(barrier, inc=1, device_id=(d, 1 - t), device_id_type=MESH)
+        count += 1
+
+    @pl.when(o > 0)
+    def _():
+        pl.semaphore_signal(barrier, inc=1, device_id=(d - GROUP, t), device_id_type=MESH)
+
+    @pl.when(o < outer - 1)
+    def _():
+        pl.semaphore_signal(barrier, inc=1, device_id=(d + GROUP, t), device_id_type=MESH)
+
+    neighbours = (o + outer - 1) // outer + (2 * outer - 2 - o) // outer
+    pl.semaphore_wait(barrier, count + neighbours)
+
+
+class Hops:
+    def __init__(self, outer, steps, sent, came):
+        d, t, o, _ = place()
+        self.moves = []
+        for n, (k, from_left, from_right, to_left, to_right) in enumerate(steps):
+            back = outer - 1 - o
+            right = pltpu.make_async_remote_copy(
+                from_left, to_left, sent.at[2 * n], came.at[2 * n], device_id=(d + GROUP, t), device_id_type=MESH
+            )
+            left = pltpu.make_async_remote_copy(
+                from_right,
+                to_right,
+                sent.at[2 * n + 1],
+                came.at[2 * n + 1],
+                device_id=(d - GROUP, t),
+                device_id_type=MESH,
+            )
+            self.moves.append((right, (o >= k - 1) & (back >= 1), o >= k))
+            self.moves.append((left, (back >= k - 1) & (o >= 1), back >= k))
+
+    def start(self):
+        for copy, sends, _ in self.moves:
+            pl.when(sends)(copy.start)
+
+    def wait(self):
+        for copy, sends, receives in self.moves:
+            pl.when(sends)(copy.wait_send)
+            pl.when(receives)(copy.wait_recv)
+
+
+def to_x(src, dst, sent, came):
+    d, t, _, _ = place()
+    return pltpu.make_async_remote_copy(src, dst, sent, came, device_id=(d, 1 - t), device_id_type=MESH)
+
+
+def to_dp(m, src, dst, sent, came):
+    d, t, _, _ = place()
+    return pltpu.make_async_remote_copy(src, dst, sent, came, device_id=(flip(d, m), t), device_id_type=MESH)
+
+
+def remote_call(kernel, name, collective_id, out_shape, in_specs, out_specs, args, scratch, flops):
+    return pl.pallas_call(
+        kernel,
+        name=name,
+        out_shape=out_shape,
+        in_specs=in_specs,
+        out_specs=out_specs,
+        scratch_shapes=list(scratch),
+        compiler_params=pltpu.CompilerParams(
+            vmem_limit_bytes=VMEM_LIMIT, collective_id=collective_id, has_side_effects=True
+        ),
+        cost_estimate=pl.CostEstimate(flops=flops, bytes_accessed=8 << 20, transcendentals=0),
+    )(*args)
+
+
+def attention_kernel(outer, q_block, n_steps, len_ref, own_ref, other_ref, w_ref, cos_ref, sin_ref, x_ref, gain_ref, *refs):
+    width = w_ref.shape[1] // 2
+    heads = width // 2
+    dy_refs, refs = refs[:2], refs[2:]
+    sources, refs = refs[:n_steps], refs[n_steps:]
+    qkv_ref, lse_ref, attn_ref, come_ref, hidden_ref, na_ref, nb_ref = refs[:7]
+    refs = refs[7:]
+    dy_outs, refs = refs[:4], refs[4:]
+    to_left, refs = refs[:n_steps], refs[n_steps:]
+    to_right, refs = refs[:n_steps], refs[n_steps:]
+    send_ref, s_hop, r_hop, s_dy, r_dy, s_at, r_at = refs
+    d, t, o, i = place()
+    length = len_ref[0]
+    rows = own_ref.shape[0]
+    groups = width // (2 * LANES)
+    greet(outer, (2,), True)
+    hops = Hops(outer, [(1, s, s, l, r) for s, l, r in zip(sources, to_left, to_right, strict=True)], s_hop, r_hop)
+    hops.start()
+    ax, bx, ay, by = dy_outs
+    dys = [
+        to_x(dy_refs[0], ax, s_dy.at[0], r_dy.at[0]),
+        to_dp(2, dy_refs[1], by, s_dy.at[1], r_dy.at[1]),
+        to_x(dy_refs[1], bx, s_dy.at[2], r_dy.at[2]),
+        to_dp(2, dy_refs[0], ay, s_dy.at[3], r_dy.at[3]),
+    ]
+
+    block = 256
+    key_lanes = lax.broadcasted_iota(jnp.int32, (block, LANES), 1) < HD
+    for part in range(2):
+        for b in range(rows // block):
+            at = pl.multiple_of((t if part == 0 else 1 - t) * rows + b * block, block)
+            projected = mm((own_ref if part == 0 else other_ref)[b * block : (b + 1) * block], w_ref[:, :width])
+            cosine, sine = cos_ref[pl.ds(at, block), :], sin_ref[pl.ds(at, block), :]
+            for g in range(groups):
+                q = projected[:, g * 2 * LANES : g * 2 * LANES + LANES]
+                kv = projected[:, g * 2 * LANES + LANES : (g + 1) * 2 * LANES]
+                q = q * cosine + swap_halves(q) * sine
+                kv = jnp.where(key_lanes, kv * cosine + swap_halves(kv) * sine, kv)
+                qkv_ref[pl.ds(at, block), g * 2 * LANES : g * 2 * LANES + LANES] = q.astype(BF)
+                qkv_ref[pl.ds(at, block), g * 2 * LANES + LANES : (g + 1) * 2 * LANES] = kv.astype(BF)
+
+    for copy in dys:
+        copy.start()
+
+    def exchange(g):
+        lanes = pl.ds(pl.multiple_of(g * LANES, LANES), LANES)
+        return to_x(send_ref.at[:, lanes], come_ref.at[:, lanes], s_at.at[g], r_at.at[g])
+
+    def per_group(g, carry):
+        q_lanes = pl.ds(pl.multiple_of(g * 2 * LANES, LANES), LANES)
+        kv_lanes = pl.ds(pl.multiple_of(g * 2 * LANES + LANES, LANES), LANES)
+        o_lanes = pl.ds(pl.multiple_of(g * LANES, LANES), LANES)
+        keys, values = doubled(qkv_ref[:, kv_lanes])
+        for b in range(2 * rows // q_block):
+            start, n_keys = b * q_block, (b + 1) * q_block
+            q = head_pair(qkv_ref[start : start + q_block, q_lanes])
+            scores = mm_nt(keys[:n_keys], q) * (1.0 / math.sqrt(HD))
+            scores = jnp.where(allowed(n_keys, q_block, start, length), scores, NEGATIVE)
+            largest = jnp.max(scores, axis=0, keepdims=True)
+            expon = jnp.exp(scores - largest)
+            totals = jnp.sum(expon, axis=0, keepdims=True)
+            probs = (expon * (1.0 / totals)).astype(BF)
+            mixed = head_join(mm_tn(probs, values[:n_keys])).astype(BF)
+            lse_ref[g, b : b + 1, :] = largest + jnp.log(totals)
+            half, inner = start // rows, start % rows
+
+            @pl.when(t == half)
+            def _():
+                attn_ref[inner : inner + q_block, o_lanes] = mixed
+
+            @pl.when(t != half)
+            def _():
+                send_ref[inner : inner + q_block, o_lanes] = mixed
+
+        exchange(g).start()
+        return carry
+
+    lax.fori_loop(0, groups, per_group, 0)
+
+    def settle(g, carry):
+        exchange(g).wait()
+        return carry
+
+    for p, normed_ref in enumerate((na_ref, nb_ref)):
+        at = slice(p * rows // 2, (p + 1) * rows // 2)
+        hidden_ref[at] = x_ref[at].astype(F32) + mm_nt(attn_ref[at], w_ref[:, width : width + heads])
+    lax.fori_loop(0, groups, settle, 0)
+    for p, normed_ref in enumerate((na_ref, nb_ref)):
+        at = slice(p * rows // 2, (p + 1) * rows // 2)
+        hidden = hidden_ref[at] + mm_nt(come_ref[at], w_ref[:, width + heads :])
+        inverse = lax.rsqrt(jnp.mean(hidden * hidden, axis=-1, keepdims=True) + EPSILON)
+        hidden_ref[at] = hidden
+        normed_ref[...] = (hidden * inverse * gain_ref[...]).astype(BF)
+    for copy in dys:
+        copy.wait()
+    hops.wait()
+
+
+def attention(outer, q_block, length, own, other, weights_full, cosine, sine, x, gain, dys, sources):
+    rows, groups = own.shape[0], weights_full.shape[1] // (4 * LANES)
+    n = len(sources)
+    piece = jax.ShapeDtypeStruct((rows // 2, D), BF)
+    weights = [jax.ShapeDtypeStruct(s.shape, BF) for s in sources]
+    out = remote_call(
+        functools.partial(attention_kernel, outer, q_block, n),
+        "attention",
+        1,
+        [
+            jax.ShapeDtypeStruct((2 * rows, groups * 2 * LANES), BF),
+            jax.ShapeDtypeStruct((groups, 2 * rows // q_block, 2 * q_block), F32),
+            jax.ShapeDtypeStruct((rows, groups * LANES), BF),
+            jax.ShapeDtypeStruct((rows, groups * LANES), BF),
+            jax.ShapeDtypeStruct((rows, D), F32),
+            piece,
+            piece,
+        ]
+        + [piece] * 4
+        + weights * 2,
+        [SMEM] + [VM] * 7 + [ANY] * (2 + n),
+        [VM] * 7 + [ANY] * (4 + 2 * n),
+        (length, own, other, weights_full, cosine, sine, x, gain.reshape(1, D), *dys, *sources),
+        [
+            pltpu.VMEM((rows, groups * LANES), BF),
+            pltpu.SemaphoreType.DMA((2 * n,)),
+            pltpu.SemaphoreType.DMA((2 * n,)),
+            pltpu.SemaphoreType.DMA((4,)),
+            pltpu.SemaphoreType.DMA((4,)),
+            pltpu.SemaphoreType.DMA((groups,)),
+            pltpu.SemaphoreType.DMA((groups,)),
+        ],
+        30 << 30,
+    )
+    return out[:7], out[7:11], out[11 : 11 + n], out[11 + n :]
+
+
+def one_hot_rows(pos, gate, j, n_rows):
+    rank = lax.broadcasted_iota(jnp.int32, (CAP, n_rows), 0)
+    chosen = rank == pos[j : j + 1, :]
+    return jnp.where(chosen, 1.0 if gate is None else gate[j : j + 1, :], 0.0).astype(BF)
+
+
+def spread_kernel(outer, steps, pos_ref, gate_ref, na_ref, nb_ref, *refs):
+    n_steps = len(steps)
+    dy_refs, refs = refs[:6], refs[6:]
+    from_left, refs = refs[:n_steps], refs[n_steps:]
+    from_right, refs = refs[:n_steps], refs[n_steps:]
+    n_ref, dyx_ref, og_ref = refs[:3]
+    refs = refs[3:]
+    to_left, refs = refs[:n_steps], refs[n_steps:]
+    to_right, refs = refs[:n_steps], refs[n_steps:]
+    held, s_hop, r_hop, s_n, r_n, s_d, r_d, l_sem = refs
+    height = na_ref.shape[0]
+    n_experts = og_ref.shape[1]
+    greet(outer, (1, 2), True)
+    n_ax = to_x(na_ref, n_ref.at[0, 1], s_n.at[0], r_n.at[0])
+    n_by = to_dp(2, nb_ref, n_ref.at[1, 2], s_n.at[1], r_n.at[1])
+    n_bx = to_x(nb_ref, n_ref.at[0, 3], s_n.at[2], r_n.at[2])
+    n_ay = to_dp(2, na_ref, n_ref.at[1, 0], s_n.at[3], r_n.at[3])
+    n_axy = to_dp(2, n_ref.at[0, 1], n_ref.at[1, 1], s_n.at[4], r_n.at[4])
+    n_bxy = to_x(n_ref.at[1, 2], n_ref.at[1, 3], s_n.at[5], r_n.at[5])
+    core = {}
+    for n, (s, p) in enumerate([(s, p) for s in range(2) for p in range(4)]):
+        source = na_ref if (s, p) == (0, 0) else nb_ref if (s, p) == (0, 2) else n_ref.at[s, p]
+        core[s, p] = to_dp(1, source, n_ref.at[2 + s, p], s_n.at[6 + n], r_n.at[6 + n])
+    for copy in (n_ax, n_by, n_bx, n_ay):
+        copy.start()
+    d_a, d_b, d_ax, d_bx, d_ay, d_by = dy_refs
+    d_axy = to_dp(2, d_ax, dyx_ref.at[0, 1], s_d.at[0], r_d.at[0])
+    d_bxy = to_x(d_by, dyx_ref.at[0, 3], s_d.at[1], r_d.at[1])
+    d_axy.start()
+    d_bxy.start()
+    d_near = [[d_a, d_ax, d_b, d_bx], [d_ay, dyx_ref.at[0, 1], d_by, dyx_ref.at[0, 3]]]
+    d_core = {}
+    for n, (s, p) in enumerate([(s, p) for s in range(2) for p in range(4)]):
+        d_core[s, p] = to_dp(1, d_near[s][p], dyx_ref.at[1 + s, p], s_d.at[2 + n], r_d.at[2 + n])
+    for key in ((0, 0), (0, 1), (0, 2), (0, 3), (1, 0), (1, 2)):
+        d_core[key].start()
+    core[0, 0].start()
+    core[0, 2].start()
+    hops = Hops(
+        outer,
+        [(k, a, b, l, r) for k, a, b, l, r in zip(steps, from_left, from_right, to_left, to_right, strict=True)],
+        s_hop,
+        r_hop,
+    )
+    hops.start()
+
+    def load(s):
+        pieces = d_near[s] if s < 2 else [dyx_ref.at[s - 1, p] for p in range(4)]
+        return [
+            pltpu.make_async_copy(piece, held.at[pl.ds(p * height, height)], l_sem.at[p])
+            for p, piece in enumerate(pieces)
+        ]
+
+    def give(s):
+        copies = load(s)
+        for c in copies:
+            c.start()
+        for c in copies:
+            c.wait()
+
+        def one(j, carry):
+            rank = lax.broadcasted_iota(jnp.int32, (CAP, 4 * height), 0)
+            chosen = rank == pos_ref[s, pl.ds(j, 1), :]
+            one_hot = jnp.where(chosen, gate_ref[s, pl.ds(j, 1), :], 0.0).astype(BF)
+            og_ref[s, j] = mm(one_hot, held[...]).astype(BF)
+            return carry
+
+        lax.fori_loop(0, n_experts, one, 0)
+
+    give(0)
+    n_ax.wait()
+    n_by.wait()
+    n_axy.start()
+    n_bxy.start()
+    core[0, 1].start()
+    core[1, 2].start()
+    d_axy.wait()
+    d_bxy.wait()
+    d_core[1, 1].start()
+    d_core[1, 3].start()
+    give(1)
+    n_bx.wait()
+    n_ay.wait()
+    core[0, 3].start()
+    core[1, 0].start()
+    for p in range(4):
+        d_core[0, p].wait()
+    give(2)
+    n_axy.wait()
+    n_bxy.wait()
+    core[1, 1].start()
+    core[1, 3].start()
+    for p in range(4):
+        d_core[1, p].wait()
+    give(3)
+    for key in core:
+        core[key].wait()
+    hops.wait()
+
+
+def spread(outer, pos, gate, normed, dys, steps, from_left, from_right):
+    height = normed[0].shape[0]
+    n, n_experts = len(steps), pos.shape[1]
+    weights = [jax.ShapeDtypeStruct(s.shape, BF) for s in from_left]
+    out = remote_call(
+        functools.partial(spread_kernel, outer, steps),
+        "spread",
+        2,
+        [
+            jax.ShapeDtypeStruct((GROUP, 4, height, D), BF),
+            jax.ShapeDtypeStruct((3, 4, height, D), BF),
+            jax.ShapeDtypeStruct((GROUP, n_experts, CAP, D), BF),
+        ]
+        + weights * 2,
+        [VM] * 2 + [ANY] * (2 + 6 + 2 * n),
+        [ANY, ANY, VM] + [ANY] * (2 * n),
+        (pos, gate, *normed, *dys, *from_left, *from_right),
+        [
+            pltpu.VMEM((4 * height, D), BF),
+            pltpu.SemaphoreType.DMA((2 * n,)),
+            pltpu.SemaphoreType.DMA((2 * n,)),
+            pltpu.SemaphoreType.DMA((14,)),
+            pltpu.SemaphoreType.DMA((14,)),
+            pltpu.SemaphoreType.DMA((10,)),
+            pltpu.SemaphoreType.DMA((10,)),
+            pltpu.SemaphoreType.DMA((4,)),
+        ],
+        12 << 30,
+    )
+    return out[0], out[2], out[3 : 3 + n], out[3 + n :]
+
+
+def hand_out_kernel(outer, steps, pos_ref, na_ref, nb_ref, n_ref, *refs):
+    n_steps = len(steps)
+    from_left, refs = refs[:n_steps], refs[n_steps:]
+    from_right, refs = refs[:n_steps], refs[n_steps:]
+    x_ref, refs = refs[0], refs[1:]
+    to_left, refs = refs[:n_steps], refs[n_steps:]
+    to_right, refs = refs[:n_steps], refs[n_steps:]
+    held, s_hop, r_hop, l_sem = refs
+    height = na_ref.shape[0]
+    n_experts = x_ref.shape[1]
+    greet(outer, (), False)
+    hops = Hops(
+        outer,
+        [(k, a, b, l, r) for k, a, b, l, r in zip(steps, from_left, from_right, to_left, to_right, strict=True)],
+        s_hop,
+        r_hop,
+    )
+    hops.start()
+
+    def load(s):
+        pieces = [na_ref, n_ref.at[0, 1], nb_ref, n_ref.at[0, 3]] if s == 0 else [n_ref.at[s, p] for p in range(4)]
+        return [
+            pltpu.make_async_copy(piece, held.at[s % 2, pl.ds(p * height, height)], l_sem.at[s % 2, p])
+            for p, piece in enumerate(pieces)
+        ]
+
+    for c in load(0):
+        c.start()
+    for s in range(GROUP):
+        if s + 1 < GROUP:
+            for c in load(s + 1):
+                c.start()
+        for c in load(s):
+            c.wait()
+
+        def one(j, carry, s=s):
+            rank = lax.broadcasted_iota(jnp.int32, (CAP, 4 * height), 0)
+            one_hot = jnp.where(rank == pos_ref[s, pl.ds(j, 1), :], 1.0, 0.0).astype(BF)
+            x_ref[s, j] = mm(one_hot, held[s % 2]).astype(BF)
+            return carry
+
+        lax.fori_loop(0, n_experts, one, 0)
+    hops.wait()
+
+
+def hand_out(outer, pos, normed, gathered, steps, from_left, from_right):
+    height = normed[0].shape[0]
+    n, n_experts = len(steps), pos.shape[1]
+    weights = [jax.ShapeDtypeStruct(s.shape, BF) for s in from_left]
+    out = remote_call(
+        functools.partial(hand_out_kernel, outer, steps),
+        "hand_out",
+        3,
+        [jax.ShapeDtypeStruct((GROUP, n_experts, CAP, D), BF)] + weights * 2,
+        [VM] + [ANY] * (3 + 2 * n),
+        [VM] + [ANY] * (2 * n),
+        (pos, *normed, gathered, *from_left, *from_right),
+        [
+            pltpu.VMEM((2, 4 * height, D), BF),
+            pltpu.SemaphoreType.DMA((2 * n,)),
+            pltpu.SemaphoreType.DMA((2 * n,)),
+            pltpu.SemaphoreType.DMA((2, 4)),
+        ],
+        12 << 30,
+    )
+    return out[0], out[1 : 1 + n], out[1 + n :]
+
+
+def expert_step_kernel(j, outer, in_rows, down_rows, steps, x_ref, g_ref, own, *refs):
+    n_hops, n_steps = outer - 1, len(steps)
+    lefts, refs = refs[:n_hops], refs[n_hops:]
+    rights, refs = refs[:n_hops], refs[n_hops:]
+    from_left, refs = refs[:n_steps], refs[n_steps:]
+    from_right, refs = refs[:n_steps], refs[n_steps:]
+    y_ref, dx_ref, dw_ref = refs[:3]
+    refs = refs[3:]
+    to_left, refs = refs[:n_steps], refs[n_steps:]
+    to_right, refs = refs[:n_steps], refs[n_steps:]
+    x_all, g_all, w_in, w_down, act_all, gug_all, sem_x, sem_g, sem_w, sem_d, s_hop, r_hop = refs
+    _, _, o, i = place()
+    if n_steps:
+        greet(outer, (), False)
+        hops = Hops(
+            outer,
+            [(k, a, b, l, r) for k, a, b, l, r in zip(steps, from_left, from_right, to_left, to_right, strict=True)],
+            s_hop,
+            r_hop,
+        )
+        hops.start()
+
+    def rows_of(source, held, sems):
+        return [
+            pltpu.make_async_copy(source.at[n, j], held.at[pl.ds(n * CAP, CAP)], sems.at[n]) for n in range(GROUP)
+        ]
+
+    def weight_copies(source, at, slot):
+        made = []
+        for m in range(GROUP):
+            where = at * GROUP + flip(i, m)
+            made.append(
+                pltpu.make_async_copy(
+                    source.at[m, pl.ds(0, in_rows)],
+                    w_in.at[pl.ds(pl.multiple_of(where * in_rows, in_rows), in_rows)],
+                    sem_w.at[slot * GROUP + m],
+                )
+            )
+            made.append(
+                pltpu.make_async_copy(
+                    source.at[m, pl.ds(in_rows, down_rows)],
+                    w_down.at[pl.ds(pl.multiple_of(where * down_rows, down_rows), down_rows)],
+                    sem_d.at[slot * GROUP + m],
+                )
+            )
+        return made
+
+    def each_weight(act):
+        act(weight_copies(own, o, 0))
+        for k in range(1, outer):
+
+            @pl.when(o >= k)
+            def _():
+                act(weight_copies(lefts[k - 1], o - k, k))
+
+            @pl.when(o + k < outer)
+            def _():
+                act(weight_copies(rights[k - 1], o + k, n_hops + k))
+
+    def start(made):
+        for c in made:
+            c.start()
+
+    def wait(made):
+        for c in made:
+            c.wait()
+
+    each_weight(start)
+    copy_x, copy_g = rows_of(x_ref, x_all, sem_x), rows_of(g_ref, g_all, sem_g)
+    start(copy_x)
+    start(copy_g)
+    each_weight(wait)
+    wait(copy_x)
+    wait(copy_g)
+
+    def per_slot(s, carry):
+        at = pl.ds(pl.multiple_of(s * CAP, CAP), CAP)
+        gate_up = mm(x_all[at, :], w_in[...])
+        g, u = gate_up[:, :FF], gate_up[:, FF:]
+        sigma = 1.0 / (1.0 + jnp.exp(-g))
+        silu = g * sigma
+        act = (silu * u).astype(BF)
+        act_all[at, :] = act
+        y_ref[s] = mm(act, w_down[...]).astype(BF)
+        act_grad = mm_nt(g_all[at, :], w_down[...])
+        gug_all[at, :FF] = (act_grad * u * sigma * (1.0 + g * (1.0 - sigma))).astype(BF)
+        gug_all[at, FF:] = (act_grad * silu).astype(BF)
+        dx_ref[s] = mm_nt(gug_all[at, :], w_in[...]).astype(BF)
+        return carry
+
+    lax.fori_loop(0, GROUP, per_slot, 0)
+    for c in range(outer):
+        part = mm_tn(x_all[:, c * GROUP * in_rows : (c + 1) * GROUP * in_rows], gug_all[...]).astype(BF)
+        for r in range(GROUP):
+            dw_ref[c, flip(i, r), :in_rows, :] = part[r * in_rows : (r + 1) * in_rows]
+        part = mm_tn(act_all[:, c * GROUP * down_rows : (c + 1) * GROUP * down_rows], g_all[...]).astype(BF)
+        for r in range(GROUP):
+            dw_ref[c, flip(i, r), in_rows:, :] = part[r * down_rows : (r + 1) * down_rows]
+    if n_steps:
+        hops.wait()
+
+
+def expert_step(j, outer, in_rows, down_rows, x, g, own, lefts, rights, steps, from_left, from_right):
+    n_hops, n = outer - 1, len(steps)
+    total = GROUP * CAP
+    packed = in_rows + down_rows
+    weights = [jax.ShapeDtypeStruct(s.shape, BF) for s in from_left]
+    shapes = [
+        jax.ShapeDtypeStruct((GROUP, CAP, D), BF),
+        jax.ShapeDtypeStruct((GROUP, CAP, D), BF),
+        jax.ShapeDtypeStruct((outer, GROUP, packed, D), BF),
+    ] + weights * 2
+    in_specs = [ANY] * (3 + 2 * n_hops + 2 * n)
+    out_specs = [VM] * 3 + [ANY] * (2 * n)
+    args = (x, g, own, *lefts, *rights, *from_left, *from_right)
+    scratch = [
+        pltpu.VMEM((total, D), BF),
+        pltpu.VMEM((total, D), BF),
+        pltpu.VMEM((D, 2 * FF), BF),
+        pltpu.VMEM((FF, D), BF),
+        pltpu.VMEM((total, FF), BF),
+        pltpu.VMEM((total, 2 * FF), BF),
+        pltpu.SemaphoreType.DMA((GROUP,)),
+        pltpu.SemaphoreType.DMA((GROUP,)),
+        pltpu.SemaphoreType.DMA(((1 + 2 * n_hops) * GROUP,)),
+        pltpu.SemaphoreType.DMA(((1 + 2 * n_hops) * GROUP,)),
+        pltpu.SemaphoreType.DMA((max(1, 2 * n),)),
+        pltpu.SemaphoreType.DMA((max(1, 2 * n),)),
+    ]
+    kernel = functools.partial(expert_step_kernel, j, outer, in_rows, down_rows, steps)
+    flops = 18 * total * D * FF
+    if n:
+        out = remote_call(kernel, "expert_step", 4 + j, shapes, in_specs, out_specs, args, scratch, flops)
+    else:
+        out = call(kernel, "expert_last", shapes, in_specs, out_specs, args, scratch=scratch, flops=flops, moved=15 << 20)
+    return out[:3], out[3 : 3 + n], out[3 + n :]
+
+
+def layer(
     tokens,
     cotangent,
     lengths,
@@ -603,16 +1178,10 @@
     def beside(v):
         return lax.ppermute(v, "tensor", [(0, 1), (1, 0)])
 
-    def chain(v):
+    def hop(pairs):
         up = [(a, a + GROUP) for a in range(n_dp - GROUP)]
         down = [(b, a) for a, b in up]
-        lefts, rights = [], []
-        a = b = v
-        for _ in range(outer - 1):
-            a, b = lax.ppermute(a, "dp", up), lax.ppermute(b, "dp", down)
-            lefts.append(a)
-            rights.append(b)
-        return lefts, rights
+        return [(lax.ppermute(a, "dp", up), lax.ppermute(b, "dp", down)) for a, b in pairs]
 
     def gather_group(pieces):
         if pair:
@@ -624,42 +1193,6 @@
             slot = lax.all_gather(pieces[0], "tensor", axis=0, tiled=True)
             slots = [[slot], [across(slot, 2)]]
         return slots + [[across(p, 1) for p in s] for s in slots]
-
-    qkv_full = lax.all_gather(qkv_weight.reshape(qkv_weight.shape[0], width), "dp", axis=0, tiled=True)
-    out_full = lax.all_gather(attn_out_weight.T, "dp", axis=0, tiled=True)
-    blocks = pack_weights(idx, expert_in_weight, expert_out_weight)
-    moved_weights = []
-    for per_expert in blocks:
-        own = jnp.stack([per_expert[0]] + [across(per_expert[m], m) for m in range(1, GROUP)])
-        moved_weights.append((own, *chain(own)))
-    if pair:
-        out_parts = [out_full, beside(out_full)]
-    else:
-        gathered = lax.all_gather(out_full, "tensor", axis=0)
-        out_parts = [gathered[k] for k in range(n_tensor)]
-
-    x = tokens.astype(F32)
-    inverse_one = lax.rsqrt(jnp.mean(x * x, axis=-1, keepdims=True) + EPSILON)
-    normed_one = (x * inverse_one * first_gain).astype(BF)
-    if pair:
-        other = beside(normed_one)
-        normed_all = jnp.where(
-            t == 0,
-            jnp.concatenate([normed_one, other], axis=0),
-            jnp.concatenate([other, normed_one], axis=0),
-        )
-    else:
-        normed_all = lax.all_gather(normed_one, "tensor", axis=0, tiled=True)
-    cosine, sine = rope_tables(slot_rows)
-    qkv = qkv_project(normed_all, qkv_full, cosine, sine)
-    *attended, lse = attend(idx, qkv, 2 if pair else 1, q_block)
-    if pair:
-        attn_parts = [attended[0], beside(attended[1])]
-    else:
-        heads = attended[0].shape[1]
-        exchanged = lax.all_to_all(attended[0].reshape(n_tensor, rows, heads), "tensor", 0, 0)
-        attn_parts = [exchanged[k] for k in range(n_tensor)]
-    hidden, *normed_two = project_out(tokens, second_gain, attn_parts, out_parts, 2 if pair else 1)
 
     positions = t * rows + jnp.arange(rows, dtype=jnp.int32)
     valid_rows = positions < length
@@ -690,21 +1223,134 @@
     pos = jnp.where(named, ranks, -1.0).astype(jnp.int32)
     pos_columns, gate_columns = jnp.swapaxes(pos, 1, 2), jnp.swapaxes(own_gates, 1, 2)
 
+    x = tokens.astype(F32)
+    inverse_one = lax.rsqrt(jnp.mean(x * x, axis=-1, keepdims=True) + EPSILON)
+    normed_one = (x * inverse_one * first_gain).astype(BF)
+    cosine, sine = rope_tables(slot_rows)
     dy = jnp.where(valid_rows[:, None], cotangent, jnp.zeros_like(cotangent))
-    dy_slots = gather_group([dy[:half], dy[half:]] if pair else [dy])
-    out_grads = [dispatch(pos[s], own_gates[s], dy_slots[s], True) for s in range(GROUP)]
-    normed_slots = gather_group(normed_two)
-    expert_rows = [dispatch(pos[s], own_gates[s], normed_slots[s], False) for s in range(GROUP)]
-
     expert_outs, row_grads, weight_grads = [], [], []
-    for j in range(own_experts):
-        own, lefts, rights = moved_weights[j]
-        y, dx, dw = expert(
-            idx, j, outer, in_rows, down_rows, expert_rows, out_grads, own, lefts, rights
+    if pair and outer == 4:
+        other = beside(normed_one)
+        out_shard = attn_out_weight.T
+        shards = jnp.concatenate([qkv_weight.reshape(-1, width), out_shard, beside(out_shard)], axis=1)
+        weights_full = lax.all_gather(shards, "dp", axis=0, tiled=True)
+        by_distance = pack_weights(idx, expert_in_weight, expert_out_weight)
+        by_distance = [by_distance[0]] + [across(by_distance[m], m) for m in range(1, GROUP)]
+        own_weights = [jnp.stack([v[j] for v in by_distance]) for j in range(own_experts)]
+        dys = [dy[:half], dy[half:]]
+        main, dy_moved, one_l, one_r = attention(
+            outer, q_block, lengths, normed_one, other, weights_full, cosine, sine, tokens, second_gain, dys, own_weights[:3]
         )
-        expert_outs.append(y)
-        row_grads.append(dx)
-        weight_grads.append(dw)
+        qkv, lse, attn_own, attn_other, hidden, *normed_two = main
+        attn_parts = [attn_own, attn_other]
+        gathered, out_grads, moved_l, moved_r = spread(
+            outer,
+            pos,
+            own_gates,
+            normed_two,
+            [*dys, *dy_moved],
+            (1, 2, 2),
+            [own_weights[3], one_l[0], one_l[1]],
+            [own_weights[3], one_r[0], one_r[1]],
+        )
+        one_l, one_r = [*one_l, moved_l[0]], [*one_r, moved_r[0]]
+        two_l, two_r = [*moved_l[1:]], [*moved_r[1:]]
+        expert_rows, moved_l, moved_r = hand_out(
+            outer, pos, normed_two, gathered, (3, 2), [two_l[0], one_l[2]], [two_r[0], one_r[2]]
+        )
+        three_l, three_r = [moved_l[0]], [moved_r[0]]
+        two_l.append(moved_l[1])
+        two_r.append(moved_r[1])
+        plans = [
+            ((3, 2), [two_l[1], one_l[3]], [two_r[1], one_r[3]]),
+            ((3,), [two_l[2]], [two_r[2]]),
+            None,
+            ((), [], []),
+        ]
+        for j in range(own_experts):
+            plan = plans[j] or ((3,), [two_l[3]], [two_r[3]])
+            (y, dx, dw), moved_l, moved_r = expert_step(
+                j,
+                outer,
+                in_rows,
+                down_rows,
+                expert_rows,
+                out_grads,
+                own_weights[j],
+                [one_l[j], two_l[j], three_l[j]],
+                [one_r[j], two_r[j], three_r[j]],
+                *plan,
+            )
+            three_l.extend(moved_l[:1])
+            three_r.extend(moved_r[:1])
+            two_l.extend(moved_l[1:])
+            two_r.extend(moved_r[1:])
+            expert_outs.append(y)
+            row_grads.append(dx)
+            weight_grads.append(dw)
+        qkv_full = weights_full[:, :width]
+        out_parts = [weights_full[:, width : width + width // 2], weights_full[:, width + width // 2 :]]
+    else:
+        qkv_full = lax.all_gather(qkv_weight.reshape(qkv_weight.shape[0], width), "dp", axis=0, tiled=True)
+        out_full = lax.all_gather(attn_out_weight.T, "dp", axis=0, tiled=True)
+        by_distance = pack_weights(idx, expert_in_weight, expert_out_weight)
+        by_distance = [by_distance[0]] + [across(by_distance[m], m) for m in range(1, GROUP)]
+        own_weights = [jnp.stack([v[j] for v in by_distance]) for j in range(own_experts)]
+        hops = [hop([(own, own) for own in own_weights])]
+        if pair:
+            out_parts = [out_full, beside(out_full)]
+        else:
+            gathered = lax.all_gather(out_full, "tensor", axis=0)
+            out_parts = [gathered[k] for k in range(n_tensor)]
+
+        if pair:
+            other = beside(normed_one)
+            normed_all = jnp.where(
+                t == 0,
+                jnp.concatenate([normed_one, other], axis=0),
+                jnp.concatenate([other, normed_one], axis=0),
+            )
+        else:
+            normed_all = lax.all_gather(normed_one, "tensor", axis=0, tiled=True)
+        qkv = qkv_project(normed_all, qkv_full, cosine, sine)
+        *attended, lse = attend(idx, qkv, 2 if pair else 1, q_block)
+        if pair:
+            attn_parts = [attended[0], beside(attended[1])]
+        else:
+            heads = attended[0].shape[1]
+            exchanged = lax.all_to_all(attended[0].reshape(n_tensor, rows, heads), "tensor", 0, 0)
+            attn_parts = [exchanged[k] for k in range(n_tensor)]
+        attn_parts, hops[0] = lax.optimization_barrier((attn_parts, hops[0]))
+        if outer > 2:
+            hops.append(hop(hops[0]))
+        hidden, *normed_two = project_out(tokens, second_gain, attn_parts, out_parts, 2 if pair else 1)
+
+        dy_slots = gather_group([dy[:half], dy[half:]] if pair else [dy])
+        out_grads = [dispatch(pos[s], own_gates[s], dy_slots[s], True) for s in range(GROUP)]
+        normed_slots = gather_group(normed_two)
+        normed_slots, out_grads, hops = lax.optimization_barrier((normed_slots, out_grads, hops))
+        while len(hops) < outer - 1:
+            hops.append(hop(hops[-1]))
+        expert_rows = [dispatch(pos[s], own_gates[s], normed_slots[s], False) for s in range(GROUP)]
+
+        for j in range(own_experts):
+            if j:
+                idx, expert_outs[-1] = lax.optimization_barrier((idx, expert_outs[-1]))
+            y, dx, dw = expert(
+                idx,
+                j,
+                outer,
+                in_rows,
+                down_rows,
+                expert_rows,
+                out_grads,
+                own_weights[j],
+                [h[j][0] for h in hops],
+                [h[j][1] for h in hops],
+            )
+            expert_outs.append(y)
+            row_grads.append(dx)
+            weight_grads.append(dw)
 
     def sum_group(sources, scaled):
         def part(s, add, n_outs):
@@ -822,7 +1468,7 @@
         P("tensor", "dp", None),
     )
     return jax.shard_map(
-        body,
+        layer,
         mesh=mesh,
         in_specs=placed,
         out_specs=(

time: 980 us -> 697 us (0.71)
  waiting for transfers between devices: 436 us -> 135 us
  Pallas kernels: 255 us -> 393 us
  starting transfers between devices: 151 us -> 49.5 us
  local copies, waits for them, and re-layouts: 43.7 us -> 29.7 us
    pallas_call x2 -> x6, Pallas kernels: 26.8 us -> 280 us  [remote_call(): pl.pallas_call(kernel, name=name, out_shape=out_shape, in_specs=in_specs,...]
    ppermute x24 -> x0, waiting for transfers between devices: 250 us -> none  [chain(): a, b = (lax.ppermute(a, 'dp', up), lax.ppermute(b, 'dp', down))]
    pallas_call x23 -> x11, Pallas kernels: 204 us -> 89.3 us  [call(): pl.pallas_call(kernel, name=name, out_shape=out_shape, in_specs=in_specs,...]
    ppermute x24 -> x0, starting transfers between devices: 67.3 us -> none  [chain(): a, b = (lax.ppermute(a, 'dp', up), lax.ppermute(b, 'dp', down))]
    ppermute x63 -> x32, waiting for transfers between devices: 95.3 us -> 53.8 us  [across(): return lax.ppermute(v, 'dp', [(a, a ^ m) for a in range(n_dp)])]
    ppermute x63 -> x32, starting transfers between devices: 65.6 us -> 38.4 us  [across(): return lax.ppermute(v, 'dp', [(a, a ^ m) for a in range(n_dp)])]
    squeeze x10 -> x0, local copies, waits for them, and re-layouts: 15 us -> none  [the longest x5 8.63 us: body(): pos[s]]
    ppermute x20 -> x13, waiting for transfers between devices: 57.9 us -> 52 us  [beside(): return lax.ppermute(v, 'tensor', [(0, 1), (1, 0)])]
  transfers between devices with their start and end apart: 115 -> 52, of which waited for: 41 -> 17; matrix products, arithmetic and copies ran while one was open for 10% -> 13% of each run, Pallas kernels for 24% -> 29%
where the time goes in v2:
time: 697 us; the launch traced here: 685 us
  Pallas kernels  393 us (56%)
  waiting for transfers between devices  135 us (19%)
  starting transfers between devices  49.5 us (7%)
  other arithmetic  41.2 us (6%)
  local copies, waits for them, and re-layouts  29.7 us (4%)
  matrix products  21 us (3%)
  between operations  15.9 us (2%)
    pallas_call x6, Pallas kernels, remote_call(): pl.pallas_call(kernel, name=name, out_shape=out_shape, in_specs=in_specs,...  280 us
    pallas_call x11, Pallas kernels, call(): pl.pallas_call(kernel, name=name, out_shape=out_shape, in_specs=in_specs,...  89.3 us
    ppermute x32, waiting for transfers between devices, across(): return lax.ppermute(v, 'dp', [(a, a ^ m) for a in range(n_dp)])  53.8 us
    ppermute x13, waiting for transfers between devices, beside(): return lax.ppermute(v, 'tensor', [(0, 1), (1, 0)])  52 us
    ppermute x32, starting transfers between devices, across(): return lax.ppermute(v, 'dp', [(a, a ^ m) for a in range(n_dp)])  38.4 us
    reduce_scatter x1, waiting for transfers between devices, layer(): lax.psum_scatter(qkv_part.astype(BF), 'dp', scatter_dimension=0, tiled=True)  29.1 us
    pallas_call x1, Pallas kernels, attend_back(): pl.pallas_call(functools.partial(attend_back_kernel, q_block, parts), nam...  23.9 us
  transfers between devices with their start and end apart: 52, of which 17 were waited for; matrix products, arithmetic and copies ran while one was open for 13% of the time, Pallas kernels for 29%

profile of v2, /device:TPU:9, one launch (start us, length us, event | category | flops | bytes accessed | tf_op | source)
XLA Modules:
  0.0 685.5 jit_solution(17517777748490933913)
XLA Ops:
  10.6 1.6 pad_maximum_fusion.7
  15.8 1.5 fusion.7
  20.1 4.6 pack_weights.1
  24.6 2.5 collective-permute-start.2
  29.6 1.9 fusion.29
  33.3 18.8 %collective-permute-done.6 = bf16[32,1024]{1,0:T(8,128)(2,1)S(1)} collective-permute-done((bf16[32,1024]{1,0:T(8,128)(2,1)S(1)}, bf16[32,1024]{1,0:T(8,128)(2,1)S(1)}, u32[]{:S(2)}, u32[]{:S(2)}) %collective-permute-start.6) | collective-permute-done | bytes 65568 | tf_op jit(solution)/shard_map/ppermute | solution.py:1176
  52.1 1.7 collective-permute-start.8
  53.7 1.9 pad_maximum_fusion.5
  55.6 2.1 collective-permute-start.4
  64.5 11.9 %collective-permute-done.4 = bf16[4,96,1024]{2,1,0:T(8,128)(2,1)} collective-permute-done((bf16[4,96,1024]{2,1,0:T(8,128)(2,1)}, bf16[4,96,1024]{2,1,0:T(8,128)(2,1)}, u32[]{:S(2)}, u32[]{:S(2)}) %collective-permute-start.4) | collective-permute-done | bytes 786464 | tf_op jit(solution)/shard_map/ppermute | solution.py:1176
  81.1 60.1 %attention.1 = (bf16[1024,1024]{1,0:T(8,128)(2,1)}, f32[4,4,512]{2,1,0:T(4,128)}, bf16[512,512]{1,0:T(8,128)(2,1)}, bf16[512,512]{1,0:T(8,128)(2,1)}, f32[512,10...) custom-call(s32[1]{0:T(128)} %copy.48.len_ref, ...), custom_call_target="tpu_custom_call" | custom-call | flops 32212254720 | bytes 8388608 | tf_op jit(solution)/shard_map/attention/pallas_call | solution.py:653
  141.2 58.6 %spread.1 = (bf16[4,4,256,1024]{3,2,1,0:T(8,128)(2,1)}, bf16[3,4,256,1024]{3,2,1,0:T(8,128)(2,1)}, bf16[4,4,288,1024]{3,2,1,0:T(8,128)(2,1)}, bf16[4,96,1024]{2,...) custom-call(s32[4,4,1024]{2,1,0:T(4,128)} %copy.42.pos_ref, ...), custom_call_target="tpu_custom_call" | custom-call | flops 12884901888 | bytes 8388608 | tf_op jit(solution)/shard_map/spread/pallas_call | solution.py:653
  199.8 37.4 %hand_out.1 = (bf16[4,4,288,1024]{3,2,1,0:T(8,128)(2,1)}, bf16[4,96,1024]{2,1,0:T(8,128)(2,1)}, bf16[4,96,1024]{2,1,0:T(8,128)(2,1)}, bf16[4,96,1024]{2,1,0:T(8,128)(2,1)}, bf16[4,96,1024]{2,1,0:T(8,128)(2,1)}) custom-call(s32[4,4,1024]{2,1,0:T(4,128)} %copy.42.pos_ref, bf16[256,1024]{1,0:T(8,128)(2,1)} %get-tuple-element.90.na_ref, ...), custom_call_target="tpu_custom_call" | custom-call | flops 12884901888 | bytes 8388608 | tf_op jit(solution)/shard_map/hand_out/pallas_call | solution.py:653
  237.2 37.6 %expert_step.3 = (bf16[4,288,1024]{2,1,0:T(8,128)(2,1)}, bf16[4,288,1024]{2,1,0:T(8,128)(2,1)}, bf16[4,4,96,1024]{3,2,1,0:T(8,128)(2,1)}, bf16[4,96,1024]{2,1,0:...) custom-call(bf16[4,4,288,1024]{3,2,1,0:T(8,128)(2,1)} %get-tuple-element.105, ...), custom_call_target="tpu_custom_call" | custom-call | flops 10871635968 | bytes 8388608 | tf_op jit(solution)/shard_map/expert_step/pallas_call | solution.py:653
  274.9 33.0 %expert_step.4 = (bf16[4,288,1024]{2,1,0:T(8,128)(2,1)}, bf16[4,288,1024]{2,1,0:T(8,128)(2,1)}, bf16[4,4,96,1024]{3,2,1,0:T(8,128)(2,1)}, bf16[4,96,1024]{2,1,0:T(8,128)(2,1)}, bf16[4,96,1024]{2,1,0:T(8,128)(2,1)}) custom-call(bf16[4,4,288,1024]{3,2,1,0:T(8,128)(2,1)} %get-tuple-element.105.x_ref, bf16[4,4,288,1024]{3,2,1,0:T(8,128)(2,1)} %get-tuple-element.106.g_ref, ...), custom_call_target="tpu_custom_call" | custom-call | flops 10871635968 | bytes 8388608 | tf_op jit(solution)/shard_map/expert_step/pallas_call | solution.py:653
  308.0 53.3 %expert_step.5 = (bf16[4,288,1024]{2,1,0:T(8,128)(2,1)}, bf16[4,288,1024]{2,1,0:T(8,128)(2,1)}, bf16[4,4,96,1024]{3,2,1,0:T(8,128)(2,1)}, bf16[4,96,1024]{2,1,0:T(8,128)(2,1)}, bf16[4,96,1024]{2,1,0:T(8,128)(2,1)}) custom-call(bf16[4,4,288,1024]{3,2,1,0:T(8,128)(2,1)} %get-tuple-element.105.x_ref, bf16[4,4,288,1024]{3,2,1,0:T(8,128)(2,1)} %get-tuple-element.106.g_ref, ...), custom_call_target="tpu_custom_call" | custom-call | flops 10871635968 | bytes 8388608 | tf_op jit(solution)/shard_map/expert_step/pallas_call | solution.py:653
  364.2 19.2 %expert_last.1 = (bf16[4,288,1024]{2,1,0:T(8,128)(2,1)}, bf16[4,288,1024]{2,1,0:T(8,128)(2,1)}, bf16[4,4,96,1024]{3,2,1,0:T(8,128)(2,1)}) custom-call(bf16[4,4,288,1024]{3,2,1,0:T(8,128)(2,1)} %get-tuple-element.105.x_ref, bf16[4,4,288,1024]{3,2,1,0:T(8,128)(2,1)} %get-tuple-element.106.g_ref, bf16[4,96,1024]{2,1,0:T(8,128)(2,1)} %pad_maximum_fusion.4.refs_6_.refs_9_.own, ...), custom_call_target="tpu_custom_call" | custom-call | flops 10871635968 | bytes 15728640 | tf_op jit(solution)/shard_map/expert_last/pallas_call | solution.py:45
  383.4 7.2 %combine.4 = bf16[1024,1024]{1,0:T(8,128)(2,1)} custom-call(s32[1024,4]{1,0:T(8,128)} %get-tuple-element.170.pos_ref, f32[1024,4]{1,0:T(8,128)} %get-tuple-element.166.gate_ref, bf16[4,288,1024]{2,1,0:T(8,128)(2,1)} %get-tuple-element.135.refs_0_, bf16[4,288,1024]{2,1,0:T(8,128)(2,1)} %get-tuple-element.136.refs_1_, ...), custom_call_target="tpu_custom_call" | custom-call | flops 2415919104 | bytes 5242880 | tf_op jit(solution)/shard_map/combine/pallas_call | solution.py:45
  390.6 5.4 collective-permute-start.17
  396.0 7.1 %combine.6 = bf16[1024,1024]{1,0:T(8,128)(2,1)} custom-call(s32[1024,4]{1,0:T(8,128)} %get-tuple-element.171.pos_ref, f32[1024,4]{1,0:T(8,128)} %get-tuple-element.167.gate_ref, bf16[4,288,1024]{2,1,0:T(8,128)(2,1)} %get-tuple-element.135.refs_0_, bf16[4,288,1024]{2,1,0:T(8,128)(2,1)} %get-tuple-element.136.refs_1_, ...), custom_call_target="tpu_custom_call" | custom-call | flops 2415919104 | bytes 5242880 | tf_op jit(solution)/shard_map/combine/pallas_call | solution.py:45
  403.3 7.1 %combine_scaled.4 = bf16[1024,1024]{1,0:T(8,128)(2,1)} custom-call(s32[1024,4]{1,0:T(8,128)} %get-tuple-element.170.pos_ref, f32[1024,4]{1,0:T(8,128)} %get-tuple-element.166.gate_ref, bf16[4,288,1024]{2,1,0:T(8,128)(2,1)} %get-tuple-element.113.refs_0_, bf16[4,288,1024]{2,1,0:T(8,128)(2,1)} %get-tuple-element.118.refs_1_, ...), custom_call_target="tpu_custom_call" | custom-call | flops 2415919104 | bytes 5242880 | tf_op jit(solution)/shard_map/combine_scaled/pallas_call | solution.py:45
  410.9 7.3 %combine_scaled.6 = bf16[1024,1024]{1,0:T(8,128)(2,1)} custom-call(s32[1024,4]{1,0:T(8,128)} %get-tuple-element.171.pos_ref, f32[1024,4]{1,0:T(8,128)} %get-tuple-element.167.gate_ref, bf16[4,288,1024]{2,1,0:T(8,128)(2,1)} %get-tuple-element.113.refs_0_, bf16[4,288,1024]{2,1,0:T(8,128)(2,1)} %get-tuple-element.118.refs_1_, ...), custom_call_target="tpu_custom_call" | custom-call | flops 2415919104 | bytes 5242880 | tf_op jit(solution)/shard_map/combine_scaled/pallas_call | solution.py:45
  419.4 3.0 fusion.38
  422.4 7.4 %combine.5 = (bf16[256,1024]{1,0:T(8,128)(2,1)}, bf16[256,1024]{1,0:T(8,128)(2,1)}, bf16[256,1024]{1,0:T(8,128)(2,1)}, bf16[256,1024]{1,0:T(8,128)(2,1)}) custom-call(s32[1024,4]{1,0:T(8,128)} %get-tuple-element.173.pos_ref, f32[1024,4]{1,0:T(8,128)} %get-tuple-element.169.gate_ref, bf16[4,288,1024]{2,1,0:T(8,128)(2,1)} %get-tuple-element.135.refs_0_, ...), custom_call_target="tpu_custom_call" | custom-call | flops 2415919104 | bytes 5242880 | tf_op jit(solution)/shard_map/combine/pallas_call | solution.py:45
  431.1 7.8 %combine.7 = (bf16[256,1024]{1,0:T(8,128)(2,1)}, bf16[256,1024]{1,0:T(8,128)(2,1)}, bf16[256,1024]{1,0:T(8,128)(2,1)}, bf16[256,1024]{1,0:T(8,128)(2,1)}) custom-call(s32[1024,4]{1,0:T(8,128)} %get-tuple-element.172.pos_ref, f32[1024,4]{1,0:T(8,128)} %get-tuple-element.168.gate_ref, bf16[4,288,1024]{2,1,0:T(8,128)(2,1)} %get-tuple-element.135.refs_0_, ...), custom_call_target="tpu_custom_call" | custom-call | flops 2415919104 | bytes 5242880 | tf_op jit(solution)/shard_map/combine/pallas_call | solution.py:45
  440.3 7.5 %combine_scaled.5 = (bf16[256,1024]{1,0:T(8,128)(2,1)}, bf16[256,1024]{1,0:T(8,128)(2,1)}, bf16[256,1024]{1,0:T(8,128)(2,1)}, bf16[256,1024]{1,0:T(8,128)(2,1)}) custom-call(s32[1024,4]{1,0:T(8,128)} %get-tuple-element.173.pos_ref, f32[1024,4]{1,0:T(8,128)} %get-tuple-element.169.gate_ref, bf16[4,288,1024]{2,1,0:T(8,128)(2,1)} %get-tuple-element.113.refs_0_, ...), custom_call_target="tpu_custom_call" | custom-call | flops 2415919104 | bytes 5242880 | tf_op jit(solution)/shard_map/combine_scaled/pallas_call | solution.py:45
  449.5 7.4 %combine_scaled.7 = (bf16[256,1024]{1,0:T(8,128)(2,1)}, bf16[256,1024]{1,0:T(8,128)(2,1)}, bf16[256,1024]{1,0:T(8,128)(2,1)}, bf16[256,1024]{1,0:T(8,128)(2,1)}) custom-call(s32[1024,4]{1,0:T(8,128)} %get-tuple-element.172.pos_ref, f32[1024,4]{1,0:T(8,128)} %get-tuple-element.168.gate_ref, bf16[4,288,1024]{2,1,0:T(8,128)(2,1)} %get-tuple-element.113.refs_0_, ...), custom_call_target="tpu_custom_call" | custom-call | flops 2415919104 | bytes 5242880 | tf_op jit(solution)/shard_map/combine_scaled/pallas_call | solution.py:45
  457.0 1.5 collective-permute-start.12
  458.4 2.1 add_convert_fusion.3.refs_2_
  463.1 8.9 %collective-permute-done.23 = bf16[256,1024]{1,0:T(8,128)(2,1)} collective-permute-done((bf16[256,1024]{1,0:T(8,128)(2,1)}, bf16[256,1024]{1,0:T(8,128)(2,1)}, u32[]{:S(2)}, u32[]{:S(2)}) %collective-permute-start.23) | collective-permute-done | bytes 524320 | tf_op jit(solution)/shard_map/ppermute | solution.py:1179
  473.6 2.0 add_convert_fusion.5.refs_0_
  477.2 17.1 %collective-permute-done.21.refs_1_ = bf16[256,1024]{1,0:T(8,128)(2,1)S(1)} collective-permute-done((bf16[256,1024]{1,0:T(8,128)(2,1)S(1)}, bf16[256,1024]{1,0:T(8,128)(2,1)S(1)}, u32[]{:S(2)}, u32[]{:S(2)}) %collective-permute-start.21) | collective-permute-done | bytes 524320 | tf_op jit(solution)/shard_map/ppermute | solution.py:1179
  495.3 6.6 hidden_back.1
  504.7 3.1 convolution_convert_fusion
  507.8 9.6 %collective-permute-done.25.refs_1_ = bf16[512,512]{1,0:T(8,128)(2,1)} collective-permute-done((bf16[512,512]{1,0:T(8,128)(2,1)}, bf16[512,512]{1,0:T(8,128)(2,1)}, u32[]{:S(2)}, u32[]{:S(2)}) %collective-permute-start.25) | collective-permute-done | bytes 524320 | tf_op jit(solution)/shard_map/ppermute | solution.py:1179
  517.6 23.9 %attend_back.1 = (bf16[512,1024]{1,0:T(8,128)(2,1)}, bf16[512,1024]{1,0:T(8,128)(2,1)}) custom-call(s32[4]{0:T(128)} %pad_add_fusion.idx_ref, bf16[1024,1024]{1,0:T(8,128)(2,1)} %get-tuple-element.148.qkv_ref, f32[4,4,512]{2,1,0:T(4,128)} %get-tuple-element.149.lse_ref, f32[1024,128]{1,0:T(8,128)} %get-tuple-element.220.cos_ref, ...), custom_call_target="tpu_custom_call" | custom-call | flops 32212254720 | bytes 6291456 | tf_op jit(solution)/shard_map/attend_back/pallas_call | solution.py:233
  541.5 4.3 fusion.23
  550.3 2.6 add_convert_fusion.1
  553.2 15.0 %collective-permute-done.26 = bf16[512,1024]{1,0:T(8,128)(2,1)} collective-permute-done((bf16[512,1024]{1,0:T(8,128)(2,1)}, bf16[512,1024]{1,0:T(8,128)(2,1)}, u32[]{:S(2)}, u32[]{:S(2)}) %collective-permute-start.26) | collective-permute-done | bytes 1048608 | tf_op jit(solution)/shard_map/ppermute | solution.py:1179
  568.2 5.1 fusion.6
  575.8 4.8 collective-permute-start.28
  580.7 2.5 fusion.47
  583.7 3.9 add_convert_fusion
  587.6 1.9 collective-permute-start.30
  591.0 2.7 collective-permute-start.31
  593.6 3.5 fusion.9
  597.8 2.0 slice_bitcast_fusion.23
  599.7 2.5 collective-permute-start.41
  602.8 2.0 slice_bitcast_fusion.22
  606.0 2.0 slice_bitcast_fusion.21
  608.0 1.7 collective-permute-start.43
  613.1 1.5 convert_bitcast_fusion.1
  614.6 2.3 collective-permute-done.42
  617.1 4.0 collective-permute-done.38
  621.5 3.8 collective-permute-done.43
  625.8 3.8 collective-permute-done.39
  629.9 3.9 collective-permute-done.44
  635.3 2.6 collective-permute-done.40
  638.7 2.4 gather_fusion
  641.1 2.3 bitcast_select_fusion
  643.3 1.6 slice_convert_fusion.1
  644.9 2.5 slice_convert_fusion
  647.4 29.1 %reduce-scatter.7.cloned.1.call-done = bf16[64,1024]{1,0:T(8,128)(2,1)} async-done(((bf16[1024,1024]{1,0:T(8,128)(2,1)}), bf16[64,1024]{1,0:T(8,128)(2,1)}) %reduce-scatter.7.cloned.1.call-update) | async-done | bytes 131088 | tf_op jit(solution)/shard_map/reduce_scatter | solution.py:1432
  676.5 1.7 reshape.117
  (212 shorter events, 62.1 us)
Async XLA Ops:
  7.2 10.7 %copy-start = (bf16[512,1024]{1,0:T(8,128)(2,1)S(1)}, bf16[512,1024]{1,0:T(8,128)(2,1)}, u32[]{:S(2)}) copy-start(bf16[512,1024]{1,0:T(8,128)(2,1)} %x_ref.1) | copy-start | bytes 3145732
  7.2 10.7 %copy-start.27 = (f32[1024]{0:T(1024)S(1)}, f32[1024]{0:T(1024)}, u32[]{:S(2)}) copy-start(f32[1024]{0:T(1024)} %param.16) | copy-start | bytes 12292
  7.2 73.9 %all-gather.2.cloned.1.call-start = ((), (), s32[]{:S(2)}) async-start(), calls=%async_computation.6 | async-start | bytes 4456448 | tf_op jit(solution)/shard_map/all_gather | solution.py:1236
  7.2 3.4 collective-permute-start.1
  12.2 585.6 %reduce-scatter.11.cloned.1.call-start = ((), (), s32[]{:S(2)}) async-start(), calls=%async_computation.9 | async-start | bytes 3932160 | tf_op jit(solution)/shard_map/reduce_scatter | solution.py:1416
  12.9 15.5 %copy-start.29 = (pred[512]{0:T(512)(128)(4,1)}, pred[512]{0:T(512)(128)(4,1)S(1)}, u32[]{:S(2)}) copy-start(pred[512]{0:T(512)(128)(4,1)S(1)} %add_compare_fusion.1) | copy-start | bytes 1540
  14.5 17.0 %collective-permute-start.5 = (bf16[32,512]{1,0:T(8,128)(2,1)S(1)}, bf16[32,512]{1,0:T(8,128)(2,1)S(1)}, u32[]{:S(2)}, u32[]{:S(2)}) collective-permute-start(bf16[32,512]{1,0:T(8,128)(2,1)S(1)} %select_convert_fusion.1), channel_id=1, source_target_pairs={{0,1},{1,0},{2,3},{3,2},{4,5},{5,4},{6,7},{7,6},{8,9},{9,8},{10,11... | collective-permute-start | bytes 98312 | tf_op jit(solution)/shard_map/ppermute | solution.py:1179
  19.2 61.9 %collective-permute-start = (bf16[512,1024]{1,0:T(8,128)(2,1)}, bf16[512,1024]{1,0:T(8,128)(2,1)}, u32[]{:S(2)}, u32[]{:S(2)}) collective-permute-start(bf16[512,1024]{1,0:T(8,128)(2,1)} %fusion.5.own_ref), channel_id=1, source_target_pairs={{0,1},{1,0},{2,3},{3,2},{4,5},{5,4},{6,7},{7,6},{8,9},{9,8},{10,11... | collective-permute-start | bytes 3145736 | tf_op jit(solution)/shard_map/ppermute | solution.py:1179
  24.6 37.3 %collective-permute-start.2 = (bf16[4,96,1024]{2,1,0:T(8,128)(2,1)}, bf16[4,96,1024]{2,1,0:T(8,128)(2,1)}, u32[]{:S(2)}, u32[]{:S(2)}) collective-permute-start(bf16[4,96,1024]{2,1,0:T(8,128)(2,1)} %get-tuple-element.86), channel_id=1, source_target_pairs={{0,2},{2,0},{4,6},{6,4},{8,10},{10,8},{12,14},{14,12},{16,18},{18,... | collective-permute-start | bytes 2359304 | tf_op jit(solution)/shard_map/ppermute | solution.py:1176
  27.1 36.1 %collective-permute-start.3 = (bf16[4,96,1024]{2,1,0:T(8,128)(2,1)}, bf16[4,96,1024]{2,1,0:T(8,128)(2,1)}, u32[]{:S(2)}, u32[]{:S(2)}) collective-permute-start(bf16[4,96,1024]{2,1,0:T(8,128)(2,1)} %get-tuple-element.87), channel_id=1, source_target_pairs={{0,4},{2,6},{4,0},{6,2},{8,12},{10,14},{12,8},{14,10},{16,20},{18,... | collective-permute-start | bytes 2359304 | tf_op jit(solution)/shard_map/ppermute | solution.py:1176
  31.6 20.5 %collective-permute-start.6 = (bf16[32,1024]{1,0:T(8,128)(2,1)S(1)}, bf16[32,1024]{1,0:T(8,128)(2,1)S(1)}, u32[]{:S(2)}, u32[]{:S(2)}) collective-permute-start(bf16[32,1024]{1,0:T(8,128)(2,1)S(1)} %get-tuple-element.209), channel_id=1, source_target_pairs={{0,4},{2,6},{4,0},{6,2},{8,12},{10,14},{12,8},{14,10},{16,20},{18,... | collective-permute-start | bytes 196616 | tf_op jit(solution)/shard_map/ppermute | solution.py:1176
  32.7 22.9 %collective-permute-start.7 = (bf16[32,1024]{1,0:T(8,128)(2,1)S(1)}, bf16[32,1024]{1,0:T(8,128)(2,1)S(1)}, u32[]{:S(2)}, u32[]{:S(2)}) collective-permute-start(bf16[32,1024]{1,0:T(8,128)(2,1)S(1)} %get-tuple-element.209), channel_id=1, source_target_pairs={{0,2},{2,0},{4,6},{6,4},{8,10},{10,8},{12,14},{14,12},{16,18},{18,... | collective-permute-start | bytes 196616 | tf_op jit(solution)/shard_map/ppermute | solution.py:1176
  52.1 5.6 collective-permute-start.8
  55.6 20.9 %collective-permute-start.4 = (bf16[4,96,1024]{2,1,0:T(8,128)(2,1)}, bf16[4,96,1024]{2,1,0:T(8,128)(2,1)}, u32[]{:S(2)}, u32[]{:S(2)}) collective-permute-start(bf16[4,96,1024]{2,1,0:T(8,128)(2,1)} %get-tuple-element.88), channel_id=1, source_target_pairs={{0,6},{2,4},{4,2},{6,0},{8,14},{10,12},{12,10},{14,8},{16,22},{18,... | collective-permute-start | bytes 2359304 | tf_op jit(solution)/shard_map/ppermute | solution.py:1176
  61.9 15.8 %copy-start.9 = (bf16[1,96,1024]{2,1,0:T(8,128)(2,1)S(1)}, bf16[1,96,1024]{2,1,0:T(8,128)(2,1)}, u32[]{:S(2)}) copy-start(bf16[1,96,1024]{2,1,0:T(8,128)(2,1)} %get-tuple-element.192) | copy-start | bytes 589828
  63.2 15.6 %copy-start.8 = (bf16[1,96,1024]{2,1,0:T(8,128)(2,1)S(1)}, bf16[1,96,1024]{2,1,0:T(8,128)(2,1)}, u32[]{:S(2)}) copy-start(bf16[1,96,1024]{2,1,0:T(8,128)(2,1)} %get-tuple-element.193) | copy-start | bytes 589828
  274.9 327.9 %reduce-scatter.13.cloned.1.call-start = ((), (), s32[]{:S(2)}) async-start(), calls=%async_computation.10 | async-start | bytes 3932160 | tf_op jit(solution)/shard_map/reduce_scatter | solution.py:1416
  308.0 298.0 %reduce-scatter.15.cloned.1.call-start = ((), (), s32[]{:S(2)}) async-start(), calls=%async_computation.11 | async-start | bytes 3932160 | tf_op jit(solution)/shard_map/reduce_scatter | solution.py:1416
  361.3 248.4 %reduce-scatter.17.cloned.1.call-start = ((), (), s32[]{:S(2)}) async-start(), calls=%async_computation.12 | async-start | bytes 3932160 | tf_op jit(solution)/shard_map/reduce_scatter | solution.py:1416
  390.6 31.8 %collective-permute-start.17 = (bf16[1024,1024]{1,0:T(8,128)(2,1)}, bf16[1024,1024]{1,0:T(8,128)(2,1)}, u32[]{:S(2)}, u32[]{:S(2)}) collective-permute-start(bf16[1024,1024]{1,0:T(8,128)(2,1)} %combine.4), channel_id=1, source_target_pairs={{0,2},{2,0},{4,6},{6,4},{8,10},{10,8},{12,14},{14,12},{16,18},{18,... | collective-permute-start | bytes 6291464 | tf_op jit(solution)/shard_map/ppermute | solution.py:1176
  403.1 28.0 %collective-permute-start.18 = (bf16[1024,1024]{1,0:T(8,128)(2,1)}, bf16[1024,1024]{1,0:T(8,128)(2,1)}, u32[]{:S(2)}, u32[]{:S(2)}) collective-permute-start(bf16[1024,1024]{1,0:T(8,128)(2,1)} %combine.6), channel_id=1, source_target_pairs={{0,2},{2,0},{4,6},{6,4},{8,10},{10,8},{12,14},{14,12},{16,18},{18,... | collective-permute-start | bytes 6291464 | tf_op jit(solution)/shard_map/ppermute | solution.py:1176
  410.4 29.9 %collective-permute-start.9 = (bf16[1024,1024]{1,0:T(8,128)(2,1)}, bf16[1024,1024]{1,0:T(8,128)(2,1)}, u32[]{:S(2)}, u32[]{:S(2)}) collective-permute-start(bf16[1024,1024]{1,0:T(8,128)(2,1)} %combine_scaled.4), channel_id=1, source_target_pairs={{0,2},{2,0},{4,6},{6,4},{8,10},{10,8},{12,14},{14,12},{16,18},{18,... | collective-permute-start | bytes 6291464 | tf_op jit(solution)/shard_map/ppermute | solution.py:1176
  418.3 29.9 %collective-permute-start.10 = (bf16[1024,1024]{1,0:T(8,128)(2,1)}, bf16[1024,1024]{1,0:T(8,128)(2,1)S(1)}, u32[]{:S(2)}, u32[]{:S(2)}) collective-permute-start(bf16[1024,1024]{1,0:T(8,128)(2,1)} %combine_scaled.6), channel_id=1, source_target_pairs={{0,2},{2,0},{4,6},{6,4},{8,10},{10,8},{12,14},{14,12},{16,18},{18,... | collective-permute-start | bytes 6291464 | tf_op jit(solution)/shard_map/ppermute | solution.py:1176
  419.3 193.8 %reduce-scatter.9.cloned.1.call-start = ((), (), s32[]{:S(2)}) async-start(), calls=%async_computation.8 | async-start | bytes 1114112 | tf_op jit(solution)/shard_map/reduce_scatter | solution.py:1433
  429.8 27.1 %collective-permute-start.22 = (bf16[256,1024]{1,0:T(8,128)(2,1)}, bf16[256,1024]{1,0:T(8,128)(2,1)}, u32[]{:S(2)}, u32[]{:S(2)}) collective-permute-start(bf16[256,1024]{1,0:T(8,128)(2,1)} %get-tuple-element.144), channel_id=1, source_target_pairs={{0,1},{1,0},{2,3},{3,2},{4,5},{5,4},{6,7},{7,6},{8,9},{9,8},{10,11... | collective-permute-start | bytes 1572872 | tf_op jit(solution)/shard_map/ppermute | solution.py:1179
  438.9 21.6 %collective-permute-start.20 = (bf16[256,1024]{1,0:T(8,128)(2,1)}, bf16[256,1024]{1,0:T(8,128)(2,1)}, u32[]{:S(2)}, u32[]{:S(2)}) collective-permute-start(bf16[256,1024]{1,0:T(8,128)(2,1)} %get-tuple-element.142), channel_id=1, source_target_pairs={{0,4},{2,6},{4,0},{6,2},{8,12},{10,14},{12,8},{14,10},{16,20},{18,... | collective-permute-start | bytes 1572872 | tf_op jit(solution)/shard_map/ppermute | solution.py:1176
  447.8 100.3 %collective-permute-start.14 = (bf16[256,1024]{1,0:T(8,128)(2,1)}, bf16[256,1024]{1,0:T(8,128)(2,1)S(1)}, u32[]{:S(2)}, u32[]{:S(2)}) collective-permute-start(bf16[256,1024]{1,0:T(8,128)(2,1)} %get-tuple-element.132), channel_id=1, source_target_pairs={{0,1},{1,0},{2,3},{3,2},{4,5},{5,4},{6,7},{7,6},{8,9},{9,8},{10,11... | collective-permute-start | bytes 1572872 | tf_op jit(solution)/shard_map/ppermute | solution.py:1179
  448.0 25.2 %collective-permute-start.19 = (bf16[256,1024]{1,0:T(8,128)(2,1)}, bf16[256,1024]{1,0:T(8,128)(2,1)}, u32[]{:S(2)}, u32[]{:S(2)}) collective-permute-start(bf16[256,1024]{1,0:T(8,128)(2,1)} %get-tuple-element.140), channel_id=1, source_target_pairs={{0,4},{2,6},{4,0},{6,2},{8,12},{10,14},{12,8},{14,10},{16,20},{18,... | collective-permute-start | bytes 1572872 | tf_op jit(solution)/shard_map/ppermute | solution.py:1176
  448.2 13.6 %copy-start.16 = (bf16[256,1024]{1,0:T(8,128)(2,1)S(1)}, bf16[256,1024]{1,0:T(8,128)(2,1)}, u32[]{:S(2)}) copy-start(bf16[256,1024]{1,0:T(8,128)(2,1)} %get-tuple-element.141) | copy-start | bytes 1572868
  448.2 23.8 %collective-permute-start.23 = (bf16[256,1024]{1,0:T(8,128)(2,1)}, bf16[256,1024]{1,0:T(8,128)(2,1)}, u32[]{:S(2)}, u32[]{:S(2)}) collective-permute-start(bf16[256,1024]{1,0:T(8,128)(2,1)} %get-tuple-element.146), channel_id=1, source_target_pairs={{0,1},{1,0},{2,3},{3,2},{4,5},{5,4},{6,7},{7,6},{8,9},{9,8},{10,11... | collective-permute-start | bytes 1572872 | tf_op jit(solution)/shard_map/ppermute | solution.py:1179
  456.9 15.1 %copy-start.17 = (bf16[256,1024]{1,0:T(8,128)(2,1)S(1)}, bf16[256,1024]{1,0:T(8,128)(2,1)}, u32[]{:S(2)}) copy-start(bf16[256,1024]{1,0:T(8,128)(2,1)} %get-tuple-element.145) | copy-start | bytes 1572868
  457.0 18.7 %collective-permute-start.12 = (bf16[256,1024]{1,0:T(8,128)(2,1)}, bf16[256,1024]{1,0:T(8,128)(2,1)S(1)}, u32[]{:S(2)}, u32[]{:S(2)}) collective-permute-start(bf16[256,1024]{1,0:T(8,128)(2,1)} %get-tuple-element.130), channel_id=1, source_target_pairs={{0,4},{2,6},{4,0},{6,2},{8,12},{10,14},{12,8},{14,10},{16,20},{18,... | collective-permute-start | bytes 1572872 | tf_op jit(solution)/shard_map/ppermute | solution.py:1176
  458.4 15.2 %copy-start.13 = (bf16[256,1024]{1,0:T(8,128)(2,1)S(1)}, bf16[256,1024]{1,0:T(8,128)(2,1)}, u32[]{:S(2)}) copy-start(bf16[256,1024]{1,0:T(8,128)(2,1)} %get-tuple-element.139) | copy-start | bytes 1572868
  460.5 42.8 %collective-permute-start.15 = (bf16[256,1024]{1,0:T(8,128)(2,1)}, bf16[256,1024]{1,0:T(8,128)(2,1)S(1)}, u32[]{:S(2)}, u32[]{:S(2)}) collective-permute-start(bf16[256,1024]{1,0:T(8,128)(2,1)} %get-tuple-element.134), channel_id=1, source_target_pairs={{0,1},{1,0},{2,3},{3,2},{4,5},{5,4},{6,7},{7,6},{8,9},{9,8},{10,11... | collective-permute-start | bytes 1572872 | tf_op jit(solution)/shard_map/ppermute | solution.py:1179
  461.8 15.3 %copy-start.15 = (bf16[256,1024]{1,0:T(8,128)(2,1)S(1)}, bf16[256,1024]{1,0:T(8,128)(2,1)}, u32[]{:S(2)}) copy-start(bf16[256,1024]{1,0:T(8,128)(2,1)} %get-tuple-element.129) | copy-start | bytes 1572868
  472.0 22.4 %collective-permute-start.21 = (bf16[256,1024]{1,0:T(8,128)(2,1)S(1)}, bf16[256,1024]{1,0:T(8,128)(2,1)S(1)}, u32[]{:S(2)}, u32[]{:S(2)}) collective-permute-start(bf16[256,1024]{1,0:T(8,128)(2,1)S(1)} %add_convert_fusion.4), channel_id=1, source_target_pairs={{0,1},{1,0},{2,3},{3,2},{4,5},{5,4},{6,7},{7,6},{8,9},{9,8},{10,11... | collective-permute-start | bytes 1572872 | tf_op jit(solution)/shard_map/ppermute | solution.py:1179
  473.2 21.1 %collective-permute-start.24 = (bf16[256,1024]{1,0:T(8,128)(2,1)S(1)}, bf16[256,1024]{1,0:T(8,128)(2,1)S(1)}, u32[]{:S(2)}, u32[]{:S(2)}) collective-permute-start(bf16[256,1024]{1,0:T(8,128)(2,1)S(1)} %add_convert_fusion.2), channel_id=1, source_target_pairs={{0,4},{2,6},{4,0},{6,2},{8,12},{10,14},{12,8},{14,10},{16,20},{18,... | collective-permute-start | bytes 1572872 | tf_op jit(solution)/shard_map/ppermute | solution.py:1176
  475.7 70.2 %collective-permute-start.11 = (bf16[256,1024]{1,0:T(8,128)(2,1)}, bf16[256,1024]{1,0:T(8,128)(2,1)S(1)}, u32[]{:S(2)}, u32[]{:S(2)}) collective-permute-start(bf16[256,1024]{1,0:T(8,128)(2,1)} %get-tuple-element.128), channel_id=1, source_target_pairs={{0,4},{2,6},{4,0},{6,2},{8,12},{10,14},{12,8},{14,10},{16,20},{18,... | collective-permute-start | bytes 1572872 | tf_op jit(solution)/shard_map/ppermute | solution.py:1176
  494.4 53.5 %collective-permute-start.13 = (bf16[256,1024]{1,0:T(8,128)(2,1)S(1)}, bf16[256,1024]{1,0:T(8,128)(2,1)S(1)}, u32[]{:S(2)}, u32[]{:S(2)}) collective-permute-start(bf16[256,1024]{1,0:T(8,128)(2,1)S(1)} %add_convert_fusion.8), channel_id=1, source_target_pairs={{0,1},{1,0},{2,3},{3,2},{4,5},{5,4},{6,7},{7,6},{8,9},{9,8},{10,11... | collective-permute-start | bytes 1572872 | tf_op jit(solution)/shard_map/ppermute | solution.py:1179
  502.0 15.4 %collective-permute-start.25 = (bf16[512,512]{1,0:T(8,128)(2,1)}, bf16[512,512]{1,0:T(8,128)(2,1)}, u32[]{:S(2)}, u32[]{:S(2)}) collective-permute-start(bf16[512,512]{1,0:T(8,128)(2,1)} %get-tuple-element.151), channel_id=1, source_target_pairs={{0,1},{1,0},{2,3},{3,2},{4,5},{5,4},{6,7},{7,6},{8,9},{9,8},{10,11... | collective-permute-start | bytes 1572872 | tf_op jit(solution)/shard_map/ppermute | solution.py:1179
  504.3 43.8 %collective-permute-start.16 = (bf16[256,1024]{1,0:T(8,128)(2,1)}, bf16[256,1024]{1,0:T(8,128)(2,1)S(1)}, u32[]{:S(2)}, u32[]{:S(2)}) collective-permute-start(bf16[256,1024]{1,0:T(8,128)(2,1)} %add_convert_fusion.6), channel_id=1, source_target_pairs={{0,4},{2,6},{4,0},{6,2},{8,12},{10,14},{12,8},{14,10},{16,20},{18,... | collective-permute-start | bytes 1572872 | tf_op jit(solution)/shard_map/ppermute | solution.py:1176
  517.3 32.9 %collective-permute-start.32 = (bf16[1024,512]{1,0:T(8,128)(2,1)}, bf16[1024,512]{1,0:T(8,128)(2,1)}, u32[]{:S(2)}, u32[]{:S(2)}) collective-permute-start(bf16[1024,512]{1,0:T(8,128)(2,1)} %convolution_convert_fusion), channel_id=1, source_target_pairs={{0,1},{1,0},{2,3},{3,2},{4,5},{5,4},{6,7},{7,6},{8,9},{9,8},{10,11... | collective-permute-start | bytes 3145736 | tf_op jit(solution)/shard_map/ppermute | solution.py:1179
  545.8 22.3 %collective-permute-start.26 = (bf16[512,1024]{1,0:T(8,128)(2,1)}, bf16[512,1024]{1,0:T(8,128)(2,1)}, u32[]{:S(2)}, u32[]{:S(2)}) collective-permute-start(bf16[512,1024]{1,0:T(8,128)(2,1)} %fusion.23), channel_id=1, source_target_pairs={{0,1},{1,0},{2,3},{3,2},{4,5},{5,4},{6,7},{7,6},{8,9},{9,8},{10,11... | collective-permute-start | bytes 3145736 | tf_op jit(solution)/shard_map/ppermute | solution.py:1179
  550.2 17.9 %copy-start.1 = (bf16[512,1024]{1,0:T(8,128)(2,1)S(1)}, bf16[512,1024]{1,0:T(8,128)(2,1)}, u32[]{:S(2)}) copy-start(bf16[512,1024]{1,0:T(8,128)(2,1)} %x_ref.1) | copy-start | bytes 3145732
  550.2 17.9 %copy-start.24 = (f32[512]{0:T(512)S(1)}, f32[512]{0:T(512)}, u32[]{:S(2)}) copy-start(f32[512]{0:T(512)} %copy-done.23) | copy-start | bytes 6148
  550.2 17.9 %copy-start.28 = (f32[1024]{0:T(1024)S(1)}, f32[1024]{0:T(1024)}, u32[]{:S(2)}) copy-start(f32[1024]{0:T(1024)} %param.16) | copy-start | bytes 12292
  552.9 123.6 %reduce-scatter.7.cloned.1.call-start = ((), (), s32[]{:S(2)}) async-start(), calls=%async_computation.7 | async-start | bytes 2228224 | tf_op jit(solution)/shard_map/reduce_scatter | solution.py:1432
  573.2 2.6 collective-permute-start.27
  575.8 7.3 %collective-permute-start.28 = (f32[2,1024]{1,0:T(2,128)S(1)}, f32[2,1024]{1,0:T(2,128)S(1)}, u32[]{:S(2)}, u32[]{:S(2)}) collective-permute-start(f32[2,1024]{1,0:T(2,128)S(1)} %fusion.36), channel_id=1, source_target_pairs={{0,2},{2,0},{4,6},{6,4},{8,10},{10,8},{12,14},{14,12},{16,18},{18,... | collective-permute-start | bytes 24584 | tf_op jit(solution)/shard_map/ppermute | solution.py:1176
  583.2 4.4 collective-permute-start.29
  587.6 3.3 collective-permute-start.30
  591.0 6.2 collective-permute-start.31
  599.7 11.2 %collective-permute-start.41 = (bf16[96,1024]{1,0:T(8,128)(2,1)S(1)}, bf16[96,1024]{1,0:T(8,128)(2,1)S(1)}, u32[]{:S(2)}, u32[]{:S(2)}) collective-permute-start(bf16[96,1024]{1,0:T(8,128)(2,1)S(1)} %get-tuple-element.177), channel_id=1, source_target_pairs={{0,6},{2,4},{4,2},{6,0},{8,14},{10,12},{12,10},{14,8},{16,22},{18,... | collective-permute-start | bytes 589832 | tf_op jit(solution)/shard_map/ppermute | solution.py:1176
  602.2 10.6 %collective-permute-start.37 = (bf16[96,1024]{1,0:T(8,128)(2,1)}, bf16[96,1024]{1,0:T(8,128)(2,1)S(1)}, u32[]{:S(2)}, u32[]{:S(2)}) collective-permute-start(bf16[96,1024]{1,0:T(8,128)(2,1)} %get-tuple-element.178), channel_id=1, source_target_pairs={{0,4},{2,6},{4,0},{6,2},{8,12},{10,14},{12,8},{14,10},{16,20},{18,... | collective-permute-start | bytes 589832 | tf_op jit(solution)/shard_map/ppermute | solution.py:1176
  604.8 12.1 %collective-permute-start.42 = (bf16[96,1024]{1,0:T(8,128)(2,1)}, bf16[96,1024]{1,0:T(8,128)(2,1)S(1)}, u32[]{:S(2)}, u32[]{:S(2)}) collective-permute-start(bf16[96,1024]{1,0:T(8,128)(2,1)} %get-tuple-element.181), channel_id=1, source_target_pairs={{0,6},{2,4},{4,2},{6,0},{8,14},{10,12},{12,10},{14,8},{16,22},{18,... | collective-permute-start | bytes 589832 | tf_op jit(solution)/shard_map/ppermute | solution.py:1176
  605.1 16.0 %collective-permute-start.38 = (bf16[96,1024]{1,0:T(8,128)(2,1)S(1)}, bf16[96,1024]{1,0:T(8,128)(2,1)S(1)}, u32[]{:S(2)}, u32[]{:S(2)}) collective-permute-start(bf16[96,1024]{1,0:T(8,128)(2,1)S(1)} %get-tuple-element.182), channel_id=1, source_target_pairs={{0,4},{2,6},{4,0},{6,2},{8,12},{10,14},{12,8},{14,10},{16,20},{18,... | collective-permute-start | bytes 589832 | tf_op jit(solution)/shard_map/ppermute | solution.py:1176
  608.0 17.4 %collective-permute-start.43 = (bf16[96,1024]{1,0:T(8,128)(2,1)}, bf16[96,1024]{1,0:T(8,128)(2,1)S(1)}, u32[]{:S(2)}, u32[]{:S(2)}) collective-permute-start(bf16[96,1024]{1,0:T(8,128)(2,1)} %get-tuple-element.185), channel_id=1, source_target_pairs={{0,6},{2,4},{4,2},{6,0},{8,14},{10,12},{12,10},{14,8},{16,22},{18,... | collective-permute-start | bytes 589832 | tf_op jit(solution)/shard_map/ppermute | solution.py:1176
  611.0 18.6 %collective-permute-start.39 = (bf16[96,1024]{1,0:T(8,128)(2,1)S(1)}, bf16[96,1024]{1,0:T(8,128)(2,1)S(1)}, u32[]{:S(2)}, u32[]{:S(2)}) collective-permute-start(bf16[96,1024]{1,0:T(8,128)(2,1)S(1)} %get-tuple-element.186), channel_id=1, source_target_pairs={{0,4},{2,6},{4,0},{6,2},{8,12},{10,14},{12,8},{14,10},{16,20},{18,... | collective-permute-start | bytes 589832 | tf_op jit(solution)/shard_map/ppermute | solution.py:1176
  612.8 21.0 %collective-permute-start.44 = (bf16[96,1024]{1,0:T(8,128)(2,1)S(1)}, bf16[96,1024]{1,0:T(8,128)(2,1)}, u32[]{:S(2)}, u32[]{:S(2)}) collective-permute-start(bf16[96,1024]{1,0:T(8,128)(2,1)S(1)} %get-tuple-element.189), channel_id=1, source_target_pairs={{0,6},{2,4},{4,2},{6,0},{8,14},{10,12},{12,10},{14,8},{16,22},{18,... | collective-permute-start | bytes 589832 | tf_op jit(solution)/shard_map/ppermute | solution.py:1176
  616.9 21.1 %collective-permute-start.40 = (bf16[96,1024]{1,0:T(8,128)(2,1)S(1)}, bf16[96,1024]{1,0:T(8,128)(2,1)S(1)}, u32[]{:S(2)}, u32[]{:S(2)}) collective-permute-start(bf16[96,1024]{1,0:T(8,128)(2,1)S(1)} %get-tuple-element.190), channel_id=1, source_target_pairs={{0,4},{2,6},{4,0},{6,2},{8,12},{10,14},{12,8},{14,10},{16,20},{18,... | collective-permute-start | bytes 589832 | tf_op jit(solution)/shard_map/ppermute | solution.py:1176
  621.1 17.0 %collective-permute-start.33 = (bf16[96,1024]{1,0:T(8,128)(2,1)S(1)}, bf16[96,1024]{1,0:T(8,128)(2,1)S(1)}, u32[]{:S(2)}, u32[]{:S(2)}) collective-permute-start(bf16[96,1024]{1,0:T(8,128)(2,1)S(1)} %get-tuple-element.179), channel_id=1, source_target_pairs={{0,2},{2,0},{4,6},{6,4},{8,10},{10,8},{12,14},{14,12},{16,18},{18,... | collective-permute-start | bytes 589832 | tf_op jit(solution)/shard_map/ppermute | solution.py:1176
  625.3 12.8 %collective-permute-start.34 = (bf16[96,1024]{1,0:T(8,128)(2,1)S(1)}, bf16[96,1024]{1,0:T(8,128)(2,1)S(1)}, u32[]{:S(2)}, u32[]{:S(2)}) collective-permute-start(bf16[96,1024]{1,0:T(8,128)(2,1)S(1)} %get-tuple-element.183), channel_id=1, source_target_pairs={{0,2},{2,0},{4,6},{6,4},{8,10},{10,8},{12,14},{14,12},{16,18},{18,... | collective-permute-start | bytes 589832 | tf_op jit(solution)/shard_map/ppermute | solution.py:1176
  629.5 8.6 %collective-permute-start.35 = (bf16[96,1024]{1,0:T(8,128)(2,1)S(1)}, bf16[96,1024]{1,0:T(8,128)(2,1)S(1)}, u32[]{:S(2)}, u32[]{:S(2)}) collective-permute-start(bf16[96,1024]{1,0:T(8,128)(2,1)S(1)} %get-tuple-element.187), channel_id=1, source_target_pairs={{0,2},{2,0},{4,6},{6,4},{8,10},{10,8},{12,14},{14,12},{16,18},{18,... | collective-permute-start | bytes 589832 | tf_op jit(solution)/shard_map/ppermute | solution.py:1176
  633.9 4.2 collective-permute-start.36
  (21 other events, 91.3 us)
Sparse Core Ops, SparseCore 0:
  12.3 58.4 all-gather.1
  275.0 84.3 reduce-scatter.10
  361.7 60.6 reduce-scatter.12
  424.5 60.2 reduce-scatter.14
  487.6 60.2 reduce-scatter.16
  553.0 58.5 reduce-scatter.8
  615.7 60.6 reduce-scatter.6

commit v3 on v2

--- a/solution.py
+++ b/solution.py
@@ -639,6 +639,17 @@
             pl.when(receives)(copy.wait_recv)
 
 
+def greet_all(outer):
+    d, t, o, i = place()
+    barrier = pltpu.get_barrier_semaphore()
+    for m in range(1, GROUP):
+        pl.semaphore_signal(barrier, inc=1, device_id=(flip(d, m), t), device_id_type=MESH)
+    pl.semaphore_signal(barrier, inc=1, device_id=(d, 1 - t), device_id_type=MESH)
+    for k in range(1, outer):
+        pl.semaphore_signal(barrier, inc=1, device_id=((o + k) % outer * GROUP + i, t), device_id_type=MESH)
+    pl.semaphore_wait(barrier, GROUP - 1 + outer)
+
+
 def to_x(src, dst, sent, came):
     d, t, _, _ = place()
     return pltpu.make_async_remote_copy(src, dst, sent, came, device_id=(d, 1 - t), device_id_type=MESH)
@@ -1005,20 +1016,26 @@
     return out[0], out[1 : 1 + n], out[1 + n :]
 
 
-def expert_step_kernel(j, outer, in_rows, down_rows, steps, x_ref, g_ref, own, *refs):
-    n_hops, n_steps = outer - 1, len(steps)
+def expert_step_kernel(j, outer, in_rows, down_rows, steps, sum_steps, x_ref, g_ref, own, *refs):
+    n_hops, n_steps, n_sums = outer - 1, len(steps), len(sum_steps)
     lefts, refs = refs[:n_hops], refs[n_hops:]
     rights, refs = refs[:n_hops], refs[n_hops:]
     from_left, refs = refs[:n_steps], refs[n_steps:]
     from_right, refs = refs[:n_steps], refs[n_steps:]
+    dws, refs = refs[:n_sums], refs[n_sums:]
+    was_l, refs = refs[:n_sums], refs[n_sums:]
+    was_r, refs = refs[:n_sums], refs[n_sums:]
     y_ref, dx_ref, dw_ref = refs[:3]
     refs = refs[3:]
     to_left, refs = refs[:n_steps], refs[n_steps:]
     to_right, refs = refs[:n_steps], refs[n_steps:]
-    x_all, g_all, w_in, w_down, act_all, gug_all, sem_x, sem_g, sem_w, sem_d, s_hop, r_hop = refs
+    sum_left, refs = refs[:n_sums], refs[n_sums:]
+    sum_right, refs = refs[:n_sums], refs[n_sums:]
+    x_all, g_all, w_in, w_down, act_all, gug_all, sem_x, sem_g, sem_w, sem_d, s_hop, r_hop = refs[:12]
     _, _, o, i = place()
+    greet(outer, (), False)
+    sums = Sums(outer, sum_steps, dws, was_l, was_r, sum_left, sum_right, *refs[12:])
     if n_steps:
-        greet(outer, (), False)
         hops = Hops(
             outer,
             [(k, a, b, l, r) for k, a, b, l, r in zip(steps, from_left, from_right, to_left, to_right, strict=True)],
@@ -1072,10 +1089,12 @@
         for c in made:
             c.wait()
 
+    sums.load()
     each_weight(start)
     copy_x, copy_g = rows_of(x_ref, x_all, sem_x), rows_of(g_ref, g_all, sem_g)
     start(copy_x)
     start(copy_g)
+    sums.send()
     each_weight(wait)
     wait(copy_x)
     wait(copy_g)
@@ -1105,10 +1124,12 @@
             dw_ref[c, flip(i, r), in_rows:, :] = part[r * down_rows : (r + 1) * down_rows]
     if n_steps:
         hops.wait()
-
-
-def expert_step(j, outer, in_rows, down_rows, x, g, own, lefts, rights, steps, from_left, from_right):
-    n_hops, n = outer - 1, len(steps)
+    sums.wait()
+
+
+def expert_step(j, outer, in_rows, down_rows, x, g, own, lefts, rights, hop_plan, sum_plan):
+    (steps, from_left, from_right), (sum_steps, dws, was_l, was_r) = hop_plan, sum_plan
+    n_hops, n, n_sums = outer - 1, len(steps), len(sum_steps)
     total = GROUP * CAP
     packed = in_rows + down_rows
     weights = [jax.ShapeDtypeStruct(s.shape, BF) for s in from_left]
@@ -1116,31 +1137,735 @@
         jax.ShapeDtypeStruct((GROUP, CAP, D), BF),
         jax.ShapeDtypeStruct((GROUP, CAP, D), BF),
         jax.ShapeDtypeStruct((outer, GROUP, packed, D), BF),
-    ] + weights * 2
-    in_specs = [ANY] * (3 + 2 * n_hops + 2 * n)
-    out_specs = [VM] * 3 + [ANY] * (2 * n)
-    args = (x, g, own, *lefts, *rights, *from_left, *from_right)
-    scratch = [
-        pltpu.VMEM((total, D), BF),
-        pltpu.VMEM((total, D), BF),
-        pltpu.VMEM((D, 2 * FF), BF),
-        pltpu.VMEM((FF, D), BF),
-        pltpu.VMEM((total, FF), BF),
-        pltpu.VMEM((total, 2 * FF), BF),
-        pltpu.SemaphoreType.DMA((GROUP,)),
-        pltpu.SemaphoreType.DMA((GROUP,)),
-        pltpu.SemaphoreType.DMA(((1 + 2 * n_hops) * GROUP,)),
-        pltpu.SemaphoreType.DMA(((1 + 2 * n_hops) * GROUP,)),
-        pltpu.SemaphoreType.DMA((max(1, 2 * n),)),
-        pltpu.SemaphoreType.DMA((max(1, 2 * n),)),
+    ] + weights * 2 + [jax.ShapeDtypeStruct((GROUP, packed, D), BF)] * (2 * n_sums)
+    out = remote_call(
+        functools.partial(expert_step_kernel, j, outer, in_rows, down_rows, steps, sum_steps),
+        "expert_step",
+        4 + j,
+        shapes,
+        [ANY] * (3 + 2 * n_hops + 2 * n + 3 * n_sums),
+        [VM] * 3 + [ANY] * (2 * n + 2 * n_sums),
+        (x, g, own, *lefts, *rights, *from_left, *from_right, *dws, *was_l, *was_r),
+        [
+            pltpu.VMEM((total, D), BF),
+            pltpu.VMEM((total, D), BF),
+            pltpu.VMEM((D, 2 * FF), BF),
+            pltpu.VMEM((FF, D), BF),
+            pltpu.VMEM((total, FF), BF),
+            pltpu.VMEM((total, 2 * FF), BF),
+            pltpu.SemaphoreType.DMA((GROUP,)),
+            pltpu.SemaphoreType.DMA((GROUP,)),
+            pltpu.SemaphoreType.DMA(((1 + 2 * n_hops) * GROUP,)),
+            pltpu.SemaphoreType.DMA(((1 + 2 * n_hops) * GROUP,)),
+            pltpu.SemaphoreType.DMA((max(1, 2 * n),)),
+            pltpu.SemaphoreType.DMA((max(1, 2 * n),)),
+            *sums_scratch(n_sums, packed),
+        ],
+        18 * total * D * FF,
+    )
+    out, rest = out[:3], out[3:]
+    return out, rest[:n], rest[n : 2 * n], rest[2 * n : 2 * n + n_sums], rest[2 * n + n_sums :]
+
+
+class Sums:
+    def __init__(self, outer, steps, dws, was_left, was_right, to_left, to_right, message, term, loaded, added, sent, came):
+        d, t, o, _ = place()
+        back = outer - 1 - o
+        self.moves = []
+        for n, s in enumerate(steps):
+            for side, near, target, was, to, peer in (
+                (0, o, outer - s + o, was_left, to_left, d + GROUP),
+                (1, back, s - 1 - back, was_right, to_right, d - GROUP),
+            ):
+                k = 2 * n + side
+                own = pltpu.make_async_copy(dws[n].at[target], message.at[k], loaded.at[k])
+                before = None if s == 1 else pltpu.make_async_copy(was[n], term.at[side], added.at[k])
+                move = pltpu.make_async_remote_copy(
+                    message.at[k], to[n], sent.at[k], came.at[k], device_id=(peer, t), device_id_type=MESH
+                )
+                sends, adds = near <= s - 1, (near <= s - 1) & (near >= 1)
+                receives = (near >= 1) & (near <= s)
+                self.moves.append((own, before, move, sends, adds, receives, message.at[k], term.at[side]))
+
+    def load(self):
+        for own, _, _, sends, *_ in self.moves:
+            pl.when(sends)(own.start)
+
+    def send(self):
+        for n in range(0, len(self.moves), 2):
+            pair = self.moves[n : n + 2]
+            for _, before, _, _, adds, *_ in pair:
+                if before is not None:
+                    pl.when(adds)(before.start)
+            for own, before, move, sends, adds, _, message, term in pair:
+                pl.when(sends)(own.wait)
+                if before is not None:
+
+                    @pl.when(adds)
+                    def _(before=before, message=message, term=term):
+                        before.wait()
+
+                        def one(m, carry):
+                            message[m] = (message[m].astype(F32) + term[m].astype(F32)).astype(BF)
+                            return carry
+
+                        lax.fori_loop(0, GROUP, one, 0)
+
+                pl.when(sends)(move.start)
+
+    def wait(self):
+        for _, _, move, sends, _, receives, *_ in self.moves:
+            pl.when(sends)(move.wait_send)
+            pl.when(receives)(move.wait_recv)
+
+
+def sums_scratch(n, packed):
+    n = max(1, n)
+    return [
+        pltpu.VMEM((2 * n, GROUP, packed, D), BF),
+        pltpu.VMEM((2, GROUP, packed, D), BF),
+        pltpu.SemaphoreType.DMA((2 * n,)),
+        pltpu.SemaphoreType.DMA((2 * n,)),
+        pltpu.SemaphoreType.DMA((2 * n,)),
+        pltpu.SemaphoreType.DMA((2 * n,)),
     ]
-    kernel = functools.partial(expert_step_kernel, j, outer, in_rows, down_rows, steps)
-    flops = 18 * total * D * FF
-    if n:
-        out = remote_call(kernel, "expert_step", 4 + j, shapes, in_specs, out_specs, args, scratch, flops)
-    else:
-        out = call(kernel, "expert_last", shapes, in_specs, out_specs, args, scratch=scratch, flops=flops, moved=15 << 20)
-    return out[:3], out[3 : 3 + n], out[3 + n :]
+
+
+def again(scratch):
+    return [pltpu.SemaphoreType.DMA(s.shape) for s in scratch[2:]]
+
+
+class Final:
+    def __init__(self, outer, dw, left, right, mine, term, target, loaded, sent, came, kept):
+        _, _, o, _ = place()
+        self.from_left, self.from_right = o >= 1, o < outer - 1
+        self.mine, self.term = mine, term
+        self.own = pltpu.make_async_copy(dw.at[o], mine, loaded.at[0])
+        self.left = pltpu.make_async_copy(left, term.at[0], loaded.at[1])
+        self.right = pltpu.make_async_copy(right, term.at[1], loaded.at[2])
+        self.moves = [to_dp(m, mine.at[m], target.at[m], sent.at[m - 1], came.at[m - 1]) for m in range(1, GROUP)]
+        self.keep = pltpu.make_async_copy(mine.at[0], target.at[0], kept)
+
+    def send(self):
+        self.own.start()
+        pl.when(self.from_left)(self.left.start)
+        pl.when(self.from_right)(self.right.start)
+        self.own.wait()
+
+        def add(k):
+            def one(m, carry):
+                self.mine[m] = (self.mine[m].astype(F32) + self.term[k, m].astype(F32)).astype(BF)
+                return carry
+
+            lax.fori_loop(0, GROUP, one, 0)
+
+        @pl.when(self.from_left)
+        def _():
+            self.left.wait()
+            add(0)
+
+        @pl.when(self.from_right)
+        def _():
+            self.right.wait()
+            add(1)
+
+        for move in self.moves:
+            move.start()
+        self.keep.start()
+
+    def wait(self):
+        for move in self.moves:
+            move.wait()
+        self.keep.wait()
+
+
+def final_scratch(packed):
+    return [
+        pltpu.VMEM((GROUP, packed, D), BF),
+        pltpu.SemaphoreType.DMA((3,)),
+        pltpu.SemaphoreType.DMA((GROUP - 1,)),
+        pltpu.SemaphoreType.DMA((GROUP - 1,)),
+        pltpu.SemaphoreType.DMA,
+    ]
+
+
+class Mixer:
+    def __init__(self, sources, pos_ref, gate_ref, held, sems):
+        self.sources, self.pos, self.gate, self.held, self.sems = sources, pos_ref, gate_ref, held, sems
+
+    def copies(self, slot, buffer):
+        return [
+            pltpu.make_async_copy(
+                source.at[slot], self.held.at[buffer, pl.ds(j * CAP, CAP)], self.sems.at[buffer * len(self.sources) + j]
+            )
+            for j, source in enumerate(self.sources)
+        ]
+
+    def load(self, slot, buffer):
+        for c in self.copies(slot, buffer):
+            c.start()
+
+    def mix(self, slot, buffer, out, add=None):
+        for c in self.copies(slot, buffer):
+            c.wait()
+        n_experts = len(self.sources)
+        width = n_experts * CAP
+        block = 256
+
+        def one(b, carry):
+            at = pl.ds(pl.multiple_of(b * block, block), block)
+            targets = []
+            for j in range(n_experts):
+                target = self.pos[slot, at, j : j + 1]
+                targets.append(jnp.where(target >= 0, target + j * CAP, -1))
+            tiles = []
+            for first in range(0, width, LANES):
+                size = min(LANES, width - first)
+                lane = first + lax.broadcasted_iota(jnp.int32, (block, size), 1)
+                tile = jnp.zeros((block, size), F32)
+                for j in range(first // CAP, (first + size - 1) // CAP + 1):
+                    value = 1.0 if self.gate is None else self.gate[slot, at, j : j + 1]
+                    tile = jnp.where(lane == targets[j], value, tile)
+                tiles.append(tile.astype(BF))
+            total = mm(jnp.concatenate(tiles, axis=1), self.held[buffer])
+            if add is not None:
+                total = total + add[at, :].astype(F32)
+            out[at, :] = total.astype(BF)
+            return carry
+
+        lax.fori_loop(0, out.shape[0] // block, one, 0)
+
+
+class GroupSum:
+    def __init__(self, far, come, near, come_ab, last_ab, sent, came):
+        self.far, self.come, self.near, self.come_ab, self.last_ab = far, come, near, come_ab, last_ab
+        q = near.shape[1] // 4
+        self.q = q
+        self.core = [to_dp(1, far.at[s], come.at[s], sent.at[s], came.at[s]) for s in range(2)]
+        self.a = to_dp(2, near.at[1, pl.ds(0, 2 * q)], come_ab.at[0], sent.at[2], came.at[2])
+        self.b = [
+            to_x(near.at[s, pl.ds(3 * q, q)], come_ab.at[1, pl.ds(s * q, q)], sent.at[3 + s], came.at[3 + s])
+            for s in range(2)
+        ]
+        self.last = [
+            to_x(near.at[0, pl.ds(q, q)], last_ab.at[0], sent.at[5], came.at[5]),
+            to_dp(2, near.at[1, pl.ds(2 * q, q)], last_ab.at[1], sent.at[6], came.at[6]),
+        ]
+
+    def second(self):
+        q, near, come_ab = self.q, self.near, self.come_ab
+        self.a.wait_recv()
+        near[0, q : 2 * q] = (near[0, q : 2 * q].astype(F32) + come_ab[0, q : 2 * q].astype(F32)).astype(BF)
+        self.last[0].start()
+        self.b[1].wait_recv()
+        near[1, 2 * q : 3 * q] = (near[1, 2 * q : 3 * q].astype(F32) + come_ab[1, q : 2 * q].astype(F32)).astype(BF)
+        self.last[1].start()
+        self.b[0].wait_recv()
+
+    def terms(self, p):
+        q = self.q
+        self.last[p].wait_recv()
+        return (
+            self.near[0, 2 * p * q : 2 * p * q + q].astype(F32)
+            + self.come_ab[p, :q].astype(F32)
+            + self.last_ab[p].astype(F32)
+        )
+
+    def sent(self):
+        for copy in (*self.core, self.a, *self.b, *self.last):
+            copy.wait_send()
+
+
+def group_scratch(rows, n_experts):
+    return [
+        pltpu.VMEM((2, n_experts * CAP, D), BF),
+        pltpu.VMEM((2, rows, D), BF),
+        pltpu.VMEM((2, rows, D), BF),
+        pltpu.VMEM((2, rows, D), BF),
+        pltpu.VMEM((2, rows // 2, D), BF),
+        pltpu.VMEM((2, rows // 4, D), BF),
+        pltpu.SemaphoreType.DMA((2 * n_experts,)),
+        pltpu.SemaphoreType.DMA((7,)),
+        pltpu.SemaphoreType.DMA((7,)),
+    ]
+
+
+def mix_and_sum(mixer, group):
+    mixer.load(2, 0)
+    mixer.load(3, 1)
+    mixer.mix(2, 0, group.far.at[0])
+    group.core[0].start()
+    mixer.load(1, 0)
+    mixer.mix(3, 1, group.far.at[1])
+    group.core[1].start()
+    mixer.load(0, 1)
+    group.core[1].wait_recv()
+    mixer.mix(1, 0, group.near.at[1], group.come.at[1])
+    group.a.start()
+    group.b[1].start()
+    group.core[0].wait_recv()
+    mixer.mix(0, 1, group.near.at[0], group.come.at[0])
+    group.b[0].start()
+    group.second()
+
+
+def rows_back_kernel(outer, first, then, pos_ref, valid_ref, hidden_ref, cot_ref, gain_ref, w_ref, *refs):
+    n_experts, n1, n2 = pos_ref.shape[2], len(first), len(then)
+    sources, refs = refs[:n_experts], refs[n_experts:]
+    dws, refs = refs[:n1], refs[n1:]
+    was_l, refs = refs[:n1], refs[n1:]
+    was_r, refs = refs[:n1], refs[n1:]
+    grad_ref, low_ref, gain_grad_ref, own_ref, come_ref = refs[:5]
+    refs = refs[5:]
+    to_l, refs = refs[: n1 + n2], refs[n1 + n2 :]
+    to_r, refs = refs[: n1 + n2], refs[n1 + n2 :]
+    (held, far, come, near, come_ab, last_ab, l_sem, s_sem, r_sem), refs = refs[:9], refs[9:]
+    sums_a, refs = refs[:6], refs[6:]
+    sums_b, refs = (*sums_a[:2], *refs[:4]), refs[4:]
+    send_ref, s_at, r_at = refs
+    greet(outer, (1, 2), True)
+    one = Sums(outer, first, dws, was_l, was_r, to_l[:n1], to_r[:n1], *sums_a)
+    two = Sums(
+        outer,
+        [s for s, _ in then],
+        [dws[k] for _, k in then],
+        [to_l[k] for _, k in then],
+        [to_r[k] for _, k in then],
+        to_l[n1:],
+        to_r[n1:],
+        *sums_b,
+    )
+    group = GroupSum(far, come, near, come_ab, last_ab, s_sem, r_sem)
+    mixer = Mixer(sources, pos_ref, None, held, l_sem)
+    one.load()
+    one.send()
+    mix_and_sum(mixer, group)
+    one.wait()
+    two.load()
+    two.send()
+    rows = hidden_ref.shape[0] // 2
+    width = w_ref.shape[1] // 2
+    heads = width // 2
+    gain = gain_ref[...]
+    gain_grad = jnp.zeros((1, D), F32)
+    for p in range(2):
+        at = slice(p * rows, (p + 1) * rows)
+        hidden = hidden_ref[at]
+        normed_grad = group.terms(p)
+        inverse = lax.rsqrt(jnp.mean(hidden * hidden, axis=-1, keepdims=True) + EPSILON)
+        gain_grad = gain_grad + jnp.sum(normed_grad * (hidden * inverse), axis=0, keepdims=True)
+        scaled = normed_grad * gain
+        back = inverse * scaled - hidden * (
+            inverse * inverse * inverse * jnp.mean(scaled * hidden, axis=-1, keepdims=True)
+        )
+        dy = jnp.where(valid_ref[at] > 0, cot_ref[at].astype(F32), 0.0)
+        total = dy + back
+        grad_ref[at] = total
+        low = total.astype(BF)
+        low_ref[at] = low
+        send_ref[at] = mm(low, w_ref[:, width + heads :]).astype(BF)
+    gain_grad_ref[...] = gain_grad
+    away = to_x(send_ref, come_ref, s_at, r_at)
+    away.start()
+    own_ref[...] = mm(low_ref[...], w_ref[:, width : width + heads]).astype(BF)
+    group.sent()
+    away.wait()
+    two.wait()
+
+
+def rows_back(outer, pos, valid, hidden, cotangent, gain, weights_full, sources, first, then, dws, was_l, was_r):
+    rows, heads = hidden.shape[0], weights_full.shape[1] // 4
+    n = len(first) + len(then)
+    packed = dws[0].shape[2]
+    hop = [jax.ShapeDtypeStruct((GROUP, packed, D), BF)] * (2 * n)
+    half = jax.ShapeDtypeStruct((rows, heads), BF)
+    out = remote_call(
+        functools.partial(rows_back_kernel, outer, first, then),
+        "rows_back",
+        10,
+        [
+            jax.ShapeDtypeStruct((rows, D), F32),
+            jax.ShapeDtypeStruct((rows, D), BF),
+            jax.ShapeDtypeStruct((1, D), F32),
+            half,
+            half,
+        ]
+        + hop,
+        [VM] * 6 + [ANY] * (len(sources) + 3 * len(first)),
+        [VM] * 5 + [ANY] * (2 * n),
+        (pos, valid, hidden, cotangent, gain.reshape(1, D), weights_full, *sources, *dws, *was_l, *was_r),
+        [
+            *group_scratch(2 * rows, len(sources)),
+            *sums_scratch(len(first), packed),
+            *again(sums_scratch(len(first), packed)),
+            pltpu.VMEM((rows, heads), BF),
+            pltpu.SemaphoreType.DMA,
+            pltpu.SemaphoreType.DMA,
+        ],
+        20 << 30,
+    )
+    return out[:5], out[5 : 5 + n], out[5 + n :]
+
+
+def attention_back_kernel(outer, q_block, steps, len_ref, qkv_ref, lse_ref, cos_ref, sin_ref, own_ref, other_ref, *refs):
+    n = len(steps)
+    dws, refs = refs[:n], refs[n:]
+    was_l, refs = refs[:n], refs[n:]
+    was_r, refs = refs[:n], refs[n:]
+    f_dw, f_left, f_right, refs = *refs[:3], refs[3:]
+    outs, fin_ref, refs = refs[:2], refs[2], refs[3:]
+    to_l, refs = refs[:n], refs[n:]
+    to_r, refs = refs[:n], refs[n:]
+    do_ref, dq_ref, dk_ref, dv_ref = refs[:4]
+    sums_refs, final_refs = refs[4:10], refs[10:]
+    _, t, _, _ = place()
+    greet(outer, (1, 2, 3), False)
+    sums = Sums(outer, steps, dws, was_l, was_r, to_l, to_r, *sums_refs)
+    final = Final(outer, f_dw, f_left, f_right, final_refs[0], sums_refs[1], fin_ref, *final_refs[1:])
+    sums.load()
+    sums.send()
+    final.send()
+    length = len_ref[0]
+    rows, own_rows = qkv_ref.shape[0], own_ref.shape[0]
+    groups = own_ref.shape[1] // LANES
+    scale = 1.0 / math.sqrt(HD)
+
+    def per_group(g, carry):
+        q_lanes = pl.ds(pl.multiple_of(g * 2 * LANES, LANES), LANES)
+        kv_lanes = pl.ds(pl.multiple_of(g * 2 * LANES + LANES, LANES), LANES)
+        o_lanes = pl.ds(pl.multiple_of(g * LANES, LANES), LANES)
+        for half, grad_ref in ((t, own_ref), (1 - t, other_ref)):
+            do_ref[pl.ds(pl.multiple_of(half * own_rows, own_rows), own_rows), :] = grad_ref[:, o_lanes]
+        keys, values = doubled(qkv_ref[:, kv_lanes])
+        dk_ref[...] = jnp.zeros_like(dk_ref)
+        dv_ref[...] = jnp.zeros_like(dv_ref)
+        for b in range(rows // q_block):
+            start, n_keys = b * q_block, (b + 1) * q_block
+            q = head_pair(qkv_ref[start : start + q_block, q_lanes])
+            grad = head_pair(do_ref[start : start + q_block, :])
+            scores = mm_nt(keys[:n_keys], q) * scale
+            probs = jnp.where(
+                allowed(n_keys, q_block, start, length), jnp.exp(scores - lse_ref[g, b : b + 1, :]), 0.0
+            )
+            prob_grad = mm_nt(values[:n_keys], grad)
+            center = jnp.sum(probs * prob_grad, axis=0, keepdims=True)
+            score_grad = (probs * (prob_grad - center)).astype(BF)
+            dq_ref[start : start + q_block, :] = head_join(mm_tn(score_grad, keys[:n_keys])) * scale
+            dk_ref[:n_keys, :] += mm(score_grad, q)
+            dv_ref[:n_keys, :] += mm(probs.astype(BF), grad)
+        for p, half in enumerate((t, 1 - t)):
+            at = pl.ds(pl.multiple_of(half * own_rows, own_rows), own_rows)
+            cosine, sine = cos_ref[at, :], sin_ref[at, :]
+            dq = dq_ref[at, :]
+            outs[p][:, q_lanes] = (dq * cosine - swap_halves(dq) * sine).astype(BF)
+            dk, dv = dk_ref[at, :] * scale, dv_ref[at, :]
+            dk = dk + pltpu.roll(dk, HD, 1)
+            dv = dv + pltpu.roll(dv, HD, 1)
+            dk = dk * cosine - swap_halves(dk) * sine
+            first = lax.broadcasted_iota(jnp.int32, dk.shape, 1) < HD
+            outs[p][:, kv_lanes] = jnp.where(first, dk, dv).astype(BF)
+        return carry
+
+    lax.fori_loop(0, groups, per_group, 0)
+    final.wait()
+    sums.wait()
+
+
+def attention_back(outer, q_block, length, qkv, lse, cosine, sine, grads, steps, dws, was_l, was_r, final):
+    rows, width = qkv.shape
+    n = len(steps)
+    packed = dws[0].shape[2]
+    hop = jax.ShapeDtypeStruct((GROUP, packed, D), BF)
+    out = remote_call(
+        functools.partial(attention_back_kernel, outer, q_block, steps),
+        "attention_back",
+        12,
+        [jax.ShapeDtypeStruct((rows // 2, width), BF)] * 2 + [hop] * (1 + 2 * n),
+        [SMEM] + [VM] * 6 + [ANY] * (3 * n + 3),
+        [VM] * 2 + [ANY] * (1 + 2 * n),
+        (length, qkv, lse, cosine, sine, *grads, *dws, *was_l, *was_r, *final),
+        [
+            pltpu.VMEM((rows, LANES), BF),
+            pltpu.VMEM((rows, LANES), F32),
+            pltpu.VMEM((rows, LANES), F32),
+            pltpu.VMEM((rows, LANES), F32),
+            *sums_scratch(n, packed),
+            *final_scratch(packed),
+        ],
+        30 << 30,
+    )
+    return out[:2], out[2], out[3 : 3 + n], out[3 + n :]
+
+
+def finish_kernel(outer, in_rows, len_ref, pos_ref, gate_ref, valid_ref, hidden_ref, hgrad_ref, x_ref, gain_ref, w_any, *refs):
+    (no_ref, nx_ref, po_ref, px_ref, ao_ref, sg_ref), refs = refs[:6], refs[6:]
+    n_experts = pos_ref.shape[2]
+    ys, refs = refs[:n_experts], refs[n_experts:]
+    dws, refs = refs[:3], refs[3:]
+    done, refs = refs[:2], refs[2:]
+    was_l, refs = refs[:2], refs[2:]
+    was_r, refs = refs[:2], refs[2:]
+    out_ref, tgrad_ref, gains_ref, qkv_ref, outw_ref = refs[:5]
+    fins, to_l, to_r, refs = refs[5:8], refs[8:11], refs[11:14], refs[14:]
+    (held, far, come, near, come_ab, last_ab, l_sem, s_sem, r_sem), refs = refs[:9], refs[9:]
+    sums_a, refs = refs[:6], refs[6:]
+    sums_b, refs = (*sums_a[:2], *refs[:4]), refs[4:]
+    final_refs, refs = [refs[5 * k : 5 * k + 5] for k in range(3)], refs[15:]
+    part_ref, theirs_ref, p_send, p_recv = refs[:4]
+    refs = refs[4:]
+    qp, q_core, q_y, q_z, q_send, q_recv = refs[:6]
+    g_buf, g_come, g_z, g_send, g_recv, w_ref, w_sem = refs[6:]
+    d, t, o, i = place()
+    y, c = i // 2, i % 2
+    rows = hidden_ref.shape[0]
+    width = w_ref.shape[1]
+    w_copy = pltpu.make_async_copy(w_any.at[:, pl.ds(0, width)], w_ref, w_sem)
+    w_copy.start()
+    greet_all(outer)
+    sums = Sums(outer, (2, 3), [dws[2], dws[1]], was_l, was_r, to_l[:2], to_r[:2], *sums_a)
+    last = Sums(outer, (3,), [dws[2]], to_l[:1], to_r[:1], to_l[2:], to_r[2:], *sums_b)
+    came = [done, (to_l[1], to_r[1]), (to_l[2], to_r[2])]
+    finals = [
+        Final(outer, dws[k], *came[k], final_refs[k][0], sums_a[1], fins[k], *final_refs[k][1:]) for k in range(3)
+    ]
+    group = GroupSum(far, come, near, come_ab, last_ab, s_sem, r_sem)
+    mixer = Mixer(ys, pos_ref, gate_ref, held, l_sem)
+    sums.load()
+    sums.send()
+
+    w_copy.wait()
+    part_ref[...] = mm_nt(px_ref[...], w_ref[...]).astype(BF)
+    exchange = to_x(part_ref, theirs_ref, p_send, p_recv)
+    exchange.start()
+
+    each = qkv_ref.shape[0]
+
+    def weights_block(k, carry):
+        lanes = pl.ds(pl.multiple_of(k * GROUP * each, GROUP * each), GROUP * each)
+        total = (mm_tn(no_ref[:, lanes], po_ref[...]) + mm_tn(nx_ref[:, lanes], px_ref[...])).astype(BF)
+        for r in range(GROUP):
+            qp[k, r // 2, r % 2, :, :width] = total[r * each : (r + 1) * each]
+            at = pl.ds(pl.multiple_of((k * GROUP + r) * each, each), each)
+            qp[k, r // 2, r % 2, :, width:] = ao_ref[at, :]
+        return carry
+
+    lax.fori_loop(0, outer, weights_block, 0)
+    to_core = to_dp(1, qp.at[:, :, 1 - c], q_core, q_send.at[0], q_recv.at[0])
+    to_core.start()
+    finals[0].send()
+
+    mixer.load(2, 0)
+    mixer.load(3, 1)
+    mixer.mix(2, 0, group.far.at[0])
+    group.core[0].start()
+    mixer.load(1, 0)
+    to_core.wait()
+
+    def add_core(k, carry):
+        for r in range(2):
+            qp[k, r, c] = (qp[k, r, c].astype(F32) + q_core[k, r].astype(F32)).astype(BF)
+        return carry
+
+    lax.fori_loop(0, outer, add_core, 0)
+    to_y = to_dp(2, qp.at[:, 1 - y, c], q_y, q_send.at[1], q_recv.at[1])
+    to_y.start()
+    mixer.mix(3, 1, group.far.at[1])
+    group.core[1].start()
+    mixer.load(0, 1)
+
+    exchange.wait()
+    gain_grad = jnp.zeros((1, D), F32)
+    quarter = rows // 4
+    for p in range(4):
+        at = slice(p * quarter, (p + 1) * quarter)
+        normed_grad = mm_nt(po_ref[at], w_ref[:, :width]).astype(BF).astype(F32) + theirs_ref[at].astype(F32)
+        x = x_ref[at].astype(F32)
+        inverse = lax.rsqrt(jnp.mean(x * x, axis=-1, keepdims=True) + EPSILON)
+        gain_grad = gain_grad + jnp.sum(normed_grad * (x * inverse), axis=0, keepdims=True)
+        scaled = normed_grad * gain_ref[...]
+        tgrad_ref[at] = (
+            hgrad_ref[at]
+            + inverse * scaled
+            - x * (inverse * inverse * inverse * jnp.mean(scaled * x, axis=-1, keepdims=True))
+        )
+    g_buf[0, 0:1, :] = gain_grad
+    g_buf[0, 1:2, :] = sg_ref[...]
+    g_buf[0, 2:8, :] = jnp.zeros((6, D), F32)
+    g_moves = [
+        to_x(g_buf.at[0], g_come.at[0], g_send.at[0], g_recv.at[0]),
+        to_dp(1, g_buf.at[1], g_come.at[1], g_send.at[1], g_recv.at[1]),
+        to_dp(2, g_buf.at[2], g_come.at[2], g_send.at[2], g_recv.at[2]),
+    ]
+    g_moves[0].start()
+    g_moves[0].wait()
+    g_buf[1] = g_buf[0] + g_come[0]
+    g_moves[1].start()
+    to_y.wait()
+
+    def add_y(k, carry):
+        qp[k, y, c] = (qp[k, y, c].astype(F32) + q_y[k].astype(F32)).astype(BF)
+        return carry
+
+    lax.fori_loop(0, outer, add_y, 0)
+    z_moves = []
+    for k in range(1, outer):
+        peer = (o + k) % outer
+        z_moves.append(
+            pltpu.make_async_remote_copy(
+                qp.at[peer, y, c],
+                q_z.at[k - 1],
+                q_send.at[1 + k],
+                q_recv.at[1 + k],
+                device_id=(peer * GROUP + i, t),
+                device_id_type=MESH,
+            )
+        )
+    for move in z_moves:
+        move.start()
+    group.core[1].wait_recv()
+    mixer.mix(1, 0, group.near.at[1], group.come.at[1])
+    group.a.start()
+    group.b[1].start()
+    sums.wait()
+    last.load()
+    last.send()
+    g_moves[1].wait()
+    g_buf[2] = g_buf[1] + g_come[1]
+    g_moves[2].start()
+    group.core[0].wait_recv()
+    mixer.mix(0, 1, group.near.at[0], group.come.at[0])
+    group.b[0].start()
+    g_moves[2].wait()
+    g_z[0] = g_buf[2] + g_come[2]
+    gz_moves = []
+    for k in range(1, outer):
+        peer = (o + k) % outer
+        gz_moves.append(
+            pltpu.make_async_remote_copy(
+                g_z.at[0],
+                g_z.at[k],
+                g_send.at[2 + k],
+                g_recv.at[2 + k],
+                device_id=(peer * GROUP + i, t),
+                device_id_type=MESH,
+            )
+        )
+    for move in gz_moves:
+        move.start()
+    group.second()
+    finals[1].send()
+    for move in z_moves:
+        move.wait()
+    total = qp[o, y, c].astype(F32)
+    for k in range(1, outer):
+        total = total + q_z[k - 1].astype(F32)
+    qkv_ref[...] = total[:, :width]
+    outw_ref[...] = total[:, width:]
+    for move in gz_moves:
+        move.wait()
+    gains = g_z[(o + outer) % outer]
+    for k in range(1, outer):
+        gains = gains + g_z[(o - k + outer) % outer]
+    gains_ref[...] = gains
+    for p in range(2):
+        at = slice(p * rows // 2, (p + 1) * rows // 2)
+        out_ref[at] = jnp.where(valid_ref[at] > 0, hidden_ref[at] + group.terms(p), 0.0).astype(BF)
+    last.wait()
+    finals[2].send()
+    group.sent()
+    for final in finals:
+        final.wait()
+
+
+def finish(outer, in_rows, length, pos, gate, valid, hidden, hgrad, x, gain, weights_full, extra, ys, dws, done, was_l, was_r):
+    rows = hidden.shape[0]
+    n = len(ys)
+    packed = dws[0].shape[2]
+    width = weights_full.shape[1] // 2
+    heads = width // 2
+    each = D // (outer * GROUP)
+    hop = jax.ShapeDtypeStruct((GROUP, packed, D), BF)
+    columns = width + heads
+    return remote_call(
+        functools.partial(finish_kernel, outer, in_rows),
+        "finish",
+        11,
+        [
+            jax.ShapeDtypeStruct((rows, D), BF),
+            jax.ShapeDtypeStruct((rows, D), F32),
+            jax.ShapeDtypeStruct((8, D), F32),
+            jax.ShapeDtypeStruct((each, width), F32),
+            jax.ShapeDtypeStruct((each, heads), F32),
+        ]
+        + [hop] * 9,
+        [SMEM] + [VM] * 7 + [ANY] + [VM] * 6 + [ANY] * (n + 9),
+        [VM] * 5 + [ANY] * 9,
+        (length, pos, gate, valid, hidden, hgrad, x, gain.reshape(1, D), weights_full, *extra, *ys, *dws, *done, *was_l, *was_r),
+        [
+            *group_scratch(2 * rows, n),
+            *sums_scratch(2, packed),
+            *again(sums_scratch(1, packed)),
+            *final_scratch(packed) * 3,
+            pltpu.VMEM((rows, D), BF),
+            pltpu.VMEM((rows, D), BF),
+            pltpu.SemaphoreType.DMA,
+            pltpu.SemaphoreType.DMA,
+            pltpu.VMEM((outer, 2, 2, each, columns), BF),
+            pltpu.VMEM((outer, 2, each, columns), BF),
+            pltpu.VMEM((outer, each, columns), BF),
+            pltpu.VMEM((outer - 1, each, columns), BF),
+            pltpu.SemaphoreType.DMA((1 + outer,)),
+            pltpu.SemaphoreType.DMA((1 + outer,)),
+            pltpu.VMEM((3, 8, D), F32),
+            pltpu.VMEM((3, 8, D), F32),
+            pltpu.VMEM((outer, 8, D), F32),
+            pltpu.SemaphoreType.DMA((2 + outer,)),
+            pltpu.SemaphoreType.DMA((2 + outer,)),
+            pltpu.VMEM((D, width), BF),
+            pltpu.SemaphoreType.DMA,
+        ],
+        30 << 30,
+    )
+
+
+def settle_kernel(n, in_rows, idx_ref, *refs):
+    sources, (in_ref, down_ref) = refs[:n], refs[n:]
+    j = pl.program_id(0)
+    for k in range(n):
+
+        @pl.when(j == k)
+        def _(k=k):
+            in_ref[0] = sources[k][0, :in_rows, :].astype(F32)
+            down_ref[0] = sources[k][0, in_rows:, :].astype(F32)
+
+
+def settle_experts(idx, fins, in_rows):
+    n = len(fins)
+    _, packed, _ = fins[0].shape
+    experts = n * GROUP
+
+    def source(k):
+        return lambda j, m, idx_ref: (jnp.where(j == k, m, jnp.where(j < k, 0, GROUP - 1)), 0, 0)
+
+    def target(j, m, idx_ref):
+        return ((idx_ref[1] ^ m) * n + j, 0, 0)
+
+    return pl.pallas_call(
+        functools.partial(settle_kernel, n, in_rows),
+        name="settle_experts",
+        out_shape=[
+            jax.ShapeDtypeStruct((experts, in_rows, D), F32),
+            jax.ShapeDtypeStruct((experts, packed - in_rows, D), F32),
+        ],
+        grid_spec=pltpu.PrefetchScalarGridSpec(
+            num_scalar_prefetch=1,
+            grid=(n, GROUP),
+            in_specs=[pl.BlockSpec((1, packed, D), source(k)) for k in range(n)],
+            out_specs=[pl.BlockSpec((1, in_rows, D), target), pl.BlockSpec((1, packed - in_rows, D), target)],
+        ),
+        compiler_params=pltpu.CompilerParams(vmem_limit_bytes=VMEM_LIMIT),
+        cost_estimate=pl.CostEstimate(flops=0, bytes_accessed=9 << 20, transcendentals=0),
+    )(idx, *fins)
 
 
 def layer(
@@ -1261,15 +1986,17 @@
         three_l, three_r = [moved_l[0]], [moved_r[0]]
         two_l.append(moved_l[1])
         two_r.append(moved_r[1])
-        plans = [
-            ((3, 2), [two_l[1], one_l[3]], [two_r[1], one_r[3]]),
-            ((3,), [two_l[2]], [two_r[2]]),
-            None,
-            ((), [], []),
+        hop_plans = [
+            lambda: ((3, 2), [two_l[1], one_l[3]], [two_r[1], one_r[3]]),
+            lambda: ((3,), [two_l[2]], [two_r[2]]),
+            lambda: ((3,), [two_l[3]], [two_r[3]]),
+            lambda: ((), [], []),
         ]
+        sums_l, sums_r = [], []
         for j in range(own_experts):
-            plan = plans[j] or ((3,), [two_l[3]], [two_r[3]])
-            (y, dx, dw), moved_l, moved_r = expert_step(
+            first_grad = weight_grads[:1]
+            sum_plan = ((j,), first_grad, sums_l or first_grad, sums_r or first_grad) if j else ((), [], [], [])
+            (y, dx, dw), moved_l, moved_r, sums_l, sums_r = expert_step(
                 j,
                 outer,
                 in_rows,
@@ -1279,7 +2006,8 @@
                 own_weights[j],
                 [one_l[j], two_l[j], three_l[j]],
                 [one_r[j], two_r[j], three_r[j]],
-                *plan,
+                hop_plans[j](),
+                sum_plan,
             )
             three_l.extend(moved_l[:1])
             three_r.extend(moved_r[:1])
@@ -1288,8 +2016,71 @@
             expert_outs.append(y)
             row_grads.append(dx)
             weight_grads.append(dw)
-        qkv_full = weights_full[:, :width]
-        out_parts = [weights_full[:, width : width + width // 2], weights_full[:, width + width // 2 :]]
+        valid_column = valid_rows.astype(F32)[:, None]
+        _, dw_b, dw_c, dw_d = weight_grads
+        main, sum_l, sum_r = rows_back(
+            outer,
+            pos_columns,
+            valid_column,
+            hidden,
+            cotangent,
+            second_gain,
+            weights_full,
+            row_grads,
+            (1, 1),
+            ((2, 0), (2, 1)),
+            [dw_b, dw_c],
+            [dw_b, dw_c],
+            [dw_b, dw_c],
+        )
+        hidden_grad, branch_grad, second_gain_part, attn_grad_own, attn_grad_other = main
+        projected, fin_a, three_l, three_r = attention_back(
+            outer,
+            q_block,
+            lengths,
+            qkv,
+            lse,
+            cosine,
+            sine,
+            [attn_grad_own, attn_grad_other],
+            (3, 1),
+            [dw_b, dw_d],
+            [sum_l[2], dw_d],
+            [sum_r[2], dw_d],
+            [weight_grads[0], sums_l[0], sums_r[0]],
+        )
+        out_own, out_other = (mm_tn(branch_grad, part).astype(BF) for part in attn_parts)
+        attn_out_part = (out_own.astype(F32) + beside(out_other).astype(F32)).astype(BF)
+        output, tokens_grad, gains, qkv_grad, attn_out_grad, *fins = finish(
+            outer,
+            in_rows,
+            lengths,
+            pos_columns,
+            gate_columns,
+            valid_column,
+            hidden,
+            hidden_grad,
+            tokens,
+            first_gain,
+            weights_full,
+            [normed_one, other, *projected, attn_out_part, second_gain_part],
+            expert_outs,
+            [dw_b, dw_c, dw_d],
+            [three_l[0], three_r[0]],
+            [three_l[1], sum_l[3]],
+            [three_r[1], sum_r[3]],
+        )
+        expert_in_grad, expert_out_grad = settle_experts(idx, [fin_a, *fins[:3]], in_rows)
+        return (
+            output,
+            tokens_grad,
+            gains[0],
+            qkv_grad.reshape(qkv_weight.shape),
+            attn_out_grad.T,
+            gains[1],
+            expert_in_grad,
+            expert_out_grad,
+        )
     else:
         qkv_full = lax.all_gather(qkv_weight.reshape(qkv_weight.shape[0], width), "dp", axis=0, tiled=True)
         out_full = lax.all_gather(attn_out_weight.T, "dp", axis=0, tiled=True)

time: 697 us -> 640 us (0.918)
  Pallas kernels: 393 us -> 519 us
  waiting for transfers between devices: 135 us -> 49.8 us
  starting transfers between devices: 49.5 us -> 12.5 us
  other arithmetic: 41.2 us -> 14.7 us
  matrix products: 21 us -> 4.11 us
  local copies, waits for them, and re-layouts: 29.7 us -> 17.1 us
    pallas_call x6 -> x10, Pallas kernels: 280 us -> 503 us  [remote_call(): pl.pallas_call(kernel, name=name, out_shape=out_shape, in_specs=in_specs,...]
    pallas_call x11 -> x1, Pallas kernels: 89.3 us -> 4.52 us  [call(): pl.pallas_call(kernel, name=name, out_shape=out_shape, in_specs=in_specs,...]
    ppermute x13 -> x4, waiting for transfers between devices: 52 us -> 12 us  [beside(): return lax.ppermute(v, 'tensor', [(0, 1), (1, 0)])]
    ppermute x32 -> x6, starting transfers between devices: 38.4 us -> 6.44 us  [across(): return lax.ppermute(v, 'dp', [(a, a ^ m) for a in range(n_dp)])]
    reduce_scatter x6 -> x0, waiting for transfers between devices: 29.1 us -> none  [the longest x1 29.1 us: layer(): lax.psum_scatter(qkv_part.astype(BF), 'dp', scatter_dimension=0, tiled=True)]
    ppermute x32 -> x6, waiting for transfers between devices: 53.8 us -> 37.7 us  [across(): return lax.ppermute(v, 'dp', [(a, a ^ m) for a in range(n_dp)])]
    convert_element_type x10 -> x1, other arithmetic: 15.8 us -> 1.27 us  [layer(): (out_own.astype(F32) + beside(out_other).astype(F32)).astype(BF)]
    pallas_call x1, Pallas kernels: 23.9 us -> 11.8 us  [settle_experts(): pl.pallas_call(functools.partial(settle_kernel, n, in_rows), name='settle...]
  transfers between devices with their start and end apart: 52 -> 11, of which waited for: 17 -> 3; matrix products, arithmetic and copies ran while one was open for 13% -> 4% of each run, Pallas kernels for 29% -> 7%
where the time goes in v3:
time: 640 us; the launch traced here: 633 us
  Pallas kernels  519 us (81%)
  waiting for transfers between devices  49.8 us (8%)
  local copies, waits for them, and re-layouts  17.1 us (3%)
  between operations  15.2 us (2%)
  other arithmetic  14.7 us (2%)
  starting transfers between devices  12.5 us (2%)
    pallas_call x10, Pallas kernels, remote_call(): pl.pallas_call(kernel, name=name, out_shape=out_shape, in_specs=in_specs,...  503 us
    ppermute x6, waiting for transfers between devices, across(): return lax.ppermute(v, 'dp', [(a, a ^ m) for a in range(n_dp)])  37.7 us
  transfers between devices with their start and end apart: 11, of which 3 were waited for; matrix products, arithmetic and copies ran while one was open for 4% of the time, Pallas kernels for 7%

profile of v3, /device:TPU:9, one launch (start us, length us, event | category | flops | bytes accessed | tf_op | source)
XLA Modules:
  0.0 632.5 jit_solution(2087068226387271727)
XLA Ops:
  7.2 0.0 all-gather.2.cloned.1.call-start
  7.2 1.3 collective-permute-start.5
  8.5 0.9 copy.46
  9.4 0.0 copy-start
  9.5 1.2 collective-permute-done.5
  10.6 1.6 pad_maximum_fusion.6
  12.2 0.0 all-gather.2.cloned.1.call-update
  12.9 0.6 pad_add_fusion.idx_ref
  13.5 4.5 pack_weights.1
  18.0 0.0 copy-start.3
  18.1 1.9 collective-permute-start.6
  19.9 1.3 collective-permute-start.7
  21.2 0.5 collective-permute-start.8
  21.7 0.2 select_reduce_fusion
  21.9 1.3 collective-permute-start
  23.2 0.3 fusion.3
  23.5 2.1 fusion.19
  25.6 0.1 broadcast_select_fusion
  25.7 0.0 copy-start.10
  25.7 1.1 fusion.18
  26.8 1.9 fusion.12
  28.7 1.3 fusion.5.own_ref.refs_0_
  30.0 1.3 collective-permute-start.1
  31.3 1.8 pad_maximum_fusion.4
  33.2 0.7 collective-permute-start.2
  33.9 37.7 %collective-permute-done.1 = bf16[32,1024]{1,0:T(8,128)(2,1)S(1)} collective-permute-done((bf16[32,1024]{1,0:T(8,128)(2,1)S(1)}, bf16[32,1024]{1,0:T(8,128)(2,1)S(1)}, u32[]{:S(2)}, u32[]{:S(2)}) %collective-permute-start.1) | collective-permute-done | bytes 65568 | tf_op jit(solution)/shard_map/ppermute | solution.py:1901
  71.6 0.9 collective-permute-start.3
  72.4 0.7 fusion.11.valid_ref
  73.2 0.0 collective-permute-done.2
  73.2 1.2 collective-permute-start.4
  74.4 0.5 copy.45
  74.9 1.0 copy.41.gate_ref
  75.9 1.4 select_convert_fusion
  77.3 0.0 copy-start.1
  77.4 1.3 copy.42.pos_ref
  78.7 1.5 convert_bitcast_fusion.gate_ref
  80.1 0.0 collective-permute-done.6
  80.1 1.3 fusion.20
  81.5 1.3 fusion.21
  82.8 1.3 fusion.22
  84.1 1.0 pad_maximum_fusion.2.refs_4_.own
  85.0 1.0 pad_maximum_fusion.3.refs_6_.refs_9_.own
  86.0 1.4 pad_maximum_fusion
  87.4 10.9 %collective-permute-done.4.other_ref.refs_1_ = bf16[512,1024]{1,0:T(8,128)(2,1)} collective-permute-done((bf16[512,1024]{1,0:T(8,128)(2,1)}, bf16[512,1024]{1,0:T(8,128)(2,1)}, u32[]{:S(2)}, u32[]{:S(2)}) %collective-permute-start.4) | collective-permute-done | bytes 1048608 | tf_op jit(solution)/shard_map/ppermute | solution.py:1904
  98.3 59.7 %attention.1 = (bf16[1024,1024]{1,0:T(8,128)(2,1)}, f32[4,4,512]{2,1,0:T(4,128)}, bf16[512,512]{1,0:T(8,128)(2,1)}, bf16[512,512]{1,0:T(8,128)(2,1)}, f32[512,10...) custom-call(s32[1]{0:T(128)} %copy.50.len_ref, ...), custom_call_target="tpu_custom_call" | custom-call | flops 32212254720 | bytes 8388608 | tf_op jit(solution)/shard_map/attention/pallas_call | solution.py:664
  158.0 58.4 %spread.1 = (bf16[4,4,256,1024]{3,2,1,0:T(8,128)(2,1)}, bf16[3,4,256,1024]{3,2,1,0:T(8,128)(2,1)}, bf16[4,4,288,1024]{3,2,1,0:T(8,128)(2,1)}, bf16[4,96,1024]{2,...) custom-call(s32[4,4,1024]{2,1,0:T(4,128)} %copy.42.pos_ref, ...), custom_call_target="tpu_custom_call" | custom-call | flops 12884901888 | bytes 8388608 | tf_op jit(solution)/shard_map/spread/pallas_call | solution.py:664
  216.4 38.7 %hand_out.1 = (bf16[4,4,288,1024]{3,2,1,0:T(8,128)(2,1)}, bf16[4,96,1024]{2,1,0:T(8,128)(2,1)}, bf16[4,96,1024]{2,1,0:T(8,128)(2,1)}, bf16[4,96,1024]{2,1,0:T(8,128)(2,1)}, bf16[4,96,1024]{2,1,0:T(8,128)(2,1)}) custom-call(s32[4,4,1024]{2,1,0:T(4,128)} %copy.42.pos_ref, bf16[256,1024]{1,0:T(8,128)(2,1)} %get-tuple-element.99.na_ref, ...), custom_call_target="tpu_custom_call" | custom-call | flops 12884901888 | bytes 8388608 | tf_op jit(solution)/shard_map/hand_out/pallas_call | solution.py:664
  255.2 37.9 %expert_step.4 = (bf16[4,288,1024]{2,1,0:T(8,128)(2,1)}, bf16[4,288,1024]{2,1,0:T(8,128)(2,1)}, bf16[4,4,96,1024]{3,2,1,0:T(8,128)(2,1)}, bf16[4,96,1024]{2,1,0:...) custom-call(bf16[4,4,288,1024]{3,2,1,0:T(8,128)(2,1)} %get-tuple-element.114, ...), custom_call_target="tpu_custom_call" | custom-call | flops 10871635968 | bytes 8388608 | tf_op jit(solution)/shard_map/expert_step/pallas_call | solution.py:664
  293.1 24.0 %expert_step.5 = (bf16[4,288,1024]{2,1,0:T(8,128)(2,1)}, bf16[4,288,1024]{2,1,0:T(8,128)(2,1)}, bf16[4,4,96,1024]{3,2,1,0:T(8,128)(2,1)}, bf16[4,96,1024]{2,1,0:...) custom-call(bf16[4,4,288,1024]{3,2,1,0:T(8,128)(2,1)} %get-tuple-element.114, ...), custom_call_target="tpu_custom_call" | custom-call | flops 10871635968 | bytes 8388608 | tf_op jit(solution)/shard_map/expert_step/pallas_call | solution.py:664
  317.1 23.4 %expert_step.6 = (bf16[4,288,1024]{2,1,0:T(8,128)(2,1)}, bf16[4,288,1024]{2,1,0:T(8,128)(2,1)}, bf16[4,4,96,1024]{3,2,1,0:T(8,128)(2,1)}, bf16[4,96,1024]{2,1,0:...) custom-call(bf16[4,4,288,1024]{3,2,1,0:T(8,128)(2,1)} %get-tuple-element.114, ...), custom_call_target="tpu_custom_call" | custom-call | flops 10871635968 | bytes 8388608 | tf_op jit(solution)/shard_map/expert_step/pallas_call | solution.py:664
  340.5 22.9 %expert_step.7 = (bf16[4,288,1024]{2,1,0:T(8,128)(2,1)}, bf16[4,288,1024]{2,1,0:T(8,128)(2,1)}, bf16[4,4,96,1024]{3,2,1,0:T(8,128)(2,1)}, bf16[4,96,1024]{2,1,0:T(8,128)(2,1)}, bf16[4,96,1024]{2,1,0:T(8,128)(2,1)}) custom-call(bf16[4,4,288,1024]{3,2,1,0:T(8,128)(2,1)} %get-tuple-element.114.x_ref, bf16[4,4,288,1024]{3,2,1,0:T(8,128)(2,1)} %get-tuple-element.115.g_ref, ...), custom_call_target="tpu_custom_call" | custom-call | flops 10871635968 | bytes 8388608 | tf_op jit(solution)/shard_map/expert_step/pallas_call | solution.py:664
  363.4 92.2 %rows_back.1 = (f32[512,1024]{1,0:T(8,128)}, bf16[512,1024]{1,0:T(8,128)(2,1)}, f32[1,1024]{1,0:T(1,128)}, bf16[512,512]{1,0:T(8,128)(2,1)}, bf16[512,512]{1,0:T...) custom-call(s32[4,1024,4]{2,1,0:T(8,128)} %bitcast.34, ...), custom_call_target="tpu_custom_call" | custom-call | flops 21474836480 | bytes 8388608 | tf_op jit(solution)/shard_map/rows_back/pallas_call | solution.py:664
  455.6 2.0 convolution_convert_fusion
  457.6 2.3 collective-permute-start.9
  459.9 39.8 %attention_back.1 = (bf16[512,1024]{1,0:T(8,128)(2,1)}, bf16[512,1024]{1,0:T(8,128)(2,1)}, bf16[4,96,1024]{2,1,0:T(8,128)(2,1)}, bf16[4,96,1024]{2,1,0:T(8,128)(...) custom-call(s32[1]{0:T(128)} %copy.50.len_ref, ...), custom_call_target="tpu_custom_call" | custom-call | flops 32212254720 | bytes 8388608 | tf_op jit(solution)/shard_map/attention_back/pallas_call | solution.py:664
  499.6 0.7 convolution_convert_fusion.1
  500.4 1.3 add_convert_fusion.refs_4_
  501.7 105.7 %finish.1 = (bf16[512,1024]{1,0:T(8,128)(2,1)}, f32[512,1024]{1,0:T(8,128)}, f32[8,1024]{1,0:T(8,128)}, f32[64,1024]{1,0:T(8,128)}, f32[64,512]{1,0:T(8,128)}, /...) custom-call(s32[1]{0:T(128)} %copy.50.len_ref, ...), custom_call_target="tpu_custom_call" | custom-call | flops 32212254720 | bytes 8388608 | tf_op jit(solution)/shard_map/finish/pallas_call | solution.py:664
  607.4 1.9 reshape.76
  609.3 1.4 fusion.23
  610.7 11.8 %settle_experts.1 = (f32[16,64,1024]{2,1,0:T(8,128)}, f32[16,32,1024]{2,1,0:T(8,128)}) custom-call(s32[4]{0:T(128)} %pad_add_fusion.idx_ref, bf16[4,96,1024]{2,1,0:T(8,128)(2,1)} %get-tuple-element.174.refs_0_, bf16[4,96,1024]{2,1,0:T(8,128)(2,1)} %get-tuple-element.175.refs_1_, bf16[4,96,1024]{2,1,0:T(8,128)(2,1)} %get-tuple-element.176.refs_2_, ...), custom_call_target="tpu_custom_call" | custom-call | bytes 9437184 | tf_op jit(solution)/shard_map/settle_experts/pallas_call | solution.py:1853
  622.6 1.0 copy.51
  623.5 1.3 copy.52
  624.9 0.7 copy.53
  (40 shorter events, 0.1 us)
Async XLA Ops:
  7.2 91.1 %all-gather.2.cloned.1.call-start = ((), (), s32[]{:S(2)}) async-start(), calls=%async_computation | async-start | bytes 4456448 | tf_op jit(solution)/shard_map/all_gather | solution.py:1961
  7.2 3.4 collective-permute-start.5
  8.5 13.2 %copy-start.9 = (bf16[512,8]{0,1:T(8,128)(2,1)S(1)}, bf16[512,8]{0,1:T(8,128)(2,1)}, u32[]{:S(2)}) copy-start(bf16[512,8]{0,1:T(8,128)(2,1)} %param.15) | copy-start | bytes 24580
  8.5 13.2 %copy-start.8 = (s32[512,8]{0,1:T(8,128)S(1)}, s32[512,8]{0,1:T(8,128)}, u32[]{:S(2)}) copy-start(s32[512,8]{0,1:T(8,128)} %param.14) | copy-start | bytes 49156
  9.4 13.7 %copy-start = (bf16[512,1024]{1,0:T(8,128)(2,1)S(1)}, bf16[512,1024]{1,0:T(8,128)(2,1)}, u32[]{:S(2)}) copy-start(bf16[512,1024]{1,0:T(8,128)(2,1)} %x_ref.3) | copy-start | bytes 3145732
  18.0 7.5 %copy-start.3 = (bf16[512,1024]{1,0:T(8,128)(2,1)S(1)}, bf16[512,1024]{1,0:T(8,128)(2,1)}, u32[]{:S(2)}) copy-start(bf16[512,1024]{1,0:T(8,128)(2,1)} %cot_ref.1) | copy-start | bytes 3145732
  18.1 62.1 %collective-permute-start.6 = (bf16[4,96,1024]{2,1,0:T(8,128)(2,1)}, bf16[4,96,1024]{2,1,0:T(8,128)(2,1)}, u32[]{:S(2)}, u32[]{:S(2)}) collective-permute-start(bf16[4,96,1024]{2,1,0:T(8,128)(2,1)} %get-tuple-element.95), channel_id=1, source_target_pairs={{0,2},{2,0},{4,6},{6,4},{8,10},{10,8},{12,14},{14,12},{16,18},{18,... | collective-permute-start | bytes 2359304 | tf_op jit(solution)/shard_map/ppermute | solution.py:1901
  19.9 61.5 %collective-permute-start.7 = (bf16[4,96,1024]{2,1,0:T(8,128)(2,1)}, bf16[4,96,1024]{2,1,0:T(8,128)(2,1)}, u32[]{:S(2)}, u32[]{:S(2)}) collective-permute-start(bf16[4,96,1024]{2,1,0:T(8,128)(2,1)} %get-tuple-element.96), channel_id=1, source_target_pairs={{0,4},{2,6},{4,0},{6,2},{8,12},{10,14},{12,8},{14,10},{16,20},{18,... | collective-permute-start | bytes 2359304 | tf_op jit(solution)/shard_map/ppermute | solution.py:1901
  21.2 61.6 %collective-permute-start.8 = (bf16[4,96,1024]{2,1,0:T(8,128)(2,1)}, bf16[4,96,1024]{2,1,0:T(8,128)(2,1)}, u32[]{:S(2)}, u32[]{:S(2)}) collective-permute-start(bf16[4,96,1024]{2,1,0:T(8,128)(2,1)} %get-tuple-element.97), channel_id=1, source_target_pairs={{0,6},{2,4},{4,2},{6,0},{8,14},{10,12},{12,10},{14,8},{16,22},{18,... | collective-permute-start | bytes 2359304 | tf_op jit(solution)/shard_map/ppermute | solution.py:1901
  21.9 8.1 %collective-permute-start = (bf16[32,512]{1,0:T(8,128)(2,1)S(1)}, bf16[32,512]{1,0:T(8,128)(2,1)S(1)}, u32[]{:S(2)}, u32[]{:S(2)}) collective-permute-start(bf16[32,512]{1,0:T(8,128)(2,1)S(1)} %select_convert_fusion.1), channel_id=1, source_target_pairs={{0,1},{1,0},{2,3},{3,2},{4,5},{5,4},{6,7},{7,6},{8,9},{9,8},{10,11... | collective-permute-start | bytes 98312 | tf_op jit(solution)/shard_map/ppermute | solution.py:1904
  25.7 3.0 copy-start.10
  30.0 41.6 %collective-permute-start.1 = (bf16[32,1024]{1,0:T(8,128)(2,1)S(1)}, bf16[32,1024]{1,0:T(8,128)(2,1)S(1)}, u32[]{:S(2)}, u32[]{:S(2)}) collective-permute-start(bf16[32,1024]{1,0:T(8,128)(2,1)S(1)} %get-tuple-element.199), channel_id=1, source_target_pairs={{0,4},{2,6},{4,0},{6,2},{8,12},{10,14},{12,8},{14,10},{16,20},{18,... | collective-permute-start | bytes 196616 | tf_op jit(solution)/shard_map/ppermute | solution.py:1901
  33.2 40.0 %collective-permute-start.2 = (bf16[32,1024]{1,0:T(8,128)(2,1)S(1)}, bf16[32,1024]{1,0:T(8,128)(2,1)S(1)}, u32[]{:S(2)}, u32[]{:S(2)}) collective-permute-start(bf16[32,1024]{1,0:T(8,128)(2,1)S(1)} %get-tuple-element.199), channel_id=1, source_target_pairs={{0,2},{2,0},{4,6},{6,4},{8,10},{10,8},{12,14},{14,12},{16,18},{18,... | collective-permute-start | bytes 196616 | tf_op jit(solution)/shard_map/ppermute | solution.py:1901
  71.6 2.8 collective-permute-start.3
  73.2 25.1 %collective-permute-start.4 = (bf16[512,1024]{1,0:T(8,128)(2,1)}, bf16[512,1024]{1,0:T(8,128)(2,1)}, u32[]{:S(2)}, u32[]{:S(2)}) collective-permute-start(bf16[512,1024]{1,0:T(8,128)(2,1)} %fusion.5.own_ref.refs_0_), channel_id=1, source_target_pairs={{0,1},{1,0},{2,3},{3,2},{4,5},{5,4},{6,7},{7,6},{8,9},{9,8},{10,11... | collective-permute-start | bytes 3145736 | tf_op jit(solution)/shard_map/ppermute | solution.py:1904
  77.3 2.8 copy-start.1
  80.1 3.9 copy-start.6
  81.4 3.6 copy-start.5
  363.4 92.2 %copy-start.13 = (bf16[512,512]{1,0:T(8,128)(2,1)S(1)}, bf16[512,512]{1,0:T(8,128)(2,1)}, u32[]{:S(2)}) copy-start(bf16[512,512]{1,0:T(8,128)(2,1)} %get-tuple-element.157) | copy-start | bytes 1572868
  457.6 42.8 %collective-permute-start.9 = (bf16[1024,512]{1,0:T(8,128)(2,1)S(1)}, bf16[1024,512]{1,0:T(8,128)(2,1)S(1)}, u32[]{:S(2)}, u32[]{:S(2)}) collective-permute-start(bf16[1024,512]{1,0:T(8,128)(2,1)S(1)} %convolution_convert_fusion), channel_id=1, source_target_pairs={{0,1},{1,0},{2,3},{3,2},{4,5},{5,4},{6,7},{7,6},{8,9},{9,8},{10,11... | collective-permute-start | bytes 3145736 | tf_op jit(solution)/shard_map/ppermute | solution.py:1904
  459.9 39.8 %copy-start.11 = (bf16[512,1024]{1,0:T(8,128)(2,1)S(1)}, bf16[512,1024]{1,0:T(8,128)(2,1)}, u32[]{:S(2)}) copy-start(bf16[512,1024]{1,0:T(8,128)(2,1)} %get-tuple-element.155) | copy-start | bytes 3145732
  459.9 39.8 %copy-start.12 = (bf16[512,512]{1,0:T(8,128)(2,1)S(1)}, bf16[512,512]{1,0:T(8,128)(2,1)}, u32[]{:S(2)}) copy-start(bf16[512,512]{1,0:T(8,128)(2,1)} %get-tuple-element.156) | copy-start | bytes 1572868
  607.4 15.1 %copy-start.4 = (bf16[512,1024]{1,0:T(8,128)(2,1)S(1)}, bf16[512,1024]{1,0:T(8,128)(2,1)}, u32[]{:S(2)}) copy-start(bf16[512,1024]{1,0:T(8,128)(2,1)} %get-tuple-element.221) | copy-start | bytes 3145732
  610.7 12.8 %copy-start.2 = (f32[512,1024]{1,0:T(8,128)S(1)}, f32[512,1024]{1,0:T(8,128)}, u32[]{:S(2)}) copy-start(f32[512,1024]{1,0:T(8,128)} %get-tuple-element.222) | copy-start | bytes 6291460
  623.5 1.3 copy-start.7
Sparse Core Ops, SparseCore 0:
  12.3 67.4 all-gather.1

commit v4 on v3

--- a/solution.py
+++ b/solution.py
@@ -675,30 +675,280 @@
     )(*args)
 
 
+def collect_kernel(outer, in_rows, down_rows, shard_ref, normed_ref, gates_ref, freq_ref, in_ref, down_ref, *refs):
+    w_ref, other_ref, cos_ref, sin_ref, pos_ref, gate_ref, posc_ref, gatec_ref = refs[:8]
+    own_refs, packed_refs, to_left, to_right = refs[8:10], refs[10:12], refs[12], refs[13]
+    packed, gates_all, before, l_w, l_in, l_down, l_own = refs[14:21]
+    s_z, r_z, s_y, r_y, s_c, r_c, s_x, r_x, s_g, r_g, s_a, r_a, s_hop, r_hop = refs[21:]
+    d, t, o, i = place()
+    each = shard_ref.shape[0]
+    width = w_ref.shape[1] // 2
+    own_width = shard_ref.shape[1]
+    n_local = in_ref.shape[0]
+    n = n_local // GROUP
+    slot_rows = gates_all.shape[2]
+    half = slot_rows // 4
+
+    def block(which, index):
+        return pl.ds(pl.multiple_of((which * GROUP + index) * each, each), each)
+
+    def lanes(h):
+        return pl.ds(h * width, width)
+
+    local = pltpu.make_async_copy(shard_ref, w_ref.at[block(o, i), pl.ds(0, own_width)], l_w)
+    local.start()
+    packs = []
+    for j in range(n):
+        for m in range(GROUP):
+            source, k = flip(i, m) * n + j, j * GROUP + m
+            packs.append(
+                (
+                    pltpu.make_async_copy(in_ref.at[source], packed.at[j, m, pl.ds(0, in_rows)], l_in.at[k]),
+                    pltpu.make_async_copy(down_ref.at[source], packed.at[j, m, pl.ds(in_rows, down_rows)], l_down.at[k]),
+                )
+            )
+    for pair in packs:
+        for c in pair:
+            c.start()
+    greet_all(outer)
+
+    x_moves = [
+        to_x(shard_ref.at[:, pl.ds(width, own_width - width)], w_ref.at[block(o, i), pl.ds(own_width, 2 * width - own_width)], s_x.at[0], r_x.at[0]),
+        to_x(normed_ref, other_ref, s_x.at[1], r_x.at[1]),
+    ]
+    g_x = [
+        to_x(
+            gates_ref.at[:, pl.ds(p * half, half)],
+            gates_all.at[0, :, pl.ds((2 * p + 1) * half, half)],
+            s_g.at[p],
+            r_g.at[p],
+        )
+        for p in range(2)
+    ]
+    g_y = to_dp(2, gates_all.at[0], gates_all.at[1], s_g.at[2], r_g.at[2])
+    g_c = [to_dp(1, gates_all.at[s], gates_all.at[2 + s], s_g.at[3 + s], r_g.at[3 + s]) for s in range(2)]
+
+    def z_move(k, h):
+        peer = (o + k) % outer
+        source = shard_ref.at[:, pl.ds(0, width)] if h == 0 else w_ref.at[block(o, i), lanes(1)]
+        return pltpu.make_async_remote_copy(
+            source,
+            w_ref.at[block(o, i), lanes(h)],
+            s_z.at[2 * k - 2 + h],
+            r_z.at[2 * k - 2 + h],
+            device_id=(peer * GROUP + i, t),
+            device_id_type=MESH,
+        )
+
+    def near_source(b, h):
+        if b == 0 and h == 0:
+            return shard_ref.at[:, pl.ds(0, width)]
+        return w_ref.at[block((o + outer - b) % outer, i), lanes(h)]
+
+    def y_move(b, h):
+        target = w_ref.at[block((o + outer - b) % outer, i), lanes(h)]
+        return to_dp(2, near_source(b, h), target, s_y.at[2 * b + h], r_y.at[2 * b + h])
+
+    def c_move(b, far, h):
+        target = w_ref.at[block((o + outer - b) % outer, flip(i, 2) if far else i), lanes(h)]
+        source = target if far else near_source(b, h)
+        k = (2 * b + far) * 2 + h
+        return to_dp(1, source, target, s_c.at[k], r_c.at[k])
+
+    def weights_move(j, m):
+        return to_dp(m, packed.at[j, m], own_refs[j].at[m], s_a.at[3 * j + m - 1], r_a.at[3 * j + m - 1])
+
+    keeps = [pltpu.make_async_copy(packed.at[j, 0], own_refs[j].at[0], l_own.at[j]) for j in range(2)]
+    stays = [pltpu.make_async_copy(packed.at[2 + j], packed_refs[j], l_own.at[2 + j]) for j in range(2)]
+    hops = Hops(outer, [(1, own_refs[0], own_refs[0], to_left, to_right)], s_hop, r_hop)
+
+    def packed_there(j):
+        for pair in packs[j * GROUP : (j + 1) * GROUP]:
+            for c in pair:
+                c.wait()
+
+    x_moves[0].start()
+    for c in g_x:
+        c.start()
+    for k in range(1, outer):
+        z_move(k, 0).start()
+    y_move(0, 0).start()
+    c_move(0, 0, 0).start()
+    packed_there(0)
+    for m in range(1, GROUP):
+        weights_move(0, m).start()
+    keeps[0].start()
+    x_moves[1].start()
+    local.wait()
+    x_moves[0].wait()
+    for k in range(1, outer):
+        z_move(k, 1).start()
+    packed_there(1)
+    keeps[1].start()
+    for j in range(2):
+        packed_there(2 + j)
+        stays[j].start()
+    gates_all[0, :, 0:half] = gates_ref[:, 0:half]
+    gates_all[0, :, 2 * half : 3 * half] = gates_ref[:, half:]
+    angles = lax.broadcasted_iota(jnp.int32, (slot_rows, LANES), 0).astype(F32) * freq_ref[...]
+    lane = lax.broadcasted_iota(jnp.int32, (slot_rows, LANES), 1)
+    cos_ref[...] = jnp.cos(angles)
+    sin_ref[...] = jnp.where(lane % HD < HD // 2, -jnp.sin(angles), jnp.sin(angles))
+    for c in g_x:
+        c.wait()
+    g_y.start()
+    g_c[0].start()
+    for k in range(1, outer):
+        z_move(k, 0).wait_recv()
+        y_move(k, 0).start()
+        c_move(k, 0, 0).start()
+    for m in range(1, GROUP):
+        weights_move(1, m).start()
+    for b in range(1):
+        y_move(b, 1).start()
+        c_move(b, 0, 1).start()
+    before[...] = (
+        lax.broadcasted_iota(jnp.int32, before.shape, 0) < lax.broadcasted_iota(jnp.int32, before.shape, 1)
+    ).astype(F32).astype(BF)
+    keeps[0].wait()
+    for m in range(1, GROUP):
+        weights_move(0, m).wait_recv()
+    hops.start()
+    g_y.wait()
+    g_c[1].start()
+    for k in range(1, outer):
+        z_move(k, 1).wait_recv()
+        y_move(k, 1).start()
+        c_move(k, 0, 1).start()
+    for b in range(outer):
+        y_move(b, 0).wait_recv()
+        c_move(b, 1, 0).start()
+    for c in g_c:
+        c.wait()
+    n_all = gates_all.shape[1]
+    first = t * n_local + i * n
+    pick = (
+        lax.broadcasted_iota(jnp.int32, (8, n_all), 1) == lax.broadcasted_iota(jnp.int32, (8, n_all), 0) + first
+    ).astype(F32).astype(BF)
+    for s in range(GROUP):
+        gate = mm(pick, gates_all[s])
+        rank = mm((gate > 0).astype(F32).astype(BF), before[...])
+        gate_ref[s] = gate[:n]
+        pos_ref[s] = jnp.where(gate > 0, rank, -1.0).astype(jnp.int32)[:n]
+        gate = lax.dot_general(gates_all[s], pick, (((0,), (1,)), ((), ())), preferred_element_type=F32)
+        rank = mm_tn(before[...], (gate > 0).astype(F32).astype(BF))
+        gatec_ref[s] = gate[:, :n]
+        posc_ref[s] = jnp.where(gate > 0, rank, -1.0).astype(jnp.int32)[:, :n]
+    for b in range(outer):
+        y_move(b, 1).wait_recv()
+        c_move(b, 1, 1).start()
+    for k in range(1, outer):
+        for h in range(2):
+            z_move(k, h).wait_send()
+    for b in range(outer):
+        for h in range(2):
+            y_move(b, h).wait_send()
+            c_move(b, 0, h).wait()
+            c_move(b, 1, h).wait()
+    for m in range(1, GROUP):
+        weights_move(0, m).wait_send()
+        weights_move(1, m).wait()
+    x_moves[1].wait()
+    keeps[1].wait()
+    for c in stays:
+        c.wait()
+    hops.wait()
+
+
+def collect(outer, shard, normed, gates, frequency, expert_in, expert_down):
+    each, own_width = shard.shape
+    width = own_width * 2 // 3
+    rows = normed.shape[0]
+    experts, in_rows, _ = expert_in.shape
+    down_rows = expert_down.shape[1]
+    n = experts // GROUP
+    packed = in_rows + down_rows
+    hop = jax.ShapeDtypeStruct((GROUP, packed, D), BF)
+    dma = pltpu.SemaphoreType.DMA
+    out = remote_call(
+        functools.partial(collect_kernel, outer, in_rows, down_rows),
+        "collect",
+        13,
+        [
+            jax.ShapeDtypeStruct((D, 2 * width), BF),
+            jax.ShapeDtypeStruct((rows, D), BF),
+            jax.ShapeDtypeStruct((2 * rows, LANES), F32),
+            jax.ShapeDtypeStruct((2 * rows, LANES), F32),
+            jax.ShapeDtypeStruct((GROUP, n, 2 * rows), jnp.int32),
+            jax.ShapeDtypeStruct((GROUP, n, 2 * rows), F32),
+            jax.ShapeDtypeStruct((GROUP, 2 * rows, n), jnp.int32),
+            jax.ShapeDtypeStruct((GROUP, 2 * rows, n), F32),
+        ]
+        + [hop] * 6,
+        [VM] * 4 + [ANY] * 2,
+        [VM] * 8 + [ANY] * 6,
+        (shard, normed, gates, frequency, expert_in, expert_down),
+        [
+            pltpu.VMEM((n, GROUP, packed, D), BF),
+            pltpu.VMEM((GROUP, gates.shape[0], 2 * rows), BF),
+            pltpu.VMEM((2 * rows, 2 * rows), BF),
+            dma,
+            dma((experts,)),
+            dma((experts,)),
+            dma((4,)),
+            dma((2 * outer - 2,)),
+            dma((2 * outer - 2,)),
+            dma((2 * outer,)),
+            dma((2 * outer,)),
+            dma((4 * outer,)),
+            dma((4 * outer,)),
+            dma((2,)),
+            dma((2,)),
+            dma((5,)),
+            dma((5,)),
+            dma((6,)),
+            dma((6,)),
+            dma((2,)),
+            dma((2,)),
+        ],
+        4 << 30,
+    )
+    return out[:8], out[8:10], out[10:12], out[12], out[13]
+
+
 def attention_kernel(outer, q_block, n_steps, len_ref, own_ref, other_ref, w_ref, cos_ref, sin_ref, x_ref, gain_ref, *refs):
     width = w_ref.shape[1] // 2
     heads = width // 2
-    dy_refs, refs = refs[:2], refs[2:]
-    sources, refs = refs[:n_steps], refs[n_steps:]
+    cot_ref, ready, packed_refs, refs = refs[0], refs[1], refs[2:4], refs[4:]
     qkv_ref, lse_ref, attn_ref, come_ref, hidden_ref, na_ref, nb_ref = refs[:7]
     refs = refs[7:]
-    dy_outs, refs = refs[:4], refs[4:]
+    dy_outs, own_refs, refs = refs[:4], refs[4:6], refs[6:]
     to_left, refs = refs[:n_steps], refs[n_steps:]
     to_right, refs = refs[:n_steps], refs[n_steps:]
-    send_ref, s_hop, r_hop, s_dy, r_dy, s_at, r_at = refs
+    send_ref, s_hop, r_hop, s_later, r_later, s_dy, r_dy, s_at, r_at, s_a, r_a, l_own = refs
     d, t, o, i = place()
     length = len_ref[0]
     rows = own_ref.shape[0]
     groups = width // (2 * LANES)
-    greet(outer, (2,), True)
-    hops = Hops(outer, [(1, s, s, l, r) for s, l, r in zip(sources, to_left, to_right, strict=True)], s_hop, r_hop)
+    greet(outer, (1, 2, 3), True)
+    hops = Hops(outer, [(1, ready, ready, to_left[0], to_right[0])], s_hop, r_hop)
+    later = Hops(outer, [(1, own_refs[k], own_refs[k], to_left[1 + k], to_right[1 + k]) for k in range(2)], s_later, r_later)
+    keeps = [pltpu.make_async_copy(packed_refs[k].at[0], own_refs[k].at[0], l_own.at[k]) for k in range(2)]
+    weights = [
+        to_dp(m, packed_refs[k].at[m], own_refs[k].at[m], s_a.at[3 * k + m - 1], r_a.at[3 * k + m - 1])
+        for k in range(2)
+        for m in range(1, GROUP)
+    ]
     hops.start()
+    for copy in (*weights, *keeps):
+        copy.start()
     ax, bx, ay, by = dy_outs
+    dy_a, dy_b = (cot_ref.at[pl.ds(p * rows // 2, rows // 2)] for p in range(2))
     dys = [
-        to_x(dy_refs[0], ax, s_dy.at[0], r_dy.at[0]),
-        to_dp(2, dy_refs[1], by, s_dy.at[1], r_dy.at[1]),
-        to_x(dy_refs[1], bx, s_dy.at[2], r_dy.at[2]),
-        to_dp(2, dy_refs[0], ay, s_dy.at[3], r_dy.at[3]),
+        to_x(dy_a, ax, s_dy.at[0], r_dy.at[0]),
+        to_dp(2, dy_b, by, s_dy.at[1], r_dy.at[1]),
+        to_x(dy_b, bx, s_dy.at[2], r_dy.at[2]),
+        to_dp(2, dy_a, ay, s_dy.at[3], r_dy.at[3]),
     ]
 
     block = 256
@@ -750,6 +1000,13 @@
                 send_ref[inner : inner + q_block, o_lanes] = mixed
 
         exchange(g).start()
+
+        @pl.when(g == groups // 2)
+        def _():
+            for copy in (*weights, *keeps):
+                copy.wait()
+            later.start()
+
         return carry
 
     lax.fori_loop(0, groups, per_group, 0)
@@ -771,13 +1028,14 @@
     for copy in dys:
         copy.wait()
     hops.wait()
-
-
-def attention(outer, q_block, length, own, other, weights_full, cosine, sine, x, gain, dys, sources):
+    later.wait()
+
+
+def attention(outer, q_block, length, own, other, weights_full, cosine, sine, x, gain, cotangent, ready, packed):
     rows, groups = own.shape[0], weights_full.shape[1] // (4 * LANES)
-    n = len(sources)
+    n = 3
     piece = jax.ShapeDtypeStruct((rows // 2, D), BF)
-    weights = [jax.ShapeDtypeStruct(s.shape, BF) for s in sources]
+    hop = jax.ShapeDtypeStruct(ready.shape, BF)
     out = remote_call(
         functools.partial(attention_kernel, outer, q_block, n),
         "attention",
@@ -792,22 +1050,27 @@
             piece,
         ]
         + [piece] * 4
-        + weights * 2,
-        [SMEM] + [VM] * 7 + [ANY] * (2 + n),
-        [VM] * 7 + [ANY] * (4 + 2 * n),
-        (length, own, other, weights_full, cosine, sine, x, gain.reshape(1, D), *dys, *sources),
+        + [hop] * (2 + 2 * n),
+        [SMEM] + [VM] * 7 + [ANY] * 4,
+        [VM] * 7 + [ANY] * (6 + 2 * n),
+        (length, own, other, weights_full, cosine, sine, x, gain.reshape(1, D), cotangent, ready, *packed),
         [
             pltpu.VMEM((rows, groups * LANES), BF),
-            pltpu.SemaphoreType.DMA((2 * n,)),
-            pltpu.SemaphoreType.DMA((2 * n,)),
+            pltpu.SemaphoreType.DMA((2,)),
+            pltpu.SemaphoreType.DMA((2,)),
+            pltpu.SemaphoreType.DMA((4,)),
+            pltpu.SemaphoreType.DMA((4,)),
             pltpu.SemaphoreType.DMA((4,)),
             pltpu.SemaphoreType.DMA((4,)),
             pltpu.SemaphoreType.DMA((groups,)),
             pltpu.SemaphoreType.DMA((groups,)),
+            pltpu.SemaphoreType.DMA((6,)),
+            pltpu.SemaphoreType.DMA((6,)),
+            pltpu.SemaphoreType.DMA((2,)),
         ],
         30 << 30,
     )
-    return out[:7], out[7:11], out[11 : 11 + n], out[11 + n :]
+    return out[:7], out[7:11], out[11:13], out[13 : 13 + n], out[13 + n :]
 
 
 def one_hot_rows(pos, gate, j, n_rows):
@@ -818,7 +1081,7 @@
 
 def spread_kernel(outer, steps, pos_ref, gate_ref, na_ref, nb_ref, *refs):
     n_steps = len(steps)
-    dy_refs, refs = refs[:6], refs[6:]
+    cot_ref, dy_refs, refs = refs[0], refs[1:5], refs[5:]
     from_left, refs = refs[:n_steps], refs[n_steps:]
     from_right, refs = refs[:n_steps], refs[n_steps:]
     n_ref, dyx_ref, og_ref = refs[:3]
@@ -841,7 +1104,8 @@
         core[s, p] = to_dp(1, source, n_ref.at[2 + s, p], s_n.at[6 + n], r_n.at[6 + n])
     for copy in (n_ax, n_by, n_bx, n_ay):
         copy.start()
-    d_a, d_b, d_ax, d_bx, d_ay, d_by = dy_refs
+    d_a, d_b = (cot_ref.at[pl.ds(p * height, height)] for p in range(2))
+    d_ax, d_bx, d_ay, d_by = dy_refs
     d_axy = to_dp(2, d_ax, dyx_ref.at[0, 1], s_d.at[0], r_d.at[0])
     d_bxy = to_x(d_by, dyx_ref.at[0, 3], s_d.at[1], r_d.at[1])
     d_axy.start()
@@ -930,7 +1194,7 @@
             jax.ShapeDtypeStruct((GROUP, n_experts, CAP, D), BF),
         ]
         + weights * 2,
-        [VM] * 2 + [ANY] * (2 + 6 + 2 * n),
+        [VM] * 2 + [ANY] * (2 + 5 + 2 * n),
         [ANY, ANY, VM] + [ANY] * (2 * n),
         (pos, gate, *normed, *dys, *from_left, *from_right),
         [
@@ -1925,47 +2189,34 @@
     chosen = expert_ids.T[None] == jnp.arange(n_experts, dtype=jnp.int32)[:, None, None]
     gates = jnp.sum(jnp.where(chosen, gate_values.T[None].astype(F32), 0.0), axis=1)
     gates = jnp.where(valid_rows[None, :], gates, 0.0).astype(BF)
-    if pair:
-        gates_x = beside(gates)
-        slot_gates = jnp.concatenate(
-            [gates[:, :half], gates_x[:, :half], gates[:, half:], gates_x[:, half:]], axis=1
-        )
-    else:
-        slot_gates = lax.all_gather(gates, "tensor", axis=1, tiled=True)
-    gates_y = across(slot_gates, 2)
-    all_gates = jnp.stack([slot_gates, gates_y, across(slot_gates, 1), across(gates_y, 1)])
-    own_gates = lax.dynamic_slice_in_dim(
-        all_gates, t * experts_local + i * own_experts, own_experts, axis=1
-    ).astype(F32)
-    named = own_gates > 0
-    before = (
-        lax.broadcasted_iota(jnp.int32, (slot_rows, slot_rows), 0)
-        < lax.broadcasted_iota(jnp.int32, (slot_rows, slot_rows), 1)
-    ).astype(BF)
-    ranks = jnp.dot(
-        named.astype(BF).reshape(GROUP * own_experts, slot_rows), before, preferred_element_type=F32
-    ).reshape(GROUP, own_experts, slot_rows)
-    pos = jnp.where(named, ranks, -1.0).astype(jnp.int32)
-    pos_columns, gate_columns = jnp.swapaxes(pos, 1, 2), jnp.swapaxes(own_gates, 1, 2)
-
     x = tokens.astype(F32)
     inverse_one = lax.rsqrt(jnp.mean(x * x, axis=-1, keepdims=True) + EPSILON)
     normed_one = (x * inverse_one * first_gain).astype(BF)
-    cosine, sine = rope_tables(slot_rows)
-    dy = jnp.where(valid_rows[:, None], cotangent, jnp.zeros_like(cotangent))
     expert_outs, row_grads, weight_grads = [], [], []
     if pair and outer == 4:
-        other = beside(normed_one)
-        out_shard = attn_out_weight.T
-        shards = jnp.concatenate([qkv_weight.reshape(-1, width), out_shard, beside(out_shard)], axis=1)
-        weights_full = lax.all_gather(shards, "dp", axis=0, tiled=True)
-        by_distance = pack_weights(idx, expert_in_weight, expert_out_weight)
-        by_distance = [by_distance[0]] + [across(by_distance[m], m) for m in range(1, GROUP)]
-        own_weights = [jnp.stack([v[j] for v in by_distance]) for j in range(own_experts)]
-        dys = [dy[:half], dy[half:]]
-        main, dy_moved, one_l, one_r = attention(
-            outer, q_block, lengths, normed_one, other, weights_full, cosine, sine, tokens, second_gain, dys, own_weights[:3]
+        frequency = THETA ** (-(jnp.arange(HD // 2).astype(F32) * 2.0 / HD))
+        shard = jnp.concatenate([qkv_weight.reshape(-1, width), attn_out_weight.T], axis=1)
+        main, ready, packed, first_l, first_r = collect(
+            outer, shard, normed_one, gates, jnp.tile(frequency, 4)[None, :], expert_in_weight, expert_out_weight
         )
+        weights_full, other, cosine, sine, pos, own_gates, pos_columns, gate_columns = main
+        main, dy_moved, later, one_l, one_r = attention(
+            outer,
+            q_block,
+            lengths,
+            normed_one,
+            other,
+            weights_full,
+            cosine,
+            sine,
+            tokens,
+            second_gain,
+            cotangent,
+            ready[1],
+            packed,
+        )
+        own_weights = [*ready, *later]
+        one_l, one_r = [first_l, *one_l], [first_r, *one_r]
         qkv, lse, attn_own, attn_other, hidden, *normed_two = main
         attn_parts = [attn_own, attn_other]
         gathered, out_grads, moved_l, moved_r = spread(
@@ -1973,21 +2224,20 @@
             pos,
             own_gates,
             normed_two,
-            [*dys, *dy_moved],
-            (1, 2, 2),
-            [own_weights[3], one_l[0], one_l[1]],
-            [own_weights[3], one_r[0], one_r[1]],
+            [cotangent, *dy_moved],
+            (2, 2, 2),
+            one_l[:3],
+            one_r[:3],
         )
-        one_l, one_r = [*one_l, moved_l[0]], [*one_r, moved_r[0]]
-        two_l, two_r = [*moved_l[1:]], [*moved_r[1:]]
+        two_l, two_r = [*moved_l], [*moved_r]
         expert_rows, moved_l, moved_r = hand_out(
-            outer, pos, normed_two, gathered, (3, 2), [two_l[0], one_l[2]], [two_r[0], one_r[2]]
+            outer, pos, normed_two, gathered, (3, 2), [two_l[0], one_l[3]], [two_r[0], one_r[3]]
         )
         three_l, three_r = [moved_l[0]], [moved_r[0]]
         two_l.append(moved_l[1])
         two_r.append(moved_r[1])
         hop_plans = [
-            lambda: ((3, 2), [two_l[1], one_l[3]], [two_r[1], one_r[3]]),
+            lambda: ((3,), [two_l[1]], [two_r[1]]),
             lambda: ((3,), [two_l[2]], [two_r[2]]),
             lambda: ((3,), [two_l[3]], [two_r[3]]),
             lambda: ((), [], []),
@@ -2011,8 +2261,6 @@
             )
             three_l.extend(moved_l[:1])
             three_r.extend(moved_r[:1])
-            two_l.extend(moved_l[1:])
-            two_r.extend(moved_r[1:])
             expert_outs.append(y)
             row_grads.append(dx)
             weight_grads.append(dw)
@@ -2082,6 +2330,31 @@
             expert_out_grad,
         )
     else:
+        if pair:
+            gates_x = beside(gates)
+            slot_gates = jnp.concatenate(
+                [gates[:, :half], gates_x[:, :half], gates[:, half:], gates_x[:, half:]], axis=1
+            )
+        else:
+            slot_gates = lax.all_gather(gates, "tensor", axis=1, tiled=True)
+        gates_y = across(slot_gates, 2)
+        all_gates = jnp.stack([slot_gates, gates_y, across(slot_gates, 1), across(gates_y, 1)])
+        own_gates = lax.dynamic_slice_in_dim(
+            all_gates, t * experts_local + i * own_experts, own_experts, axis=1
+        ).astype(F32)
+        named = own_gates > 0
+        before = (
+            lax.broadcasted_iota(jnp.int32, (slot_rows, slot_rows), 0)
+            < lax.broadcasted_iota(jnp.int32, (slot_rows, slot_rows), 1)
+        ).astype(BF)
+        ranks = jnp.dot(
+            named.astype(BF).reshape(GROUP * own_experts, slot_rows), before, preferred_element_type=F32
+        ).reshape(GROUP, own_experts, slot_rows)
+        pos = jnp.where(named, ranks, -1.0).astype(jnp.int32)
+        pos_columns, gate_columns = jnp.swapaxes(pos, 1, 2), jnp.swapaxes(own_gates, 1, 2)
+
+        cosine, sine = rope_tables(slot_rows)
+        dy = jnp.where(valid_rows[:, None], cotangent, jnp.zeros_like(cotangent))
         qkv_full = lax.all_gather(qkv_weight.reshape(qkv_weight.shape[0], width), "dp", axis=0, tiled=True)
         out_full = lax.all_gather(attn_out_weight.T, "dp", axis=0, tiled=True)
         by_distance = pack_weights(idx, expert_in_weight, expert_out_weight)

time: 640 us -> 584 us (0.912)
  waiting for transfers between devices: 49.8 us -> 0.01 us
  Pallas kernels: 519 us -> 554 us
  between operations: 15.2 us -> 1.75 us
  starting transfers between devices: 12.5 us -> 0.62 us
  local copies, waits for them, and re-layouts: 17.1 us -> 7.79 us
  other arithmetic: 14.7 us -> 7.72 us
    pallas_call x10 -> x11, Pallas kernels: 503 us -> 542 us  [remote_call(): pl.pallas_call(kernel, name=name, out_shape=out_shape, in_specs=in_specs,...]
    ppermute x6 -> x0, waiting for transfers between devices: 37.7 us -> none  [across(): return lax.ppermute(v, 'dp', [(a, a ^ m) for a in range(n_dp)])]
    ppermute x4 -> x1, waiting for transfers between devices: 12 us -> 0.01 us  [beside(): return lax.ppermute(v, 'tensor', [(0, 1), (1, 0)])]
    slice x7 -> x0, local copies, waits for them, and re-layouts: 7.06 us -> none  [the longest x4 5.98 us: layer(): v[j]]
    ppermute x6 -> x0, starting transfers between devices: 6.44 us -> none  [across(): return lax.ppermute(v, 'dp', [(a, a ^ m) for a in range(n_dp)])]
  transfers between devices with their start and end apart: 11 -> 1, of which waited for: 3 -> 0; matrix products, arithmetic and copies ran while one was open for 4% -> 0% of each run, Pallas kernels for 7% -> 7%
where the time goes in v4:
time: 584 us; the launch traced here: 577 us
  Pallas kernels  554 us (95%)
  local copies, waits for them, and re-layouts  7.79 us (1%)
  other arithmetic  7.72 us (1%)
    pallas_call x11, Pallas kernels, remote_call(): pl.pallas_call(kernel, name=name, out_shape=out_shape, in_specs=in_specs,...  542 us
    pallas_call x1, Pallas kernels, settle_experts(): pl.pallas_call(functools.partial(settle_kernel, n, in_rows), name='settle...  11.8 us
  transfers between devices with their start and end apart: 1, of which 0 were waited for; matrix products, arithmetic and copies ran while one was open for 0% of the time, Pallas kernels for 7%

profile of v4, /device:TPU:9, one launch (start us, length us, event | category | flops | bytes accessed | tf_op | source)
XLA Modules:
  0.0 576.8 jit_solution(16960006118014340032)
XLA Ops:
  0.6 0.0 copy-start
  0.6 0.0 copy-start.4
  1.4 0.7 convert_bitcast_fusion
  2.1 1.5 fusion
  3.6 0.9 copy.19
  4.6 0.6 broadcast_in_dim_tile.3.freq_ref
  5.2 0.7 fusion.3.valid_ref
  5.9 0.9 select_reduce_fusion
  6.8 0.6 select_convert_fusion.gates_ref
  7.4 0.0 copy-done
  7.4 2.0 fusion.2.normed_ref.own_ref.refs_0_
  9.4 0.0 copy-done.4
  9.4 0.7 pad_maximum_fusion.shard_ref
  10.1 53.3 %collect.1 = (bf16[1024,2048]{1,0:T(8,128)(2,1)}, bf16[512,1024]{1,0:T(8,128)(2,1)}, f32[1024,128]{1,0:T(8,128)}, f32[1024,128]{1,0:T(8,128)}, s32[4,4,1024]{2,1...) custom-call(bf16[64,1536]{1,0:T(8,128)(2,1)} %pad_maximum_fusion.sha, ...), custom_call_target="tpu_custom_call" | custom-call | flops 4294967296 | bytes 8388608 | tf_op jit(solution)/shard_map/collect/pallas_call | solution.py:664
  63.4 62.7 %attention.1 = (bf16[1024,1024]{1,0:T(8,128)(2,1)}, f32[4,4,512]{2,1,0:T(4,128)}, bf16[512,512]{1,0:T(8,128)(2,1)}, bf16[512,512]{1,0:T(8,128)(2,1)}, f32[512,10...) custom-call(s32[1]{0:T(128)} %copy.23.len_ref, ...), custom_call_target="tpu_custom_call" | custom-call | flops 32212254720 | bytes 8388608 | tf_op jit(solution)/shard_map/attention/pallas_call | solution.py:664
  126.1 58.0 %spread.1 = (bf16[4,4,256,1024]{3,2,1,0:T(8,128)(2,1)}, bf16[3,4,256,1024]{3,2,1,0:T(8,128)(2,1)}, bf16[4,4,288,1024]{3,2,1,0:T(8,128)(2,1)}, bf16[4,96,1024]{2,...) custom-call(s32[4,4,1024]{2,1,0:T(4,128)} %get-tuple-element.114.pos, ...), custom_call_target="tpu_custom_call" | custom-call | flops 12884901888 | bytes 8388608 | tf_op jit(solution)/shard_map/spread/pallas_call | solution.py:664
  184.1 38.6 %hand_out.1 = (bf16[4,4,288,1024]{3,2,1,0:T(8,128)(2,1)}, bf16[4,96,1024]{2,1,0:T(8,128)(2,1)}, bf16[4,96,1024]{2,1,0:T(8,128)(2,1)}, bf16[4,96,1024]{2,1,0:T(8,128)(2,1)}, bf16[4,96,1024]{2,1,0:T(8,128)(2,1)}) custom-call(s32[4,4,1024]{2,1,0:T(4,128)} %get-tuple-element.114.pos_ref, bf16[256,1024]{1,0:T(8,128)(2,1)} %get-tuple-element.115.na_ref, ...), custom_call_target="tpu_custom_call" | custom-call | flops 12884901888 | bytes 8388608 | tf_op jit(solution)/shard_map/hand_out/pallas_call | solution.py:664
  222.7 22.5 %expert_step.4 = (bf16[4,288,1024]{2,1,0:T(8,128)(2,1)}, bf16[4,288,1024]{2,1,0:T(8,128)(2,1)}, bf16[4,4,96,1024]{3,2,1,0:T(8,128)(2,1)}, bf16[4,96,1024]{2,1,0:T(8,128)(2,1)}, bf16[4,96,1024]{2,1,0:T(8,128)(2,1)}) custom-call(bf16[4,4,288,1024]{3,2,1,0:T(8,128)(2,1)} %get-tuple-element.133.x_ref, bf16[4,4,288,1024]{3,2,1,0:T(8,128)(2,1)} %get-tuple-element.134.g_ref, ...), custom_call_target="tpu_custom_call" | custom-call | flops 10871635968 | bytes 8388608 | tf_op jit(solution)/shard_map/expert_step/pallas_call | solution.py:664
  245.2 23.4 %expert_step.5 = (bf16[4,288,1024]{2,1,0:T(8,128)(2,1)}, bf16[4,288,1024]{2,1,0:T(8,128)(2,1)}, bf16[4,4,96,1024]{3,2,1,0:T(8,128)(2,1)}, bf16[4,96,1024]{2,1,0:...) custom-call(bf16[4,4,288,1024]{3,2,1,0:T(8,128)(2,1)} %get-tuple-element.133, ...), custom_call_target="tpu_custom_call" | custom-call | flops 10871635968 | bytes 8388608 | tf_op jit(solution)/shard_map/expert_step/pallas_call | solution.py:664
  268.6 23.8 %expert_step.6 = (bf16[4,288,1024]{2,1,0:T(8,128)(2,1)}, bf16[4,288,1024]{2,1,0:T(8,128)(2,1)}, bf16[4,4,96,1024]{3,2,1,0:T(8,128)(2,1)}, bf16[4,96,1024]{2,1,0:...) custom-call(bf16[4,4,288,1024]{3,2,1,0:T(8,128)(2,1)} %get-tuple-element.133, ...), custom_call_target="tpu_custom_call" | custom-call | flops 10871635968 | bytes 8388608 | tf_op jit(solution)/shard_map/expert_step/pallas_call | solution.py:664
  292.4 23.2 %expert_step.7 = (bf16[4,288,1024]{2,1,0:T(8,128)(2,1)}, bf16[4,288,1024]{2,1,0:T(8,128)(2,1)}, bf16[4,4,96,1024]{3,2,1,0:T(8,128)(2,1)}, bf16[4,96,1024]{2,1,0:T(8,128)(2,1)}, bf16[4,96,1024]{2,1,0:T(8,128)(2,1)}) custom-call(bf16[4,4,288,1024]{3,2,1,0:T(8,128)(2,1)} %get-tuple-element.133.x_ref, bf16[4,4,288,1024]{3,2,1,0:T(8,128)(2,1)} %get-tuple-element.134.g_ref, ...), custom_call_target="tpu_custom_call" | custom-call | flops 10871635968 | bytes 8388608 | tf_op jit(solution)/shard_map/expert_step/pallas_call | solution.py:664
  315.6 0.0 copy-start.6
  315.6 91.8 %rows_back.1 = (f32[512,1024]{1,0:T(8,128)}, bf16[512,1024]{1,0:T(8,128)(2,1)}, f32[1,1024]{1,0:T(1,128)}, bf16[512,512]{1,0:T(8,128)(2,1)}, bf16[512,512]{1,0:T...) custom-call(s32[4,1024,4]{2,1,0:T(8,128)} %get-tuple-element.104.pos, ...), custom_call_target="tpu_custom_call" | custom-call | flops 21474836480 | bytes 8388608 | tf_op jit(solution)/shard_map/rows_back/pallas_call | solution.py:664
  407.4 0.0 copy-done.6
  407.4 2.0 convolution_convert_fusion
  409.4 0.6 collective-permute-start
  410.0 0.0 copy-start.5
  410.0 39.9 %attention_back.1 = (bf16[512,1024]{1,0:T(8,128)(2,1)}, bf16[512,1024]{1,0:T(8,128)(2,1)}, bf16[4,96,1024]{2,1,0:T(8,128)(2,1)}, bf16[4,96,1024]{2,1,0:T(8,128)(...) custom-call(s32[1]{0:T(128)} %copy.23.len_ref, ...), custom_call_target="tpu_custom_call" | custom-call | flops 32212254720 | bytes 8388608 | tf_op jit(solution)/shard_map/attention_back/pallas_call | solution.py:664
  449.9 0.6 pad_add_fusion.idx_ref
  450.5 0.0 collective-permute-done
  450.5 0.0 copy-done.5
  450.5 2.8 add_convert_fusion.refs_4_
  453.3 105.2 %finish.1 = (bf16[512,1024]{1,0:T(8,128)(2,1)}, f32[512,1024]{1,0:T(8,128)}, f32[8,1024]{1,0:T(8,128)}, f32[64,1024]{1,0:T(8,128)}, f32[64,512]{1,0:T(8,128)}, /...) custom-call(s32[1]{0:T(128)} %copy.23.len_ref, ...), custom_call_target="tpu_custom_call" | custom-call | flops 32212254720 | bytes 8388608 | tf_op jit(solution)/shard_map/finish/pallas_call | solution.py:664
  558.5 0.0 copy-start.2
  558.5 1.9 reshape.66
  560.4 1.4 fusion.4
  561.8 0.0 copy-start.1
  561.8 11.8 %settle_experts.1 = (f32[16,64,1024]{2,1,0:T(8,128)}, f32[16,32,1024]{2,1,0:T(8,128)}) custom-call(s32[4]{0:T(128)} %pad_add_fusion.idx_ref, bf16[4,96,1024]{2,1,0:T(8,128)(2,1)} %get-tuple-element.194.refs_0_, bf16[4,96,1024]{2,1,0:T(8,128)(2,1)} %get-tuple-element.195.refs_1_, bf16[4,96,1024]{2,1,0:T(8,128)(2,1)} %get-tuple-element.196.refs_2_, ...), custom_call_target="tpu_custom_call" | custom-call | bytes 9437184 | tf_op jit(solution)/shard_map/settle_experts/pallas_call | solution.py:2117
  573.6 0.0 copy-done.2
  573.7 1.0 copy.24
  574.6 0.0 copy-done.1
  574.6 0.0 copy-start.3
  574.6 1.3 copy.25
  575.9 0.0 copy-done.3
  575.9 0.7 copy.26
  (4 shorter events, 0.0 us)
Async XLA Ops:
  0.6 6.8 %copy-start = (bf16[512,1024]{1,0:T(8,128)(2,1)S(1)}, bf16[512,1024]{1,0:T(8,128)(2,1)}, u32[]{:S(2)}) copy-start(bf16[512,1024]{1,0:T(8,128)(2,1)} %x_ref.3) | copy-start | bytes 3145732
  0.6 8.7 %copy-start.4 = (bf16[512,64]{0,1:T(8,128)(2,1)S(1)}, bf16[512,64]{0,1:T(8,128)(2,1)}, u32[]{:S(2)}) copy-start(bf16[512,64]{0,1:T(8,128)(2,1)} %param.18) | copy-start | bytes 196612
  315.6 91.8 %copy-start.6 = (bf16[512,512]{1,0:T(8,128)(2,1)S(1)}, bf16[512,512]{1,0:T(8,128)(2,1)}, u32[]{:S(2)}) copy-start(bf16[512,512]{1,0:T(8,128)(2,1)} %get-tuple-element.177) | copy-start | bytes 1572868
  409.4 41.1 %collective-permute-start = (bf16[1024,512]{1,0:T(8,128)(2,1)S(1)}, bf16[1024,512]{1,0:T(8,128)(2,1)S(1)}, u32[]{:S(2)}, u32[]{:S(2)}) collective-permute-start(bf16[1024,512]{1,0:T(8,128)(2,1)S(1)} %convolution_convert_fusion), channel_id=1, source_target_pairs={{0,1},{1,0},{2,3},{3,2},{4,5},{5,4},{6,7},{7,6},{8,9},{9,8},{10,11... | collective-permute-start | bytes 3145736 | tf_op jit(solution)/shard_map/ppermute | solution.py:2168
  410.0 40.5 %copy-start.5 = (bf16[512,1024]{1,0:T(8,128)(2,1)S(1)}, bf16[512,1024]{1,0:T(8,128)(2,1)}, u32[]{:S(2)}) copy-start(bf16[512,1024]{1,0:T(8,128)(2,1)} %get-tuple-element.175) | copy-start | bytes 3145732
  558.5 15.1 %copy-start.2 = (bf16[512,1024]{1,0:T(8,128)(2,1)S(1)}, bf16[512,1024]{1,0:T(8,128)(2,1)}, u32[]{:S(2)}) copy-start(bf16[512,1024]{1,0:T(8,128)(2,1)} %get-tuple-element.210) | copy-start | bytes 3145732
  561.8 12.8 %copy-start.1 = (f32[512,1024]{1,0:T(8,128)S(1)}, f32[512,1024]{1,0:T(8,128)}, u32[]{:S(2)}) copy-start(f32[512,1024]{1,0:T(8,128)} %get-tuple-element.211) | copy-start | bytes 6291460
  574.6 1.3 copy-start.3

commit v5 on v4

--- a/solution.py
+++ b/solution.py
@@ -1379,13 +1379,20 @@
         return carry
 
     lax.fori_loop(0, GROUP, per_slot, 0)
-    for c in range(outer):
-        part = mm_tn(x_all[:, c * GROUP * in_rows : (c + 1) * GROUP * in_rows], gug_all[...]).astype(BF)
+    in_block, down_block = GROUP * in_rows, GROUP * down_rows
+
+    def per_owner(c, carry):
+        lanes = pl.ds(pl.multiple_of(c * in_block, in_block), in_block)
+        part = mm_tn(x_all[:, lanes], gug_all[...]).astype(BF)
         for r in range(GROUP):
             dw_ref[c, flip(i, r), :in_rows, :] = part[r * in_rows : (r + 1) * in_rows]
-        part = mm_tn(act_all[:, c * GROUP * down_rows : (c + 1) * GROUP * down_rows], g_all[...]).astype(BF)
+        lanes = pl.ds(pl.multiple_of(c * down_block, down_block), down_block)
+        part = mm_tn(act_all[:, lanes], g_all[...]).astype(BF)
         for r in range(GROUP):
             dw_ref[c, flip(i, r), in_rows:, :] = part[r * down_rows : (r + 1) * down_rows]
+        return carry
+
+    lax.fori_loop(0, outer, per_owner, 0)
     if n_steps:
         hops.wait()
     sums.wait()
@@ -1601,117 +1608,139 @@
 
 
 class GroupSum:
-    def __init__(self, far, come, near, come_ab, last_ab, sent, came):
-        self.far, self.come, self.near, self.come_ab, self.last_ab = far, come, near, come_ab, last_ab
-        q = near.shape[1] // 4
-        self.q = q
-        self.core = [to_dp(1, far.at[s], come.at[s], sent.at[s], came.at[s]) for s in range(2)]
-        self.a = to_dp(2, near.at[1, pl.ds(0, 2 * q)], come_ab.at[0], sent.at[2], came.at[2])
+    def __init__(self, near, q, middle, mine, come_ab, last_ab, sent, came):
+        self.middle, self.mine, self.come_ab, self.last_ab, self.q = middle, mine, come_ab, last_ab, q
+        self.a = [
+            to_dp(2, near.at[1, pl.ds(s * q, q)], come_ab.at[0, pl.ds(s * q, q)], sent.at[s], came.at[s]) for s in range(2)
+        ]
         self.b = [
-            to_x(near.at[s, pl.ds(3 * q, q)], come_ab.at[1, pl.ds(s * q, q)], sent.at[3 + s], came.at[3 + s])
+            to_x(near.at[s, pl.ds(3 * q, q)], come_ab.at[1, pl.ds(s * q, q)], sent.at[2 + s], came.at[2 + s])
             for s in range(2)
         ]
         self.last = [
-            to_x(near.at[0, pl.ds(q, q)], last_ab.at[0], sent.at[5], came.at[5]),
-            to_dp(2, near.at[1, pl.ds(2 * q, q)], last_ab.at[1], sent.at[6], came.at[6]),
+            to_x(middle[0], last_ab.at[0], sent.at[4], came.at[4]),
+            to_dp(2, middle[1], last_ab.at[1], sent.at[5], came.at[5]),
         ]
 
     def second(self):
-        q, near, come_ab = self.q, self.near, self.come_ab
-        self.a.wait_recv()
-        near[0, q : 2 * q] = (near[0, q : 2 * q].astype(F32) + come_ab[0, q : 2 * q].astype(F32)).astype(BF)
-        self.last[0].start()
-        self.b[1].wait_recv()
-        near[1, 2 * q : 3 * q] = (near[1, 2 * q : 3 * q].astype(F32) + come_ab[1, q : 2 * q].astype(F32)).astype(BF)
-        self.last[1].start()
-        self.b[0].wait_recv()
+        q = self.q
+        for p, first in enumerate((self.a[1], self.b[1])):
+            first.wait_recv()
+            self.middle[p][...] = (
+                self.middle[p][...].astype(F32) + self.come_ab[p, q : 2 * q].astype(F32)
+            ).astype(BF)
+            self.last[p].start()
 
     def terms(self, p):
-        q = self.q
+        (self.a, self.b)[p][0].wait_recv()
         self.last[p].wait_recv()
         return (
-            self.near[0, 2 * p * q : 2 * p * q + q].astype(F32)
-            + self.come_ab[p, :q].astype(F32)
-            + self.last_ab[p].astype(F32)
+            self.mine[p][...].astype(F32) + self.come_ab[p, : self.q].astype(F32) + self.last_ab[p].astype(F32)
         )
 
     def sent(self):
-        for copy in (*self.core, self.a, *self.b, *self.last):
+        for copy in (*self.a, *self.b, *self.last):
             copy.wait_send()
 
 
-def group_scratch(rows, n_experts):
+def group_scratch(rows):
     return [
-        pltpu.VMEM((2, n_experts * CAP, D), BF),
-        pltpu.VMEM((2, rows, D), BF),
-        pltpu.VMEM((2, rows, D), BF),
-        pltpu.VMEM((2, rows, D), BF),
         pltpu.VMEM((2, rows // 2, D), BF),
         pltpu.VMEM((2, rows // 4, D), BF),
-        pltpu.SemaphoreType.DMA((2 * n_experts,)),
-        pltpu.SemaphoreType.DMA((7,)),
-        pltpu.SemaphoreType.DMA((7,)),
+        pltpu.SemaphoreType.DMA((6,)),
+        pltpu.SemaphoreType.DMA((6,)),
     ]
 
 
-def mix_and_sum(mixer, group):
-    mixer.load(2, 0)
-    mixer.load(3, 1)
-    mixer.mix(2, 0, group.far.at[0])
-    group.core[0].start()
-    mixer.load(1, 0)
-    mixer.mix(3, 1, group.far.at[1])
-    group.core[1].start()
-    mixer.load(0, 1)
-    group.core[1].wait_recv()
-    mixer.mix(1, 0, group.near.at[1], group.come.at[1])
-    group.a.start()
-    group.b[1].start()
-    group.core[0].wait_recv()
-    mixer.mix(0, 1, group.near.at[0], group.come.at[0])
-    group.b[0].start()
-    group.second()
-
-
-def rows_back_kernel(outer, first, then, pos_ref, valid_ref, hidden_ref, cot_ref, gain_ref, w_ref, *refs):
+def rows_back_kernel(outer, first, then, pos_ref, gate_ref, valid_ref, hidden_ref, cot_ref, gain_ref, w_any, *refs):
     n_experts, n1, n2 = pos_ref.shape[2], len(first), len(then)
     sources, refs = refs[:n_experts], refs[n_experts:]
-    dws, refs = refs[:n1], refs[n1:]
+    ys, refs = refs[:n_experts], refs[n_experts:]
+    dws, refs = refs[: n1 + 1], refs[n1 + 1 :]
     was_l, refs = refs[:n1], refs[n1:]
     was_r, refs = refs[:n1], refs[n1:]
-    grad_ref, low_ref, gain_grad_ref, own_ref, come_ref = refs[:5]
-    refs = refs[5:]
+    f_dw, f_left, f_right, refs = *refs[:3], refs[3:]
+    grad_ref, low_ref, gain_grad_ref, own_ref, come_ref, mixed, fin_ref = refs[:7]
+    refs = refs[7:]
     to_l, refs = refs[: n1 + n2], refs[n1 + n2 :]
     to_r, refs = refs[: n1 + n2], refs[n1 + n2 :]
-    (held, far, come, near, come_ab, last_ab, l_sem, s_sem, r_sem), refs = refs[:9], refs[9:]
+    (held, far, come, mixed_come, near, l_sem, s_core, r_core), refs = refs[:8], refs[8:]
+    (come_ab, last_ab, s_sem, r_sem), refs = refs[:4], refs[4:]
     sums_a, refs = refs[:6], refs[6:]
     sums_b, refs = (*sums_a[:2], *refs[:4]), refs[4:]
-    send_ref, s_at, r_at = refs
-    greet(outer, (1, 2), True)
-    one = Sums(outer, first, dws, was_l, was_r, to_l[:n1], to_r[:n1], *sums_a)
+    send_ref, s_at, r_at, w_ref, w_sem = refs[:5]
+    final_refs = refs[5:]
+    heads = w_ref.shape[1] // 2
+    w_copy = pltpu.make_async_copy(w_any.at[:, pl.ds(2 * heads, 2 * heads)], w_ref, w_sem)
+    w_copy.start()
+    mixer = Mixer(sources, pos_ref, None, held, l_sem)
+    mixer.load(3, 0)
+    mixer.load(2, 1)
+    greet(outer, (1, 2, 3), True)
+    one = Sums(outer, first, dws[:n1], was_l, was_r, to_l[:n1], to_r[:n1], *sums_a)
+    final = Final(outer, f_dw, f_left, f_right, final_refs[0], sums_a[1], fin_ref, *final_refs[1:])
     two = Sums(
         outer,
         [s for s, _ in then],
         [dws[k] for _, k in then],
-        [to_l[k] for _, k in then],
-        [to_r[k] for _, k in then],
+        [None if s == 1 else to_l[k] for s, k in then],
+        [None if s == 1 else to_r[k] for s, k in then],
         to_l[n1:],
         to_r[n1:],
         *sums_b,
     )
-    group = GroupSum(far, come, near, come_ab, last_ab, s_sem, r_sem)
-    mixer = Mixer(sources, pos_ref, None, held, l_sem)
+    q = near.shape[1] // 4
+    group = GroupSum(
+        near,
+        q,
+        [near.at[0, pl.ds(q, q)], near.at[1, pl.ds(2 * q, q)]],
+        [near.at[0, pl.ds(0, q)], near.at[0, pl.ds(2 * q, q)]],
+        come_ab,
+        last_ab,
+        s_sem,
+        r_sem,
+    )
+    core = [to_dp(1, far.at[s], come.at[s], s_core.at[s], r_core.at[s]) for s in range(2)]
+    mixed_core = [to_dp(1, far.at[s], mixed_come.at[s], s_core.at[2 + s], r_core.at[2 + s]) for s in range(2)]
     one.load()
     one.send()
-    mix_and_sum(mixer, group)
+    final.send()
+    mixer.mix(3, 0, far.at[1])
+    core[1].start()
+    mixer.load(1, 0)
+    mixer.mix(2, 1, far.at[0])
+    core[0].start()
+    mixer.load(0, 1)
+    core[1].wait_recv()
+    mixer.mix(1, 0, near.at[1], come.at[1])
+    group.a[1].start()
+    group.b[1].start()
+    group.a[0].start()
+    outputs = Mixer(ys, pos_ref, gate_ref, held, l_sem)
+    outputs.load(3, 0)
+    core[0].wait_recv()
+    mixer.mix(0, 1, near.at[0], come.at[0])
+    group.b[0].start()
+    outputs.load(2, 1)
+    core[1].wait_send()
+    outputs.mix(3, 0, far.at[1])
+    mixed_core[1].start()
+    outputs.load(1, 0)
+    group.second()
+    core[0].wait_send()
+    outputs.mix(2, 1, far.at[0])
+    mixed_core[0].start()
+    outputs.load(0, 1)
     one.wait()
     two.load()
     two.send()
+    mixed_core[1].wait_recv()
+    outputs.mix(1, 0, mixed.at[1], mixed_come.at[1])
+    w_copy.wait()
     rows = hidden_ref.shape[0] // 2
-    width = w_ref.shape[1] // 2
-    heads = width // 2
     gain = gain_ref[...]
     gain_grad = jnp.zeros((1, D), F32)
+    aways = []
     for p in range(2):
         at = slice(p * rows, (p + 1) * rows)
         hidden = hidden_ref[at]
@@ -1727,22 +1756,33 @@
         grad_ref[at] = total
         low = total.astype(BF)
         low_ref[at] = low
-        send_ref[at] = mm(low, w_ref[:, width + heads :]).astype(BF)
+        send_ref[at] = mm(low, w_ref[:, heads:]).astype(BF)
+        part = pl.ds(p * rows, rows)
+        aways.append(to_x(send_ref.at[part], come_ref.at[part], s_at.at[p], r_at.at[p]))
+        aways[p].start()
     gain_grad_ref[...] = gain_grad
-    away = to_x(send_ref, come_ref, s_at, r_at)
-    away.start()
-    own_ref[...] = mm(low_ref[...], w_ref[:, width : width + heads]).astype(BF)
+    mixed_core[0].wait_recv()
+    outputs.mix(0, 1, mixed.at[0], mixed_come.at[0])
+    own_ref[...] = mm(low_ref[...], w_ref[:, :heads]).astype(BF)
     group.sent()
-    away.wait()
+    for copy in mixed_core:
+        copy.wait_send()
+    for away in aways:
+        away.wait()
+    final.wait()
     two.wait()
 
 
-def rows_back(outer, pos, valid, hidden, cotangent, gain, weights_full, sources, first, then, dws, was_l, was_r):
+def rows_back(
+    outer, pos, gate, valid, hidden, cotangent, gain, weights_full, sources, ys, first, then, dws, was_l, was_r, final
+):
     rows, heads = hidden.shape[0], weights_full.shape[1] // 4
-    n = len(first) + len(then)
+    n, n_experts = len(first) + len(then), len(sources)
     packed = dws[0].shape[2]
     hop = [jax.ShapeDtypeStruct((GROUP, packed, D), BF)] * (2 * n)
     half = jax.ShapeDtypeStruct((rows, heads), BF)
+    most = max(len(first), len(then))
+    slots = pltpu.VMEM((2, 2 * rows, D), BF)
     out = remote_call(
         functools.partial(rows_back_kernel, outer, first, then),
         "rows_back",
@@ -1753,42 +1793,70 @@
             jax.ShapeDtypeStruct((1, D), F32),
             half,
             half,
+            jax.ShapeDtypeStruct((2, 2 * rows, D), BF),
         ]
+        + hop[:1]
         + hop,
-        [VM] * 6 + [ANY] * (len(sources) + 3 * len(first)),
-        [VM] * 5 + [ANY] * (2 * n),
-        (pos, valid, hidden, cotangent, gain.reshape(1, D), weights_full, *sources, *dws, *was_l, *was_r),
+        [VM] * 6 + [ANY] * (4 + 2 * n_experts + len(dws) + 2 * len(first)),
+        [VM] * 6 + [ANY] * (1 + 2 * n),
+        (pos, gate, valid, hidden, cotangent, gain.reshape(1, D), weights_full, *sources, *ys, *dws, *was_l, *was_r, *final),
         [
-            *group_scratch(2 * rows, len(sources)),
-            *sums_scratch(len(first), packed),
-            *again(sums_scratch(len(first), packed)),
+            pltpu.VMEM((2, n_experts * CAP, D), BF),
+            slots,
+            slots,
+            slots,
+            slots,
+            pltpu.SemaphoreType.DMA((2 * n_experts,)),
+            pltpu.SemaphoreType.DMA((4,)),
+            pltpu.SemaphoreType.DMA((4,)),
+            *group_scratch(2 * rows),
+            *sums_scratch(most, packed),
+            *again(sums_scratch(most, packed)),
             pltpu.VMEM((rows, heads), BF),
+            pltpu.SemaphoreType.DMA((2,)),
+            pltpu.SemaphoreType.DMA((2,)),
+            pltpu.VMEM((D, 2 * heads), BF),
             pltpu.SemaphoreType.DMA,
-            pltpu.SemaphoreType.DMA,
+            *final_scratch(packed),
         ],
-        20 << 30,
+        30 << 30,
     )
-    return out[:5], out[5 : 5 + n], out[5 + n :]
-
-
-def attention_back_kernel(outer, q_block, steps, len_ref, qkv_ref, lse_ref, cos_ref, sin_ref, own_ref, other_ref, *refs):
+    return out[:6], out[6], out[7 : 7 + n], out[7 + n :]
+
+
+def attention_back_kernel(
+    outer, q_block, steps, len_ref, qkv_ref, lse_ref, cos_ref, sin_ref, own_ref, other_ref, hidden_ref, valid_ref, *refs
+):
     n = len(steps)
+    mixed, refs = refs[0], refs[1:]
     dws, refs = refs[:n], refs[n:]
     was_l, refs = refs[:n], refs[n:]
     was_r, refs = refs[:n], refs[n:]
-    f_dw, f_left, f_right, refs = *refs[:3], refs[3:]
-    outs, fin_ref, refs = refs[:2], refs[2], refs[3:]
+    outs, out_ref, refs = refs[:2], refs[2], refs[3:]
     to_l, refs = refs[:n], refs[n:]
     to_r, refs = refs[:n], refs[n:]
     do_ref, dq_ref, dk_ref, dv_ref = refs[:4]
-    sums_refs, final_refs = refs[4:10], refs[10:]
+    sums_refs, refs = refs[4:10], refs[10:]
+    middle, mine, l_sem, come_ab, last_ab, s_sem, r_sem = refs
     _, t, _, _ = place()
-    greet(outer, (1, 2, 3), False)
+    q = middle.shape[1]
+    loads = [
+        pltpu.make_async_copy(mixed.at[0, pl.ds(q, q)], middle.at[0], l_sem.at[0]),
+        pltpu.make_async_copy(mixed.at[1, pl.ds(2 * q, q)], middle.at[1], l_sem.at[1]),
+        pltpu.make_async_copy(mixed.at[0, pl.ds(0, q)], mine.at[0], l_sem.at[2]),
+        pltpu.make_async_copy(mixed.at[0, pl.ds(2 * q, q)], mine.at[1], l_sem.at[3]),
+    ]
+    for c in loads:
+        c.start()
+    greet(outer, (2,), True)
+    group = GroupSum(
+        mixed, q, [middle.at[0], middle.at[1]], [mine.at[0], mine.at[1]], come_ab, last_ab, s_sem, r_sem
+    )
+    for copy in (group.a[1], group.b[1], group.a[0], group.b[0]):
+        copy.start()
     sums = Sums(outer, steps, dws, was_l, was_r, to_l, to_r, *sums_refs)
-    final = Final(outer, f_dw, f_left, f_right, final_refs[0], sums_refs[1], fin_ref, *final_refs[1:])
     sums.load()
     sums.send()
-    final.send()
     length = len_ref[0]
     rows, own_rows = qkv_ref.shape[0], own_ref.shape[0]
     groups = own_ref.shape[1] // LANES
@@ -1828,14 +1896,26 @@
             dk = dk * cosine - swap_halves(dk) * sine
             first = lax.broadcasted_iota(jnp.int32, dk.shape, 1) < HD
             outs[p][:, kv_lanes] = jnp.where(first, dk, dv).astype(BF)
+
+        @pl.when(g == groups // 2)
+        def _():
+            for c in loads:
+                c.wait()
+            group.second()
+
         return carry
 
     lax.fori_loop(0, groups, per_group, 0)
-    final.wait()
+    for p in range(2):
+        at = slice(p * q, (p + 1) * q)
+        out_ref[at] = jnp.where(valid_ref[at] > 0, hidden_ref[at] + group.terms(p), 0.0).astype(BF)
+    group.sent()
     sums.wait()
 
 
-def attention_back(outer, q_block, length, qkv, lse, cosine, sine, grads, steps, dws, was_l, was_r, final):
+def attention_back(
+    outer, q_block, length, qkv, lse, cosine, sine, grads, hidden, valid, mixed, steps, dws, was_l, was_r
+):
     rows, width = qkv.shape
     n = len(steps)
     packed = dws[0].shape[2]
@@ -1844,242 +1924,257 @@
         functools.partial(attention_back_kernel, outer, q_block, steps),
         "attention_back",
         12,
-        [jax.ShapeDtypeStruct((rows // 2, width), BF)] * 2 + [hop] * (1 + 2 * n),
-        [SMEM] + [VM] * 6 + [ANY] * (3 * n + 3),
-        [VM] * 2 + [ANY] * (1 + 2 * n),
-        (length, qkv, lse, cosine, sine, *grads, *dws, *was_l, *was_r, *final),
+        [jax.ShapeDtypeStruct((rows // 2, width), BF)] * 2
+        + [jax.ShapeDtypeStruct((rows // 2, D), BF)]
+        + [hop] * (2 * n),
+        [SMEM] + [VM] * 8 + [ANY] * (3 * n + 1),
+        [VM] * 3 + [ANY] * (2 * n),
+        (length, qkv, lse, cosine, sine, *grads, hidden, valid, mixed, *dws, *was_l, *was_r),
         [
             pltpu.VMEM((rows, LANES), BF),
             pltpu.VMEM((rows, LANES), F32),
             pltpu.VMEM((rows, LANES), F32),
             pltpu.VMEM((rows, LANES), F32),
             *sums_scratch(n, packed),
-            *final_scratch(packed),
+            pltpu.VMEM((2, rows // 4, D), BF),
+            pltpu.VMEM((2, rows // 4, D), BF),
+            pltpu.SemaphoreType.DMA((4,)),
+            *group_scratch(rows),
         ],
         30 << 30,
     )
-    return out[:2], out[2], out[3 : 3 + n], out[3 + n :]
-
-
-def finish_kernel(outer, in_rows, len_ref, pos_ref, gate_ref, valid_ref, hidden_ref, hgrad_ref, x_ref, gain_ref, w_any, *refs):
-    (no_ref, nx_ref, po_ref, px_ref, ao_ref, sg_ref), refs = refs[:6], refs[6:]
-    n_experts = pos_ref.shape[2]
-    ys, refs = refs[:n_experts], refs[n_experts:]
+    return out[:3], out[3 : 3 + n], out[3 + n :]
+
+
+def over_outer(outer, source, target, sent, came, base):
+    _, t, o, i = place()
+    return [
+        pltpu.make_async_remote_copy(
+            source((o + k) % outer),
+            target(k),
+            sent.at[base + k],
+            came.at[base + k],
+            device_id=((o + k) % outer * GROUP + i, t),
+            device_id_type=MESH,
+        )
+        for k in range(1, outer)
+    ]
+
+
+class Spread:
+    def __init__(self, outer, terms, come_core, come_y, come_z, sent, came):
+        _, _, self.o, i = place()
+        self.outer, self.terms, self.come_core, self.come_y, self.come_z = outer, terms, come_core, come_y, come_z
+        y, c = i // 2, i % 2
+        self.y, self.c = y, c
+        self.core = to_dp(1, terms.at[:, :, 1 - c], come_core, sent.at[0], came.at[0])
+        self.side = to_dp(2, terms.at[:, 1 - y, c], come_y, sent.at[1], came.at[1])
+        self.moves = over_outer(outer, lambda peer: terms.at[peer, y, c], lambda k: come_z.at[k - 1], sent, came, 1)
+
+    def over_core(self):
+        self.core.start()
+
+    def over_y(self):
+        self.core.wait()
+
+        def add(k, carry):
+            for r in range(2):
+                self.terms[k, r, self.c] = (
+                    self.terms[k, r, self.c].astype(F32) + self.come_core[k, r].astype(F32)
+                ).astype(BF)
+            return carry
+
+        lax.fori_loop(0, self.outer, add, 0)
+        self.side.start()
+
+    def over_z(self):
+        self.side.wait()
+
+        def add(k, carry):
+            self.terms[k, self.y, self.c] = (
+                self.terms[k, self.y, self.c].astype(F32) + self.come_y[k].astype(F32)
+            ).astype(BF)
+            return carry
+
+        lax.fori_loop(0, self.outer, add, 0)
+        for move in self.moves:
+            move.start()
+
+    def total(self):
+        for move in self.moves:
+            move.wait()
+        total = self.terms[self.o, self.y, self.c].astype(F32)
+        for k in range(1, self.outer):
+            total = total + self.come_z[k - 1].astype(F32)
+        return total
+
+
+def spread_scratch(outer, each, columns):
+    return [
+        pltpu.VMEM((outer, 2, 2, each, columns), BF),
+        pltpu.VMEM((outer, 2, each, columns), BF),
+        pltpu.VMEM((outer, each, columns), BF),
+        pltpu.VMEM((outer - 1, each, columns), BF),
+        pltpu.SemaphoreType.DMA((1 + outer,)),
+        pltpu.SemaphoreType.DMA((1 + outer,)),
+    ]
+
+
+def finish_kernel(outer, hgrad_ref, x_ref, gain_ref, w_any, *refs):
+    (no_ref, nx_ref, po_ref, px_ref, oo_ref, ox_ref, sg_ref), refs = refs[:7], refs[7:]
     dws, refs = refs[:3], refs[3:]
     done, refs = refs[:2], refs[2:]
     was_l, refs = refs[:2], refs[2:]
     was_r, refs = refs[:2], refs[2:]
-    out_ref, tgrad_ref, gains_ref, qkv_ref, outw_ref = refs[:5]
-    fins, to_l, to_r, refs = refs[5:8], refs[8:11], refs[11:14], refs[14:]
-    (held, far, come, near, come_ab, last_ab, l_sem, s_sem, r_sem), refs = refs[:9], refs[9:]
-    sums_a, refs = refs[:6], refs[6:]
-    sums_b, refs = (*sums_a[:2], *refs[:4]), refs[4:]
+    tgrad_ref, gains_ref, qkv_ref, outw_ref = refs[:4]
+    fins, to_l, to_r, refs = refs[4:7], refs[7:9], refs[9:11], refs[11:]
+    sums_refs, refs = [refs[:6], refs[6:12]], refs[12:]
     final_refs, refs = [refs[5 * k : 5 * k + 5] for k in range(3)], refs[15:]
-    part_ref, theirs_ref, p_send, p_recv = refs[:4]
-    refs = refs[4:]
-    qp, q_core, q_y, q_z, q_send, q_recv = refs[:6]
-    g_buf, g_come, g_z, g_send, g_recv, w_ref, w_sem = refs[6:]
+    part_ref, theirs_ref, p_send, p_recv, out_ref, come_ref, c_send, c_recv = refs[:8]
+    q_refs, o_refs, refs = refs[8:14], refs[14:20], refs[20:]
+    g_buf, g_come, g_z, g_send, g_recv, w_ref, w_sem = refs
     d, t, o, i = place()
-    y, c = i // 2, i % 2
-    rows = hidden_ref.shape[0]
+    rows = hgrad_ref.shape[0]
     width = w_ref.shape[1]
     w_copy = pltpu.make_async_copy(w_any.at[:, pl.ds(0, width)], w_ref, w_sem)
     w_copy.start()
     greet_all(outer)
-    sums = Sums(outer, (2, 3), [dws[2], dws[1]], was_l, was_r, to_l[:2], to_r[:2], *sums_a)
-    last = Sums(outer, (3,), [dws[2]], to_l[:1], to_r[:1], to_l[2:], to_r[2:], *sums_b)
-    came = [done, (to_l[1], to_r[1]), (to_l[2], to_r[2])]
+    sums = [
+        Sums(outer, (3,), [dws[1 + k]], [was_l[k]], [was_r[k]], [to_l[k]], [to_r[k]], *sums_refs[k]) for k in range(2)
+    ]
+    came = [done, (to_l[0], to_r[0]), (to_l[1], to_r[1])]
     finals = [
-        Final(outer, dws[k], *came[k], final_refs[k][0], sums_a[1], fins[k], *final_refs[k][1:]) for k in range(3)
+        Final(outer, dws[k], *came[k], final_refs[k][0], sums_refs[0][1], fins[k], *final_refs[k][1:]) for k in range(3)
     ]
-    group = GroupSum(far, come, near, come_ab, last_ab, s_sem, r_sem)
-    mixer = Mixer(ys, pos_ref, gate_ref, held, l_sem)
-    sums.load()
-    sums.send()
+    for one in sums:
+        one.load()
+    for one in sums:
+        one.send()
+    whole, part = Spread(outer, *q_refs), Spread(outer, *o_refs)
+    each, heads = outw_ref.shape
+
+    def out_block(k, carry):
+        for r in range(GROUP):
+            at = pl.ds(pl.multiple_of((k * GROUP + r) * each, each), each)
+            part.terms[k, r // 2, r % 2, :, :heads] = oo_ref[at, :]
+            part.terms[k, r // 2, r % 2, :, heads:] = ox_ref[at, :]
+        return carry
+
+    lax.fori_loop(0, outer, out_block, 0)
+    part.over_core()
 
     w_copy.wait()
     part_ref[...] = mm_nt(px_ref[...], w_ref[...]).astype(BF)
     exchange = to_x(part_ref, theirs_ref, p_send, p_recv)
     exchange.start()
 
-    each = qkv_ref.shape[0]
-
     def weights_block(k, carry):
         lanes = pl.ds(pl.multiple_of(k * GROUP * each, GROUP * each), GROUP * each)
         total = (mm_tn(no_ref[:, lanes], po_ref[...]) + mm_tn(nx_ref[:, lanes], px_ref[...])).astype(BF)
         for r in range(GROUP):
-            qp[k, r // 2, r % 2, :, :width] = total[r * each : (r + 1) * each]
-            at = pl.ds(pl.multiple_of((k * GROUP + r) * each, each), each)
-            qp[k, r // 2, r % 2, :, width:] = ao_ref[at, :]
+            whole.terms[k, r // 2, r % 2] = total[r * each : (r + 1) * each]
         return carry
 
+    part.over_y()
     lax.fori_loop(0, outer, weights_block, 0)
-    to_core = to_dp(1, qp.at[:, :, 1 - c], q_core, q_send.at[0], q_recv.at[0])
-    to_core.start()
+    whole.over_core()
     finals[0].send()
-
-    mixer.load(2, 0)
-    mixer.load(3, 1)
-    mixer.mix(2, 0, group.far.at[0])
-    group.core[0].start()
-    mixer.load(1, 0)
-    to_core.wait()
-
-    def add_core(k, carry):
-        for r in range(2):
-            qp[k, r, c] = (qp[k, r, c].astype(F32) + q_core[k, r].astype(F32)).astype(BF)
-        return carry
-
-    lax.fori_loop(0, outer, add_core, 0)
-    to_y = to_dp(2, qp.at[:, 1 - y, c], q_y, q_send.at[1], q_recv.at[1])
-    to_y.start()
-    mixer.mix(3, 1, group.far.at[1])
-    group.core[1].start()
-    mixer.load(0, 1)
+    whole.over_y()
+    part.over_z()
+    sums[0].wait()
+    finals[1].send()
 
     exchange.wait()
-    gain_grad = jnp.zeros((1, D), F32)
     quarter = rows // 4
-    for p in range(4):
-        at = slice(p * quarter, (p + 1) * quarter)
-        normed_grad = mm_nt(po_ref[at], w_ref[:, :width]).astype(BF).astype(F32) + theirs_ref[at].astype(F32)
-        x = x_ref[at].astype(F32)
+
+    def norm_rows(p, gain_grad):
+        at = pl.ds(pl.multiple_of(p * quarter, quarter), quarter)
+        normed_grad = mm_nt(po_ref[at, :], w_ref[...]).astype(BF).astype(F32) + theirs_ref[at, :].astype(F32)
+        x = x_ref[at, :].astype(F32)
         inverse = lax.rsqrt(jnp.mean(x * x, axis=-1, keepdims=True) + EPSILON)
-        gain_grad = gain_grad + jnp.sum(normed_grad * (x * inverse), axis=0, keepdims=True)
         scaled = normed_grad * gain_ref[...]
-        tgrad_ref[at] = (
-            hgrad_ref[at]
+        tgrad_ref[at, :] = (
+            hgrad_ref[at, :]
             + inverse * scaled
             - x * (inverse * inverse * inverse * jnp.mean(scaled * x, axis=-1, keepdims=True))
         )
-    g_buf[0, 0:1, :] = gain_grad
+        return gain_grad + jnp.sum(normed_grad * (x * inverse), axis=0, keepdims=True)
+
+    g_buf[0, 0:1, :] = lax.fori_loop(0, 4, norm_rows, jnp.zeros((1, D), F32))
     g_buf[0, 1:2, :] = sg_ref[...]
     g_buf[0, 2:8, :] = jnp.zeros((6, D), F32)
     g_moves = [
-        to_x(g_buf.at[0], g_come.at[0], g_send.at[0], g_recv.at[0]),
-        to_dp(1, g_buf.at[1], g_come.at[1], g_send.at[1], g_recv.at[1]),
-        to_dp(2, g_buf.at[2], g_come.at[2], g_send.at[2], g_recv.at[2]),
+        to_dp(1, g_buf.at[0], g_come.at[0], g_send.at[0], g_recv.at[0]),
+        to_dp(2, g_buf.at[1], g_come.at[1], g_send.at[1], g_recv.at[1]),
+        to_x(g_buf.at[2], g_come.at[2], g_send.at[2], g_recv.at[2]),
     ]
     g_moves[0].start()
+    whole.over_z()
     g_moves[0].wait()
     g_buf[1] = g_buf[0] + g_come[0]
     g_moves[1].start()
-    to_y.wait()
-
-    def add_y(k, carry):
-        qp[k, y, c] = (qp[k, y, c].astype(F32) + q_y[k].astype(F32)).astype(BF)
-        return carry
-
-    lax.fori_loop(0, outer, add_y, 0)
-    z_moves = []
-    for k in range(1, outer):
-        peer = (o + k) % outer
-        z_moves.append(
-            pltpu.make_async_remote_copy(
-                qp.at[peer, y, c],
-                q_z.at[k - 1],
-                q_send.at[1 + k],
-                q_recv.at[1 + k],
-                device_id=(peer * GROUP + i, t),
-                device_id_type=MESH,
-            )
-        )
-    for move in z_moves:
-        move.start()
-    group.core[1].wait_recv()
-    mixer.mix(1, 0, group.near.at[1], group.come.at[1])
-    group.a.start()
-    group.b[1].start()
-    sums.wait()
-    last.load()
-    last.send()
+    sums[1].wait()
+    finals[2].send()
     g_moves[1].wait()
     g_buf[2] = g_buf[1] + g_come[1]
     g_moves[2].start()
-    group.core[0].wait_recv()
-    mixer.mix(0, 1, group.near.at[0], group.come.at[0])
-    group.b[0].start()
+    out = part.total()
+    outw_ref[...] = out[:, :heads]
+    out_ref[...] = out[:, heads:].astype(BF)
+    to_other = to_x(out_ref, come_ref, c_send, c_recv)
+    to_other.start()
     g_moves[2].wait()
     g_z[0] = g_buf[2] + g_come[2]
-    gz_moves = []
-    for k in range(1, outer):
-        peer = (o + k) % outer
-        gz_moves.append(
-            pltpu.make_async_remote_copy(
-                g_z.at[0],
-                g_z.at[k],
-                g_send.at[2 + k],
-                g_recv.at[2 + k],
-                device_id=(peer * GROUP + i, t),
-                device_id_type=MESH,
-            )
-        )
+    gz_moves = over_outer(outer, lambda peer: g_z.at[0], lambda k: g_z.at[k], g_send, g_recv, 2)
     for move in gz_moves:
         move.start()
-    group.second()
-    finals[1].send()
-    for move in z_moves:
-        move.wait()
-    total = qp[o, y, c].astype(F32)
-    for k in range(1, outer):
-        total = total + q_z[k - 1].astype(F32)
-    qkv_ref[...] = total[:, :width]
-    outw_ref[...] = total[:, width:]
+    qkv_ref[...] = whole.total()
+    to_other.wait()
+    outw_ref[...] = outw_ref[...] + come_ref[...].astype(F32)
     for move in gz_moves:
         move.wait()
     gains = g_z[(o + outer) % outer]
     for k in range(1, outer):
         gains = gains + g_z[(o - k + outer) % outer]
     gains_ref[...] = gains
-    for p in range(2):
-        at = slice(p * rows // 2, (p + 1) * rows // 2)
-        out_ref[at] = jnp.where(valid_ref[at] > 0, hidden_ref[at] + group.terms(p), 0.0).astype(BF)
-    last.wait()
-    finals[2].send()
-    group.sent()
     for final in finals:
         final.wait()
 
 
-def finish(outer, in_rows, length, pos, gate, valid, hidden, hgrad, x, gain, weights_full, extra, ys, dws, done, was_l, was_r):
-    rows = hidden.shape[0]
-    n = len(ys)
+def finish(outer, hgrad, x, gain, weights_full, extra, dws, done, was_l, was_r):
+    rows = hgrad.shape[0]
     packed = dws[0].shape[2]
     width = weights_full.shape[1] // 2
     heads = width // 2
     each = D // (outer * GROUP)
     hop = jax.ShapeDtypeStruct((GROUP, packed, D), BF)
-    columns = width + heads
     return remote_call(
-        functools.partial(finish_kernel, outer, in_rows),
+        functools.partial(finish_kernel, outer),
         "finish",
         11,
         [
-            jax.ShapeDtypeStruct((rows, D), BF),
             jax.ShapeDtypeStruct((rows, D), F32),
             jax.ShapeDtypeStruct((8, D), F32),
             jax.ShapeDtypeStruct((each, width), F32),
             jax.ShapeDtypeStruct((each, heads), F32),
         ]
-        + [hop] * 9,
-        [SMEM] + [VM] * 7 + [ANY] + [VM] * 6 + [ANY] * (n + 9),
-        [VM] * 5 + [ANY] * 9,
-        (length, pos, gate, valid, hidden, hgrad, x, gain.reshape(1, D), weights_full, *extra, *ys, *dws, *done, *was_l, *was_r),
+        + [hop] * 7,
+        [VM] * 3 + [ANY] + [VM] * 7 + [ANY] * 9,
+        [VM] * 4 + [ANY] * 7,
+        (hgrad, x, gain.reshape(1, D), weights_full, *extra, *dws, *done, *was_l, *was_r),
         [
-            *group_scratch(2 * rows, n),
-            *sums_scratch(2, packed),
-            *again(sums_scratch(1, packed)),
+            *sums_scratch(1, packed) * 2,
             *final_scratch(packed) * 3,
             pltpu.VMEM((rows, D), BF),
             pltpu.VMEM((rows, D), BF),
             pltpu.SemaphoreType.DMA,
             pltpu.SemaphoreType.DMA,
-            pltpu.VMEM((outer, 2, 2, each, columns), BF),
-            pltpu.VMEM((outer, 2, each, columns), BF),
-            pltpu.VMEM((outer, each, columns), BF),
-            pltpu.VMEM((outer - 1, each, columns), BF),
-            pltpu.SemaphoreType.DMA((1 + outer,)),
-            pltpu.SemaphoreType.DMA((1 + outer,)),
+            pltpu.VMEM((each, heads), BF),
+            pltpu.VMEM((each, heads), BF),
+            pltpu.SemaphoreType.DMA,
+            pltpu.SemaphoreType.DMA,
+            *spread_scratch(outer, each, width),
+            *spread_scratch(outer, each, 2 * heads),
             pltpu.VMEM((3, 8, D), F32),
             pltpu.VMEM((3, 8, D), F32),
             pltpu.VMEM((outer, 8, D), F32),
@@ -2092,44 +2187,48 @@
     )
 
 
-def settle_kernel(n, in_rows, idx_ref, *refs):
-    sources, (in_ref, down_ref) = refs[:n], refs[n:]
-    j = pl.program_id(0)
-    for k in range(n):
-
-        @pl.when(j == k)
-        def _(k=k):
-            in_ref[0] = sources[k][0, :in_rows, :].astype(F32)
-            down_ref[0] = sources[k][0, in_rows:, :].astype(F32)
+def settle_kernel(in_rows, idx_ref, *refs):
+    n = len(refs) - 7
+    sources, (in_ref, down_ref, held, wide_in, wide_down, l_sem, s_sem) = refs[:n], refs[n:]
+    loads = [pltpu.make_async_copy(source, held.at[j], l_sem.at[j]) for j, source in enumerate(sources)]
+    for c in loads:
+        c.start()
+    stores = []
+    for j in range(n):
+        loads[j].wait()
+        for m in range(GROUP):
+            k = j * GROUP + m
+            at = (idx_ref[1] ^ m) * n + j
+            wide_in[k] = held[j, m, :in_rows, :].astype(F32)
+            wide_down[k] = held[j, m, in_rows:, :].astype(F32)
+            stores.append(pltpu.make_async_copy(wide_in.at[k], in_ref.at[at], s_sem.at[2 * k]))
+            stores.append(pltpu.make_async_copy(wide_down.at[k], down_ref.at[at], s_sem.at[2 * k + 1]))
+            for c in stores[-2:]:
+                c.start()
+    for c in stores:
+        c.wait()
 
 
 def settle_experts(idx, fins, in_rows):
     n = len(fins)
     _, packed, _ = fins[0].shape
-    experts = n * GROUP
-
-    def source(k):
-        return lambda j, m, idx_ref: (jnp.where(j == k, m, jnp.where(j < k, 0, GROUP - 1)), 0, 0)
-
-    def target(j, m, idx_ref):
-        return ((idx_ref[1] ^ m) * n + j, 0, 0)
-
-    return pl.pallas_call(
-        functools.partial(settle_kernel, n, in_rows),
-        name="settle_experts",
-        out_shape=[
-            jax.ShapeDtypeStruct((experts, in_rows, D), F32),
-            jax.ShapeDtypeStruct((experts, packed - in_rows, D), F32),
+    experts, down_rows = n * GROUP, packed - in_rows
+    return call(
+        functools.partial(settle_kernel, in_rows),
+        "settle_experts",
+        [jax.ShapeDtypeStruct((experts, in_rows, D), F32), jax.ShapeDtypeStruct((experts, down_rows, D), F32)],
+        [SMEM] + [ANY] * n,
+        [ANY] * 2,
+        (idx, *fins),
+        scratch=[
+            pltpu.VMEM((n, GROUP, packed, D), BF),
+            pltpu.VMEM((experts, in_rows, D), F32),
+            pltpu.VMEM((experts, down_rows, D), F32),
+            pltpu.SemaphoreType.DMA((n,)),
+            pltpu.SemaphoreType.DMA((2 * experts,)),
         ],
-        grid_spec=pltpu.PrefetchScalarGridSpec(
-            num_scalar_prefetch=1,
-            grid=(n, GROUP),
-            in_specs=[pl.BlockSpec((1, packed, D), source(k)) for k in range(n)],
-            out_specs=[pl.BlockSpec((1, in_rows, D), target), pl.BlockSpec((1, packed - in_rows, D), target)],
-        ),
-        compiler_params=pltpu.CompilerParams(vmem_limit_bytes=VMEM_LIMIT),
-        cost_estimate=pl.CostEstimate(flops=0, bytes_accessed=9 << 20, transcendentals=0),
-    )(idx, *fins)
+        moved=9 << 20,
+    )
 
 
 def layer(
@@ -2246,6 +2345,9 @@
         for j in range(own_experts):
             first_grad = weight_grads[:1]
             sum_plan = ((j,), first_grad, sums_l or first_grad, sums_r or first_grad) if j else ((), [], [], [])
+            if j == own_experts - 1:
+                second_grad = weight_grads[1]
+                sum_plan = ((j, 1), weight_grads[:2], [*sums_l, second_grad], [*sums_r, second_grad])
             (y, dx, dw), moved_l, moved_r, sums_l, sums_r = expert_step(
                 j,
                 outer,
@@ -2266,23 +2368,26 @@
             weight_grads.append(dw)
         valid_column = valid_rows.astype(F32)[:, None]
         _, dw_b, dw_c, dw_d = weight_grads
-        main, sum_l, sum_r = rows_back(
+        main, fin_a, sum_l, sum_r = rows_back(
             outer,
             pos_columns,
+            gate_columns,
             valid_column,
             hidden,
             cotangent,
             second_gain,
             weights_full,
             row_grads,
-            (1, 1),
-            ((2, 0), (2, 1)),
-            [dw_b, dw_c],
-            [dw_b, dw_c],
-            [dw_b, dw_c],
+            expert_outs,
+            (2, 1),
+            ((2, 1), (1, 2)),
+            [dw_b, dw_c, dw_d],
+            [sums_l[1], dw_c],
+            [sums_r[1], dw_c],
+            [weight_grads[0], sums_l[0], sums_r[0]],
         )
-        hidden_grad, branch_grad, second_gain_part, attn_grad_own, attn_grad_other = main
-        projected, fin_a, three_l, three_r = attention_back(
+        hidden_grad, branch_grad, second_gain_part, attn_grad_own, attn_grad_other, mixed = main
+        (projected_own, projected_other, output), three_l, three_r = attention_back(
             outer,
             q_block,
             lengths,
@@ -2291,32 +2396,26 @@
             cosine,
             sine,
             [attn_grad_own, attn_grad_other],
-            (3, 1),
+            hidden,
+            valid_column,
+            mixed,
+            (3, 2),
             [dw_b, dw_d],
-            [sum_l[2], dw_d],
-            [sum_r[2], dw_d],
-            [weight_grads[0], sums_l[0], sums_r[0]],
+            [sum_l[0], sum_l[3]],
+            [sum_r[0], sum_r[3]],
         )
         out_own, out_other = (mm_tn(branch_grad, part).astype(BF) for part in attn_parts)
-        attn_out_part = (out_own.astype(F32) + beside(out_other).astype(F32)).astype(BF)
-        output, tokens_grad, gains, qkv_grad, attn_out_grad, *fins = finish(
+        tokens_grad, gains, qkv_grad, attn_out_grad, *fins = finish(
             outer,
-            in_rows,
-            lengths,
-            pos_columns,
-            gate_columns,
-            valid_column,
-            hidden,
             hidden_grad,
             tokens,
             first_gain,
             weights_full,
-            [normed_one, other, *projected, attn_out_part, second_gain_part],
-            expert_outs,
+            [normed_one, other, projected_own, projected_other, out_own, out_other, second_gain_part],
             [dw_b, dw_c, dw_d],
             [three_l[0], three_r[0]],
-            [three_l[1], sum_l[3]],
-            [three_r[1], sum_r[3]],
+            [sum_l[2], three_l[1]],
+            [sum_r[2], three_r[1]],
         )
         expert_in_grad, expert_out_grad = settle_experts(idx, [fin_a, *fins[:3]], in_rows)
         return (

time: 584 us -> 550 us (0.942)
  Pallas kernels: 554 us -> 519 us
    pallas_call x11, Pallas kernels: 542 us -> 514 us  [remote_call(): pl.pallas_call(kernel, name=name, out_shape=out_shape, in_specs=in_specs,...]
    pallas_call x1, Pallas kernels: 11.8 us -> 4.88 us  [call(): pl.pallas_call(kernel, name=name, out_shape=out_shape, in_specs=in_specs,...]
  transfers between devices with their start and end apart: 1 -> 0, of which waited for: 0 -> 0; matrix products, arithmetic and copies ran while one was open for 0% -> 0% of each run, Pallas kernels for 7% -> 0%
where the time goes in v5:
time: 550 us; the launch traced here: 540 us
  Pallas kernels  519 us (94%)
  other arithmetic  8.27 us (2%)
  local copies, waits for them, and re-layouts  5.86 us (1%)
    pallas_call x11, Pallas kernels, remote_call(): pl.pallas_call(kernel, name=name, out_shape=out_shape, in_specs=in_specs,...  514 us

profile of v5, /device:TPU:9, one launch (start us, length us, event | category | flops | bytes accessed | tf_op | source)
XLA Modules:
  0.0 539.6 jit_solution(9786460412920419335)
XLA Ops:
  0.6 0.0 copy-start.3
  0.6 0.0 copy-start.5
  1.4 0.7 convert_bitcast_fusion
  2.1 0.9 select_reduce_fusion
  2.9 0.6 select_convert_fusion.gates_ref
  3.6 1.5 fusion
  5.1 2.5 fusion.2.normed_ref.own_ref.refs_0_
  7.6 0.0 copy-done.3
  7.6 0.0 copy-done.5
  7.6 0.7 pad_maximum_fusion.shard_ref
  8.3 0.6 broadcast_in_dim_tile.3.freq_ref
  8.9 53.3 %collect.1 = (bf16[1024,2048]{1,0:T(8,128)(2,1)}, bf16[512,1024]{1,0:T(8,128)(2,1)}, f32[1024,128]{1,0:T(8,128)}, f32[1024,128]{1,0:T(8,128)}, s32[4,4,1024]{2,1...) custom-call(bf16[64,1536]{1,0:T(8,128)(2,1)} %pad_maximum_fusion.sha, ...), custom_call_target="tpu_custom_call" | custom-call | flops 4294967296 | bytes 8388608 | tf_op jit(solution)/shard_map/collect/pallas_call | solution.py:664
  62.2 62.6 %attention.1 = (bf16[1024,1024]{1,0:T(8,128)(2,1)}, f32[4,4,512]{2,1,0:T(4,128)}, bf16[512,512]{1,0:T(8,128)(2,1)}, bf16[512,512]{1,0:T(8,128)(2,1)}, f32[512,10...) custom-call(s32[1]{0:T(128)} %copy.23.len_ref, ...), custom_call_target="tpu_custom_call" | custom-call | flops 32212254720 | bytes 8388608 | tf_op jit(solution)/shard_map/attention/pallas_call | solution.py:664
  124.9 57.9 %spread.1 = (bf16[4,4,256,1024]{3,2,1,0:T(8,128)(2,1)}, bf16[3,4,256,1024]{3,2,1,0:T(8,128)(2,1)}, bf16[4,4,288,1024]{3,2,1,0:T(8,128)(2,1)}, bf16[4,96,1024]{2,...) custom-call(s32[4,4,1024]{2,1,0:T(4,128)} %get-tuple-element.121.pos, ...), custom_call_target="tpu_custom_call" | custom-call | flops 12884901888 | bytes 8388608 | tf_op jit(solution)/shard_map/spread/pallas_call | solution.py:664
  182.8 38.5 %hand_out.1 = (bf16[4,4,288,1024]{3,2,1,0:T(8,128)(2,1)}, bf16[4,96,1024]{2,1,0:T(8,128)(2,1)}, bf16[4,96,1024]{2,1,0:T(8,128)(2,1)}, bf16[4,96,1024]{2,1,0:T(8,128)(2,1)}, bf16[4,96,1024]{2,1,0:T(8,128)(2,1)}) custom-call(s32[4,4,1024]{2,1,0:T(4,128)} %get-tuple-element.121.pos_ref, bf16[256,1024]{1,0:T(8,128)(2,1)} %get-tuple-element.122.na_ref, ...), custom_call_target="tpu_custom_call" | custom-call | flops 12884901888 | bytes 8388608 | tf_op jit(solution)/shard_map/hand_out/pallas_call | solution.py:664
  221.4 23.3 %expert_step.4 = (bf16[4,288,1024]{2,1,0:T(8,128)(2,1)}, bf16[4,288,1024]{2,1,0:T(8,128)(2,1)}, bf16[4,4,96,1024]{3,2,1,0:T(8,128)(2,1)}, bf16[4,96,1024]{2,1,0:T(8,128)(2,1)}, bf16[4,96,1024]{2,1,0:T(8,128)(2,1)}) custom-call(bf16[4,4,288,1024]{3,2,1,0:T(8,128)(2,1)} %get-tuple-element.140.x_ref, bf16[4,4,288,1024]{3,2,1,0:T(8,128)(2,1)} %get-tuple-element.141.g_ref, ...), custom_call_target="tpu_custom_call" | custom-call | flops 10871635968 | bytes 8388608 | tf_op jit(solution)/shard_map/expert_step/pallas_call | solution.py:664
  244.7 23.3 %expert_step.5 = (bf16[4,288,1024]{2,1,0:T(8,128)(2,1)}, bf16[4,288,1024]{2,1,0:T(8,128)(2,1)}, bf16[4,4,96,1024]{3,2,1,0:T(8,128)(2,1)}, bf16[4,96,1024]{2,1,0:...) custom-call(bf16[4,4,288,1024]{3,2,1,0:T(8,128)(2,1)} %get-tuple-element.140, ...), custom_call_target="tpu_custom_call" | custom-call | flops 10871635968 | bytes 8388608 | tf_op jit(solution)/shard_map/expert_step/pallas_call | solution.py:664
  268.0 23.9 %expert_step.6 = (bf16[4,288,1024]{2,1,0:T(8,128)(2,1)}, bf16[4,288,1024]{2,1,0:T(8,128)(2,1)}, bf16[4,4,96,1024]{3,2,1,0:T(8,128)(2,1)}, bf16[4,96,1024]{2,1,0:...) custom-call(bf16[4,4,288,1024]{3,2,1,0:T(8,128)(2,1)} %get-tuple-element.140, ...), custom_call_target="tpu_custom_call" | custom-call | flops 10871635968 | bytes 8388608 | tf_op jit(solution)/shard_map/expert_step/pallas_call | solution.py:664
  291.9 37.7 %expert_step.7 = (bf16[4,288,1024]{2,1,0:T(8,128)(2,1)}, bf16[4,288,1024]{2,1,0:T(8,128)(2,1)}, bf16[4,4,96,1024]{3,2,1,0:T(8,128)(2,1)}, bf16[4,96,1024]{2,1,0:...) custom-call(bf16[4,4,288,1024]{3,2,1,0:T(8,128)(2,1)} %get-tuple-element.140, ...), custom_call_target="tpu_custom_call" | custom-call | flops 10871635968 | bytes 8388608 | tf_op jit(solution)/shard_map/expert_step/pallas_call | solution.py:664
  329.6 0.7 fusion.3.valid_ref
  330.4 0.0 copy-start.8
  330.4 80.5 %rows_back.1 = (f32[512,1024]{1,0:T(8,128)}, bf16[512,1024]{1,0:T(8,128)(2,1)}, f32[1,1024]{1,0:T(1,128)}, bf16[512,512]{1,0:T(8,128)(2,1)}, bf16[512,512]{1,0:T...) custom-call(s32[4,1024,4]{2,1,0:T(8,128)} %get-tuple-element.118.pos, ...), custom_call_target="tpu_custom_call" | custom-call | flops 32212254720 | bytes 8388608 | tf_op jit(solution)/shard_map/rows_back/pallas_call | solution.py:664
  410.8 0.0 copy-start.6
  410.8 0.0 copy-start.7
  410.8 0.0 copy-done.8
  410.9 3.1 convolution_convert_fusion.refs_5_
  413.9 0.0 copy-done.6
  413.9 0.0 copy-done.7
  413.9 1.7 convolution_convert_fusion.1.refs_4_
  415.6 41.7 %attention_back.1 = (bf16[512,1024]{1,0:T(8,128)(2,1)}, bf16[512,1024]{1,0:T(8,128)(2,1)}, bf16[512,1024]{1,0:T(8,128)(2,1)}, bf16[4,96,1024]{2,1,0:T(8,128)(2,1...) custom-call(s32[1]{0:T(128)} %copy.23.len_ref, ...), custom_call_target="tpu_custom_call" | custom-call | flops 32212254720 | bytes 8388608 | tf_op jit(solution)/shard_map/attention_back/pallas_call | solution.py:664
  457.4 71.1 %finish.1 = (f32[512,1024]{1,0:T(8,128)}, f32[8,1024]{1,0:T(8,128)}, f32[64,1024]{1,0:T(8,128)}, f32[64,512]{1,0:T(8,128)}, bf16[4,96,1024]{2,1,0:T(8,128)(2,1)}...) custom-call(f32[512,1024]{1,0:T(8,128)} %get-tuple-element.187.hgrad, ...), custom_call_target="tpu_custom_call" | custom-call | flops 32212254720 | bytes 8388608 | tf_op jit(solution)/shard_map/finish/pallas_call | solution.py:664
  528.5 0.0 copy-start.2
  528.5 0.0 copy-start.1
  528.5 0.6 pad_add_fusion.idx_ref
  529.1 0.0 copy-start
  529.1 4.9 settle_experts.1
  534.0 0.0 copy-done.2
  534.0 0.8 reshape.66
  534.8 1.4 fusion.4
  536.3 0.0 copy-done.1
  536.3 1.0 copy.24
  537.2 0.0 copy-done
  537.2 0.0 copy-start.4
  537.2 1.3 copy.25
  538.6 0.0 copy-done.4
  538.6 0.7 copy.26
  (5 shorter events, 0.0 us)
Async XLA Ops:
  0.6 7.0 %copy-start.3 = (bf16[64,4,256]{2,1,0:T(4,128)(2,1)S(1)}, bf16[64,4,256]{2,1,0:T(4,128)(2,1)}, u32[]{:S(2)}) copy-start(bf16[64,4,256]{2,1,0:T(4,128)(2,1)} %param.17) | copy-start | bytes 393220
  0.6 7.0 %copy-start.5 = (bf16[512,64]{0,1:T(8,128)(2,1)S(1)}, bf16[512,64]{0,1:T(8,128)(2,1)}, u32[]{:S(2)}) copy-start(bf16[512,64]{0,1:T(8,128)(2,1)} %param.18) | copy-start | bytes 196612
  330.4 80.5 %copy-start.8 = (bf16[512,512]{1,0:T(8,128)(2,1)S(1)}, bf16[512,512]{1,0:T(8,128)(2,1)}, u32[]{:S(2)}) copy-start(bf16[512,512]{1,0:T(8,128)(2,1)} %get-tuple-element.192) | copy-start | bytes 1572868
  410.8 3.1 copy-start.6
  410.8 3.1 copy-start.7
  528.5 5.5 %copy-start.2 = (f32[64,1024]{1,0:T(8,128)S(1)}, f32[64,1024]{1,0:T(8,128)}, u32[]{:S(2)}) copy-start(f32[64,1024]{1,0:T(8,128)} %get-tuple-element.202) | copy-start | bytes 786436
  528.5 7.8 %copy-start.1 = (bf16[512,1024]{1,0:T(8,128)(2,1)S(1)}, bf16[512,1024]{1,0:T(8,128)(2,1)}, u32[]{:S(2)}) copy-start(bf16[512,1024]{1,0:T(8,128)(2,1)} %get-tuple-element.220) | copy-start | bytes 3145732
  529.1 8.1 %copy-start = (f32[512,1024]{1,0:T(8,128)S(1)}, f32[512,1024]{1,0:T(8,128)}, u32[]{:S(2)}) copy-start(f32[512,1024]{1,0:T(8,128)} %get-tuple-element.221) | copy-start | bytes 6291460
  537.2 1.3 copy-start.4

commit v6 on v5

--- a/solution.py
+++ b/solution.py
@@ -790,10 +790,19 @@
         stays[j].start()
     gates_all[0, :, 0:half] = gates_ref[:, 0:half]
     gates_all[0, :, 2 * half : 3 * half] = gates_ref[:, half:]
-    angles = lax.broadcasted_iota(jnp.int32, (slot_rows, LANES), 0).astype(F32) * freq_ref[...]
-    lane = lax.broadcasted_iota(jnp.int32, (slot_rows, LANES), 1)
-    cos_ref[...] = jnp.cos(angles)
-    sin_ref[...] = jnp.where(lane % HD < HD // 2, -jnp.sin(angles), jnp.sin(angles))
+    block_rows = 128
+
+    def table(b, carry):
+        at = pl.ds(pl.multiple_of(b * block_rows, block_rows), block_rows)
+        row = b * block_rows + lax.broadcasted_iota(jnp.int32, (block_rows, LANES), 0)
+        angles = row.astype(F32) * freq_ref[...]
+        lane = lax.broadcasted_iota(jnp.int32, (block_rows, LANES), 1)
+        sine = jnp.sin(angles)
+        cos_ref[at, :] = jnp.cos(angles)
+        sin_ref[at, :] = jnp.where(lane % HD < HD // 2, -sine, sine)
+        return carry
+
+    lax.fori_loop(0, slot_rows // block_rows, table, 0)
     for c in g_x:
         c.wait()
     g_y.start()
@@ -953,10 +962,12 @@
 
     block = 256
     key_lanes = lax.broadcasted_iota(jnp.int32, (block, LANES), 1) < HD
-    for part in range(2):
-        for b in range(rows // block):
+    for part, source in enumerate((own_ref, other_ref)):
+
+        def project(b, carry, part=part, source=source):
+            here = pl.ds(pl.multiple_of(b * block, block), block)
             at = pl.multiple_of((t if part == 0 else 1 - t) * rows + b * block, block)
-            projected = mm((own_ref if part == 0 else other_ref)[b * block : (b + 1) * block], w_ref[:, :width])
+            projected = mm(source[here, :], w_ref[:, :width])
             cosine, sine = cos_ref[pl.ds(at, block), :], sin_ref[pl.ds(at, block), :]
             for g in range(groups):
                 q = projected[:, g * 2 * LANES : g * 2 * LANES + LANES]
@@ -965,6 +976,9 @@
                 kv = jnp.where(key_lanes, kv * cosine + swap_halves(kv) * sine, kv)
                 qkv_ref[pl.ds(at, block), g * 2 * LANES : g * 2 * LANES + LANES] = q.astype(BF)
                 qkv_ref[pl.ds(at, block), g * 2 * LANES + LANES : (g + 1) * 2 * LANES] = kv.astype(BF)
+            return carry
+
+        lax.fori_loop(0, rows // block, project, 0)
 
     for copy in dys:
         copy.start()
@@ -1084,13 +1098,14 @@
     cot_ref, dy_refs, refs = refs[0], refs[1:5], refs[5:]
     from_left, refs = refs[:n_steps], refs[n_steps:]
     from_right, refs = refs[:n_steps], refs[n_steps:]
-    n_ref, dyx_ref, og_ref = refs[:3]
+    n_ref, dyx_ref, og_out = refs[:3]
     refs = refs[3:]
     to_left, refs = refs[:n_steps], refs[n_steps:]
     to_right, refs = refs[:n_steps], refs[n_steps:]
-    held, s_hop, r_hop, s_n, r_n, s_d, r_d, l_sem = refs
+    held, s_hop, r_hop, s_n, r_n, s_d, r_d, l_sem, og_ref, o_sem = refs
     height = na_ref.shape[0]
     n_experts = og_ref.shape[1]
+    leave = [pltpu.make_async_copy(og_ref.at[s % 2], og_out.at[s], o_sem.at[s]) for s in range(GROUP)]
     greet(outer, (1, 2), True)
     n_ax = to_x(na_ref, n_ref.at[0, 1], s_n.at[0], r_n.at[0])
     n_by = to_dp(2, nb_ref, n_ref.at[1, 2], s_n.at[1], r_n.at[1])
@@ -1139,15 +1154,18 @@
             c.start()
         for c in copies:
             c.wait()
+        if s >= 2:
+            leave[s - 2].wait()
 
         def one(j, carry):
             rank = lax.broadcasted_iota(jnp.int32, (CAP, 4 * height), 0)
             chosen = rank == pos_ref[s, pl.ds(j, 1), :]
             one_hot = jnp.where(chosen, gate_ref[s, pl.ds(j, 1), :], 0.0).astype(BF)
-            og_ref[s, j] = mm(one_hot, held[...]).astype(BF)
+            og_ref[s % 2, j] = mm(one_hot, held[...]).astype(BF)
             return carry
 
         lax.fori_loop(0, n_experts, one, 0)
+        leave[s].start()
 
     give(0)
     n_ax.wait()
@@ -1177,6 +1195,8 @@
     give(3)
     for key in core:
         core[key].wait()
+    for s in range(2, GROUP):
+        leave[s].wait()
     hops.wait()
 
 
@@ -1195,7 +1215,7 @@
         ]
         + weights * 2,
         [VM] * 2 + [ANY] * (2 + 5 + 2 * n),
-        [ANY, ANY, VM] + [ANY] * (2 * n),
+        [ANY] * (3 + 2 * n),
         (pos, gate, *normed, *dys, *from_left, *from_right),
         [
             pltpu.VMEM((4 * height, D), BF),
@@ -1206,6 +1226,8 @@
             pltpu.SemaphoreType.DMA((10,)),
             pltpu.SemaphoreType.DMA((10,)),
             pltpu.SemaphoreType.DMA((4,)),
+            pltpu.VMEM((2, n_experts, CAP, D), BF),
+            pltpu.SemaphoreType.DMA((GROUP,)),
         ],
         12 << 30,
     )
@@ -1216,10 +1238,11 @@
     n_steps = len(steps)
     from_left, refs = refs[:n_steps], refs[n_steps:]
     from_right, refs = refs[:n_steps], refs[n_steps:]
-    x_ref, refs = refs[0], refs[1:]
+    x_out, refs = refs[0], refs[1:]
     to_left, refs = refs[:n_steps], refs[n_steps:]
     to_right, refs = refs[:n_steps], refs[n_steps:]
-    held, s_hop, r_hop, l_sem = refs
+    held, s_hop, r_hop, l_sem, x_ref, o_sem = refs
+    leave = [pltpu.make_async_copy(x_ref.at[s % 2], x_out.at[s], o_sem.at[s]) for s in range(GROUP)]
     height = na_ref.shape[0]
     n_experts = x_ref.shape[1]
     greet(outer, (), False)
@@ -1246,14 +1269,19 @@
                 c.start()
         for c in load(s):
             c.wait()
+        if s >= 2:
+            leave[s - 2].wait()
 
         def one(j, carry, s=s):
             rank = lax.broadcasted_iota(jnp.int32, (CAP, 4 * height), 0)
             one_hot = jnp.where(rank == pos_ref[s, pl.ds(j, 1), :], 1.0, 0.0).astype(BF)
-            x_ref[s, j] = mm(one_hot, held[s % 2]).astype(BF)
+            x_ref[s % 2, j] = mm(one_hot, held[s % 2]).astype(BF)
             return carry
 
         lax.fori_loop(0, n_experts, one, 0)
+        leave[s].start()
+    for s in range(2, GROUP):
+        leave[s].wait()
     hops.wait()
 
 
@@ -1267,13 +1295,15 @@
         3,
         [jax.ShapeDtypeStruct((GROUP, n_experts, CAP, D), BF)] + weights * 2,
         [VM] + [ANY] * (3 + 2 * n),
-        [VM] + [ANY] * (2 * n),
+        [ANY] * (1 + 2 * n),
         (pos, *normed, gathered, *from_left, *from_right),
         [
             pltpu.VMEM((2, 4 * height, D), BF),
             pltpu.SemaphoreType.DMA((2 * n,)),
             pltpu.SemaphoreType.DMA((2 * n,)),
             pltpu.SemaphoreType.DMA((2, 4)),
+            pltpu.VMEM((2, n_experts, CAP, D), BF),
+            pltpu.SemaphoreType.DMA((GROUP,)),
         ],
         12 << 30,
     )
@@ -1289,16 +1319,17 @@
     dws, refs = refs[:n_sums], refs[n_sums:]
     was_l, refs = refs[:n_sums], refs[n_sums:]
     was_r, refs = refs[:n_sums], refs[n_sums:]
-    y_ref, dx_ref, dw_ref = refs[:3]
+    y_out, dx_out, dw_out = refs[:3]
     refs = refs[3:]
     to_left, refs = refs[:n_steps], refs[n_steps:]
     to_right, refs = refs[:n_steps], refs[n_steps:]
     sum_left, refs = refs[:n_sums], refs[n_sums:]
     sum_right, refs = refs[:n_sums], refs[n_sums:]
     x_all, g_all, w_in, w_down, act_all, gug_all, sem_x, sem_g, sem_w, sem_d, s_hop, r_hop = refs[:12]
+    (y_ref, dx_ref, dw_ref, o_sem), refs = refs[12:16], refs[16:]
     _, _, o, i = place()
     greet(outer, (), False)
-    sums = Sums(outer, sum_steps, dws, was_l, was_r, sum_left, sum_right, *refs[12:])
+    sums = Sums(outer, sum_steps, dws, was_l, was_r, sum_left, sum_right, *refs)
     if n_steps:
         hops = Hops(
             outer,
@@ -1376,7 +1407,18 @@
         gug_all[at, :FF] = (act_grad * u * sigma * (1.0 + g * (1.0 - sigma))).astype(BF)
         gug_all[at, FF:] = (act_grad * silu).astype(BF)
         dx_ref[s] = mm_nt(gug_all[at, :], w_in[...]).astype(BF)
+        for copy in leaving(s):
+            copy.start()
         return carry
+
+    def leaving(s):
+        return (
+            pltpu.make_async_copy(y_ref.at[s], y_out.at[s], o_sem.at[0, s]),
+            pltpu.make_async_copy(dx_ref.at[s], dx_out.at[s], o_sem.at[1, s]),
+        )
+
+    def gradient(c):
+        return pltpu.make_async_copy(dw_ref.at[c], dw_out.at[c], o_sem.at[2, c])
 
     lax.fori_loop(0, GROUP, per_slot, 0)
     in_block, down_block = GROUP * in_rows, GROUP * down_rows
@@ -1390,9 +1432,15 @@
         part = mm_tn(act_all[:, lanes], g_all[...]).astype(BF)
         for r in range(GROUP):
             dw_ref[c, flip(i, r), in_rows:, :] = part[r * down_rows : (r + 1) * down_rows]
+        gradient(c).start()
         return carry
 
     lax.fori_loop(0, outer, per_owner, 0)
+    for s in range(GROUP):
+        for copy in leaving(s):
+            copy.wait()
+    for c in range(outer):
+        gradient(c).wait()
     if n_steps:
         hops.wait()
     sums.wait()
@@ -1415,7 +1463,7 @@
         4 + j,
         shapes,
         [ANY] * (3 + 2 * n_hops + 2 * n + 3 * n_sums),
-        [VM] * 3 + [ANY] * (2 * n + 2 * n_sums),
+        [ANY] * (3 + 2 * n + 2 * n_sums),
         (x, g, own, *lefts, *rights, *from_left, *from_right, *dws, *was_l, *was_r),
         [
             pltpu.VMEM((total, D), BF),
@@ -1430,6 +1478,10 @@
             pltpu.SemaphoreType.DMA(((1 + 2 * n_hops) * GROUP,)),
             pltpu.SemaphoreType.DMA((max(1, 2 * n),)),
             pltpu.SemaphoreType.DMA((max(1, 2 * n),)),
+            pltpu.VMEM((GROUP, CAP, D), BF),
+            pltpu.VMEM((GROUP, CAP, D), BF),
+            pltpu.VMEM((outer, GROUP, packed, D), BF),
+            pltpu.SemaphoreType.DMA((3, max(GROUP, outer))),
             *sums_scratch(n_sums, packed),
         ],
         18 * total * D * FF,
@@ -1700,73 +1752,94 @@
         s_sem,
         r_sem,
     )
-    core = [to_dp(1, far.at[s], come.at[s], s_core.at[s], r_core.at[s]) for s in range(2)]
-    mixed_core = [to_dp(1, far.at[s], mixed_come.at[s], s_core.at[2 + s], r_core.at[2 + s]) for s in range(2)]
+    def core(s):
+        return to_dp(1, far.at[s], come.at[s], s_core.at[s], r_core.at[s])
+
+    def mixed_core(s):
+        return to_dp(1, far.at[s], mixed_come.at[s], s_core.at[2 + s], r_core.at[2 + s])
+
+    outputs = Mixer(ys, pos_ref, gate_ref, held, l_sem)
+    rows = hidden_ref.shape[0] // 2
+    aways = [
+        to_x(
+            send_ref.at[pl.ds(p * rows, rows)], come_ref.at[pl.ds(p * rows, rows)], s_at.at[p], r_at.at[p]
+        )
+        for p in range(2)
+    ]
+
+    def phase(mixer, base, target, add, ahead, behind):
+        def body(k, carry):
+            s = 1 - k
+            ahead(s, k)
+            mixer.mix(base + s, k, target.at[s], None if add is None else add.at[s])
+            behind(s, k)
+            return carry
+
+        lax.fori_loop(0, 2, body, 0)
+
+    def far_behind(s, k):
+        core(s).start()
+        mixer.load(s, k)
+
+    def near_behind(s, k):
+        @pl.when(s == 1)
+        def _():
+            group.a[1].start()
+            group.b[1].start()
+            group.a[0].start()
+
+        pl.when(s == 0)(group.b[0].start)
+        outputs.load(2 + s, k)
+
+    def mixed_ahead(s, k):
+        core(s).wait_send()
+        pl.when(k == 1)(group.second)
+
+    def mixed_behind(s, k):
+        mixed_core(s).start()
+        outputs.load(s, k)
+
+    def back():
+        gain = gain_ref[...]
+        gain_grad = jnp.zeros((1, D), F32)
+        for p in range(2):
+            at = slice(p * rows, (p + 1) * rows)
+            hidden = hidden_ref[at]
+            normed_grad = group.terms(p)
+            inverse = lax.rsqrt(jnp.mean(hidden * hidden, axis=-1, keepdims=True) + EPSILON)
+            gain_grad = gain_grad + jnp.sum(normed_grad * (hidden * inverse), axis=0, keepdims=True)
+            scaled = normed_grad * gain
+            back = inverse * scaled - hidden * (
+                inverse * inverse * inverse * jnp.mean(scaled * hidden, axis=-1, keepdims=True)
+            )
+            dy = jnp.where(valid_ref[at] > 0, cot_ref[at].astype(F32), 0.0)
+            total = dy + back
+            grad_ref[at] = total
+            low = total.astype(BF)
+            low_ref[at] = low
+            send_ref[at] = mm(low, w_ref[:, heads:]).astype(BF)
+            aways[p].start()
+        gain_grad_ref[...] = gain_grad
+
+    def last_ahead(s, k):
+        mixed_core(s).wait_recv()
+        pl.when(k == 1)(back)
+
     one.load()
     one.send()
     final.send()
-    mixer.mix(3, 0, far.at[1])
-    core[1].start()
-    mixer.load(1, 0)
-    mixer.mix(2, 1, far.at[0])
-    core[0].start()
-    mixer.load(0, 1)
-    core[1].wait_recv()
-    mixer.mix(1, 0, near.at[1], come.at[1])
-    group.a[1].start()
-    group.b[1].start()
-    group.a[0].start()
-    outputs = Mixer(ys, pos_ref, gate_ref, held, l_sem)
-    outputs.load(3, 0)
-    core[0].wait_recv()
-    mixer.mix(0, 1, near.at[0], come.at[0])
-    group.b[0].start()
-    outputs.load(2, 1)
-    core[1].wait_send()
-    outputs.mix(3, 0, far.at[1])
-    mixed_core[1].start()
-    outputs.load(1, 0)
-    group.second()
-    core[0].wait_send()
-    outputs.mix(2, 1, far.at[0])
-    mixed_core[0].start()
-    outputs.load(0, 1)
+    phase(mixer, 2, far, None, lambda s, k: None, far_behind)
+    phase(mixer, 0, near, come, lambda s, k: core(s).wait_recv(), near_behind)
+    phase(outputs, 2, far, None, mixed_ahead, mixed_behind)
     one.wait()
     two.load()
     two.send()
-    mixed_core[1].wait_recv()
-    outputs.mix(1, 0, mixed.at[1], mixed_come.at[1])
     w_copy.wait()
-    rows = hidden_ref.shape[0] // 2
-    gain = gain_ref[...]
-    gain_grad = jnp.zeros((1, D), F32)
-    aways = []
-    for p in range(2):
-        at = slice(p * rows, (p + 1) * rows)
-        hidden = hidden_ref[at]
-        normed_grad = group.terms(p)
-        inverse = lax.rsqrt(jnp.mean(hidden * hidden, axis=-1, keepdims=True) + EPSILON)
-        gain_grad = gain_grad + jnp.sum(normed_grad * (hidden * inverse), axis=0, keepdims=True)
-        scaled = normed_grad * gain
-        back = inverse * scaled - hidden * (
-            inverse * inverse * inverse * jnp.mean(scaled * hidden, axis=-1, keepdims=True)
-        )
-        dy = jnp.where(valid_ref[at] > 0, cot_ref[at].astype(F32), 0.0)
-        total = dy + back
-        grad_ref[at] = total
-        low = total.astype(BF)
-        low_ref[at] = low
-        send_ref[at] = mm(low, w_ref[:, heads:]).astype(BF)
-        part = pl.ds(p * rows, rows)
-        aways.append(to_x(send_ref.at[part], come_ref.at[part], s_at.at[p], r_at.at[p]))
-        aways[p].start()
-    gain_grad_ref[...] = gain_grad
-    mixed_core[0].wait_recv()
-    outputs.mix(0, 1, mixed.at[0], mixed_come.at[0])
+    phase(outputs, 0, mixed, mixed_come, last_ahead, lambda s, k: None)
     own_ref[...] = mm(low_ref[...], w_ref[:, :heads]).astype(BF)
     group.sent()
-    for copy in mixed_core:
-        copy.wait_send()
+    for s in range(2):
+        mixed_core(s).wait_send()
     for away in aways:
         away.wait()
     final.wait()

time: 550 us -> 530 us (0.964)
  Pallas kernels: 519 us -> 500 us
    pallas_call x11, Pallas kernels: 514 us -> 495 us  [remote_call(): pl.pallas_call(kernel, name=name, out_shape=out_shape, in_specs=in_specs,...]
where the time goes in v6:
time: 530 us; the launch traced here: 521 us
  Pallas kernels  500 us (94%)
  other arithmetic  8.27 us (2%)
  local copies, waits for them, and re-layouts  5.86 us (1%)
    pallas_call x11, Pallas kernels, remote_call(): pl.pallas_call(kernel, name=name, out_shape=out_shape, in_specs=in_specs,...  495 us

profile of v6, /device:TPU:9, one launch (start us, length us, event | category | flops | bytes accessed | tf_op | source)
XLA Modules:
  0.0 521.1 jit_solution(17152602317425757155)
XLA Ops:
  0.6 0.0 copy-start.3
  0.6 0.0 copy-start.5
  1.4 0.7 convert_bitcast_fusion
  2.1 0.9 select_reduce_fusion
  2.9 0.6 select_convert_fusion.gates_ref
  3.6 1.5 fusion
  5.1 2.5 fusion.2.normed_ref.own_ref.refs_0_
  7.6 0.0 copy-done.3
  7.6 0.0 copy-done.5
  7.6 0.7 pad_maximum_fusion.shard_ref
  8.3 0.6 broadcast_in_dim_tile.3.freq_ref
  8.9 53.3 %collect.1 = (bf16[1024,2048]{1,0:T(8,128)(2,1)}, bf16[512,1024]{1,0:T(8,128)(2,1)}, f32[1024,128]{1,0:T(8,128)}, f32[1024,128]{1,0:T(8,128)}, s32[4,4,1024]{2,1...) custom-call(bf16[64,1536]{1,0:T(8,128)(2,1)} %pad_maximum_fusion.sha, ...), custom_call_target="tpu_custom_call" | custom-call | flops 4294967296 | bytes 8388608 | tf_op jit(solution)/shard_map/collect/pallas_call | solution.py:664
  62.2 62.6 %attention.1 = (bf16[1024,1024]{1,0:T(8,128)(2,1)}, f32[4,4,512]{2,1,0:T(4,128)}, bf16[512,512]{1,0:T(8,128)(2,1)}, bf16[512,512]{1,0:T(8,128)(2,1)}, f32[512,10...) custom-call(s32[1]{0:T(128)} %copy.23.len_ref, ...), custom_call_target="tpu_custom_call" | custom-call | flops 32212254720 | bytes 8388608 | tf_op jit(solution)/shard_map/attention/pallas_call | solution.py:664
  124.9 55.2 %spread.1 = (bf16[4,4,256,1024]{3,2,1,0:T(8,128)(2,1)}, bf16[3,4,256,1024]{3,2,1,0:T(8,128)(2,1)}, bf16[4,4,288,1024]{3,2,1,0:T(8,128)(2,1)}, bf16[4,96,1024]{2,...) custom-call(s32[4,4,1024]{2,1,0:T(4,128)} %get-tuple-element.121.pos, ...), custom_call_target="tpu_custom_call" | custom-call | flops 12884901888 | bytes 8388608 | tf_op jit(solution)/shard_map/spread/pallas_call | solution.py:664
  180.1 34.3 %hand_out.1 = (bf16[4,4,288,1024]{3,2,1,0:T(8,128)(2,1)}, bf16[4,96,1024]{2,1,0:T(8,128)(2,1)}, bf16[4,96,1024]{2,1,0:T(8,128)(2,1)}, bf16[4,96,1024]{2,1,0:T(8,128)(2,1)}, bf16[4,96,1024]{2,1,0:T(8,128)(2,1)}) custom-call(s32[4,4,1024]{2,1,0:T(4,128)} %get-tuple-element.121.pos_ref, bf16[256,1024]{1,0:T(8,128)(2,1)} %get-tuple-element.122.na_ref, ...), custom_call_target="tpu_custom_call" | custom-call | flops 12884901888 | bytes 8388608 | tf_op jit(solution)/shard_map/hand_out/pallas_call | solution.py:664
  214.3 21.1 %expert_step.4 = (bf16[4,288,1024]{2,1,0:T(8,128)(2,1)}, bf16[4,288,1024]{2,1,0:T(8,128)(2,1)}, bf16[4,4,96,1024]{3,2,1,0:T(8,128)(2,1)}, bf16[4,96,1024]{2,1,0:T(8,128)(2,1)}, bf16[4,96,1024]{2,1,0:T(8,128)(2,1)}) custom-call(bf16[4,4,288,1024]{3,2,1,0:T(8,128)(2,1)} %get-tuple-element.140.x_ref, bf16[4,4,288,1024]{3,2,1,0:T(8,128)(2,1)} %get-tuple-element.141.g_ref, ...), custom_call_target="tpu_custom_call" | custom-call | flops 10871635968 | bytes 8388608 | tf_op jit(solution)/shard_map/expert_step/pallas_call | solution.py:664
  235.4 19.9 %expert_step.5 = (bf16[4,288,1024]{2,1,0:T(8,128)(2,1)}, bf16[4,288,1024]{2,1,0:T(8,128)(2,1)}, bf16[4,4,96,1024]{3,2,1,0:T(8,128)(2,1)}, bf16[4,96,1024]{2,1,0:...) custom-call(bf16[4,4,288,1024]{3,2,1,0:T(8,128)(2,1)} %get-tuple-element.140, ...), custom_call_target="tpu_custom_call" | custom-call | flops 10871635968 | bytes 8388608 | tf_op jit(solution)/shard_map/expert_step/pallas_call | solution.py:664
  255.3 20.2 %expert_step.6 = (bf16[4,288,1024]{2,1,0:T(8,128)(2,1)}, bf16[4,288,1024]{2,1,0:T(8,128)(2,1)}, bf16[4,4,96,1024]{3,2,1,0:T(8,128)(2,1)}, bf16[4,96,1024]{2,1,0:...) custom-call(bf16[4,4,288,1024]{3,2,1,0:T(8,128)(2,1)} %get-tuple-element.140, ...), custom_call_target="tpu_custom_call" | custom-call | flops 10871635968 | bytes 8388608 | tf_op jit(solution)/shard_map/expert_step/pallas_call | solution.py:664
  275.6 34.1 %expert_step.7 = (bf16[4,288,1024]{2,1,0:T(8,128)(2,1)}, bf16[4,288,1024]{2,1,0:T(8,128)(2,1)}, bf16[4,4,96,1024]{3,2,1,0:T(8,128)(2,1)}, bf16[4,96,1024]{2,1,0:...) custom-call(bf16[4,4,288,1024]{3,2,1,0:T(8,128)(2,1)} %get-tuple-element.140, ...), custom_call_target="tpu_custom_call" | custom-call | flops 10871635968 | bytes 8388608 | tf_op jit(solution)/shard_map/expert_step/pallas_call | solution.py:664
  309.7 0.7 fusion.3.valid_ref
  310.5 0.0 copy-start.8
  310.5 80.8 %rows_back.1 = (f32[512,1024]{1,0:T(8,128)}, bf16[512,1024]{1,0:T(8,128)(2,1)}, f32[1,1024]{1,0:T(1,128)}, bf16[512,512]{1,0:T(8,128)(2,1)}, bf16[512,512]{1,0:T...) custom-call(s32[4,1024,4]{2,1,0:T(8,128)} %get-tuple-element.118.pos, ...), custom_call_target="tpu_custom_call" | custom-call | flops 32212254720 | bytes 8388608 | tf_op jit(solution)/shard_map/rows_back/pallas_call | solution.py:664
  391.3 0.0 copy-start.6
  391.3 0.0 copy-start.7
  391.3 0.0 copy-done.8
  391.3 3.1 convolution_convert_fusion.refs_5_
  394.4 0.0 copy-done.6
  394.4 0.0 copy-done.7
  394.4 1.7 convolution_convert_fusion.1.refs_4_
  396.1 41.6 %attention_back.1 = (bf16[512,1024]{1,0:T(8,128)(2,1)}, bf16[512,1024]{1,0:T(8,128)(2,1)}, bf16[512,1024]{1,0:T(8,128)(2,1)}, bf16[4,96,1024]{2,1,0:T(8,128)(2,1...) custom-call(s32[1]{0:T(128)} %copy.23.len_ref, ...), custom_call_target="tpu_custom_call" | custom-call | flops 32212254720 | bytes 8388608 | tf_op jit(solution)/shard_map/attention_back/pallas_call | solution.py:664
  437.7 72.2 %finish.1 = (f32[512,1024]{1,0:T(8,128)}, f32[8,1024]{1,0:T(8,128)}, f32[64,1024]{1,0:T(8,128)}, f32[64,512]{1,0:T(8,128)}, bf16[4,96,1024]{2,1,0:T(8,128)(2,1)}...) custom-call(f32[512,1024]{1,0:T(8,128)} %get-tuple-element.187.hgrad, ...), custom_call_target="tpu_custom_call" | custom-call | flops 32212254720 | bytes 8388608 | tf_op jit(solution)/shard_map/finish/pallas_call | solution.py:664
  509.9 0.0 copy-start.2
  509.9 0.0 copy-start.1
  510.0 0.6 pad_add_fusion.idx_ref
  510.6 0.0 copy-start
  510.6 4.9 settle_experts.1
  515.4 0.0 copy-done.2
  515.4 0.8 reshape.66
  516.3 1.4 fusion.4
  517.7 0.0 copy-done.1
  517.7 1.0 copy.24
  518.7 0.0 copy-done
  518.7 0.0 copy-start.4
  518.7 1.3 copy.25
  520.0 0.0 copy-done.4
  520.0 0.7 copy.26
  (5 shorter events, 0.0 us)
Async XLA Ops:
  0.6 7.0 %copy-start.3 = (bf16[64,4,256]{2,1,0:T(4,128)(2,1)S(1)}, bf16[64,4,256]{2,1,0:T(4,128)(2,1)}, u32[]{:S(2)}) copy-start(bf16[64,4,256]{2,1,0:T(4,128)(2,1)} %param.17) | copy-start | bytes 393220
  0.6 7.0 %copy-start.5 = (bf16[512,64]{0,1:T(8,128)(2,1)S(1)}, bf16[512,64]{0,1:T(8,128)(2,1)}, u32[]{:S(2)}) copy-start(bf16[512,64]{0,1:T(8,128)(2,1)} %param.18) | copy-start | bytes 196612
  310.5 80.8 %copy-start.8 = (bf16[512,512]{1,0:T(8,128)(2,1)S(1)}, bf16[512,512]{1,0:T(8,128)(2,1)}, u32[]{:S(2)}) copy-start(bf16[512,512]{1,0:T(8,128)(2,1)} %get-tuple-element.192) | copy-start | bytes 1572868
  391.3 3.1 copy-start.6
  391.3 3.1 copy-start.7
  509.9 5.5 %copy-start.2 = (f32[64,1024]{1,0:T(8,128)S(1)}, f32[64,1024]{1,0:T(8,128)}, u32[]{:S(2)}) copy-start(f32[64,1024]{1,0:T(8,128)} %get-tuple-element.202) | copy-start | bytes 786436
  509.9 7.8 %copy-start.1 = (bf16[512,1024]{1,0:T(8,128)(2,1)S(1)}, bf16[512,1024]{1,0:T(8,128)(2,1)}, u32[]{:S(2)}) copy-start(bf16[512,1024]{1,0:T(8,128)(2,1)} %get-tuple-element.220) | copy-start | bytes 3145732
  510.6 8.1 %copy-start = (f32[512,1024]{1,0:T(8,128)S(1)}, f32[512,1024]{1,0:T(8,128)}, u32[]{:S(2)}) copy-start(f32[512,1024]{1,0:T(8,128)} %get-tuple-element.221) | copy-start | bytes 6291460
  518.7 1.3 copy-start.4

commit v7 on v6

--- a/solution.py
+++ b/solution.py
@@ -929,19 +929,24 @@
     width = w_ref.shape[1] // 2
     heads = width // 2
     cot_ref, ready, packed_refs, refs = refs[0], refs[1], refs[2:4], refs[4:]
-    qkv_ref, lse_ref, attn_ref, come_ref, hidden_ref, na_ref, nb_ref = refs[:7]
+    qkv_out, lse_ref, attn_ref, come_ref, hidden_out, na_ref, nb_ref = refs[:7]
     refs = refs[7:]
     dy_outs, own_refs, refs = refs[:4], refs[4:6], refs[6:]
     to_left, refs = refs[:n_steps], refs[n_steps:]
     to_right, refs = refs[:n_steps], refs[n_steps:]
-    send_ref, s_hop, r_hop, s_later, r_later, s_dy, r_dy, s_at, r_at, s_a, r_a, l_own = refs
+    send_ref, s_hop, r_hop, s_later, r_later, s_dy, r_dy, s_at, r_at, s_a, r_a, l_own, qkv_ref, hidden_ref, o_sem = refs
+    qkv_copy = pltpu.make_async_copy(qkv_ref, qkv_out, o_sem.at[0])
+    hidden_copy = pltpu.make_async_copy(hidden_ref, hidden_out, o_sem.at[1])
     d, t, o, i = place()
     length = len_ref[0]
     rows = own_ref.shape[0]
     groups = width // (2 * LANES)
     greet(outer, (1, 2, 3), True)
     hops = Hops(outer, [(1, ready, ready, to_left[0], to_right[0])], s_hop, r_hop)
-    later = Hops(outer, [(1, own_refs[k], own_refs[k], to_left[1 + k], to_right[1 + k]) for k in range(2)], s_later, r_later)
+    later = [
+        Hops(outer, [(1, own_refs[k], own_refs[k], to_left[1 + k], to_right[1 + k])], s_later.at[k], r_later.at[k])
+        for k in range(2)
+    ]
     keeps = [pltpu.make_async_copy(packed_refs[k].at[0], own_refs[k].at[0], l_own.at[k]) for k in range(2)]
     weights = [
         to_dp(m, packed_refs[k].at[m], own_refs[k].at[m], s_a.at[3 * k + m - 1], r_a.at[3 * k + m - 1])
@@ -1015,15 +1020,19 @@
 
         exchange(g).start()
 
-        @pl.when(g == groups // 2)
-        def _():
-            for copy in (*weights, *keeps):
-                copy.wait()
-            later.start()
+        for k in range(2):
+
+            @pl.when(g == k)
+            def _(k=k):
+                for copy in (*weights[(GROUP - 1) * k : (GROUP - 1) * (k + 1)], keeps[k]):
+                    copy.wait()
+                later[k].start()
 
         return carry
 
     lax.fori_loop(0, groups, per_group, 0)
+
+    qkv_copy.start()
 
     def settle(g, carry):
         exchange(g).wait()
@@ -1039,10 +1048,14 @@
         inverse = lax.rsqrt(jnp.mean(hidden * hidden, axis=-1, keepdims=True) + EPSILON)
         hidden_ref[at] = hidden
         normed_ref[...] = (hidden * inverse * gain_ref[...]).astype(BF)
+    hidden_copy.start()
     for copy in dys:
         copy.wait()
     hops.wait()
-    later.wait()
+    for one in later:
+        one.wait()
+    qkv_copy.wait()
+    hidden_copy.wait()
 
 
 def attention(outer, q_block, length, own, other, weights_full, cosine, sine, x, gain, cotangent, ready, packed):
@@ -1066,20 +1079,23 @@
         + [piece] * 4
         + [hop] * (2 + 2 * n),
         [SMEM] + [VM] * 7 + [ANY] * 4,
-        [VM] * 7 + [ANY] * (6 + 2 * n),
+        [ANY] + [VM] * 3 + [ANY] + [VM] * 2 + [ANY] * (6 + 2 * n),
         (length, own, other, weights_full, cosine, sine, x, gain.reshape(1, D), cotangent, ready, *packed),
         [
             pltpu.VMEM((rows, groups * LANES), BF),
             pltpu.SemaphoreType.DMA((2,)),
             pltpu.SemaphoreType.DMA((2,)),
-            pltpu.SemaphoreType.DMA((4,)),
-            pltpu.SemaphoreType.DMA((4,)),
+            pltpu.SemaphoreType.DMA((2, 2)),
+            pltpu.SemaphoreType.DMA((2, 2)),
             pltpu.SemaphoreType.DMA((4,)),
             pltpu.SemaphoreType.DMA((4,)),
             pltpu.SemaphoreType.DMA((groups,)),
             pltpu.SemaphoreType.DMA((groups,)),
             pltpu.SemaphoreType.DMA((6,)),
             pltpu.SemaphoreType.DMA((6,)),
+            pltpu.SemaphoreType.DMA((2,)),
+            pltpu.VMEM((2 * rows, groups * 2 * LANES), BF),
+            pltpu.VMEM((rows, D), F32),
             pltpu.SemaphoreType.DMA((2,)),
         ],
         30 << 30,
@@ -1712,7 +1728,7 @@
     was_l, refs = refs[:n1], refs[n1:]
     was_r, refs = refs[:n1], refs[n1:]
     f_dw, f_left, f_right, refs = *refs[:3], refs[3:]
-    grad_ref, low_ref, gain_grad_ref, own_ref, come_ref, mixed, fin_ref = refs[:7]
+    grad_ref, low_ref, gain_grad_ref, own_ref, come_ref, mixed_out, fin_ref = refs[:7]
     refs = refs[7:]
     to_l, refs = refs[: n1 + n2], refs[n1 + n2 :]
     to_r, refs = refs[: n1 + n2], refs[n1 + n2 :]
@@ -1721,7 +1737,7 @@
     sums_a, refs = refs[:6], refs[6:]
     sums_b, refs = (*sums_a[:2], *refs[:4]), refs[4:]
     send_ref, s_at, r_at, w_ref, w_sem = refs[:5]
-    final_refs = refs[5:]
+    mixed, m_sem, final_refs = refs[5], refs[6], refs[7:]
     heads = w_ref.shape[1] // 2
     w_copy = pltpu.make_async_copy(w_any.at[:, pl.ds(2 * heads, 2 * heads)], w_ref, w_sem)
     w_copy.start()
@@ -1758,6 +1774,9 @@
     def mixed_core(s):
         return to_dp(1, far.at[s], mixed_come.at[s], s_core.at[2 + s], r_core.at[2 + s])
 
+    def mixed_leave(s):
+        return pltpu.make_async_copy(mixed.at[s], mixed_out.at[s], m_sem.at[s])
+
     outputs = Mixer(ys, pos_ref, gate_ref, held, l_sem)
     rows = hidden_ref.shape[0] // 2
     aways = [
@@ -1791,9 +1810,15 @@
         pl.when(s == 0)(group.b[0].start)
         outputs.load(2 + s, k)
 
+    def go_on():
+        group.second()
+        one.wait()
+        two.load()
+        two.send()
+
     def mixed_ahead(s, k):
         core(s).wait_send()
-        pl.when(k == 1)(group.second)
+        pl.when(k == 1)(go_on)
 
     def mixed_behind(s, k):
         mixed_core(s).start()
@@ -1831,11 +1856,8 @@
     phase(mixer, 2, far, None, lambda s, k: None, far_behind)
     phase(mixer, 0, near, come, lambda s, k: core(s).wait_recv(), near_behind)
     phase(outputs, 2, far, None, mixed_ahead, mixed_behind)
-    one.wait()
-    two.load()
-    two.send()
     w_copy.wait()
-    phase(outputs, 0, mixed, mixed_come, last_ahead, lambda s, k: None)
+    phase(outputs, 0, mixed, mixed_come, last_ahead, lambda s, k: mixed_leave(s).start())
     own_ref[...] = mm(low_ref[...], w_ref[:, :heads]).astype(BF)
     group.sent()
     for s in range(2):
@@ -1843,6 +1865,8 @@
     for away in aways:
         away.wait()
     final.wait()
+    for s in range(2):
+        mixed_leave(s).wait()
     two.wait()
 
 
@@ -1871,7 +1895,7 @@
         + hop[:1]
         + hop,
         [VM] * 6 + [ANY] * (4 + 2 * n_experts + len(dws) + 2 * len(first)),
-        [VM] * 6 + [ANY] * (1 + 2 * n),
+        [VM] * 5 + [ANY] * (2 + 2 * n),
         (pos, gate, valid, hidden, cotangent, gain.reshape(1, D), weights_full, *sources, *ys, *dws, *was_l, *was_r, *final),
         [
             pltpu.VMEM((2, n_experts * CAP, D), BF),
@@ -1890,6 +1914,8 @@
             pltpu.SemaphoreType.DMA((2,)),
             pltpu.VMEM((D, 2 * heads), BF),
             pltpu.SemaphoreType.DMA,
+            slots,
+            pltpu.SemaphoreType.DMA((2,)),
             *final_scratch(packed),
         ],
         30 << 30,
@@ -2093,7 +2119,7 @@
     ]
 
 
-def finish_kernel(outer, hgrad_ref, x_ref, gain_ref, w_any, *refs):
+def finish_kernel(outer, hgrad_any, x_any, gain_ref, w_any, *refs):
     (no_ref, nx_ref, po_ref, px_ref, oo_ref, ox_ref, sg_ref), refs = refs[:7], refs[7:]
     dws, refs = refs[:3], refs[3:]
     done, refs = refs[:2], refs[2:]
@@ -2105,12 +2131,18 @@
     final_refs, refs = [refs[5 * k : 5 * k + 5] for k in range(3)], refs[15:]
     part_ref, theirs_ref, p_send, p_recv, out_ref, come_ref, c_send, c_recv = refs[:8]
     q_refs, o_refs, refs = refs[8:14], refs[14:20], refs[20:]
-    g_buf, g_come, g_z, g_send, g_recv, w_ref, w_sem = refs
+    g_buf, g_come, g_z, g_send, g_recv, w_ref, w_sem, hgrad_ref, x_ref, late_sem = refs
     d, t, o, i = place()
     rows = hgrad_ref.shape[0]
     width = w_ref.shape[1]
     w_copy = pltpu.make_async_copy(w_any.at[:, pl.ds(0, width)], w_ref, w_sem)
     w_copy.start()
+    late = [
+        pltpu.make_async_copy(hgrad_any, hgrad_ref, late_sem.at[0]),
+        pltpu.make_async_copy(x_any, x_ref, late_sem.at[1]),
+    ]
+    for c in late:
+        c.start()
     greet_all(outer)
     sums = [
         Sums(outer, (3,), [dws[1 + k]], [was_l[k]], [was_r[k]], [to_l[k]], [to_r[k]], *sums_refs[k]) for k in range(2)
@@ -2123,6 +2155,11 @@
         one.load()
     for one in sums:
         one.send()
+    w_copy.wait()
+    part_ref[...] = mm_nt(px_ref[...], w_ref[...]).astype(BF)
+    exchange = to_x(part_ref, theirs_ref, p_send, p_recv)
+    exchange.start()
+    finals[0].send()
     whole, part = Spread(outer, *q_refs), Spread(outer, *o_refs)
     each, heads = outw_ref.shape
 
@@ -2136,11 +2173,6 @@
     lax.fori_loop(0, outer, out_block, 0)
     part.over_core()
 
-    w_copy.wait()
-    part_ref[...] = mm_nt(px_ref[...], w_ref[...]).astype(BF)
-    exchange = to_x(part_ref, theirs_ref, p_send, p_recv)
-    exchange.start()
-
     def weights_block(k, carry):
         lanes = pl.ds(pl.multiple_of(k * GROUP * each, GROUP * each), GROUP * each)
         total = (mm_tn(no_ref[:, lanes], po_ref[...]) + mm_tn(nx_ref[:, lanes], px_ref[...])).astype(BF)
@@ -2151,13 +2183,12 @@
     part.over_y()
     lax.fori_loop(0, outer, weights_block, 0)
     whole.over_core()
-    finals[0].send()
     whole.over_y()
     part.over_z()
-    sums[0].wait()
-    finals[1].send()
 
     exchange.wait()
+    for c in late:
+        c.wait()
     quarter = rows // 4
 
     def norm_rows(p, gain_grad):
@@ -2178,19 +2209,21 @@
     g_buf[0, 2:8, :] = jnp.zeros((6, D), F32)
     g_moves = [
         to_dp(1, g_buf.at[0], g_come.at[0], g_send.at[0], g_recv.at[0]),
-        to_dp(2, g_buf.at[1], g_come.at[1], g_send.at[1], g_recv.at[1]),
-        to_x(g_buf.at[2], g_come.at[2], g_send.at[2], g_recv.at[2]),
+        to_x(g_buf.at[1], g_come.at[1], g_send.at[1], g_recv.at[1]),
+        to_dp(2, g_buf.at[2], g_come.at[2], g_send.at[2], g_recv.at[2]),
     ]
     g_moves[0].start()
-    whole.over_z()
     g_moves[0].wait()
     g_buf[1] = g_buf[0] + g_come[0]
     g_moves[1].start()
-    sums[1].wait()
-    finals[2].send()
     g_moves[1].wait()
     g_buf[2] = g_buf[1] + g_come[1]
     g_moves[2].start()
+    sums[0].wait()
+    finals[1].send()
+    whole.over_z()
+    sums[1].wait()
+    finals[2].send()
     out = part.total()
     outw_ref[...] = out[:, :heads]
     out_ref[...] = out[:, heads:].astype(BF)
@@ -2232,7 +2265,7 @@
             jax.ShapeDtypeStruct((each, heads), F32),
         ]
         + [hop] * 7,
-        [VM] * 3 + [ANY] + [VM] * 7 + [ANY] * 9,
+        [ANY, ANY, VM, ANY] + [VM] * 7 + [ANY] * 9,
         [VM] * 4 + [ANY] * 7,
         (hgrad, x, gain.reshape(1, D), weights_full, *extra, *dws, *done, *was_l, *was_r),
         [
@@ -2255,6 +2288,9 @@
             pltpu.SemaphoreType.DMA((2 + outer,)),
             pltpu.VMEM((D, width), BF),
             pltpu.SemaphoreType.DMA,
+            pltpu.VMEM((rows, D), F32),
+            pltpu.VMEM((rows, D), BF),
+            pltpu.SemaphoreType.DMA((2,)),
         ],
         30 << 30,
     )

time: 530 us -> 523 us (0.987)
  Pallas kernels: 500 us -> 493 us
    pallas_call x11, Pallas kernels: 495 us -> 488 us  [remote_call(): pl.pallas_call(kernel, name=name, out_shape=out_shape, in_specs=in_specs,...]
where the time goes in v7:
time: 523 us; the launch traced here: 514 us
  Pallas kernels  493 us (94%)
  other arithmetic  8.27 us (2%)
  local copies, waits for them, and re-layouts  5.86 us (1%)
    pallas_call x11, Pallas kernels, remote_call(): pl.pallas_call(kernel, name=name, out_shape=out_shape, in_specs=in_specs,...  488 us

profile of v7, /device:TPU:9, one launch (start us, length us, event | category | flops | bytes accessed | tf_op | source)
XLA Modules:
  0.0 513.8 jit_solution(772651499945738870)
XLA Ops:
  0.6 0.0 copy-start.3
  0.6 0.0 copy-start.5
  1.4 0.7 convert_bitcast_fusion
  2.1 0.9 select_reduce_fusion
  2.9 0.6 select_convert_fusion.gates_ref
  3.6 1.5 fusion
  5.1 2.5 fusion.2.normed_ref.own_ref.refs_0_
  7.6 0.0 copy-done.3
  7.6 0.0 copy-done.5
  7.6 0.7 pad_maximum_fusion.shard_ref
  8.3 0.6 broadcast_in_dim_tile.3.freq_ref
  8.9 53.3 %collect.1 = (bf16[1024,2048]{1,0:T(8,128)(2,1)}, bf16[512,1024]{1,0:T(8,128)(2,1)}, f32[1024,128]{1,0:T(8,128)}, f32[1024,128]{1,0:T(8,128)}, s32[4,4,1024]{2,1...) custom-call(bf16[64,1536]{1,0:T(8,128)(2,1)} %pad_maximum_fusion.sha, ...), custom_call_target="tpu_custom_call" | custom-call | flops 4294967296 | bytes 8388608 | tf_op jit(solution)/shard_map/collect/pallas_call | solution.py:664
  62.2 59.1 %attention.1 = (bf16[1024,1024]{1,0:T(8,128)(2,1)}, f32[4,4,512]{2,1,0:T(4,128)}, bf16[512,512]{1,0:T(8,128)(2,1)}, bf16[512,512]{1,0:T(8,128)(2,1)}, f32[512,10...) custom-call(s32[1]{0:T(128)} %copy.23.len_ref, ...), custom_call_target="tpu_custom_call" | custom-call | flops 32212254720 | bytes 8388608 | tf_op jit(solution)/shard_map/attention/pallas_call | solution.py:664
  121.3 54.3 %spread.1 = (bf16[4,4,256,1024]{3,2,1,0:T(8,128)(2,1)}, bf16[3,4,256,1024]{3,2,1,0:T(8,128)(2,1)}, bf16[4,4,288,1024]{3,2,1,0:T(8,128)(2,1)}, bf16[4,96,1024]{2,...) custom-call(s32[4,4,1024]{2,1,0:T(4,128)} %get-tuple-element.121.pos, ...), custom_call_target="tpu_custom_call" | custom-call | flops 12884901888 | bytes 8388608 | tf_op jit(solution)/shard_map/spread/pallas_call | solution.py:664
  175.6 34.5 %hand_out.1 = (bf16[4,4,288,1024]{3,2,1,0:T(8,128)(2,1)}, bf16[4,96,1024]{2,1,0:T(8,128)(2,1)}, bf16[4,96,1024]{2,1,0:T(8,128)(2,1)}, bf16[4,96,1024]{2,1,0:T(8,128)(2,1)}, bf16[4,96,1024]{2,1,0:T(8,128)(2,1)}) custom-call(s32[4,4,1024]{2,1,0:T(4,128)} %get-tuple-element.121.pos_ref, bf16[256,1024]{1,0:T(8,128)(2,1)} %get-tuple-element.122.na_ref, ...), custom_call_target="tpu_custom_call" | custom-call | flops 12884901888 | bytes 8388608 | tf_op jit(solution)/shard_map/hand_out/pallas_call | solution.py:664
  210.1 21.1 %expert_step.4 = (bf16[4,288,1024]{2,1,0:T(8,128)(2,1)}, bf16[4,288,1024]{2,1,0:T(8,128)(2,1)}, bf16[4,4,96,1024]{3,2,1,0:T(8,128)(2,1)}, bf16[4,96,1024]{2,1,0:T(8,128)(2,1)}, bf16[4,96,1024]{2,1,0:T(8,128)(2,1)}) custom-call(bf16[4,4,288,1024]{3,2,1,0:T(8,128)(2,1)} %get-tuple-element.140.x_ref, bf16[4,4,288,1024]{3,2,1,0:T(8,128)(2,1)} %get-tuple-element.141.g_ref, ...), custom_call_target="tpu_custom_call" | custom-call | flops 10871635968 | bytes 8388608 | tf_op jit(solution)/shard_map/expert_step/pallas_call | solution.py:664
  231.2 19.7 %expert_step.5 = (bf16[4,288,1024]{2,1,0:T(8,128)(2,1)}, bf16[4,288,1024]{2,1,0:T(8,128)(2,1)}, bf16[4,4,96,1024]{3,2,1,0:T(8,128)(2,1)}, bf16[4,96,1024]{2,1,0:...) custom-call(bf16[4,4,288,1024]{3,2,1,0:T(8,128)(2,1)} %get-tuple-element.140, ...), custom_call_target="tpu_custom_call" | custom-call | flops 10871635968 | bytes 8388608 | tf_op jit(solution)/shard_map/expert_step/pallas_call | solution.py:664
  250.9 20.3 %expert_step.6 = (bf16[4,288,1024]{2,1,0:T(8,128)(2,1)}, bf16[4,288,1024]{2,1,0:T(8,128)(2,1)}, bf16[4,4,96,1024]{3,2,1,0:T(8,128)(2,1)}, bf16[4,96,1024]{2,1,0:...) custom-call(bf16[4,4,288,1024]{3,2,1,0:T(8,128)(2,1)} %get-tuple-element.140, ...), custom_call_target="tpu_custom_call" | custom-call | flops 10871635968 | bytes 8388608 | tf_op jit(solution)/shard_map/expert_step/pallas_call | solution.py:664
  271.2 34.2 %expert_step.7 = (bf16[4,288,1024]{2,1,0:T(8,128)(2,1)}, bf16[4,288,1024]{2,1,0:T(8,128)(2,1)}, bf16[4,4,96,1024]{3,2,1,0:T(8,128)(2,1)}, bf16[4,96,1024]{2,1,0:...) custom-call(bf16[4,4,288,1024]{3,2,1,0:T(8,128)(2,1)} %get-tuple-element.140, ...), custom_call_target="tpu_custom_call" | custom-call | flops 10871635968 | bytes 8388608 | tf_op jit(solution)/shard_map/expert_step/pallas_call | solution.py:664
  305.4 0.7 fusion.3.valid_ref
  306.2 0.0 copy-start.8
  306.2 79.8 %rows_back.1 = (f32[512,1024]{1,0:T(8,128)}, bf16[512,1024]{1,0:T(8,128)(2,1)}, f32[1,1024]{1,0:T(1,128)}, bf16[512,512]{1,0:T(8,128)(2,1)}, bf16[512,512]{1,0:T...) custom-call(s32[4,1024,4]{2,1,0:T(8,128)} %get-tuple-element.118.pos, ...), custom_call_target="tpu_custom_call" | custom-call | flops 32212254720 | bytes 8388608 | tf_op jit(solution)/shard_map/rows_back/pallas_call | solution.py:664
  386.0 0.0 copy-start.6
  386.0 0.0 copy-start.7
  386.0 0.0 copy-done.8
  386.0 3.1 convolution_convert_fusion.refs_5_
  389.0 0.0 copy-done.6
  389.1 0.0 copy-done.7
  389.1 1.7 convolution_convert_fusion.1.refs_4_
  390.8 40.5 %attention_back.1 = (bf16[512,1024]{1,0:T(8,128)(2,1)}, bf16[512,1024]{1,0:T(8,128)(2,1)}, bf16[512,1024]{1,0:T(8,128)(2,1)}, bf16[4,96,1024]{2,1,0:T(8,128)(2,1...) custom-call(s32[1]{0:T(128)} %copy.23.len_ref, ...), custom_call_target="tpu_custom_call" | custom-call | flops 32212254720 | bytes 8388608 | tf_op jit(solution)/shard_map/attention_back/pallas_call | solution.py:664
  431.3 71.3 %finish.1 = (f32[512,1024]{1,0:T(8,128)}, f32[8,1024]{1,0:T(8,128)}, f32[64,1024]{1,0:T(8,128)}, f32[64,512]{1,0:T(8,128)}, bf16[4,96,1024]{2,1,0:T(8,128)(2,1)}...) custom-call(f32[512,1024]{1,0:T(8,128)} %get-tuple-element.187.hgrad, ...), custom_call_target="tpu_custom_call" | custom-call | flops 32212254720 | bytes 8388608 | tf_op jit(solution)/shard_map/finish/pallas_call | solution.py:664
  502.6 0.0 copy-start.2
  502.6 0.0 copy-start.1
  502.7 0.6 pad_add_fusion.idx_ref
  503.3 0.0 copy-start
  503.3 4.9 settle_experts.1
  508.2 0.0 copy-done.2
  508.2 0.8 reshape.66
  509.0 1.4 fusion.4
  510.4 0.0 copy-done.1
  510.4 1.0 copy.24
  511.4 0.0 copy-done
  511.4 0.0 copy-start.4
  511.4 1.3 copy.25
  512.7 0.0 copy-done.4
  512.7 0.7 copy.26
  (5 shorter events, 0.0 us)
Async XLA Ops:
  0.6 7.0 %copy-start.3 = (bf16[64,4,256]{2,1,0:T(4,128)(2,1)S(1)}, bf16[64,4,256]{2,1,0:T(4,128)(2,1)}, u32[]{:S(2)}) copy-start(bf16[64,4,256]{2,1,0:T(4,128)(2,1)} %param.17) | copy-start | bytes 393220
  0.6 7.0 %copy-start.5 = (bf16[512,64]{0,1:T(8,128)(2,1)S(1)}, bf16[512,64]{0,1:T(8,128)(2,1)}, u32[]{:S(2)}) copy-start(bf16[512,64]{0,1:T(8,128)(2,1)} %param.18) | copy-start | bytes 196612
  306.2 79.8 %copy-start.8 = (bf16[512,512]{1,0:T(8,128)(2,1)S(1)}, bf16[512,512]{1,0:T(8,128)(2,1)}, u32[]{:S(2)}) copy-start(bf16[512,512]{1,0:T(8,128)(2,1)} %get-tuple-element.192) | copy-start | bytes 1572868
  386.0 3.1 copy-start.6
  386.0 3.1 copy-start.7
  502.6 5.5 %copy-start.2 = (f32[64,1024]{1,0:T(8,128)S(1)}, f32[64,1024]{1,0:T(8,128)}, u32[]{:S(2)}) copy-start(f32[64,1024]{1,0:T(8,128)} %get-tuple-element.202) | copy-start | bytes 786436
  502.6 7.8 %copy-start.1 = (bf16[512,1024]{1,0:T(8,128)(2,1)S(1)}, bf16[512,1024]{1,0:T(8,128)(2,1)}, u32[]{:S(2)}) copy-start(bf16[512,1024]{1,0:T(8,128)(2,1)} %get-tuple-element.220) | copy-start | bytes 3145732
  503.3 8.1 %copy-start = (f32[512,1024]{1,0:T(8,128)S(1)}, f32[512,1024]{1,0:T(8,128)}, u32[]{:S(2)}) copy-start(f32[512,1024]{1,0:T(8,128)} %get-tuple-element.221) | copy-start | bytes 6291460
  511.4 1.3 copy-start.4

commit v8 on v7

--- a/solution.py
+++ b/solution.py
@@ -1927,17 +1927,24 @@
     outer, q_block, steps, len_ref, qkv_ref, lse_ref, cos_ref, sin_ref, own_ref, other_ref, hidden_ref, valid_ref, *refs
 ):
     n = len(steps)
-    mixed, refs = refs[0], refs[1:]
+    mixed, low_any, part_anys, refs = refs[0], refs[1], refs[2:4], refs[4:]
     dws, refs = refs[:n], refs[n:]
     was_l, refs = refs[:n], refs[n:]
     was_r, refs = refs[:n], refs[n:]
-    outs, out_ref, refs = refs[:2], refs[2], refs[3:]
+    outs, out_ref, weight_refs, refs = refs[:2], refs[2], refs[3:5], refs[5:]
     to_l, refs = refs[:n], refs[n:]
     to_r, refs = refs[:n], refs[n:]
     do_ref, dq_ref, dk_ref, dv_ref = refs[:4]
     sums_refs, refs = refs[4:10], refs[10:]
-    middle, mine, l_sem, come_ab, last_ab, s_sem, r_sem = refs
+    middle, mine, l_sem, come_ab, last_ab, s_sem, r_sem, low_ref, part_refs, w_sem = refs
     _, t, _, _ = place()
+    heads_copies = [
+        pltpu.make_async_copy(low_any, low_ref, w_sem.at[0]),
+        pltpu.make_async_copy(part_anys[0], part_refs.at[0], w_sem.at[1]),
+        pltpu.make_async_copy(part_anys[1], part_refs.at[1], w_sem.at[2]),
+    ]
+    for c in heads_copies:
+        c.start()
     q = middle.shape[1]
     loads = [
         pltpu.make_async_copy(mixed.at[0, pl.ds(q, q)], middle.at[0], l_sem.at[0]),
@@ -2005,6 +2012,17 @@
         return carry
 
     lax.fori_loop(0, groups, per_group, 0)
+    for c in heads_copies:
+        c.wait()
+    block = 256
+
+    def out_weights(k, carry):
+        at = pl.ds(pl.multiple_of(k * block, block), block)
+        for p in range(2):
+            weight_refs[p][at, :] = mm_tn(low_ref[:, at], part_refs[p]).astype(BF)
+        return carry
+
+    lax.fori_loop(0, D // block, out_weights, 0)
     for p in range(2):
         at = slice(p * q, (p + 1) * q)
         out_ref[at] = jnp.where(valid_ref[at] > 0, hidden_ref[at] + group.terms(p), 0.0).astype(BF)
@@ -2013,7 +2031,7 @@
 
 
 def attention_back(
-    outer, q_block, length, qkv, lse, cosine, sine, grads, hidden, valid, mixed, steps, dws, was_l, was_r
+    outer, q_block, length, qkv, lse, cosine, sine, grads, hidden, valid, mixed, low, parts, steps, dws, was_l, was_r
 ):
     rows, width = qkv.shape
     n = len(steps)
@@ -2025,10 +2043,11 @@
         12,
         [jax.ShapeDtypeStruct((rows // 2, width), BF)] * 2
         + [jax.ShapeDtypeStruct((rows // 2, D), BF)]
+        + [jax.ShapeDtypeStruct((D, width // 2), BF)] * 2
         + [hop] * (2 * n),
-        [SMEM] + [VM] * 8 + [ANY] * (3 * n + 1),
-        [VM] * 3 + [ANY] * (2 * n),
-        (length, qkv, lse, cosine, sine, *grads, hidden, valid, mixed, *dws, *was_l, *was_r),
+        [SMEM] + [VM] * 8 + [ANY] * (3 * n + 4),
+        [VM] * 5 + [ANY] * (2 * n),
+        (length, qkv, lse, cosine, sine, *grads, hidden, valid, mixed, low, *parts, *dws, *was_l, *was_r),
         [
             pltpu.VMEM((rows, LANES), BF),
             pltpu.VMEM((rows, LANES), F32),
@@ -2039,10 +2058,13 @@
             pltpu.VMEM((2, rows // 4, D), BF),
             pltpu.SemaphoreType.DMA((4,)),
             *group_scratch(rows),
+            pltpu.VMEM((rows // 2, D), BF),
+            pltpu.VMEM((2, rows // 2, width // 2), BF),
+            pltpu.SemaphoreType.DMA((3,)),
         ],
         30 << 30,
     )
-    return out[:3], out[3 : 3 + n], out[3 + n :]
+    return out[:5], out[5 : 5 + n], out[5 + n :]
 
 
 def over_outer(outer, source, target, sent, came, base):
@@ -2496,7 +2518,7 @@
             [weight_grads[0], sums_l[0], sums_r[0]],
         )
         hidden_grad, branch_grad, second_gain_part, attn_grad_own, attn_grad_other, mixed = main
-        (projected_own, projected_other, output), three_l, three_r = attention_back(
+        (projected_own, projected_other, output, out_own, out_other), three_l, three_r = attention_back(
             outer,
             q_block,
             lengths,
@@ -2508,12 +2530,13 @@
             hidden,
             valid_column,
             mixed,
+            branch_grad,
+            attn_parts,
             (3, 2),
             [dw_b, dw_d],
             [sum_l[0], sum_l[3]],
             [sum_r[0], sum_r[3]],
         )
-        out_own, out_other = (mm_tn(branch_grad, part).astype(BF) for part in attn_parts)
         tokens_grad, gains, qkv_grad, attn_out_grad, *fins = finish(
             outer,
             hidden_grad,

time: 523 us -> 519 us (level)
  no operation moved by 1% of the time
where the time goes in v8:
time: 519 us; the launch traced here: 510 us
  Pallas kernels  494 us (95%)
  other arithmetic  8.27 us (2%)
  local copies, waits for them, and re-layouts  5.85 us (1%)
    pallas_call x11, Pallas kernels, remote_call(): pl.pallas_call(kernel, name=name, out_shape=out_shape, in_specs=in_specs,...  489 us

profile of v8, /device:TPU:9, one launch (start us, length us, event | category | flops | bytes accessed | tf_op | source)
XLA Modules:
  0.0 509.8 jit_solution(8286674156287255064)
XLA Ops:
  0.6 0.0 copy-start.3
  0.6 0.0 copy-start.5
  1.4 0.7 convert_bitcast_fusion
  2.1 0.9 select_reduce_fusion
  2.9 0.6 select_convert_fusion.gates_ref
  3.6 1.5 fusion
  5.1 2.5 fusion.2.normed_ref.own_ref.refs_0_
  7.6 0.0 copy-done.3
  7.6 0.0 copy-done.5
  7.6 0.7 pad_maximum_fusion.shard_ref
  8.3 0.6 broadcast_in_dim_tile.3.freq_ref
  8.9 53.3 %collect.1 = (bf16[1024,2048]{1,0:T(8,128)(2,1)}, bf16[512,1024]{1,0:T(8,128)(2,1)}, f32[1024,128]{1,0:T(8,128)}, f32[1024,128]{1,0:T(8,128)}, s32[4,4,1024]{2,1...) custom-call(bf16[64,1536]{1,0:T(8,128)(2,1)} %pad_maximum_fusion.sha, ...), custom_call_target="tpu_custom_call" | custom-call | flops 4294967296 | bytes 8388608 | tf_op jit(solution)/shard_map/collect/pallas_call | solution.py:664
  62.3 59.1 %attention.1 = (bf16[1024,1024]{1,0:T(8,128)(2,1)}, f32[4,4,512]{2,1,0:T(4,128)}, bf16[512,512]{1,0:T(8,128)(2,1)}, bf16[512,512]{1,0:T(8,128)(2,1)}, f32[512,10...) custom-call(s32[1]{0:T(128)} %copy.23.len_ref, ...), custom_call_target="tpu_custom_call" | custom-call | flops 32212254720 | bytes 8388608 | tf_op jit(solution)/shard_map/attention/pallas_call | solution.py:664
  121.3 54.3 %spread.1 = (bf16[4,4,256,1024]{3,2,1,0:T(8,128)(2,1)}, bf16[3,4,256,1024]{3,2,1,0:T(8,128)(2,1)}, bf16[4,4,288,1024]{3,2,1,0:T(8,128)(2,1)}, bf16[4,96,1024]{2,...) custom-call(s32[4,4,1024]{2,1,0:T(4,128)} %get-tuple-element.123.pos, ...), custom_call_target="tpu_custom_call" | custom-call | flops 12884901888 | bytes 8388608 | tf_op jit(solution)/shard_map/spread/pallas_call | solution.py:664
  175.7 34.5 %hand_out.1 = (bf16[4,4,288,1024]{3,2,1,0:T(8,128)(2,1)}, bf16[4,96,1024]{2,1,0:T(8,128)(2,1)}, bf16[4,96,1024]{2,1,0:T(8,128)(2,1)}, bf16[4,96,1024]{2,1,0:T(8,128)(2,1)}, bf16[4,96,1024]{2,1,0:T(8,128)(2,1)}) custom-call(s32[4,4,1024]{2,1,0:T(4,128)} %get-tuple-element.123.pos_ref, bf16[256,1024]{1,0:T(8,128)(2,1)} %get-tuple-element.124.na_ref, ...), custom_call_target="tpu_custom_call" | custom-call | flops 12884901888 | bytes 8388608 | tf_op jit(solution)/shard_map/hand_out/pallas_call | solution.py:664
  210.2 21.1 %expert_step.4 = (bf16[4,288,1024]{2,1,0:T(8,128)(2,1)}, bf16[4,288,1024]{2,1,0:T(8,128)(2,1)}, bf16[4,4,96,1024]{3,2,1,0:T(8,128)(2,1)}, bf16[4,96,1024]{2,1,0:T(8,128)(2,1)}, bf16[4,96,1024]{2,1,0:T(8,128)(2,1)}) custom-call(bf16[4,4,288,1024]{3,2,1,0:T(8,128)(2,1)} %get-tuple-element.142.x_ref, bf16[4,4,288,1024]{3,2,1,0:T(8,128)(2,1)} %get-tuple-element.143.g_ref, ...), custom_call_target="tpu_custom_call" | custom-call | flops 10871635968 | bytes 8388608 | tf_op jit(solution)/shard_map/expert_step/pallas_call | solution.py:664
  231.3 19.7 %expert_step.5 = (bf16[4,288,1024]{2,1,0:T(8,128)(2,1)}, bf16[4,288,1024]{2,1,0:T(8,128)(2,1)}, bf16[4,4,96,1024]{3,2,1,0:T(8,128)(2,1)}, bf16[4,96,1024]{2,1,0:...) custom-call(bf16[4,4,288,1024]{3,2,1,0:T(8,128)(2,1)} %get-tuple-element.142, ...), custom_call_target="tpu_custom_call" | custom-call | flops 10871635968 | bytes 8388608 | tf_op jit(solution)/shard_map/expert_step/pallas_call | solution.py:664
  250.9 20.3 %expert_step.6 = (bf16[4,288,1024]{2,1,0:T(8,128)(2,1)}, bf16[4,288,1024]{2,1,0:T(8,128)(2,1)}, bf16[4,4,96,1024]{3,2,1,0:T(8,128)(2,1)}, bf16[4,96,1024]{2,1,0:...) custom-call(bf16[4,4,288,1024]{3,2,1,0:T(8,128)(2,1)} %get-tuple-element.142, ...), custom_call_target="tpu_custom_call" | custom-call | flops 10871635968 | bytes 8388608 | tf_op jit(solution)/shard_map/expert_step/pallas_call | solution.py:664
  271.2 34.2 %expert_step.7 = (bf16[4,288,1024]{2,1,0:T(8,128)(2,1)}, bf16[4,288,1024]{2,1,0:T(8,128)(2,1)}, bf16[4,4,96,1024]{3,2,1,0:T(8,128)(2,1)}, bf16[4,96,1024]{2,1,0:...) custom-call(bf16[4,4,288,1024]{3,2,1,0:T(8,128)(2,1)} %get-tuple-element.142, ...), custom_call_target="tpu_custom_call" | custom-call | flops 10871635968 | bytes 8388608 | tf_op jit(solution)/shard_map/expert_step/pallas_call | solution.py:664
  305.4 0.7 fusion.3.valid_ref
  306.2 80.3 %rows_back.1 = (f32[512,1024]{1,0:T(8,128)}, bf16[512,1024]{1,0:T(8,128)(2,1)}, f32[1,1024]{1,0:T(1,128)}, bf16[512,512]{1,0:T(8,128)(2,1)}, bf16[512,512]{1,0:T...) custom-call(s32[4,1024,4]{2,1,0:T(8,128)} %get-tuple-element.120.pos, ...), custom_call_target="tpu_custom_call" | custom-call | flops 32212254720 | bytes 8388608 | tf_op jit(solution)/shard_map/rows_back/pallas_call | solution.py:664
  386.4 41.8 %attention_back.1 = (bf16[512,1024]{1,0:T(8,128)(2,1)}, bf16[512,1024]{1,0:T(8,128)(2,1)}, bf16[512,1024]{1,0:T(8,128)(2,1)}, bf16[1024,512]{1,0:T(8,128)(2,1)},...) custom-call(s32[1]{0:T(128)} %copy.23.len_ref, ...), custom_call_target="tpu_custom_call" | custom-call | flops 32212254720 | bytes 8388608 | tf_op jit(solution)/shard_map/attention_back/pallas_call | solution.py:664
  428.3 70.3 %finish.1 = (f32[512,1024]{1,0:T(8,128)}, f32[8,1024]{1,0:T(8,128)}, f32[64,1024]{1,0:T(8,128)}, f32[64,512]{1,0:T(8,128)}, bf16[4,96,1024]{2,1,0:T(8,128)(2,1)}...) custom-call(f32[512,1024]{1,0:T(8,128)} %get-tuple-element.192.hgrad, ...), custom_call_target="tpu_custom_call" | custom-call | flops 32212254720 | bytes 8388608 | tf_op jit(solution)/shard_map/finish/pallas_call | solution.py:664
  498.6 0.0 copy-start.2
  498.6 0.0 copy-start.1
  498.7 0.6 pad_add_fusion.idx_ref
  499.2 0.0 copy-start
  499.2 4.9 settle_experts.1
  504.1 0.0 copy-done.2
  504.1 0.8 reshape.66
  505.0 1.4 fusion.4
  506.4 0.0 copy-done.1
  506.4 1.0 copy.24
  507.4 0.0 copy-done
  507.4 0.0 copy-start.4
  507.4 1.3 copy.25
  508.7 0.0 copy-done.4
  508.7 0.7 copy.26
  (5 shorter events, 0.0 us)
Async XLA Ops:
  0.6 7.0 %copy-start.3 = (bf16[64,4,256]{2,1,0:T(4,128)(2,1)S(1)}, bf16[64,4,256]{2,1,0:T(4,128)(2,1)}, u32[]{:S(2)}) copy-start(bf16[64,4,256]{2,1,0:T(4,128)(2,1)} %param.17) | copy-start | bytes 393220
  0.6 7.0 %copy-start.5 = (bf16[512,64]{0,1:T(8,128)(2,1)S(1)}, bf16[512,64]{0,1:T(8,128)(2,1)}, u32[]{:S(2)}) copy-start(bf16[512,64]{0,1:T(8,128)(2,1)} %param.18) | copy-start | bytes 196612
  498.6 5.5 %copy-start.2 = (f32[64,1024]{1,0:T(8,128)S(1)}, f32[64,1024]{1,0:T(8,128)}, u32[]{:S(2)}) copy-start(f32[64,1024]{1,0:T(8,128)} %get-tuple-element.206) | copy-start | bytes 786436
  498.6 7.8 %copy-start.1 = (bf16[512,1024]{1,0:T(8,128)(2,1)S(1)}, bf16[512,1024]{1,0:T(8,128)(2,1)}, u32[]{:S(2)}) copy-start(bf16[512,1024]{1,0:T(8,128)(2,1)} %get-tuple-element.224) | copy-start | bytes 3145732
  499.2 8.1 %copy-start = (f32[512,1024]{1,0:T(8,128)S(1)}, f32[512,1024]{1,0:T(8,128)}, u32[]{:S(2)}) copy-start(f32[512,1024]{1,0:T(8,128)} %get-tuple-element.225) | copy-start | bytes 6291460
  507.4 1.3 copy-start.4
